TPU v7x, 128 devices: a whole 4x4x4 slice. The times are simulated.
128 devices in a mesh: seq: 16 (over y, z), store: 8 (over x, core).
Axes of the slice: x: 4, y: 4, z: 4, core: 2. Of those that a mesh axis runs over, the one named last changes fastest.
Arguments:
- hidden: bfloat16 [16384, 4096], P('seq'), may hold values from -6 to 6
- nbr_table: bfloat16 [64, 128, 896], P('store'), may hold values from -6 to 6
- nbr_ids: int32 [256, 2], P('seq'), may hold values from 0 to 63, as said below
- w_query: bfloat16 [4096, 4096], P(None, 'store'), may hold values from -0.09375 to 0.09375
- w_key: bfloat16 [896, 4096], P(None, 'store'), may hold values from -0.1875 to 0.1875
- w_value: bfloat16 [896, 4096], P(None, 'store'), may hold values from -0.1875 to 0.1875
- w_out: bfloat16 [4096, 4096], P('store'), may hold values from -0.125 to 0.125
- enc_query: bfloat16 [896, 896], replicated, may hold values from -0.1875 to 0.1875
- enc_key: bfloat16 [4096, 896], P('seq'), may hold values from -0.09375 to 0.09375
- enc_value: bfloat16 [4096, 896], P('seq'), may hold values from -0.09375 to 0.09375
- enc_out: bfloat16 [896, 896], replicated, may hold values from -0.1875 to 0.1875
Outputs:
- cross_out: bfloat16 [16384, 4096], P('seq', 'store')
Inputs may be any that keep to these rules, and one draw needn't show every extreme that they name: `nbr_ids`: among the spans of one index of seq (16 consecutive spans), the ids fall in each owner's range k * 8 to k * 8 + 7 exactly 4 times.
All inputs are finite; a program needn't handle non-finite values.
Results may differ from a plain program's by a relative error of at most 0.03.
Values may be sent and summed in bfloat16 or wider, within the bound.
No kernel may reach another device: no remote copies, remote signals or barrier semaphores. Data moves between devices by JAX's collectives and lax.ppermute only.
A program may use at most 128 MiB of HBM per device.

v0:
```python
import math

import jax
import jax.numpy as jnp
from jax import lax
from jax.sharding import PartitionSpec as P

D = 4096
HD = 128
E = 896
EHEADS = 14
EHD = 64
CH = 64
NLEN = 128
KNB = 2


EPSILON = 1e-06


def shifted(block, axis, distance):
    devices = range(lax.axis_size(axis))
    route = [(i - distance, i) for i in devices if i - distance in devices]
    return lax.ppermute(block, axis, route)


def encoder_block(sources, cond_keys, cond_values, enc_query, enc_out):
    count = sources.shape[0]
    source_f = sources.astype(jnp.float32)
    normed = (
        source_f * lax.rsqrt(jnp.mean(source_f * source_f, axis=-1, keepdims=True) + EPSILON)
    ).astype(jnp.bfloat16)
    queries = jnp.dot(
        normed.reshape(count * NLEN, E), enc_query, preferred_element_type=jnp.float32
    ).astype(jnp.bfloat16)
    queries = queries.reshape(count, NLEN, EHEADS, EHD)
    key_heads = cond_keys.reshape(count, CH, EHEADS, EHD)
    value_heads = cond_values.reshape(count, CH, EHEADS, EHD)
    scores = jnp.einsum(
        "nqhd,nkhd->nhqk", queries, key_heads, preferred_element_type=jnp.float32
    ) / math.sqrt(EHD)
    weights = jax.nn.softmax(scores, axis=-1).astype(jnp.bfloat16)
    mixed_heads = jnp.einsum(
        "nhqk,nkhd->nqhd", weights, value_heads, preferred_element_type=jnp.float32
    ).astype(jnp.bfloat16)
    branch = jnp.dot(
        mixed_heads.reshape(count * NLEN, E), enc_out, preferred_element_type=jnp.float32
    )
    return (source_f + branch.reshape(count, NLEN, E)).astype(jnp.bfloat16)


def body(
    hidden,
    nbr_table,
    nbr_ids,
    w_query,
    w_key,
    w_value,
    w_out,
    enc_query,
    enc_key,
    enc_value,
    enc_out,
):
    store_count = lax.axis_size("store")
    store_rank = lax.axis_index("store")
    span_count = nbr_ids.shape[0]
    row_requests = span_count * KNB
    per_owner = row_requests // store_count
    blocks_here = nbr_table.shape[0]
    token_count = hidden.shape[0]
    flat_ids = nbr_ids.reshape(-1)
    owners = flat_ids // blocks_here
    slot_index = jnp.arange(row_requests, dtype=jnp.int32)
    by_owner = jnp.sort(owners * row_requests + slot_index) % row_requests
    picked = lax.dynamic_slice_in_dim(by_owner, store_rank * per_owner, per_owner)
    sources = nbr_table[flat_ids[picked] % blocks_here]
    span_of = picked // KNB
    by_span = hidden.reshape(span_count, CH, D)
    condition = by_span[span_of].reshape(per_owner * CH, D)
    shard_rows = (
        lax.all_gather(enc_key, "seq", axis=0, tiled=True),
        lax.all_gather(enc_value, "seq", axis=0, tiled=True),
    )
    key_sum = jnp.dot(condition, shard_rows[0], preferred_element_type=jnp.float32)
    value_sum = jnp.dot(condition, shard_rows[1], preferred_element_type=jnp.float32)
    cond_keys = key_sum.astype(jnp.bfloat16).reshape(per_owner, CH, E)
    cond_values = value_sum.astype(jnp.bfloat16).reshape(per_owner, CH, E)
    encoded = encoder_block(sources, cond_keys, cond_values, enc_query, enc_out)
    head_width = w_query.shape[1]
    shard_rows = lax.all_gather(encoded, "store", axis=0, tiled=True)
    flat_rows = shard_rows.reshape(-1, E)
    keys_part = jnp.dot(flat_rows, w_key, preferred_element_type=jnp.float32).astype(jnp.bfloat16)
    values_part = jnp.dot(flat_rows, w_value, preferred_element_type=jnp.float32).astype(
        jnp.bfloat16
    )
    joined = jnp.concatenate([keys_part, values_part], axis=1)
    owner_order = joined.reshape(shard_rows.shape[0], NLEN, 2 * head_width)
    key_value = owner_order[jnp.argsort(by_owner)].reshape(span_count, KNB * NLEN, 2 * head_width)
    carried = shifted(key_value[span_count - 1], "seq", 1)
    previous = jnp.concatenate([carried[None], key_value[: span_count - 1]], axis=0)
    local_heads = head_width // HD
    queries = jnp.dot(hidden, w_query, preferred_element_type=jnp.float32).astype(jnp.bfloat16)
    queries = queries.reshape(span_count, CH, local_heads, HD)
    key_heads = previous[:, :, :head_width].reshape(span_count, KNB * NLEN, local_heads, HD)
    value_heads = previous[:, :, head_width:].reshape(span_count, KNB * NLEN, local_heads, HD)
    scores = jnp.einsum(
        "cqhd,ckhd->chqk", queries, key_heads, preferred_element_type=jnp.float32
    ) / math.sqrt(HD)
    weights = jax.nn.softmax(scores, axis=-1).astype(jnp.bfloat16)
    attended = jnp.einsum(
        "chqk,ckhd->cqhd", weights, value_heads, preferred_element_type=jnp.float32
    )
    attended = attended.astype(jnp.bfloat16).reshape(token_count, head_width)
    head_terms = jnp.dot(attended, w_out, preferred_element_type=jnp.float32)
    return lax.psum_scatter(
        head_terms.astype(jnp.bfloat16), "store", scatter_dimension=1, tiled=True
    )


def solution(mesh):
    in_specs = (
        P("seq", None),
        P("store", None, None),
        P("seq", None),
        P(None, "store"),
        P(None, "store"),
        P(None, "store"),
        P("store", None),
        P(),
        P("seq", None),
        P("seq", None),
        P(),
    )
    out_specs = P("seq", "store")
    return jax.shard_map(body, mesh=mesh, in_specs=in_specs, out_specs=out_specs, check_vma=False)
```

profile of v0, /device:TPU:9, one launch (start us, length us, event | category | flops | bytes accessed | tf_op | source)
XLA Modules:
  0.0 371.8 jit_solution(12636594940149134104)
XLA Ops:
  6.5 0.7 all-gather.6.cloned.1.call-update
  7.3 0.7 all-gather.4.cloned.1.call-update
  8.0 0.0 all-gather.8.cloned.1.call-start
  8.1 0.8 copy.34
  8.8 0.1 reshape.108
  8.9 1.6 sort.32
  10.5 0.1 compare_select_fusion.10
  10.6 0.6 gather_fusion
  11.3 0.7 gather_fusion.1
  12.0 0.3 multiply_reduce_fusion.1
  12.3 0.2 fusion.10
  12.5 2.6 convolution_convert_fusion.4
  15.1 2.4 reshape.156
  17.6 5.4 %gather_fusion.2 = bf16[4,64,4096]{2,1,0:T(8,128)(2,1)} fusion(bf16[16,64,4096]{2,1,0:T(8,128)(2,1)} %bitcast.59, s32[1024]{0:T(1024)S(1)} %get-tuple-element.14), kind=kCustom, calls=%fused_computation.2 | custom fusion | bytes 4194320 | tf_op jit(solution)/shard_map/gather | solution.py:80
  23.0 55.1 %all-gather.6.cloned.1.call-done = bf16[4096,896]{1,0:T(8,128)(2,1)} async-done(((bf16[256,896]{1,0:T(8,128)(2,1)}), bf16[4096,896]{1,0:T(8,128)(2,1)}) %all-gather.6.cloned.1.call-update) | async-done | bytes 7340048 | tf_op jit(solution)/shard_map/all_gather | solution.py:82
  78.1 6.1 %convolution_convert_fusion.6 = bf16[256,896]{1,0:T(8,128)(2,1)S(1)} fusion(bf16[256,4096]{1,0:T(8,128)(2,1)} %bitcast.54, bf16[4096,896]{1,0:T(8,128)(2,1)} %all-gather.6.cloned.1.call-done), kind=kOutput, calls=%fused_computation.37 | convolution fusion | flops 1879277568 | bytes 9895936 | tf_op jit(solution)/shard_map/dot_general | solution.py:85
  84.2 0.7 reshape.157
  84.9 2.9 fusion.8
  87.8 1.3 copy-done.3
  89.1 0.5 fusion.45
  89.6 56.6 %all-gather.4.cloned.1.call-done = bf16[4096,896]{1,0:T(8,128)(2,1)} async-done(((bf16[256,896]{1,0:T(8,128)(2,1)}), bf16[4096,896]{1,0:T(8,128)(2,1)}) %all-gather.4.cloned.1.call-update) | async-done | bytes 7340048 | tf_op jit(solution)/shard_map/all_gather | solution.py:83
  146.2 6.1 %convolution_convert_fusion.7 = bf16[256,896]{1,0:T(8,128)(2,1)S(1)} fusion(bf16[256,4096]{1,0:T(8,128)(2,1)} %bitcast.55, bf16[4096,896]{1,0:T(8,128)(2,1)} %all-gather.4.cloned.1.call-done), kind=kOutput, calls=%fused_computation.38 | convolution fusion | flops 1879277568 | bytes 9895936 | tf_op jit(solution)/shard_map/dot_general | solution.py:86
  152.3 1.7 reshape.155
  153.9 3.7 convolution_convert_fusion.5
  157.6 3.4 add_convert_fusion
  161.0 0.2 reduce-scatter.2.cloned.1.call-start
  161.3 1.7 sort.33
  163.0 43.5 %all-gather.8.cloned.1.call-done = bf16[32,128,896]{2,1,0:T(8,128)(2,1)} async-done(((bf16[4,128,896]{2,1,0:T(8,128)(2,1)}), bf16[32,128,896]{2,1,0:T(8,128)(2,1)}) %all-gather.8.cloned.1.call-update) | async-done | bytes 7340048 | tf_op jit(solution)/shard_map/all_gather | solution.py:91
  206.5 9.9 %convolution_convert_fusion.1 = bf16[4096,512]{0,1:T(8,128)(2,1)} fusion(bf16[4096,896]{1,0:T(8,128)(2,1)} %bitcast.60, bf16[896,512]{1,0:T(8,128)(2,1)} %param.16), kind=kOutput, calls=%fused_computation.10 | convolution fusion | flops 3760193536 | bytes 12451840 | tf_op jit(solution)/shard_map/dot_general | solution.py:94
  216.4 6.3 %convolution_convert_fusion.2 = bf16[4096,512]{0,1:T(8,128)(2,1)} fusion(bf16[4096,896]{1,0:T(8,128)(2,1)S(1)} %bitcast.61, bf16[896,512]{1,0:T(8,128)(2,1)S(1)} %copy-done.6), kind=kOutput, calls=%fused_computation.11 | convolution fusion | flops 3760193536 | bytes 12451840 | tf_op jit(solution)/shard_map/dot_general | solution.py:93
  222.7 7.8 %pad_maximum_fusion = bf16[4096,1024]{0,1:T(8,128)(2,1)} fusion(bf16[4096,512]{0,1:T(8,128)(2,1)} %convolution_convert_fusion.1, bf16[4096,512]{0,1:T(8,128)(2,1)} %convolution_convert_fusion.2), kind=kLoop, calls=%fused_computation.6 | loop fusion | flops 16777216 | bytes 16777216 | tf_op jit(solution)/shard_map/concatenate | solution.py:97
  230.5 11.9 %copy.58 = bf16[4096,1024]{1,0:T(8,128)(2,1)} copy(bf16[4096,1024]{0,1:T(8,128)(2,1)} %pad_maximum_fusion) | data formatting | bytes 16777216 | tf_op jit(solution)/shard_map/reshape | solution.py:98
  242.4 8.4 %gather_fusion.3 = bf16[32,128,1024]{2,1,0:T(8,128)(2,1)} fusion(bf16[32,128,1024]{2,1,0:T(8,128)(2,1)} %bitcast.51, s32[1024]{0:T(1024)S(1)} %pad_clamp_fusion), kind=kCustom, calls=%fused_computation.3 | custom fusion | bytes 16777344 | tf_op jit(solution)/shard_map/gather | solution.py:99
  250.8 1.9 slice.29
  252.7 3.2 collective-permute-start
  255.9 9.1 %convolution_convert_fusion.3 = bf16[1024,512]{1,0:T(8,128)(2,1)S(1)} fusion(bf16[1024,4096]{1,0:T(8,128)(2,1)} %param.11, bf16[4096,512]{1,0:T(8,128)(2,1)} %param.14), kind=kOutput, calls=%fused_computation.33 | convolution fusion | flops 4295491584 | bytes 13631488 | tf_op jit(solution)/shard_map/dot_general | solution.py:103
  264.9 0.5 reshape.115
  265.4 4.7 %collective-permute-done = bf16[256,1024]{1,0:T(8,128)(2,1)S(1)} collective-permute-done((bf16[256,1024]{1,0:T(8,128)(2,1)}, bf16[256,1024]{1,0:T(8,128)(2,1)S(1)}, u32[]{:S(2)}, u32[]{:S(2)}) %collective-permute-start) | collective-permute-done | bytes 524320 | tf_op jit(solution)/shard_map/ppermute | solution.py:24
  270.2 3.7 %pad_maximum_fusion.1 = (bf16[16,256,512]{2,1,0:T(8,128)(2,1)}, bf16[16,256,512]{2,1,0:T(8,128)(2,1)}) fusion(bf16[15,256,1024]{2,1,0:T(8,128)(2,1)S(1)} %bitcast.50, bf16[1,256,1024]{2,1,0:T(8,128)(2,1)S(1)} %bitcast.58), kind=kLoop, calls=%fused_computation.13 | loop fusion | flops 16777216 | bytes 16777216 | tf_op jit(solution)/shard_map/concatenate | solution.py:101
  273.9 6.4 %copy.44 = bf16[16,256,512]{1,2,0:T(8,128)(2,1)} copy(bf16[16,256,512]{2,1,0:T(8,128)(2,1)} %get-tuple-element.10) | data formatting | bytes 8388608 | tf_op jit(solution)/shard_map/slice | solution.py:105
  280.2 2.9 fusion.20
  283.1 2.0 copy-done.2
  285.1 1.6 fusion.46
  286.7 6.4 %copy.43 = bf16[16,256,512]{1,2,0:T(8,128)(2,1)} copy(bf16[16,256,512]{2,1,0:T(8,128)(2,1)} %get-tuple-element.11) | data formatting | bytes 8388608 | tf_op jit(solution)/shard_map/slice | solution.py:106
  293.1 11.9 %fusion.17 = bf16[16,64,4,128]{3,1,2,0:T(8,128)(2,1)S(1)} fusion(bf16[16,256,4,128]{1,3,2,0:T(8,128)(2,1)} %bitcast.53, f32[16,4,64]{2,1,0:T(4,128)S(1)} %fusion.46, f32[16,4,64,256]{3,2,1,0:T(8,128)} %copy-done.2), kind=kOutput, calls=%fused_computation.36 | convolution fusion | flops 274206976 | bytes 9453568 | tf_op jit(solution)/shard_map/chqk,ckhd->cqhd/dot_general | solution.py:111
  305.0 0.9 copy.48
  305.9 8.9 %convolution_convert_fusion = bf16[1024,4096]{1,0:T(8,128)(2,1)} fusion(bf16[512,4096]{1,0:T(8,128)(2,1)} %param.17, bf16[128,8,4,128]{3,2,1,0:T(4,128)(2,1)S(1)} %bitcast.56), kind=kOutput, calls=%fused_computation.9 | convolution fusion | flops 4299161600 | bytes 13631488 | tf_op jit(solution)/shard_map/dot_general | solution.py:115
  314.9 50.4 %reduce-scatter.2.cloned.1.call-done = bf16[1024,512]{1,0:T(8,128)(2,1)} async-done(((bf16[1024,4096]{1,0:T(8,128)(2,1)}), bf16[1024,512]{1,0:T(8,128)(2,1)}) %reduce-scatter.2.cloned.1.call-update) | async-done | bytes 1048592 | tf_op jit(solution)/shard_map/reduce_scatter | solution.py:116
  (28 shorter events, 0.2 us)
Async XLA Ops:
  6.5 4.8 %copy-start = (bf16[8,128,896]{2,1,0:T(8,128)(2,1)S(1)}, bf16[8,128,896]{2,1,0:T(8,128)(2,1)}, u32[]{:S(2)}) copy-start(bf16[8,128,896]{2,1,0:T(8,128)(2,1)} %param.12) | copy-start | bytes 5505028
  6.5 71.6 %all-gather.6.cloned.1.call-start = ((), (), s32[]{:S(2)}) async-start(), calls=%async_computation.2 | async-start | bytes 7798784 | tf_op jit(solution)/shard_map/all_gather | solution.py:82
  7.3 138.9 %all-gather.4.cloned.1.call-start = ((), (), s32[]{:S(2)}) async-start(), calls=%async_computation.1 | async-start | bytes 7798784 | tf_op jit(solution)/shard_map/all_gather | solution.py:83
  8.0 198.5 %all-gather.8.cloned.1.call-start = ((), (), s32[]{:S(2)}) async-start(), calls=%async_computation.3 | async-start | bytes 8257536 | tf_op jit(solution)/shard_map/all_gather | solution.py:91
  87.8 1.3 copy-start.3
  153.9 3.7 copy-start.4
  161.0 204.3 %reduce-scatter.2.cloned.1.call-start = ((), (), s32[]{:S(2)}) async-start(), calls=%async_computation.4 | async-start | bytes 9437184 | tf_op jit(solution)/shard_map/reduce_scatter | solution.py:116
  206.5 9.9 %copy-start.5 = (bf16[32,128,896]{2,1,0:T(8,128)(2,1)S(1)}, bf16[32,128,896]{2,1,0:T(8,128)(2,1)}, u32[]{:S(2)}) copy-start(bf16[32,128,896]{2,1,0:T(8,128)(2,1)} %all-gather.8.cloned.1.call-done) | copy-start | bytes 22020100
  206.5 9.9 %copy-start.6 = (bf16[896,512]{1,0:T(8,128)(2,1)S(1)}, bf16[896,512]{1,0:T(8,128)(2,1)}, u32[]{:S(2)}) copy-start(bf16[896,512]{1,0:T(8,128)(2,1)} %param.15) | copy-start | bytes 2752516
  252.7 17.5 %collective-permute-start = (bf16[256,1024]{1,0:T(8,128)(2,1)}, bf16[256,1024]{1,0:T(8,128)(2,1)S(1)}, u32[]{:S(2)}, u32[]{:S(2)}) collective-permute-start(bf16[256,1024]{1,0:T(8,128)(2,1)} %bitcast.11), channel_id=1, source_target_pairs={{0,8},{8,16},{16,24},{24,32},{32,40},{40,48},{48,56},{56,64},{64,7... | collective-permute-start | bytes 1572872 | tf_op jit(solution)/shard_map/ppermute | solution.py:24
  265.4 4.7 %slice-start = ((bf16[32,128,1024]{2,1,0:T(8,128)(2,1)}), bf16[30,128,1024]{2,1,0:T(8,128)(2,1)S(1)}, s32[]{:S(2)}) async-start(bf16[32,128,1024]{2,1,0:T(8,128)(2,1)} %gather_fusion.3), calls=%async_computation.5 | async-start | bytes 15728640 | tf_op jit(solution)/shard_map/slice | solution.py:101
  283.1 2.0 copy-start.2
  314.8 50.5 %copy-start.1 = (bf16[8,128,896]{2,1,0:T(8,128)(2,1)S(1)}, bf16[8,128,896]{2,1,0:T(8,128)(2,1)}, u32[]{:S(2)}) copy-start(bf16[8,128,896]{2,1,0:T(8,128)(2,1)} %param.12) | copy-start | bytes 5505028
Sparse Core Ops, SparseCore 0:
  9.5 68.5 all-gather.5
  80.3 65.8 all-gather.3
  161.1 45.3 all-gather.7
  315.0 50.2 reduce-scatter.1
where the time goes:
time: 374 us; the launch traced here: 372 us
  waiting for transfers between devices  212 us (57%)
  matrix products  73.7 us (20%)
  local copies, waits for them, and re-layouts  52.1 us (14%)
  other arithmetic  17.5 us (5%)
  between operations  13.3 us (4%)
    all_gather x1, waiting for transfers between devices, body(): lax.all_gather(enc_value, 'seq', axis=0, tiled=True)  56.6 us
    all_gather x1, waiting for transfers between devices, body(): lax.all_gather(enc_key, 'seq', axis=0, tiled=True)  55.1 us
    reduce_scatter x1, waiting for transfers between devices, body(): lax.psum_scatter(head_terms.astype(jnp.bfloat16), 'store', scatter_dimens...  50.4 us
    all_gather x1, waiting for transfers between devices, body(): shard_rows = lax.all_gather(encoded, 'store', axis=0, tiled=True)  43.5 us
    dot_general x1, matrix products, body(): jnp.einsum('chqk,ckhd->cqhd', weights, value_heads, preferred_element_typ...  11.9 us
    reshape x1, local copies, waits for them, and re-layouts, body(): owner_order = joined.reshape(shard_rows.shape[0], NLEN, 2 * head_width)  11.9 us
    dot_general x1, matrix products, body(): jnp.dot(flat_rows, w_value, preferred_element_type=jnp.float32)  9.94 us
    dot_general x1, matrix products, body(): jnp.dot(hidden, w_query, preferred_element_type=jnp.float32)  9.05 us
  transfers between devices with their start and end apart: 5, of which 5 were waited for; matrix products, arithmetic and copies ran while one was open for 10% of the time, Pallas kernels for 0%

commit v1 on v0

v1 whole, which is shorter than its diff:
```python
import math

import jax
import jax.numpy as jnp
from jax import lax
from jax.experimental import pallas as pl
from jax.experimental.pallas import tpu as pltpu
from jax.sharding import PartitionSpec as P

D = 4096
HD = 128
E = 896
EHEADS = 14
EHD = 64
CH = 64
NLEN = 128
KNB = 2
PAIRS = E // 128

EPSILON = 1e-06
F32 = jnp.float32
BF16 = jnp.bfloat16
REL = (0, -1, 1, 2)


def dot(a, b):
    return jnp.dot(a, b, preferred_element_type=F32)


def grid_route(side, dy, dz):
    return [
        (side * y + z, side * ((y + dy) % side) + (z + dz) % side)
        for y in range(side)
        for z in range(side)
    ]


def around(block, side, along_y):
    got = [block]
    for rel in REL[1:]:
        route = grid_route(side, -rel, 0) if along_y else grid_route(side, 0, -rel)
        got.append(lax.ppermute(block, "seq", route))
    return got


def cond_kernel(src_ref, span_ref, hidden_ref, *refs):
    a_refs, b_refs = refs[:4], refs[4:8]
    out_ref, held = refs[8], refs[9]
    step = pl.program_id(0)
    rows = hidden_ref.shape[0]
    total = None
    for i in range(4):
        for j in range(4):
            at = pl.multiple_of(src_ref[4 * i + j] * 256, 256)
            weight = jnp.concatenate([a_refs[i][j], b_refs[j][i]], axis=0)
            term = dot(hidden_ref[:, pl.ds(at, 256)], weight)
            total = term if total is None else total + term
    held[pl.ds(pl.multiple_of(step * rows, rows), rows), :] = total.astype(BF16)

    @pl.when(step == pl.num_programs(0) - 1)
    def _():
        for r in range(out_ref.shape[0]):
            at = pl.multiple_of(span_ref[r] * CH, CH)
            out_ref[r] = held[pl.ds(at, CH), :]


def cond_rows(hidden, a_parts, b_parts, sources, spans):
    tokens = hidden.shape[0]
    tile = 256
    requests = spans.shape[0]
    part = pl.BlockSpec((4, 128, 256), lambda i, s, p: (0, 0, 0), pipeline_mode=pl.Buffered(1))
    return pl.pallas_call(
        cond_kernel,
        out_shape=jax.ShapeDtypeStruct((requests, CH, 256), BF16),
        grid_spec=pltpu.PrefetchScalarGridSpec(
            num_scalar_prefetch=2,
            grid=(tokens // tile,),
            in_specs=[pl.BlockSpec((tile, D), lambda i, s, p: (i, 0))] + [part] * 8,
            out_specs=pl.BlockSpec((requests, CH, 256), lambda i, s, p: (0, 0, 0)),
            scratch_shapes=[pltpu.VMEM((tokens, 256), BF16)],
        ),
        compiler_params=pltpu.CompilerParams(
            dimension_semantics=("arbitrary",), vmem_limit_bytes=40 << 20
        ),
        cost_estimate=pl.CostEstimate(
            flops=2 * tokens * D * 256, bytes_accessed=12 << 20, transcendentals=0
        ),
        name="cond_rows",
    )(sources, spans, hidden, *a_parts, *b_parts)


def encode_kernel(query_ref, source_ref, cond_ref, out_w_ref, out_ref, mixed):
    row_head = lax.broadcasted_iota(jnp.int32, (128, 128), 0) // EHD
    col_head = lax.broadcasted_iota(jnp.int32, (128, 128), 1) // EHD
    same = row_head == col_head
    zero = jnp.zeros((128, 128), BF16)
    for p in range(PAIRS):
        keys = cond_ref[p, 0, :, :128]
        values = cond_ref[p, 0, :, 128:]
        key_pair = jnp.where(same, jnp.concatenate([keys, keys], axis=0), zero)
        value_pair = jnp.where(same, jnp.concatenate([values, values], axis=0), zero)
        query = query_ref[0, :, p * 128 : (p + 1) * 128]
        scores = lax.dot_general(
            key_pair, query, (((1,), (1,)), ((), ())), preferred_element_type=F32
        ) * (1.0 / math.sqrt(EHD))
        halves = []
        for h in range(2):
            part = scores[h * EHD : (h + 1) * EHD]
            grown = jnp.exp(part - jnp.max(part, axis=0, keepdims=True))
            halves.append((grown / jnp.sum(grown, axis=0, keepdims=True)).astype(BF16))
        weights = jnp.concatenate(halves, axis=0)
        got = lax.dot_general(
            weights, value_pair, (((0,), (0,)), ((), ())), preferred_element_type=F32
        )
        mixed[:, p * 128 : (p + 1) * 128] = got.astype(BF16)
    branch = dot(mixed[...], out_w_ref[...])
    out_ref[0] = (source_ref[0].astype(F32) + branch).astype(BF16)


def encode(enc_q, sources, cond, enc_out):
    count = sources.shape[0]
    return pl.pallas_call(
        encode_kernel,
        out_shape=jax.ShapeDtypeStruct((count, NLEN, E), BF16),
        grid=(count,),
        in_specs=[
            pl.BlockSpec((1, NLEN, E), lambda i: (i, 0, 0)),
            pl.BlockSpec((1, NLEN, E), lambda i: (i, 0, 0)),
            pl.BlockSpec((cond.shape[0], 1, CH, 256), lambda i: (0, i, 0, 0)),
            pl.BlockSpec((E, E), lambda i: (0, 0), pipeline_mode=pl.Buffered(1)),
        ],
        out_specs=pl.BlockSpec((1, NLEN, E), lambda i: (i, 0, 0)),
        scratch_shapes=[pltpu.VMEM((NLEN, E), BF16)],
        compiler_params=pltpu.CompilerParams(
            dimension_semantics=("arbitrary",), vmem_limit_bytes=24 << 20
        ),
        cost_estimate=pl.CostEstimate(
            flops=count * NLEN * E * E * 2, bytes_accessed=5 << 20, transcendentals=count << 17
        ),
        name="encode",
    )(enc_q, sources, cond, enc_out)


SPANS_STEP = 4


def decode_kernel(pos_ref, *refs):
    del pos_ref
    blocks = SPANS_STEP * KNB
    enc_refs = refs[:blocks]
    carried_ref, q_ref, wk_ref, wv_ref, wo_ref, out_ref, rows, att = refs[blocks:]
    step = pl.program_id(0)
    for m in range(blocks):
        if m < KNB:

            @pl.when(step == 0)
            def _():
                rows[m * NLEN : (m + 1) * NLEN, :] = carried_ref[m]

            @pl.when(step > 0)
            def _():
                rows[m * NLEN : (m + 1) * NLEN, :] = enc_refs[m][0]

        else:
            rows[m * NLEN : (m + 1) * NLEN, :] = enc_refs[m][0]
    width = q_ref.shape[1]
    length = KNB * NLEN
    for s in range(SPANS_STEP):
        block = rows[s * length : (s + 1) * length, :]
        keys = dot(block, wk_ref[...]).astype(BF16)
        values = dot(block, wv_ref[...]).astype(BF16)
        for h in range(width // HD):
            at = slice(h * HD, (h + 1) * HD)
            scores = lax.dot_general(
                q_ref[s * CH : (s + 1) * CH, at],
                keys[:, at],
                (((1,), (1,)), ((), ())),
                preferred_element_type=F32,
            ) * (1.0 / math.sqrt(HD))
            grown = jnp.exp(scores - jnp.max(scores, axis=-1, keepdims=True))
            weights = (grown / jnp.sum(grown, axis=-1, keepdims=True)).astype(BF16)
            att[s * CH : (s + 1) * CH, at] = dot(weights, values[:, at]).astype(BF16)
    chunk = 512
    for n in range(wo_ref.shape[1] // chunk):
        at = slice(n * chunk, (n + 1) * chunk)
        out_ref[:, at] = dot(att[...], wo_ref[:, at]).astype(BF16)


def decode(pos, encoded, carried, queries, w_key, w_value, w_out):
    tokens, width = queries.shape
    spans = tokens // CH
    steps = spans // SPANS_STEP
    blocks = SPANS_STEP * KNB
    tile = SPANS_STEP * CH

    def enc_spec(m):
        return pl.BlockSpec(
            (1, NLEN, E),
            lambda i, pos: (pos[jnp.maximum(i * blocks + m - KNB, 0)], 0, 0),
        )

    once = pl.Buffered(1)
    return pl.pallas_call(
        decode_kernel,
        out_shape=jax.ShapeDtypeStruct((tokens, D), BF16),
        grid_spec=pltpu.PrefetchScalarGridSpec(
            num_scalar_prefetch=1,
            grid=(steps,),
            in_specs=[enc_spec(m) for m in range(blocks)]
            + [
                pl.BlockSpec((KNB, NLEN, E), lambda i, pos: (0, 0, 0), pipeline_mode=once),
                pl.BlockSpec((tile, width), lambda i, pos: (i, 0)),
                pl.BlockSpec((E, width), lambda i, pos: (0, 0), pipeline_mode=once),
                pl.BlockSpec((E, width), lambda i, pos: (0, 0), pipeline_mode=once),
                pl.BlockSpec((width, D), lambda i, pos: (0, 0), pipeline_mode=once),
            ],
            out_specs=pl.BlockSpec((tile, D), lambda i, pos: (i, 0)),
            scratch_shapes=[
                pltpu.VMEM((blocks * NLEN, E), BF16),
                pltpu.VMEM((tile, width), BF16),
            ],
        ),
        compiler_params=pltpu.CompilerParams(
            dimension_semantics=("arbitrary",), vmem_limit_bytes=48 << 20
        ),
        cost_estimate=pl.CostEstimate(
            flops=2 * spans * KNB * NLEN * E * width * 2 + 2 * tokens * width * D,
            bytes_accessed=24 << 20,
            transcendentals=tokens * KNB * NLEN * (width // HD),
        ),
        name="decode",
    )(pos, *([encoded] * blocks), carried, queries, w_key, w_value, w_out)


def body(
    hidden,
    nbr_table,
    nbr_ids,
    w_query,
    w_key,
    w_value,
    w_out,
    enc_query,
    enc_key,
    enc_value,
    enc_out,
):
    store_count = lax.axis_size("store")
    store_rank = lax.axis_index("store")
    seq_count = lax.axis_size("seq")
    seq_rank = lax.axis_index("seq")
    side = math.isqrt(seq_count)
    span_count = nbr_ids.shape[0]
    row_requests = span_count * KNB
    per_owner = row_requests // store_count
    blocks_here = nbr_table.shape[0]

    pair_at = jnp.minimum(store_rank, PAIRS - 1) * 128
    weight = jnp.concatenate(
        [
            lax.dynamic_slice_in_dim(enc_key, pair_at, 128, axis=1),
            lax.dynamic_slice_in_dim(enc_value, pair_at, 128, axis=1),
        ],
        axis=1,
    )
    half = weight.shape[0] // 2
    a_four = jnp.stack(around(weight[:half], side, False))
    b_four = jnp.stack(around(weight[half:], side, True))
    a_parts = around(a_four, side, True)
    b_parts = around(b_four, side, False)
    y_at, z_at = seq_rank // side, seq_rank % side
    rel = jnp.array(REL, jnp.int32)
    from_rank = (
        side * ((y_at + rel + side) % side)[:, None] + ((z_at + rel + side) % side)[None, :]
    ).reshape(-1)

    flat_ids = nbr_ids.reshape(-1)
    slot = jnp.arange(row_requests, dtype=jnp.int32)
    rank_key = (flat_ids // blocks_here) * row_requests + slot
    pos = jnp.sum((rank_key[:, None] > rank_key[None, :]).astype(jnp.int32), axis=1)
    by_owner = jnp.sum(jnp.where(pos[None, :] == slot[:, None], slot[None, :], 0), axis=1)
    picked = lax.dynamic_slice_in_dim(by_owner, store_rank * per_owner, per_owner)
    sources = nbr_table[flat_ids[picked] % blocks_here]

    queries = dot(hidden, w_query).astype(BF16)
    source_f = sources.astype(F32)
    normed = (
        source_f * lax.rsqrt(jnp.mean(source_f * source_f, axis=-1, keepdims=True) + EPSILON)
    ).astype(BF16)
    enc_q = dot(normed.reshape(per_owner * NLEN, E), enc_query).astype(BF16)
    enc_q = enc_q.reshape(per_owner, NLEN, E)

    asked = cond_rows(hidden, a_parts, b_parts, from_rank, by_owner // KNB)
    asked = asked.reshape(store_count, per_owner, CH, 256)
    cond = lax.all_to_all(asked, "store", 0, 0, tiled=True)
    encoded = encode(enc_q, sources, cond, enc_out)
    gathered = lax.all_gather(encoded, "store", axis=0, tiled=True)
    last = gathered[lax.dynamic_slice_in_dim(pos, row_requests - KNB, KNB)]
    carried = lax.ppermute(last, "seq", [(i, i + 1) for i in range(seq_count - 1)])
    terms = decode(pos, gathered, carried, queries, w_key, w_value, w_out)
    return lax.psum_scatter(terms, "store", scatter_dimension=1, tiled=True)


def solution(mesh):
    in_specs = (
        P("seq", None),
        P("store", None, None),
        P("seq", None),
        P(None, "store"),
        P(None, "store"),
        P(None, "store"),
        P("store", None),
        P(),
        P("seq", None),
        P("seq", None),
        P(),
    )
    out_specs = P("seq", "store")
    return jax.shard_map(body, mesh=mesh, in_specs=in_specs, out_specs=out_specs, check_vma=False)
```

time: 374 us -> 241 us (0.64)
  waiting for transfers between devices: 212 us -> 118 us
  matrix products: 73.7 us -> 11.2 us
  Pallas kernels: 0 us -> 50.7 us
  local copies, waits for them, and re-layouts: 52.1 us -> 15.8 us
  starting transfers between devices: 3.47 us -> 27.9 us
  other arithmetic: 17.5 us -> 1.8 us
    all_gather x3 -> x1, waiting for transfers between devices: 155 us -> 43 us  [body(): gathered = lax.all_gather(encoded, 'store', axis=0, tiled=True)]
    dot_general x12 -> x2, matrix products: 73.7 us -> 11.2 us  [dot(): return jnp.dot(a, b, preferred_element_type=F32)]
    pallas_call x0 -> x3, Pallas kernels: none -> 50.7 us  [the longest x1 36 us: decode(): pl.pallas_call(decode_kernel, out_shape=jax.ShapeDtypeStruct((tokens, D),...]
    ppermute x1 -> x13, starting transfers between devices: 3.17 us -> 19 us  [the longest x12 15.5 us: around(): got.append(lax.ppermute(block, 'seq', route))]
    reshape x3 -> x0, local copies, waits for them, and re-layouts: 14.9 us -> none  [the longest x1 11.9 us: body(): owner_order = joined.reshape(shard_rows.shape[0], NLEN, 2 * head_width)]
    slice x5 -> x0, local copies, waits for them, and re-layouts: 14.6 us -> none  [the longest x1 6.4 us: body(): previous[:, :, head_width:].reshape(span_count, KNB * NLEN, local_heads, HD)]
    all_to_all x0 -> x1, waiting for transfers between devices: none -> 11.7 us  [body(): cond = lax.all_to_all(asked, 'store', 0, 0, tiled=True)]
    concatenate x2 -> x1, other arithmetic: 11.5 us -> 0.02 us  [body(): jnp.concatenate([lax.dynamic_slice_in_dim(enc_key, pair_at, 128, axis=1),...]
  transfers between devices with their start and end apart: 5 -> 16, of which waited for: 5 -> 7; matrix products, arithmetic and copies ran while one was open for 10% -> 6% of each run, Pallas kernels for 0% -> 0%
where the time goes in v1:
time: 241 us; the launch traced here: 239 us
  waiting for transfers between devices  118 us (49%)
  Pallas kernels  50.7 us (21%)
  starting transfers between devices  27.9 us (12%)
  local copies, waits for them, and re-layouts  15.8 us (7%)
  between operations  13.6 us (6%)
  matrix products  11.2 us (5%)
    reduce_scatter x1, waiting for transfers between devices, body(): return lax.psum_scatter(terms, 'store', scatter_dimension=1, tiled=True)  50.4 us
    all_gather x1, waiting for transfers between devices, body(): gathered = lax.all_gather(encoded, 'store', axis=0, tiled=True)  43 us
    pallas_call x1, Pallas kernels, decode(): pl.pallas_call(decode_kernel, out_shape=jax.ShapeDtypeStruct((tokens, D),...  36 us
    ppermute x12, starting transfers between devices, around(): got.append(lax.ppermute(block, 'seq', route))  15.5 us
    all_to_all x1, waiting for transfers between devices, body(): cond = lax.all_to_all(asked, 'store', 0, 0, tiled=True)  11.7 us
    dot_general x2, matrix products, dot(): return jnp.dot(a, b, preferred_element_type=F32)  11.2 us
    pallas_call x1, Pallas kernels, encode(): pl.pallas_call(encode_kernel, out_shape=jax.ShapeDtypeStruct((count, NLEN...  9.84 us
    ppermute x12, waiting for transfers between devices, around(): got.append(lax.ppermute(block, 'seq', route))  9.73 us
  transfers between devices with their start and end apart: 16, of which 7 were waited for; matrix products, arithmetic and copies ran while one was open for 6% of the time, Pallas kernels for 0%

profile of v1, /device:TPU:9, one launch (start us, length us, event | category | flops | bytes accessed | tf_op | source)
XLA Modules:
  0.0 239.3 jit_solution(9922697476653318906)
XLA Ops:
  6.5 1.0 constant_dynamic-slice_fusion
  7.6 0.1 collective-permute-start.7
  7.7 1.5 collective-permute-start.6
  9.1 3.6 %collective-permute-start.2 = (bf16[128,256]{1,0:T(8,128)(2,1)S(1)}, bf16[128,256]{1,0:T(8,128)(2,1)S(1)}, u32[]{:S(2)}, u32[]{:S(2)}) collective-permute-start(bf16[128,256]{1,0:T(8,128)(2,1)S(1)} %get-tuple-element.6), channel_id=1, source_target_pairs={{0,16},{8,24},{16,0},{24,8},{32,48},{40,56},{48,32},{56,40},{64,80... | collective-permute-start | bytes 196616 | tf_op jit(solution)/shard_map/ppermute | solution.py:42
  12.7 0.4 collective-permute-start.1
  13.2 1.0 collective-permute-start
  14.2 0.8 copy.16
  14.9 0.1 reshape.149
  15.0 0.2 convert_reduce_fusion.pos_ref
  15.2 0.1 select_reduce_fusion
  15.4 0.7 fusion.2
  16.1 0.1 broadcast_add_fusion
  16.2 0.6 gather_fusion
  16.8 3.3 %collective-permute-start.8 = (bf16[128,256]{1,0:T(8,128)(2,1)S(1)}, bf16[128,256]{1,0:T(8,128)(2,1)S(1)}, u32[]{:S(2)}, u32[]{:S(2)}) collective-permute-start(bf16[128,256]{1,0:T(8,128)(2,1)S(1)} %get-tuple-element.5), channel_id=1, source_target_pairs={{0,64},{8,72},{16,80},{24,88},{32,96},{40,104},{48,112},{56,120},{... | collective-permute-start | bytes 196616 | tf_op jit(solution)/shard_map/ppermute | solution.py:42
  20.1 0.7 collective-permute-start.5
  20.8 0.6 collective-permute-start.4
  21.4 0.9 collective-permute-start.3
  22.3 1.3 collective-permute-start.11
  23.6 1.5 collective-permute-start.10
  25.1 1.9 collective-permute-done.5.refs_3_
  27.0 0.7 collective-permute-start.9
  27.7 0.1 add.138.src_ref
  27.8 0.7 gather_fusion.1
  28.6 6.8 %collective-permute-done.4.refs_2_ = bf16[4,128,256]{2,1,0:T(8,128)(2,1)} collective-permute-done((bf16[4,128,256]{2,1,0:T(8,128)(2,1)S(1)}, bf16[4,128,256]{2,1,0:T(8,128)(2,1)}, u32[]{:S(2)}, u32[]{:S(2)}) %collective-permute-start.4) | collective-permute-done | bytes 262176 | tf_op jit(solution)/shard_map/ppermute | solution.py:42
  35.4 1.1 collective-permute-done.9.refs_5_
  36.4 3.4 %copy-done.1 = bf16[1024,4096]{1,0:T(8,128)(2,1)S(1)} copy-done((bf16[1024,4096]{1,0:T(8,128)(2,1)S(1)}, bf16[1024,4096]{1,0:T(8,128)(2,1)}, u32[]{:S(2)}) %copy-start.1) | copy-done | bytes 8388632
  39.8 4.9 %cond_rows.1 = bf16[32,64,256]{2,1,0:T(8,128)(2,1)S(1)} custom-call(s32[16]{0:T(128)S(1)} %add.138.src_ref, s32[32]{0:T(128)S(1)} %and_select_fusion.span_ref, bf16[1024,4096]{1,0:T(8,128)(2,1)S(1)} %copy-done.1, bf16[4,128,256]{2,1,0:T(8,128)(2,1)S(1)} %pad_maximum_fusion.refs_0_, bf16[4,128,256]{2,1,0:T(8,128)(2,1)} %collective-permute-done.3.refs_1_, ...), custom_call_target="tpu_custom_call" | custom-call | flops 2147483648 | bytes 12582912 | tf_op jit(solution)/shard_map/cond_rows/pallas_call | solution.py:72
  44.7 1.0 copy-done.2
  45.7 8.8 %all-to-all-start = ((bf16[8,4,64,256]{3,2,1,0:T(8,128)(2,1)}), bf16[8,4,64,256]{3,2,1,0:T(8,128)(2,1)}, u32[]{:S(2)}, u32[]{:S(2)}) async-start(bf16[8,4,64,256]{3,2,1,0:T(8,128)(2,1)} %bitcast.24), calls=%async_computation | async-start | bytes 2097152 | tf_op jit(solution)/shard_map/all_to_all | solution.py:295
  54.5 0.3 multiply_reduce_fusion
  54.8 0.2 fusion
  55.0 0.9 copy-done.8
  56.0 2.1 convolution_convert_fusion.1
  58.1 11.7 %all-to-all-done.cond_ref = bf16[8,4,64,256]{3,2,1,0:T(8,128)(2,1)} async-done(((bf16[8,4,64,256]{3,2,1,0:T(8,128)(2,1)}), bf16[8,4,64,256]{3,2,1,0:T(8,128)(2,1)}, u32[]{:S(2)}, u32[]{:S(2)}) %all-to-all-start) | async-done | bytes 1048608 | tf_op jit(solution)/shard_map/all_to_all | solution.py:295
  69.7 1.4 copy-done.4
  71.2 1.2 copy-done.7
  72.3 9.8 %encode.1 = bf16[4,128,896]{2,1,0:T(8,128)(2,1)S(1)} custom-call(bf16[4,128,896]{2,1,0:T(8,128)(2,1)S(1)} %bitcast.25, bf16[4,128,896]{2,1,0:T(8,128)(2,1)S(1)} %gather_fusion.1, bf16[8,4,64,256]{3,2,1,0:T(8,128)(2,1)} %all-to-all-done.cond_ref, bf16[896,896]{1,0:T(8,128)(2,1)S(1)} %copy-done.4), custom_call_target="tpu_custom_call" | custom-call | flops 822083584 | bytes 5242880 | tf_op jit(solution)/shard_map/encode/pallas_call | solution.py:122
  82.2 0.9 copy-done.3
  83.1 0.0 all-gather.2.cloned.1.call-update
  83.1 0.0 reduce-scatter.2.cloned.1.call-start
  83.2 0.1 compare_select_fusion
  83.3 43.0 %all-gather.2.cloned.1.call-done.refs_0_.refs_1_.refs_2_.refs_3_.refs_4_.refs_5_.refs_6_.refs_7_ = bf16[32,128,896]{2,1,0:T(8,128)(2,1)} async-done(((bf16[4,128,896]{2,1,0:T(8,128)(2,1)}), bf16[32,128,896]{2,1,0:T(8,128)(2,1)}) %all-gather.2.cloned.1.call-update) | async-done | bytes 7340048 | tf_op jit(solution)/shard_map/all_gather | solution.py:297
  126.3 3.7 %gather_fusion.2 = bf16[2,128,896]{2,1,0:T(8,128)(2,1)S(1)} fusion(bf16[32,128,896]{2,1,0:T(8,128)(2,1)} %all-gather.2.cloned.1.call-done.refs_0_.refs_1_.refs_2_.refs_3_.refs_4_.refs_5_.refs_6_.refs_7_, s32[1024]{0:T(1024)S(1)} %pad_clamp_fusion), kind=kCustom, calls=%fused_computation.2 | custom fusion | bytes 917512 | tf_op jit(solution)/shard_map/gather | solution.py:298
  130.1 3.5 %collective-permute-start.12 = (bf16[2,128,896]{2,1,0:T(8,128)(2,1)S(1)}, bf16[2,128,896]{2,1,0:T(8,128)(2,1)S(1)}, u32[]{:S(2)}, u32[]{:S(2)}) collective-permute-start(bf16[2,128,896]{2,1,0:T(8,128)(2,1)S(1)} %gather_fusion.2), channel_id=1, source_target_pairs={{0,8},{8,16},{16,24},{24,32},{32,40},{40,48},{48,56},{56,64},{64,7... | collective-permute-start | bytes 1376264 | tf_op jit(solution)/shard_map/ppermute | solution.py:299
  133.6 9.0 %convolution_convert_fusion.refs_9_ = bf16[1024,512]{1,0:T(8,128)(2,1)S(1)} fusion(bf16[1024,4096]{1,0:T(8,128)(2,1)} %hidden_ref.1, bf16[4096,512]{1,0:T(8,128)(2,1)} %param.15), kind=kOutput, calls=%fused_computation.6 | convolution fusion | flops 4295491584 | bytes 13631488 | tf_op jit(solution)/shard_map/dot_general | solution.py:27
  142.6 3.4 %collective-permute-done.12.refs_8_ = bf16[2,128,896]{2,1,0:T(8,128)(2,1)S(1)} collective-permute-done((bf16[2,128,896]{2,1,0:T(8,128)(2,1)S(1)}, bf16[2,128,896]{2,1,0:T(8,128)(2,1)S(1)}, u32[]{:S(2)}, u32[]{:S(2)}) %collective-permute-start.12) | collective-permute-done | bytes 458784 | tf_op jit(solution)/shard_map/ppermute | solution.py:299
  146.1 36.0 %decode.1 = bf16[1024,4096]{1,0:T(8,128)(2,1)} custom-call(s32[32]{0:T(128)S(1)} %convert_reduce_fusion.pos_ref, bf16[32,128,896]{2,1,0:T(8,128)(2,1)} %all-gather.2.cloned.1.call-done.refs_0_.refs_1_.refs_2_.refs_3_.refs_4_.refs_5_.refs_6_.refs_7_, ...), custom_call_target="tpu_custom_call" | custom-call | flops 11811160064 | bytes 25165824 | tf_op jit(solution)/shard_map/decode/pallas_call | solution.py:203
  182.1 50.4 %reduce-scatter.2.cloned.1.call-done = bf16[1024,512]{1,0:T(8,128)(2,1)} async-done(((bf16[1024,4096]{1,0:T(8,128)(2,1)}), bf16[1024,512]{1,0:T(8,128)(2,1)}) %reduce-scatter.2.cloned.1.call-update) | async-done | bytes 1048592 | tf_op jit(solution)/shard_map/reduce_scatter | solution.py:301
  (33 shorter events, 0.2 us)
Async XLA Ops:
  6.5 21.3 %copy-start = (bf16[8,128,896]{2,1,0:T(8,128)(2,1)S(1)}, bf16[8,128,896]{2,1,0:T(8,128)(2,1)}, u32[]{:S(2)}) copy-start(bf16[8,128,896]{2,1,0:T(8,128)(2,1)} %param.13) | copy-start | bytes 5505028
  7.6 13.8 %collective-permute-start.7 = (bf16[128,256]{1,0:T(8,128)(2,1)S(1)}, bf16[128,256]{1,0:T(8,128)(2,1)S(1)}, u32[]{:S(2)}, u32[]{:S(2)}) collective-permute-start(bf16[128,256]{1,0:T(8,128)(2,1)S(1)} %get-tuple-element.5), channel_id=1, source_target_pairs={{0,96},{8,104},{16,112},{24,120},{32,0},{40,8},{48,16},{56,24},{64... | collective-permute-start | bytes 196616 | tf_op jit(solution)/shard_map/ppermute | solution.py:42
  7.7 14.6 %collective-permute-start.6 = (bf16[128,256]{1,0:T(8,128)(2,1)S(1)}, bf16[128,256]{1,0:T(8,128)(2,1)S(1)}, u32[]{:S(2)}, u32[]{:S(2)}) collective-permute-start(bf16[128,256]{1,0:T(8,128)(2,1)S(1)} %get-tuple-element.5), channel_id=1, source_target_pairs={{0,32},{8,40},{16,48},{24,56},{32,64},{40,72},{48,80},{56,88},{64,... | collective-permute-start | bytes 196616 | tf_op jit(solution)/shard_map/ppermute | solution.py:42
  9.1 7.7 %collective-permute-start.2 = (bf16[128,256]{1,0:T(8,128)(2,1)S(1)}, bf16[128,256]{1,0:T(8,128)(2,1)S(1)}, u32[]{:S(2)}, u32[]{:S(2)}) collective-permute-start(bf16[128,256]{1,0:T(8,128)(2,1)S(1)} %get-tuple-element.6), channel_id=1, source_target_pairs={{0,16},{8,24},{16,0},{24,8},{32,48},{40,56},{48,32},{56,40},{64,80... | collective-permute-start | bytes 196616 | tf_op jit(solution)/shard_map/ppermute | solution.py:42
  12.7 7.4 %collective-permute-start.1 = (bf16[128,256]{1,0:T(8,128)(2,1)S(1)}, bf16[128,256]{1,0:T(8,128)(2,1)S(1)}, u32[]{:S(2)}, u32[]{:S(2)}) collective-permute-start(bf16[128,256]{1,0:T(8,128)(2,1)S(1)} %get-tuple-element.6), channel_id=1, source_target_pairs={{0,24},{8,0},{16,8},{24,16},{32,56},{40,32},{48,40},{56,48},{64,88... | collective-permute-start | bytes 196616 | tf_op jit(solution)/shard_map/ppermute | solution.py:42
  13.2 7.0 %collective-permute-start = (bf16[128,256]{1,0:T(8,128)(2,1)S(1)}, bf16[128,256]{1,0:T(8,128)(2,1)S(1)}, u32[]{:S(2)}, u32[]{:S(2)}) collective-permute-start(bf16[128,256]{1,0:T(8,128)(2,1)S(1)} %get-tuple-element.6), channel_id=1, source_target_pairs={{0,8},{8,16},{16,24},{24,0},{32,40},{40,48},{48,56},{56,32},{64,72... | collective-permute-start | bytes 196616 | tf_op jit(solution)/shard_map/ppermute | solution.py:42
  16.8 5.5 %collective-permute-start.8 = (bf16[128,256]{1,0:T(8,128)(2,1)S(1)}, bf16[128,256]{1,0:T(8,128)(2,1)S(1)}, u32[]{:S(2)}, u32[]{:S(2)}) collective-permute-start(bf16[128,256]{1,0:T(8,128)(2,1)S(1)} %get-tuple-element.5), channel_id=1, source_target_pairs={{0,64},{8,72},{16,80},{24,88},{32,96},{40,104},{48,112},{56,120},{... | collective-permute-start | bytes 196616 | tf_op jit(solution)/shard_map/ppermute | solution.py:42
  20.1 6.9 %collective-permute-start.5 = (bf16[4,128,256]{2,1,0:T(8,128)(2,1)S(1)}, bf16[4,128,256]{2,1,0:T(8,128)(2,1)S(1)}, u32[]{:S(2)}, u32[]{:S(2)}) collective-permute-start(bf16[4,128,256]{2,1,0:T(8,128)(2,1)S(1)} %pad_maximum_fusion.refs_0_), channel_id=1, source_target_pairs={{0,64},{8,72},{16,80},{24,88},{32,96},{40,104},{48,112},{56,120},{... | collective-permute-start | bytes 786440 | tf_op jit(solution)/shard_map/ppermute | solution.py:42
  20.8 14.5 %collective-permute-start.4 = (bf16[4,128,256]{2,1,0:T(8,128)(2,1)S(1)}, bf16[4,128,256]{2,1,0:T(8,128)(2,1)}, u32[]{:S(2)}, u32[]{:S(2)}) collective-permute-start(bf16[4,128,256]{2,1,0:T(8,128)(2,1)S(1)} %pad_maximum_fusion.refs_0_), channel_id=1, source_target_pairs={{0,96},{8,104},{16,112},{24,120},{32,0},{40,8},{48,16},{56,24},{64... | collective-permute-start | bytes 786440 | tf_op jit(solution)/shard_map/ppermute | solution.py:42
  21.4 13.9 %collective-permute-start.3 = (bf16[4,128,256]{2,1,0:T(8,128)(2,1)S(1)}, bf16[4,128,256]{2,1,0:T(8,128)(2,1)}, u32[]{:S(2)}, u32[]{:S(2)}) collective-permute-start(bf16[4,128,256]{2,1,0:T(8,128)(2,1)S(1)} %pad_maximum_fusion.refs_0_), channel_id=1, source_target_pairs={{0,32},{8,40},{16,48},{24,56},{32,64},{40,72},{48,80},{56,88},{64,... | collective-permute-start | bytes 786440 | tf_op jit(solution)/shard_map/ppermute | solution.py:42
  22.3 13.0 %collective-permute-start.11 = (bf16[4,128,256]{2,1,0:T(8,128)(2,1)S(1)}, bf16[4,128,256]{2,1,0:T(8,128)(2,1)}, u32[]{:S(2)}, u32[]{:S(2)}) collective-permute-start(bf16[4,128,256]{2,1,0:T(8,128)(2,1)S(1)} %pad_maximum_fusion.1.refs_4_), channel_id=1, source_target_pairs={{0,16},{8,24},{16,0},{24,8},{32,48},{40,56},{48,32},{56,40},{64,80... | collective-permute-start | bytes 786440 | tf_op jit(solution)/shard_map/ppermute | solution.py:42
  23.6 11.7 %collective-permute-start.10 = (bf16[4,128,256]{2,1,0:T(8,128)(2,1)S(1)}, bf16[4,128,256]{2,1,0:T(8,128)(2,1)}, u32[]{:S(2)}, u32[]{:S(2)}) collective-permute-start(bf16[4,128,256]{2,1,0:T(8,128)(2,1)S(1)} %pad_maximum_fusion.1.refs_4_), channel_id=1, source_target_pairs={{0,24},{8,0},{16,8},{24,16},{32,56},{40,32},{48,40},{56,48},{64,88... | collective-permute-start | bytes 786440 | tf_op jit(solution)/shard_map/ppermute | solution.py:42
  27.0 9.4 %collective-permute-start.9 = (bf16[4,128,256]{2,1,0:T(8,128)(2,1)S(1)}, bf16[4,128,256]{2,1,0:T(8,128)(2,1)}, u32[]{:S(2)}, u32[]{:S(2)}) collective-permute-start(bf16[4,128,256]{2,1,0:T(8,128)(2,1)S(1)} %pad_maximum_fusion.1.refs_4_), channel_id=1, source_target_pairs={{0,8},{8,16},{16,24},{24,0},{32,40},{40,48},{48,56},{56,32},{64,72... | collective-permute-start | bytes 786440 | tf_op jit(solution)/shard_map/ppermute | solution.py:42
  36.4 3.4 %copy-start.1 = (bf16[1024,4096]{1,0:T(8,128)(2,1)S(1)}, bf16[1024,4096]{1,0:T(8,128)(2,1)}, u32[]{:S(2)}) copy-start(bf16[1024,4096]{1,0:T(8,128)(2,1)} %hidden_ref.1) | copy-start | bytes 25165828
  44.7 1.0 copy-start.2
  45.7 24.0 %all-to-all-start = ((bf16[8,4,64,256]{3,2,1,0:T(8,128)(2,1)}), bf16[8,4,64,256]{3,2,1,0:T(8,128)(2,1)}, u32[]{:S(2)}, u32[]{:S(2)}) async-start(bf16[8,4,64,256]{3,2,1,0:T(8,128)(2,1)} %bitcast.24), calls=%async_computation | async-start | bytes 2097152 | tf_op jit(solution)/shard_map/all_to_all | solution.py:295
  54.5 71.8 %all-gather.2.cloned.1.call-start = ((), (), s32[]{:S(2)}) async-start(), calls=%async_computation.2 | async-start | bytes 8257536 | tf_op jit(solution)/shard_map/all_gather | solution.py:297
  54.5 1.4 copy-start.8
  69.7 1.4 copy-start.4
  71.2 1.2 copy-start.7
  82.2 0.9 copy-start.3
  83.1 149.4 %reduce-scatter.2.cloned.1.call-start = ((), (), s32[]{:S(2)}) async-start(), calls=%async_computation.3 | async-start | bytes 9437184 | tf_op jit(solution)/shard_map/reduce_scatter | solution.py:301
  130.0 16.0 %copy-start.5 = (bf16[896,512]{1,0:T(8,128)(2,1)S(1)}, bf16[896,512]{1,0:T(8,128)(2,1)}, u32[]{:S(2)}) copy-start(bf16[896,512]{1,0:T(8,128)(2,1)} %refs_10_.1) | copy-start | bytes 2752516
  130.0 16.0 %copy-start.6 = (bf16[896,512]{1,0:T(8,128)(2,1)S(1)}, bf16[896,512]{1,0:T(8,128)(2,1)}, u32[]{:S(2)}) copy-start(bf16[896,512]{1,0:T(8,128)(2,1)} %refs_11_.1) | copy-start | bytes 2752516
  130.1 16.0 %collective-permute-start.12 = (bf16[2,128,896]{2,1,0:T(8,128)(2,1)S(1)}, bf16[2,128,896]{2,1,0:T(8,128)(2,1)S(1)}, u32[]{:S(2)}, u32[]{:S(2)}) collective-permute-start(bf16[2,128,896]{2,1,0:T(8,128)(2,1)S(1)} %gather_fusion.2), channel_id=1, source_target_pairs={{0,8},{8,16},{16,24},{24,32},{32,40},{40,48},{48,56},{56,64},{64,7... | collective-permute-start | bytes 1376264 | tf_op jit(solution)/shard_map/ppermute | solution.py:299
Sparse Core Ops, SparseCore 0:
  83.3 43.0 all-gather.1
  182.2 50.2 reduce-scatter.1

commit v2 on v1

v2 whole, which is shorter than its diff:
```python
import math

import jax
import jax.numpy as jnp
from jax import lax
from jax.experimental import pallas as pl
from jax.experimental.pallas import tpu as pltpu
from jax.sharding import PartitionSpec as P

D = 4096
HD = 128
E = 896
EHEADS = 14
EHD = 64
CH = 64
NLEN = 128
KNB = 2
PAIRS = E // 128

EPSILON = 1e-06
F32 = jnp.float32
BF16 = jnp.bfloat16
REL = (0, -1, 1, 2)
FIRST = 7


def dot(a, b):
    return jnp.dot(a, b, preferred_element_type=F32)


def grid_route(side, dy, dz):
    return [
        (side * y + z, side * ((y + dy) % side) + (z + dz) % side)
        for y in range(side)
        for z in range(side)
    ]


def around(block, side, along_y):
    got = [block]
    for rel in REL[1:]:
        route = grid_route(side, -rel, 0) if along_y else grid_route(side, 0, -rel)
        got.append(lax.ppermute(block, "seq", route))
    return got


def around_x(block, chips):
    got = [block]
    for rel in REL[1:]:
        route = [
            (2 * x + core, 2 * ((x - rel) % chips) + core) for x in range(chips) for core in range(2)
        ]
        got.append(lax.ppermute(block, "store", route))
    return got


def swap_cores(block):
    count = lax.axis_size("store")
    return lax.ppermute(block, "store", [(i, i ^ 1) for i in range(count)])


def once(shape):
    return pl.BlockSpec(shape, lambda *_: (0,) * len(shape), pipeline_mode=pl.Buffered(1))


def cond_kernel(src_ref, hidden_ref, *refs):
    a_refs, b_refs = refs[:4], refs[4:8]
    out_ref, held = refs[8], refs[9]
    step = pl.program_id(0)
    rows = hidden_ref.shape[0]
    total = None
    for i in range(4):
        for j in range(4):
            at = pl.multiple_of(src_ref[4 * i + j] * 256, 256)
            weight = jnp.concatenate([a_refs[i][j], b_refs[j][i]], axis=0)
            term = dot(hidden_ref[:, pl.ds(at, 256)], weight)
            total = term if total is None else total + term
    held[pl.ds(pl.multiple_of(step * rows, rows), rows), :] = total.astype(BF16)

    @pl.when(step == pl.num_programs(0) - 1)
    def _():
        tokens = held.shape[0]
        first = FIRST * CH
        out_ref[: tokens - first, :] = held[first:, :]
        out_ref[tokens - first :, :] = held[:first, :]


def cond_rows(hidden, a_parts, b_parts, ranks):
    tokens = hidden.shape[0]
    tile = 512
    return pl.pallas_call(
        cond_kernel,
        out_shape=jax.ShapeDtypeStruct((tokens, 256), BF16),
        grid_spec=pltpu.PrefetchScalarGridSpec(
            num_scalar_prefetch=1,
            grid=(tokens // tile,),
            in_specs=[pl.BlockSpec((tile, D), lambda i, s: (i, 0))] + [once((4, 128, 256))] * 8,
            out_specs=pl.BlockSpec((tokens, 256), lambda i, s: (0, 0)),
            scratch_shapes=[pltpu.VMEM((tokens, 256), BF16)],
        ),
        compiler_params=pltpu.CompilerParams(
            dimension_semantics=("arbitrary",), vmem_limit_bytes=32 << 20
        ),
        cost_estimate=pl.CostEstimate(
            flops=2 * tokens * D * 256, bytes_accessed=12 << 20, transcendentals=0
        ),
        name="cond_rows",
    )(ranks, hidden, *a_parts, *b_parts)


def enc_query_kernel(pos_ref, *refs):
    del pos_ref
    sources, (w_ref, out_ref) = refs[:4], refs[4:]
    rows = []
    for source in sources:
        block = source[0].astype(F32)
        scale = lax.rsqrt(jnp.mean(block * block, axis=-1, keepdims=True) + EPSILON)
        rows.append((block * scale).astype(BF16))
    got = dot(jnp.concatenate(rows, axis=0), w_ref[...]).astype(BF16)
    for n in range(4):
        out_ref[n] = got[n * NLEN : (n + 1) * NLEN]


def enc_queries(pos, gathered, weight):
    count = pos.shape[0]

    def source(n):
        return pl.BlockSpec((1, NLEN, E), lambda i, pos: (pos[4 * i + n], 0, 0))

    return pl.pallas_call(
        enc_query_kernel,
        out_shape=jax.ShapeDtypeStruct((count, NLEN, E), BF16),
        grid_spec=pltpu.PrefetchScalarGridSpec(
            num_scalar_prefetch=1,
            grid=(count // 4,),
            in_specs=[source(n) for n in range(4)] + [once((E, E))],
            out_specs=pl.BlockSpec((4, NLEN, E), lambda i, pos: (i, 0, 0)),
        ),
        compiler_params=pltpu.CompilerParams(
            dimension_semantics=("arbitrary",), vmem_limit_bytes=24 << 20
        ),
        cost_estimate=pl.CostEstimate(
            flops=2 * count * NLEN * E * E, bytes_accessed=10 << 20, transcendentals=0
        ),
        name="enc_queries",
    )(pos, *([gathered] * 4), weight)


def encode_kernel(pos_ref, pair_ref, *refs):
    del pos_ref
    sources, conds = refs[:4], refs[4:12]
    query_ref, out_w_ref, out_ref, mixed = refs[12:]
    row_head = lax.broadcasted_iota(jnp.int32, (128, 128), 0) // EHD
    col_head = lax.broadcasted_iota(jnp.int32, (128, 128), 1) // EHD
    same = row_head == col_head
    zero = jnp.zeros((128, 128), BF16)
    units = [(n, j) for n in range(4) for j in range(8)]

    def two_heads(block):
        return jnp.where(same, jnp.concatenate([block, block], axis=0), zero)

    def score(n, j):
        at = pl.multiple_of(jnp.minimum(pair_ref[j], PAIRS - 1) * 128, 128)
        return lax.dot_general(
            two_heads(conds[j][n, :, :128]),
            query_ref[n, :, pl.ds(at, 128)],
            (((1,), (1,)), ((), ())),
            preferred_element_type=F32,
        ) * (1.0 / math.sqrt(EHD))

    def soften(scores):
        halves = []
        for h in range(2):
            part = scores[h * EHD : (h + 1) * EHD]
            grown = jnp.exp(part - jnp.max(part, axis=0, keepdims=True))
            halves.append((grown * (1.0 / jnp.sum(grown, axis=0, keepdims=True))).astype(BF16))
        return jnp.concatenate(halves, axis=0)

    scores = [score(n, j) for n, j in units]
    weights = [soften(x) for x in scores]
    for weight, (n, j) in zip(weights, units):
        got = lax.dot_general(
            weight,
            two_heads(conds[j][n, :, 128:]),
            (((0,), (0,)), ((), ())),
            preferred_element_type=F32,
        )
        at = pl.multiple_of(pair_ref[j] * 128, 128)
        mixed[n * NLEN : (n + 1) * NLEN, pl.ds(at, 128)] = got.astype(BF16)
    branch = dot(mixed[:, :E], out_w_ref[...])
    for n in range(4):
        rows = branch[n * NLEN : (n + 1) * NLEN]
        out_ref[n] = (sources[n][0].astype(F32) + rows).astype(BF16)


def encode(base, count, pos, pairs, queries, gathered, conds, enc_out):
    first = base // 4

    def source(n):
        return pl.BlockSpec((1, NLEN, E), lambda i, pos, pairs: (pos[base + 4 * i + n], 0, 0))

    cond = pl.BlockSpec((4, CH, 256), lambda i, pos, pairs: (first + i, 0, 0))
    return pl.pallas_call(
        encode_kernel,
        out_shape=jax.ShapeDtypeStruct((count, NLEN, E), BF16),
        grid_spec=pltpu.PrefetchScalarGridSpec(
            num_scalar_prefetch=2,
            grid=(count // 4,),
            in_specs=[source(n) for n in range(4)]
            + [cond] * 8
            + [
                pl.BlockSpec((4, NLEN, E), lambda i, pos, pairs: (first + i, 0, 0)),
                once((E, E)),
            ],
            out_specs=pl.BlockSpec((4, NLEN, E), lambda i, pos, pairs: (i, 0, 0)),
            scratch_shapes=[pltpu.VMEM((4 * NLEN, 1024), BF16)],
        ),
        compiler_params=pltpu.CompilerParams(
            dimension_semantics=("arbitrary",), vmem_limit_bytes=32 << 20
        ),
        cost_estimate=pl.CostEstimate(
            flops=count * NLEN * E * E * 3, bytes_accessed=8 << 20, transcendentals=count << 17
        ),
        name="encode",
    )(pos, pairs, *([gathered] * 4), *conds, queries, enc_out)


SPANS_STEP = 4


def decode_kernel(carries, *refs):
    own_ref, other_ref, q_ref, wk_ref, wv_ref, wo_ref = refs[:6]
    out_ref, rows, att, ks, vs = refs[-5:]
    for j in range(SPANS_STEP):
        for n, ref in enumerate((own_ref, other_ref)):
            at = slice((KNB * j + n) * NLEN, (KNB * j + n + 1) * NLEN)
            rows[at, :] = ref[j]
    if carries:

        @pl.when(pl.program_id(0) == 0)
        def _():
            rows[:NLEN, :] = refs[6][0]
            rows[NLEN : 2 * NLEN, :] = refs[7][0]

    length = KNB * NLEN
    block = rows[...]
    ks[...] = dot(block, wk_ref[...]).astype(BF16)
    units = [(s, p) for s in range(SPANS_STEP) for p in range(q_ref.shape[1] // 256)]
    empty = jnp.zeros((CH, HD), BF16)
    weights = []
    scores = []
    for s, p in units:
        pair = q_ref[s * CH : (s + 1) * CH, p * 256 : (p + 1) * 256]
        both = jnp.concatenate(
            [
                jnp.concatenate([pair[:, :HD], empty], axis=1),
                jnp.concatenate([empty, pair[:, HD:]], axis=1),
            ],
            axis=0,
        )
        scores.append(
            lax.dot_general(
                ks[s * length : (s + 1) * length, p * 256 : (p + 1) * 256],
                both,
                (((1,), (1,)), ((), ())),
                preferred_element_type=F32,
            )
            * (1.0 / math.sqrt(HD))
        )
    for score in scores:
        grown = jnp.exp(score - jnp.max(score, axis=0, keepdims=True))
        weights.append((grown * (1.0 / jnp.sum(grown, axis=0, keepdims=True))).astype(BF16))
    vs[...] = dot(block, wv_ref[...]).astype(BF16)
    for weight, (s, p) in zip(weights, units):
        got = lax.dot_general(
            weight,
            vs[s * length : (s + 1) * length, p * 256 : (p + 1) * 256],
            (((0,), (0,)), ((), ())),
            preferred_element_type=F32,
        ).astype(BF16)
        att[s * CH : (s + 1) * CH, p * 256 : p * 256 + HD] = got[:CH, :HD]
        att[s * CH : (s + 1) * CH, p * 256 + HD : (p + 1) * 256] = got[CH:, HD:]
    chunk = 512
    for n in range(wo_ref.shape[1] // chunk):
        at = slice(n * chunk, (n + 1) * chunk)
        out_ref[:, at] = dot(att[...], wo_ref[:, at]).astype(BF16)


def decode(first_span, own, other, carried, terms, queries, w_key, w_value, w_out):
    tokens, width = queries.shape
    count = own.shape[0]
    tile = SPANS_STEP * CH
    first = first_span // SPANS_STEP
    rows = SPANS_STEP * KNB * NLEN
    block = pl.BlockSpec((SPANS_STEP, NLEN, E), lambda i: (i, 0, 0))
    operands = [own, other, queries, w_key, w_value, w_out, *carried]
    specs = [
        block,
        block,
        pl.BlockSpec((tile, width), lambda i: (first + i, 0)),
        once((E, width)),
        once((E, width)),
        once((width, D)),
    ] + [once((1, NLEN, E))] * len(carried)
    aliases = {}
    if terms is not None:
        aliases = {len(operands): 0}
        operands.append(terms)
        specs.append(pl.BlockSpec(memory_space=pl.ANY))
    return pl.pallas_call(
        lambda *refs: decode_kernel(len(carried) > 0, *refs),
        out_shape=jax.ShapeDtypeStruct((tokens, D), BF16),
        grid=(count // SPANS_STEP,),
        in_specs=specs,
        out_specs=pl.BlockSpec((tile, D), lambda i: (first + i, 0)),
        scratch_shapes=[
            pltpu.VMEM((rows, E), BF16),
            pltpu.VMEM((tile, width), BF16),
            pltpu.VMEM((rows, width), BF16),
            pltpu.VMEM((rows, width), BF16),
        ],
        input_output_aliases=aliases,
        compiler_params=pltpu.CompilerParams(
            dimension_semantics=("arbitrary",), vmem_limit_bytes=40 << 20
        ),
        cost_estimate=pl.CostEstimate(
            flops=4 * count * KNB * NLEN * E * width + 2 * count * CH * width * D,
            bytes_accessed=12 << 20,
            transcendentals=count * CH * KNB * NLEN * (width // HD),
        ),
        name="decode",
    )(*operands)


def body(
    hidden,
    nbr_table,
    nbr_ids,
    w_query,
    w_key,
    w_value,
    w_out,
    enc_query,
    enc_key,
    enc_value,
    enc_out,
):
    store_count = lax.axis_size("store")
    store_rank = lax.axis_index("store")
    seq_count = lax.axis_size("seq")
    seq_rank = lax.axis_index("seq")
    side = math.isqrt(seq_count)
    chips = store_count // 2
    span_count = nbr_ids.shape[0]
    row_requests = span_count * KNB
    per_owner = row_requests // store_count
    blocks_here = nbr_table.shape[0]

    flat_ids = nbr_ids.reshape(-1)
    slot = jnp.arange(row_requests, dtype=jnp.int32)
    rank_key = (flat_ids // blocks_here) * row_requests + slot
    pos = jnp.sum((rank_key[:, None] > rank_key[None, :]).astype(jnp.int32), axis=1)
    by_owner = jnp.sum(jnp.where(pos[None, :] == slot[:, None], slot[None, :], 0), axis=1)
    picked = lax.dynamic_slice_in_dim(by_owner, store_rank * per_owner, per_owner)
    sources = nbr_table[flat_ids[picked] % blocks_here]
    gathered = lax.all_gather(sources, "store", axis=0, tiled=True)

    pair_at = jnp.minimum(store_rank, PAIRS - 1) * 128
    weight = jnp.concatenate(
        [
            lax.dynamic_slice_in_dim(enc_key, pair_at, 128, axis=1),
            lax.dynamic_slice_in_dim(enc_value, pair_at, 128, axis=1),
        ],
        axis=1,
    )
    half = weight.shape[0] // 2
    a_four = jnp.stack(around(weight[:half], side, False))
    b_four = jnp.stack(around(weight[half:], side, True))
    a_parts = around(a_four, side, True)
    b_parts = around(b_four, side, False)
    y_at, z_at = seq_rank // side, seq_rank % side
    rel = jnp.array(REL, jnp.int32)
    from_rank = (
        side * ((y_at + rel + side) % side)[:, None] + ((z_at + rel + side) % side)[None, :]
    ).reshape(-1)
    cond = cond_rows(hidden, a_parts, b_parts, from_rank).reshape(span_count, CH, 256)
    own_lane = around_x(cond, chips)
    conds = own_lane + [swap_cores(block) for block in own_lane]
    chip, core = store_rank // 2, store_rank % 2
    lane = 2 * ((chip + rel + chips) % chips)
    pairs = jnp.concatenate([lane + core, lane + 1 - core])

    spans = (jnp.arange(span_count, dtype=jnp.int32) + FIRST) % span_count
    mine = jnp.sum(
        jnp.where(slot[None, :] == (KNB * spans + core)[:, None], pos[None, :], 0), axis=1
    )
    enc_q = enc_queries(mine, gathered, enc_query)
    queries = dot(hidden, w_query).astype(BF16)
    part = span_count // 2
    high = encode(0, part, mine, pairs, enc_q, gathered, conds, enc_out)
    low = encode(part, part, mine, pairs, enc_q, gathered, conds, enc_out)
    high_other = swap_cores(high)
    low_other = swap_cores(low)
    carried = lax.ppermute(low[:1], "seq", [(i, i + 1) for i in range(seq_count - 1)])
    carried_other = swap_cores(carried)
    terms = decode(part, high, high_other, (), None, queries, w_key, w_value, w_out)
    terms = decode(
        0, low, low_other, (carried, carried_other), terms, queries, w_key, w_value, w_out
    )
    return lax.psum_scatter(terms, "store", scatter_dimension=1, tiled=True)


def solution(mesh):
    in_specs = (
        P("seq", None),
        P("store", None, None),
        P("seq", None),
        P(None, "store"),
        P(None, "store"),
        P(None, "store"),
        P("store", None),
        P(),
        P("seq", None),
        P("seq", None),
        P(),
    )
    out_specs = P("seq", "store")
    return jax.shard_map(body, mesh=mesh, in_specs=in_specs, out_specs=out_specs, check_vma=False)
```

time: 241 us -> 207 us (0.86)
  waiting for transfers between devices: 118 us -> 81.5 us
  starting transfers between devices: 27.9 us -> 37.4 us
  matrix products: 11.2 us -> 6.66 us
    all_gather x1, waiting for transfers between devices: 43 us -> 0.01 us  [body(): gathered = lax.all_gather(sources, 'store', axis=0, tiled=True)]
    ppermute x1 -> x11, starting transfers between devices: 3.49 us -> 21.7 us  [the longest x7 13.4 us: swap_cores(): return lax.ppermute(block, 'store', [(i, i ^ 1) for i in range(count)])]
    all_to_all x1 -> x0, waiting for transfers between devices: 11.7 us -> none  [body(): cond = lax.all_to_all(asked, 'store', 0, 0, tiled=True)]
    ppermute x1 -> x11, waiting for transfers between devices: 3.45 us -> 14.1 us  [the longest x3 11 us: around_x(): got.append(lax.ppermute(block, 'store', route))]
    all_to_all x1 -> x0, starting transfers between devices: 8.84 us -> none  [body(): cond = lax.all_to_all(asked, 'store', 0, 0, tiled=True)]
    pallas_call x2 -> x4, Pallas kernels: 40.9 us -> 32.1 us  [the longest x2 21.9 us: decode(): pl.pallas_call(lambda *refs: decode_kernel(len(carried) > 0, *refs), out_...]
    pallas_call x1 -> x2, Pallas kernels: 9.84 us -> 16.5 us  [encode(): pl.pallas_call(encode_kernel, out_shape=jax.ShapeDtypeStruct((count, NLEN...]
    ppermute x12, waiting for transfers between devices: 9.73 us -> 16 us  [around(): got.append(lax.ppermute(block, 'seq', route))]
  transfers between devices with their start and end apart: 16 -> 25, of which waited for: 7 -> 11; matrix products, arithmetic and copies ran while one was open for 6% -> 4% of each run, Pallas kernels for 0% -> 14%
where the time goes in v2:
time: 207 us; the launch traced here: 206 us
  waiting for transfers between devices  81.5 us (39%)
  Pallas kernels  48.6 us (23%)
  starting transfers between devices  37.4 us (18%)
  local copies, waits for them, and re-layouts  16.5 us (8%)
  between operations  13.7 us (7%)
  matrix products  6.66 us (3%)
    reduce_scatter x1, waiting for transfers between devices, body(): return lax.psum_scatter(terms, 'store', scatter_dimension=1, tiled=True)  51.3 us
    pallas_call x2, Pallas kernels, decode(): pl.pallas_call(lambda *refs: decode_kernel(len(carried) > 0, *refs), out_...  21.9 us
    pallas_call x2, Pallas kernels, encode(): pl.pallas_call(encode_kernel, out_shape=jax.ShapeDtypeStruct((count, NLEN...  16.5 us
    ppermute x12, waiting for transfers between devices, around(): got.append(lax.ppermute(block, 'seq', route))  16 us
    ppermute x12, starting transfers between devices, around(): got.append(lax.ppermute(block, 'seq', route))  15.7 us
    ppermute x7, starting transfers between devices, swap_cores(): return lax.ppermute(block, 'store', [(i, i ^ 1) for i in range(count)])  13.4 us
    unnamed x31, local copies, waits for them, and re-layouts  12.3 us
    ppermute x3, waiting for transfers between devices, around_x(): got.append(lax.ppermute(block, 'store', route))  11 us
  transfers between devices with their start and end apart: 25, of which 11 were waited for; matrix products, arithmetic and copies ran while one was open for 4% of the time, Pallas kernels for 14%

profile of v2, /device:TPU:9, one launch (start us, length us, event | category | flops | bytes accessed | tf_op | source)
XLA Modules:
  0.0 205.9 jit_solution(16980959756151665060)
XLA Ops:
  6.5 0.9 copy.17
  7.9 0.7 broadcast_add_fusion.1
  8.6 0.6 gather_fusion
  9.3 1.6 gather_fusion.1
  10.9 0.9 constant_dynamic-slice_fusion
  11.8 3.7 %collective-permute-start.2 = (bf16[128,256]{1,0:T(8,128)(2,1)S(1)}, bf16[128,256]{1,0:T(8,128)(2,1)S(1)}, u32[]{:S(2)}, u32[]{:S(2)}) collective-permute-start(bf16[128,256]{1,0:T(8,128)(2,1)S(1)} %get-tuple-element.8), channel_id=1, source_target_pairs={{0,16},{8,24},{16,0},{24,8},{32,48},{40,56},{48,32},{56,40},{64,80... | collective-permute-start | bytes 196616 | tf_op jit(solution)/shard_map/ppermute | solution.py:43
  15.5 0.4 collective-permute-start.1
  16.0 1.0 collective-permute-start
  17.2 1.8 collective-permute-done.1
  19.0 1.3 collective-permute-done
  20.3 2.1 %collective-permute-start.5 = (bf16[4,128,256]{2,1,0:T(8,128)(2,1)S(1)}, bf16[4,128,256]{2,1,0:T(8,128)(2,1)S(1)}, u32[]{:S(2)}, u32[]{:S(2)}) collective-permute-start(bf16[4,128,256]{2,1,0:T(8,128)(2,1)S(1)} %pad_maximum_fusion.refs_0_), channel_id=1, source_target_pairs={{0,64},{8,72},{16,80},{24,88},{32,96},{40,104},{48,112},{56,120},{... | collective-permute-start | bytes 786440 | tf_op jit(solution)/shard_map/ppermute | solution.py:43
  22.4 1.1 collective-permute-start.7
  23.5 0.4 collective-permute-start.6
  23.9 2.2 %collective-permute-start.8 = (bf16[128,256]{1,0:T(8,128)(2,1)S(1)}, bf16[128,256]{1,0:T(8,128)(2,1)S(1)}, u32[]{:S(2)}, u32[]{:S(2)}) collective-permute-start(bf16[128,256]{1,0:T(8,128)(2,1)S(1)} %get-tuple-element.7), channel_id=1, source_target_pairs={{0,64},{8,72},{16,80},{24,88},{32,96},{40,104},{48,112},{56,120},{... | collective-permute-start | bytes 196616 | tf_op jit(solution)/shard_map/ppermute | solution.py:43
  26.1 4.5 %collective-permute-done.7 = bf16[128,256]{1,0:T(8,128)(2,1)S(1)} collective-permute-done((bf16[128,256]{1,0:T(8,128)(2,1)S(1)}, bf16[128,256]{1,0:T(8,128)(2,1)S(1)}, u32[]{:S(2)}, u32[]{:S(2)}) %collective-permute-start.7) | collective-permute-done | bytes 65568 | tf_op jit(solution)/shard_map/ppermute | solution.py:43
  30.6 3.3 %collective-permute-start.11 = (bf16[4,128,256]{2,1,0:T(8,128)(2,1)S(1)}, bf16[4,128,256]{2,1,0:T(8,128)(2,1)S(1)}, u32[]{:S(2)}, u32[]{:S(2)}) collective-permute-start(bf16[4,128,256]{2,1,0:T(8,128)(2,1)S(1)} %pad_maximum_fusion.1.refs_4_), channel_id=1, source_target_pairs={{0,16},{8,24},{16,0},{24,8},{32,48},{40,56},{48,32},{56,40},{64,80... | collective-permute-start | bytes 786440 | tf_op jit(solution)/shard_map/ppermute | solution.py:43
  34.0 1.1 collective-permute-start.10
  35.1 0.3 collective-permute-start.9
  35.6 2.5 %collective-permute-done.4.refs_2_ = bf16[4,128,256]{2,1,0:T(8,128)(2,1)S(1)} collective-permute-done((bf16[4,128,256]{2,1,0:T(8,128)(2,1)S(1)}, bf16[4,128,256]{2,1,0:T(8,128)(2,1)S(1)}, u32[]{:S(2)}, u32[]{:S(2)}) %collective-permute-start.4) | collective-permute-done | bytes 262176 | tf_op jit(solution)/shard_map/ppermute | solution.py:43
  38.1 0.7 copy-done.9
  38.8 0.7 copy-done.11
  39.5 5.5 %collective-permute-done.10.refs_6_ = bf16[4,128,256]{2,1,0:T(8,128)(2,1)} collective-permute-done((bf16[4,128,256]{2,1,0:T(8,128)(2,1)S(1)}, bf16[4,128,256]{2,1,0:T(8,128)(2,1)}, u32[]{:S(2)}, u32[]{:S(2)}) %collective-permute-start.10) | collective-permute-done | bytes 262176 | tf_op jit(solution)/shard_map/ppermute | solution.py:43
  45.2 3.5 %copy-done.3 = bf16[1024,4096]{1,0:T(8,128)(2,1)S(1)} copy-done((bf16[1024,4096]{1,0:T(8,128)(2,1)S(1)}, bf16[1024,4096]{1,0:T(8,128)(2,1)}, u32[]{:S(2)}) %copy-start.3) | copy-done | bytes 8388632
  48.8 0.9 copy-done.10
  49.7 0.9 copy-done.12
  50.7 4.2 %cond_rows.1 = bf16[1024,256]{1,0:T(8,128)(2,1)S(1)} custom-call(s32[16]{0:T(128)S(1)} %add.185.src_ref, bf16[1024,4096]{1,0:T(8,128)(2,1)S(1)} %copy-done.3, bf16[4,128,256]{2,1,0:T(8,128)(2,1)S(1)} %pad_maximum_fusion.refs_0_, bf16[4,128,256]{2,1,0:T(8,128)(2,1)S(1)} %copy-done.10, bf16[4,128,256]{2,1,0:T(8,128)(2,1)S(1)} %collective-permute-done.4.refs_2_, ...), custom_call_target="tpu_custom_call" | custom-call | flops 2147483648 | bytes 12582912 | tf_op jit(solution)/shard_map/cond_rows/pallas_call | solution.py:91
  54.8 2.9 %collective-permute-start.14 = (bf16[16,64,256]{2,1,0:T(8,128)(2,1)S(1)}, bf16[16,64,256]{2,1,0:T(8,128)(2,1)S(1)}, u32[]{:S(2)}, u32[]{:S(2)}) collective-permute-start(bf16[16,64,256]{2,1,0:T(8,128)(2,1)S(1)} %bitcast.17), channel_id=1, source_target_pairs={{0,4},{1,5},{2,6},{3,7},{4,0},{5,1},{6,2},{7,3},{8,12},{9,13},{10,... | collective-permute-start | bytes 1572872 | tf_op jit(solution)/shard_map/ppermute | solution.py:53
  57.7 0.8 collective-permute-start.13
  58.5 0.7 collective-permute-start.12
  59.2 3.5 %collective-permute-start.15 = (bf16[16,64,256]{2,1,0:T(8,128)(2,1)S(1)}, bf16[16,64,256]{2,1,0:T(8,128)(2,1)}, u32[]{:S(2)}, u32[]{:S(2)}) collective-permute-start(bf16[16,64,256]{2,1,0:T(8,128)(2,1)S(1)} %bitcast.20), channel_id=1, source_target_pairs={{0,1},{1,0},{2,3},{3,2},{4,5},{5,4},{6,7},{7,6},{8,9},{9,8},{10,11... | collective-permute-start | bytes 1572872 | tf_op jit(solution)/shard_map/ppermute | solution.py:59
  62.7 4.4 %collective-permute-done.14.refs_7_ = bf16[16,64,256]{2,1,0:T(8,128)(2,1)S(1)} collective-permute-done((bf16[16,64,256]{2,1,0:T(8,128)(2,1)S(1)}, bf16[16,64,256]{2,1,0:T(8,128)(2,1)S(1)}, u32[]{:S(2)}, u32[]{:S(2)}) %collective-permute-start.14) | collective-permute-done | bytes 524320 | tf_op jit(solution)/shard_map/ppermute | solution.py:53
  67.2 6.9 %collective-permute-start.18 = (bf16[16,64,256]{2,1,0:T(8,128)(2,1)S(1)}, bf16[16,64,256]{2,1,0:T(8,128)(2,1)}, u32[]{:S(2)}, u32[]{:S(2)}) collective-permute-start(bf16[16,64,256]{2,1,0:T(8,128)(2,1)S(1)} %collective-permute-done.14.refs_7_), channel_id=1, source_target_pairs={{0,1},{1,0},{2,3},{3,2},{4,5},{5,4},{6,7},{7,6},{8,9},{9,8},{10,11... | collective-permute-start | bytes 1572872 | tf_op jit(solution)/shard_map/ppermute | solution.py:59
  74.1 6.5 %collective-permute-done.13.refs_6_ = bf16[16,64,256]{2,1,0:T(8,128)(2,1)S(1)} collective-permute-done((bf16[16,64,256]{2,1,0:T(8,128)(2,1)S(1)}, bf16[16,64,256]{2,1,0:T(8,128)(2,1)S(1)}, u32[]{:S(2)}, u32[]{:S(2)}) %collective-permute-start.13) | collective-permute-done | bytes 524320 | tf_op jit(solution)/shard_map/ppermute | solution.py:53
  80.6 1.6 collective-permute-start.17
  82.4 3.1 %copy-done.1 = bf16[32,128,896]{2,1,0:T(8,128)(2,1)S(1)} copy-done((bf16[32,128,896]{2,1,0:T(8,128)(2,1)S(1)}, bf16[32,128,896]{2,1,0:T(8,128)(2,1)}, u32[]{:S(2)}) %copy-start.1) | copy-done | bytes 7340056
  85.5 1.4 copy-done.6
  86.9 6.0 %enc_queries.1.refs_12_ = bf16[16,128,896]{2,1,0:T(8,128)(2,1)S(1)} custom-call(s32[16]{0:T(128)S(1)} %select_reduce_fusion.1.pos_ref, bf16[32,128,896]{2,1,0:T(8,128)(2,1)S(1)} %copy-done.1, bf16[32,128,896]{2,1,0:T(8,128)(2,1)S(1)} %copy-done.1, bf16[32,128,896]{2,1,0:T(8,128)(2,1)S(1)} %copy-done.1, bf16[32,128,896]{2,1,0:T(8,128)(2,1)S(1)} %copy-done.1, ...), custom_call_target="tpu_custom_call" | custom-call | flops 3288334336 | bytes 10485760 | tf_op jit(solution)/shard_map/enc_queries/pallas_call | solution.py:130
  93.0 8.3 %encode.3.refs_0_ = bf16[8,128,896]{2,1,0:T(8,128)(2,1)} custom-call(s32[16]{0:T(128)S(1)} %select_reduce_fusion.1.pos_ref, s32[8]{0:T(128)S(1)} %pad_add_fusion.pair_ref, bf16[32,128,896]{2,1,0:T(8,128)(2,1)S(1)} %copy-done.2, bf16[32,128,896]{2,1,0:T(8,128)(2,1)S(1)} %copy-done.2, bf16[32,128,896]{2,1,0:T(8,128)(2,1)S(1)} %copy-done.2, ...), custom_call_target="tpu_custom_call" | custom-call | flops 2466250752 | bytes 8388608 | tf_op jit(solution)/shard_map/encode/pallas_call | solution.py:203
  101.3 0.5 collective-permute-start.22
  101.8 8.2 %encode.2.refs_0_ = bf16[8,128,896]{2,1,0:T(8,128)(2,1)} custom-call(s32[16]{0:T(128)S(1)} %select_reduce_fusion.1.pos_ref, s32[8]{0:T(128)S(1)} %pad_add_fusion.pair_ref, bf16[32,128,896]{2,1,0:T(8,128)(2,1)S(1)} %copy-done.2, bf16[32,128,896]{2,1,0:T(8,128)(2,1)S(1)} %copy-done.2, bf16[32,128,896]{2,1,0:T(8,128)(2,1)S(1)} %copy-done.2, ...), custom_call_target="tpu_custom_call" | custom-call | flops 2466250752 | bytes 8388608 | tf_op jit(solution)/shard_map/encode/pallas_call | solution.py:203
  110.0 1.0 slice.18
  111.2 3.9 %collective-permute-start.20 = (bf16[1,128,896]{2,1,0:T(8,128)(2,1)S(1)}, bf16[1,128,896]{2,1,0:T(8,128)(2,1)S(1)}, u32[]{:S(2)}, u32[]{:S(2)}) collective-permute-start(bf16[1,128,896]{2,1,0:T(8,128)(2,1)S(1)} %slice.18), channel_id=1, source_target_pairs={{0,8},{8,16},{16,24},{24,32},{32,40},{40,48},{48,56},{56,64},{64,7... | collective-permute-start | bytes 688136 | tf_op jit(solution)/shard_map/ppermute | solution.py:404
  115.1 6.7 %convolution_convert_fusion.refs_2_ = bf16[1024,512]{1,0:T(8,128)(2,1)S(1)} fusion(bf16[1024,4096]{1,0:T(8,128)(2,1)S(1)} %bitcast.16, bf16[4096,512]{1,0:T(8,128)(2,1)} %param.15), kind=kOutput, calls=%fused_computation.2 | convolution fusion | flops 4295491584 | bytes 13631488 | tf_op jit(solution)/shard_map/dot_general | solution.py:28
  121.8 3.1 %collective-permute-done.20.refs_6_ = bf16[1,128,896]{2,1,0:T(8,128)(2,1)S(1)} collective-permute-done((bf16[1,128,896]{2,1,0:T(8,128)(2,1)S(1)}, bf16[1,128,896]{2,1,0:T(8,128)(2,1)S(1)}, u32[]{:S(2)}, u32[]{:S(2)}) %collective-permute-start.20) | collective-permute-done | bytes 229408 | tf_op jit(solution)/shard_map/ppermute | solution.py:404
  125.0 0.7 collective-permute-start.21
  125.7 11.0 %decode.2.refs_8_ = bf16[1024,4096]{1,0:T(8,128)(2,1)} custom-call(bf16[8,128,896]{2,1,0:T(8,128)(2,1)} %encode.3.refs_0_, bf16[8,128,896]{2,1,0:T(8,128)(2,1)} %collective-permute-done.22.refs_1_, bf16[1024,512]{1,0:T(8,128)(2,1)S(1)} %convolution_convert_fusion.refs_2_, bf16[896,512]{1,0:T(8,128)(2,1)S(1)} %copy-done.7, bf16[896,512]{1,0:T(8,128)(2,1)S(1)} %copy-done.8, ...), custom_call_target="tpu_custom_call" | custom-call | flops 5905580032 | bytes 12582912 | tf_op jit(solution)/shard_map/decode/pallas_call | solution.py:310
  136.7 11.0 %decode.3 = bf16[1024,4096]{1,0:T(8,128)(2,1)} custom-call(bf16[8,128,896]{2,1,0:T(8,128)(2,1)} %encode.2.refs_0_, bf16[8,128,896]{2,1,0:T(8,128)(2,1)S(1)} %collective-permute-done.19.refs_1_, bf16[1024,512]{1,0:T(8,128)(2,1)S(1)} %convolution_convert_fusion.refs_2_, bf16[896,512]{1,0:T(8,128)(2,1)S(1)} %copy-done.7, ...), custom_call_target="tpu_custom_call", output_to_operand_aliasing={{}: (8, {})} | custom-call | flops 5905580032 | bytes 12582912 | tf_op jit(solution)/shard_map/decode/pallas_call | solution.py:310
  147.7 51.3 %reduce-scatter.2.cloned.1.call-done = bf16[1024,512]{1,0:T(8,128)(2,1)} async-done(((bf16[1024,4096]{1,0:T(8,128)(2,1)}), bf16[1024,512]{1,0:T(8,128)(2,1)}) %reduce-scatter.2.cloned.1.call-update) | async-done | bytes 1048592 | tf_op jit(solution)/shard_map/reduce_scatter | solution.py:410
  (64 shorter events, 1.7 us)
Async XLA Ops:
  6.5 2.7 %copy-start = (bf16[8,128,896]{2,1,0:T(8,128)(2,1)S(1)}, bf16[8,128,896]{2,1,0:T(8,128)(2,1)}, u32[]{:S(2)}) copy-start(bf16[8,128,896]{2,1,0:T(8,128)(2,1)} %param.13) | copy-start | bytes 5505028
  6.5 75.9 %all-gather.3.cloned.1.call-start = ((), (), s32[]{:S(2)}) async-start(), calls=%async_computation.2 | async-start | bytes 8257536 | tf_op jit(solution)/shard_map/all_gather | solution.py:366
  10.9 188.1 %reduce-scatter.2.cloned.1.call-start = ((), (), s32[]{:S(2)}) async-start(), calls=%async_computation.1 | async-start | bytes 9437184 | tf_op jit(solution)/shard_map/reduce_scatter | solution.py:410
  11.8 5.3 %collective-permute-start.2 = (bf16[128,256]{1,0:T(8,128)(2,1)S(1)}, bf16[128,256]{1,0:T(8,128)(2,1)S(1)}, u32[]{:S(2)}, u32[]{:S(2)}) collective-permute-start(bf16[128,256]{1,0:T(8,128)(2,1)S(1)} %get-tuple-element.8), channel_id=1, source_target_pairs={{0,16},{8,24},{16,0},{24,8},{32,48},{40,56},{48,32},{56,40},{64,80... | collective-permute-start | bytes 196616 | tf_op jit(solution)/shard_map/ppermute | solution.py:43
  15.5 3.5 %collective-permute-start.1 = (bf16[128,256]{1,0:T(8,128)(2,1)S(1)}, bf16[128,256]{1,0:T(8,128)(2,1)S(1)}, u32[]{:S(2)}, u32[]{:S(2)}) collective-permute-start(bf16[128,256]{1,0:T(8,128)(2,1)S(1)} %get-tuple-element.8), channel_id=1, source_target_pairs={{0,24},{8,0},{16,8},{24,16},{32,56},{40,32},{48,40},{56,48},{64,88... | collective-permute-start | bytes 196616 | tf_op jit(solution)/shard_map/ppermute | solution.py:43
  16.0 4.3 %collective-permute-start = (bf16[128,256]{1,0:T(8,128)(2,1)S(1)}, bf16[128,256]{1,0:T(8,128)(2,1)S(1)}, u32[]{:S(2)}, u32[]{:S(2)}) collective-permute-start(bf16[128,256]{1,0:T(8,128)(2,1)S(1)} %get-tuple-element.8), channel_id=1, source_target_pairs={{0,8},{8,16},{16,24},{24,0},{32,40},{40,48},{48,56},{56,32},{64,72... | collective-permute-start | bytes 196616 | tf_op jit(solution)/shard_map/ppermute | solution.py:43
  20.3 14.8 %collective-permute-start.5 = (bf16[4,128,256]{2,1,0:T(8,128)(2,1)S(1)}, bf16[4,128,256]{2,1,0:T(8,128)(2,1)S(1)}, u32[]{:S(2)}, u32[]{:S(2)}) collective-permute-start(bf16[4,128,256]{2,1,0:T(8,128)(2,1)S(1)} %pad_maximum_fusion.refs_0_), channel_id=1, source_target_pairs={{0,64},{8,72},{16,80},{24,88},{32,96},{40,104},{48,112},{56,120},{... | collective-permute-start | bytes 786440 | tf_op jit(solution)/shard_map/ppermute | solution.py:43
  22.4 8.2 %collective-permute-start.7 = (bf16[128,256]{1,0:T(8,128)(2,1)S(1)}, bf16[128,256]{1,0:T(8,128)(2,1)S(1)}, u32[]{:S(2)}, u32[]{:S(2)}) collective-permute-start(bf16[128,256]{1,0:T(8,128)(2,1)S(1)} %get-tuple-element.7), channel_id=1, source_target_pairs={{0,96},{8,104},{16,112},{24,120},{32,0},{40,8},{48,16},{56,24},{64... | collective-permute-start | bytes 196616 | tf_op jit(solution)/shard_map/ppermute | solution.py:43
  23.5 7.1 %collective-permute-start.6 = (bf16[128,256]{1,0:T(8,128)(2,1)S(1)}, bf16[128,256]{1,0:T(8,128)(2,1)S(1)}, u32[]{:S(2)}, u32[]{:S(2)}) collective-permute-start(bf16[128,256]{1,0:T(8,128)(2,1)S(1)} %get-tuple-element.7), channel_id=1, source_target_pairs={{0,32},{8,40},{16,48},{24,56},{32,64},{40,72},{48,80},{56,88},{64,... | collective-permute-start | bytes 196616 | tf_op jit(solution)/shard_map/ppermute | solution.py:43
  23.9 6.7 %collective-permute-start.8 = (bf16[128,256]{1,0:T(8,128)(2,1)S(1)}, bf16[128,256]{1,0:T(8,128)(2,1)S(1)}, u32[]{:S(2)}, u32[]{:S(2)}) collective-permute-start(bf16[128,256]{1,0:T(8,128)(2,1)S(1)} %get-tuple-element.7), channel_id=1, source_target_pairs={{0,64},{8,72},{16,80},{24,88},{32,96},{40,104},{48,112},{56,120},{... | collective-permute-start | bytes 196616 | tf_op jit(solution)/shard_map/ppermute | solution.py:43
  26.1 12.1 %collective-permute-start.4 = (bf16[4,128,256]{2,1,0:T(8,128)(2,1)S(1)}, bf16[4,128,256]{2,1,0:T(8,128)(2,1)S(1)}, u32[]{:S(2)}, u32[]{:S(2)}) collective-permute-start(bf16[4,128,256]{2,1,0:T(8,128)(2,1)S(1)} %pad_maximum_fusion.refs_0_), channel_id=1, source_target_pairs={{0,96},{8,104},{16,112},{24,120},{32,0},{40,8},{48,16},{56,24},{64... | collective-permute-start | bytes 786440 | tf_op jit(solution)/shard_map/ppermute | solution.py:43
  30.6 7.5 %collective-permute-start.3 = (bf16[4,128,256]{2,1,0:T(8,128)(2,1)S(1)}, bf16[4,128,256]{2,1,0:T(8,128)(2,1)S(1)}, u32[]{:S(2)}, u32[]{:S(2)}) collective-permute-start(bf16[4,128,256]{2,1,0:T(8,128)(2,1)S(1)} %pad_maximum_fusion.refs_0_), channel_id=1, source_target_pairs={{0,32},{8,40},{16,48},{24,56},{32,64},{40,72},{48,80},{56,88},{64,... | collective-permute-start | bytes 786440 | tf_op jit(solution)/shard_map/ppermute | solution.py:43
  30.6 8.2 %collective-permute-start.11 = (bf16[4,128,256]{2,1,0:T(8,128)(2,1)S(1)}, bf16[4,128,256]{2,1,0:T(8,128)(2,1)S(1)}, u32[]{:S(2)}, u32[]{:S(2)}) collective-permute-start(bf16[4,128,256]{2,1,0:T(8,128)(2,1)S(1)} %pad_maximum_fusion.1.refs_4_), channel_id=1, source_target_pairs={{0,16},{8,24},{16,0},{24,8},{32,48},{40,56},{48,32},{56,40},{64,80... | collective-permute-start | bytes 786440 | tf_op jit(solution)/shard_map/ppermute | solution.py:43
  34.0 11.1 %collective-permute-start.10 = (bf16[4,128,256]{2,1,0:T(8,128)(2,1)S(1)}, bf16[4,128,256]{2,1,0:T(8,128)(2,1)}, u32[]{:S(2)}, u32[]{:S(2)}) collective-permute-start(bf16[4,128,256]{2,1,0:T(8,128)(2,1)S(1)} %pad_maximum_fusion.1.refs_4_), channel_id=1, source_target_pairs={{0,24},{8,0},{16,8},{24,16},{32,56},{40,32},{48,40},{56,48},{64,88... | collective-permute-start | bytes 786440 | tf_op jit(solution)/shard_map/ppermute | solution.py:43
  35.1 10.1 %collective-permute-start.9 = (bf16[4,128,256]{2,1,0:T(8,128)(2,1)S(1)}, bf16[4,128,256]{2,1,0:T(8,128)(2,1)}, u32[]{:S(2)}, u32[]{:S(2)}) collective-permute-start(bf16[4,128,256]{2,1,0:T(8,128)(2,1)S(1)} %pad_maximum_fusion.1.refs_4_), channel_id=1, source_target_pairs={{0,8},{8,16},{16,24},{24,0},{32,40},{40,48},{48,56},{56,32},{64,72... | collective-permute-start | bytes 786440 | tf_op jit(solution)/shard_map/ppermute | solution.py:43
  38.1 0.7 copy-start.9
  38.8 0.7 copy-start.11
  45.2 3.5 %copy-start.3 = (bf16[1024,4096]{1,0:T(8,128)(2,1)S(1)}, bf16[1024,4096]{1,0:T(8,128)(2,1)}, u32[]{:S(2)}) copy-start(bf16[1024,4096]{1,0:T(8,128)(2,1)} %hidden_ref.1) | copy-start | bytes 25165828
  48.8 0.9 copy-start.10
  49.7 0.9 copy-start.12
  54.8 12.3 %collective-permute-start.14 = (bf16[16,64,256]{2,1,0:T(8,128)(2,1)S(1)}, bf16[16,64,256]{2,1,0:T(8,128)(2,1)S(1)}, u32[]{:S(2)}, u32[]{:S(2)}) collective-permute-start(bf16[16,64,256]{2,1,0:T(8,128)(2,1)S(1)} %bitcast.17), channel_id=1, source_target_pairs={{0,4},{1,5},{2,6},{3,7},{4,0},{5,1},{6,2},{7,3},{8,12},{9,13},{10,... | collective-permute-start | bytes 1572872 | tf_op jit(solution)/shard_map/ppermute | solution.py:53
  57.7 22.8 %collective-permute-start.13 = (bf16[16,64,256]{2,1,0:T(8,128)(2,1)S(1)}, bf16[16,64,256]{2,1,0:T(8,128)(2,1)S(1)}, u32[]{:S(2)}, u32[]{:S(2)}) collective-permute-start(bf16[16,64,256]{2,1,0:T(8,128)(2,1)S(1)} %bitcast.18), channel_id=1, source_target_pairs={{0,6},{1,7},{2,0},{3,1},{4,2},{5,3},{6,4},{7,5},{8,14},{9,15},{10,... | collective-permute-start | bytes 1572872 | tf_op jit(solution)/shard_map/ppermute | solution.py:53
  58.5 23.6 %collective-permute-start.12 = (bf16[16,64,256]{2,1,0:T(8,128)(2,1)S(1)}, bf16[16,64,256]{2,1,0:T(8,128)(2,1)}, u32[]{:S(2)}, u32[]{:S(2)}) collective-permute-start(bf16[16,64,256]{2,1,0:T(8,128)(2,1)S(1)} %bitcast.19), channel_id=1, source_target_pairs={{0,2},{1,3},{2,4},{3,5},{4,6},{5,7},{6,0},{7,1},{8,10},{9,11},{10,... | collective-permute-start | bytes 1572872 | tf_op jit(solution)/shard_map/ppermute | solution.py:53
  59.2 33.7 %collective-permute-start.15 = (bf16[16,64,256]{2,1,0:T(8,128)(2,1)S(1)}, bf16[16,64,256]{2,1,0:T(8,128)(2,1)}, u32[]{:S(2)}, u32[]{:S(2)}) collective-permute-start(bf16[16,64,256]{2,1,0:T(8,128)(2,1)S(1)} %bitcast.20), channel_id=1, source_target_pairs={{0,1},{1,0},{2,3},{3,2},{4,5},{5,4},{6,7},{7,6},{8,9},{9,8},{10,11... | collective-permute-start | bytes 1572872 | tf_op jit(solution)/shard_map/ppermute | solution.py:59
  67.2 25.8 %collective-permute-start.18 = (bf16[16,64,256]{2,1,0:T(8,128)(2,1)S(1)}, bf16[16,64,256]{2,1,0:T(8,128)(2,1)}, u32[]{:S(2)}, u32[]{:S(2)}) collective-permute-start(bf16[16,64,256]{2,1,0:T(8,128)(2,1)S(1)} %collective-permute-done.14.refs_7_), channel_id=1, source_target_pairs={{0,1},{1,0},{2,3},{3,2},{4,5},{5,4},{6,7},{7,6},{8,9},{9,8},{10,11... | collective-permute-start | bytes 1572872 | tf_op jit(solution)/shard_map/ppermute | solution.py:59
  80.6 12.4 %collective-permute-start.17 = (bf16[16,64,256]{2,1,0:T(8,128)(2,1)S(1)}, bf16[16,64,256]{2,1,0:T(8,128)(2,1)}, u32[]{:S(2)}, u32[]{:S(2)}) collective-permute-start(bf16[16,64,256]{2,1,0:T(8,128)(2,1)S(1)} %collective-permute-done.13.refs_6_), channel_id=1, source_target_pairs={{0,1},{1,0},{2,3},{3,2},{4,5},{5,4},{6,7},{7,6},{8,9},{9,8},{10,11... | collective-permute-start | bytes 1572872 | tf_op jit(solution)/shard_map/ppermute | solution.py:59
  82.1 10.8 %collective-permute-start.16 = (bf16[16,64,256]{2,1,0:T(8,128)(2,1)}, bf16[16,64,256]{2,1,0:T(8,128)(2,1)}, u32[]{:S(2)}, u32[]{:S(2)}) collective-permute-start(bf16[16,64,256]{2,1,0:T(8,128)(2,1)} %collective-permute-done.12.refs_5_), channel_id=1, source_target_pairs={{0,1},{1,0},{2,3},{3,2},{4,5},{5,4},{6,7},{7,6},{8,9},{9,8},{10,11... | collective-permute-start | bytes 1572872 | tf_op jit(solution)/shard_map/ppermute | solution.py:59
  82.4 3.1 %copy-start.1 = (bf16[32,128,896]{2,1,0:T(8,128)(2,1)S(1)}, bf16[32,128,896]{2,1,0:T(8,128)(2,1)}, u32[]{:S(2)}) copy-start(bf16[32,128,896]{2,1,0:T(8,128)(2,1)} %all-gather.3.cloned.1.call-done.refs_0_.refs_1_.refs_2_.refs_3_) | copy-start | bytes 22020100
  85.5 1.4 copy-start.6
  86.9 6.1 %copy-start.2 = (bf16[32,128,896]{2,1,0:T(8,128)(2,1)S(1)}, bf16[32,128,896]{2,1,0:T(8,128)(2,1)}, u32[]{:S(2)}) copy-start(bf16[32,128,896]{2,1,0:T(8,128)(2,1)} %all-gather.3.cloned.1.call-done.refs_0_.refs_1_.refs_2_.refs_3_) | copy-start | bytes 22020100
  86.9 6.1 %copy-start.4 = (bf16[896,896]{1,0:T(8,128)(2,1)S(1)}, bf16[896,896]{1,0:T(8,128)(2,1)}, u32[]{:S(2)}) copy-start(bf16[896,896]{1,0:T(8,128)(2,1)} %refs_13_.3) | copy-start | bytes 4816900
  93.0 22.1 %slice-start = ((s8[8388608]{0:T(1024)(128)(4,1)}), s8[4194304]{0:T(1024)(128)(4,1)S(1)}, s32[]{:S(2)}) async-start(s8[8388608]{0:T(1024)(128)(4,1)} %bitcast.15), calls=%async_computation.3 | async-start | bytes 8388608
  101.3 13.8 %slice-start.1 = ((s8[8388608]{0:T(1024)(128)(4,1)}), s8[4194304]{0:T(1024)(128)(4,1)S(1)}, s32[]{:S(2)}) async-start(s8[8388608]{0:T(1024)(128)(4,1)} %bitcast.15), calls=%async_computation.4 | async-start | bytes 8388608
  101.3 24.4 %collective-permute-start.22 = (bf16[8,128,896]{2,1,0:T(8,128)(2,1)}, bf16[8,128,896]{2,1,0:T(8,128)(2,1)}, u32[]{:S(2)}, u32[]{:S(2)}) collective-permute-start(bf16[8,128,896]{2,1,0:T(8,128)(2,1)} %encode.3.refs_0_), channel_id=1, source_target_pairs={{0,1},{1,0},{2,3},{3,2},{4,5},{5,4},{6,7},{7,6},{8,9},{9,8},{10,11... | collective-permute-start | bytes 5505032 | tf_op jit(solution)/shard_map/ppermute | solution.py:59
  110.9 14.8 %copy-start.5 = (bf16[512,4096]{1,0:T(8,128)(2,1)S(1)}, bf16[512,4096]{1,0:T(8,128)(2,1)}, u32[]{:S(2)}) copy-start(bf16[512,4096]{1,0:T(8,128)(2,1)} %refs_5_.3) | copy-start | bytes 12582916
  110.9 14.7 %copy-start.7 = (bf16[896,512]{1,0:T(8,128)(2,1)S(1)}, bf16[896,512]{1,0:T(8,128)(2,1)}, u32[]{:S(2)}) copy-start(bf16[896,512]{1,0:T(8,128)(2,1)} %refs_3_.3) | copy-start | bytes 2752516
  111.0 14.7 %copy-start.8 = (bf16[896,512]{1,0:T(8,128)(2,1)S(1)}, bf16[896,512]{1,0:T(8,128)(2,1)}, u32[]{:S(2)}) copy-start(bf16[896,512]{1,0:T(8,128)(2,1)} %refs_4_.5) | copy-start | bytes 2752516
  111.0 25.7 %collective-permute-start.19 = (bf16[8,128,896]{2,1,0:T(8,128)(2,1)}, bf16[8,128,896]{2,1,0:T(8,128)(2,1)S(1)}, u32[]{:S(2)}, u32[]{:S(2)}) collective-permute-start(bf16[8,128,896]{2,1,0:T(8,128)(2,1)} %encode.2.refs_0_), channel_id=1, source_target_pairs={{0,1},{1,0},{2,3},{3,2},{4,5},{5,4},{6,7},{7,6},{8,9},{9,8},{10,11... | collective-permute-start | bytes 5505032 | tf_op jit(solution)/shard_map/ppermute | solution.py:59
  111.2 13.8 %collective-permute-start.20 = (bf16[1,128,896]{2,1,0:T(8,128)(2,1)S(1)}, bf16[1,128,896]{2,1,0:T(8,128)(2,1)S(1)}, u32[]{:S(2)}, u32[]{:S(2)}) collective-permute-start(bf16[1,128,896]{2,1,0:T(8,128)(2,1)S(1)} %slice.18), channel_id=1, source_target_pairs={{0,8},{8,16},{16,24},{24,32},{32,40},{40,48},{48,56},{56,64},{64,7... | collective-permute-start | bytes 688136 | tf_op jit(solution)/shard_map/ppermute | solution.py:404
  125.0 11.7 %collective-permute-start.21 = (bf16[1,128,896]{2,1,0:T(8,128)(2,1)S(1)}, bf16[1,128,896]{2,1,0:T(8,128)(2,1)S(1)}, u32[]{:S(2)}, u32[]{:S(2)}) collective-permute-start(bf16[1,128,896]{2,1,0:T(8,128)(2,1)S(1)} %collective-permute-done.20.refs_6_), channel_id=1, source_target_pairs={{0,1},{1,0},{2,3},{3,2},{4,5},{5,4},{6,7},{7,6},{8,9},{9,8},{10,11... | collective-permute-start | bytes 688136 | tf_op jit(solution)/shard_map/ppermute | solution.py:59
Sparse Core Ops, SparseCore 0:
  11.0 48.0 all-gather.2
  147.8 51.1 reduce-scatter.1

commit v3 on v2

--- a/solution.py
+++ b/solution.py
@@ -18,10 +18,11 @@
 PAIRS = E // 128
 
 EPSILON = 1e-06
+VMEM_LIMIT = 36 << 20
 F32 = jnp.float32
 BF16 = jnp.bfloat16
 REL = (0, -1, 1, 2)
-FIRST = 7
+FIRST = 15
 
 
 def dot(a, b):
@@ -64,15 +65,15 @@
 
 
 def cond_kernel(src_ref, hidden_ref, *refs):
-    a_refs, b_refs = refs[:4], refs[4:8]
-    out_ref, held = refs[8], refs[9]
+    a_refs, (b_ref, out_ref, held) = refs[:4], refs[4:]
     step = pl.program_id(0)
     rows = hidden_ref.shape[0]
     total = None
     for i in range(4):
         for j in range(4):
-            at = pl.multiple_of(src_ref[4 * i + j] * 256, 256)
-            weight = jnp.concatenate([a_refs[i][j], b_refs[j][i]], axis=0)
+            rank = src_ref[4 * i + j]
+            at = pl.multiple_of(rank * 256, 256)
+            weight = jnp.concatenate([a_refs[i][j], b_ref[rank]], axis=0)
             term = dot(hidden_ref[:, pl.ds(at, 256)], weight)
             total = term if total is None else total + term
     held[pl.ds(pl.multiple_of(step * rows, rows), rows), :] = total.astype(BF16)
@@ -85,7 +86,7 @@
         out_ref[tokens - first :, :] = held[:first, :]
 
 
-def cond_rows(hidden, a_parts, b_parts, ranks):
+def cond_rows(hidden, a_parts, b_all, ranks):
     tokens = hidden.shape[0]
     tile = 512
     return pl.pallas_call(
@@ -94,23 +95,24 @@
         grid_spec=pltpu.PrefetchScalarGridSpec(
             num_scalar_prefetch=1,
             grid=(tokens // tile,),
-            in_specs=[pl.BlockSpec((tile, D), lambda i, s: (i, 0))] + [once((4, 128, 256))] * 8,
+            in_specs=[pl.BlockSpec((tile, D), lambda i, s: (i, 0))] + [once((4, 128, 256))] * 4
+            + [once(b_all.shape)],
             out_specs=pl.BlockSpec((tokens, 256), lambda i, s: (0, 0)),
             scratch_shapes=[pltpu.VMEM((tokens, 256), BF16)],
         ),
         compiler_params=pltpu.CompilerParams(
-            dimension_semantics=("arbitrary",), vmem_limit_bytes=32 << 20
+            dimension_semantics=("arbitrary",), vmem_limit_bytes=VMEM_LIMIT
         ),
         cost_estimate=pl.CostEstimate(
             flops=2 * tokens * D * 256, bytes_accessed=12 << 20, transcendentals=0
         ),
         name="cond_rows",
-    )(ranks, hidden, *a_parts, *b_parts)
+    )(ranks, hidden, *a_parts, b_all)
 
 
 def enc_query_kernel(pos_ref, *refs):
     del pos_ref
-    sources, (w_ref, out_ref) = refs[:4], refs[4:]
+    sources, w_ref, out_ref = refs[:4], refs[4], refs[-1]
     rows = []
     for source in sources:
         block = source[0].astype(F32)
@@ -121,7 +123,7 @@
         out_ref[n] = got[n * NLEN : (n + 1) * NLEN]
 
 
-def enc_queries(pos, gathered, weight):
+def enc_queries(pos, gathered, weight, after):
     count = pos.shape[0]
 
     def source(n):
@@ -133,23 +135,25 @@
         grid_spec=pltpu.PrefetchScalarGridSpec(
             num_scalar_prefetch=1,
             grid=(count // 4,),
-            in_specs=[source(n) for n in range(4)] + [once((E, E))],
+            in_specs=[source(n) for n in range(4)]
+            + [once((E, E)), pl.BlockSpec(memory_space=pl.ANY)],
             out_specs=pl.BlockSpec((4, NLEN, E), lambda i, pos: (i, 0, 0)),
         ),
         compiler_params=pltpu.CompilerParams(
-            dimension_semantics=("arbitrary",), vmem_limit_bytes=24 << 20
+            dimension_semantics=("arbitrary",), vmem_limit_bytes=VMEM_LIMIT
         ),
         cost_estimate=pl.CostEstimate(
             flops=2 * count * NLEN * E * E, bytes_accessed=10 << 20, transcendentals=0
         ),
         name="enc_queries",
-    )(pos, *([gathered] * 4), weight)
+    )(pos, *([gathered] * 4), weight, after)
 
 
 def encode_kernel(pos_ref, pair_ref, *refs):
     del pos_ref
     sources, conds = refs[:4], refs[4:12]
-    query_ref, out_w_ref, out_ref, mixed = refs[12:]
+    query_ref, out_w_ref = refs[12:14]
+    out_ref, mixed = refs[-2:]
     row_head = lax.broadcasted_iota(jnp.int32, (128, 128), 0) // EHD
     col_head = lax.broadcasted_iota(jnp.int32, (128, 128), 1) // EHD
     same = row_head == col_head
@@ -193,7 +197,7 @@
         out_ref[n] = (sources[n][0].astype(F32) + rows).astype(BF16)
 
 
-def encode(base, count, pos, pairs, queries, gathered, conds, enc_out):
+def encode(base, count, pos, pairs, queries, gathered, conds, enc_out, after=()):
     first = base // 4
 
     def source(n):
@@ -202,7 +206,7 @@
     cond = pl.BlockSpec((4, CH, 256), lambda i, pos, pairs: (first + i, 0, 0))
     return pl.pallas_call(
         encode_kernel,
-        out_shape=jax.ShapeDtypeStruct((count, NLEN, E), BF16),
+        out_shape=(pltpu.HBM if after else jax.ShapeDtypeStruct)((count, NLEN, E), BF16),
         grid_spec=pltpu.PrefetchScalarGridSpec(
             num_scalar_prefetch=2,
             grid=(count // 4,),
@@ -211,26 +215,29 @@
             + [
                 pl.BlockSpec((4, NLEN, E), lambda i, pos, pairs: (first + i, 0, 0)),
                 once((E, E)),
-            ],
+            ]
+            + [pl.BlockSpec(memory_space=pl.ANY)] * len(after),
             out_specs=pl.BlockSpec((4, NLEN, E), lambda i, pos, pairs: (i, 0, 0)),
             scratch_shapes=[pltpu.VMEM((4 * NLEN, 1024), BF16)],
         ),
         compiler_params=pltpu.CompilerParams(
-            dimension_semantics=("arbitrary",), vmem_limit_bytes=32 << 20
+            dimension_semantics=("arbitrary",), vmem_limit_bytes=VMEM_LIMIT
         ),
         cost_estimate=pl.CostEstimate(
             flops=count * NLEN * E * E * 3, bytes_accessed=8 << 20, transcendentals=count << 17
         ),
         name="encode",
-    )(pos, pairs, *([gathered] * 4), *conds, queries, enc_out)
+    )(pos, pairs, *([gathered] * 4), *conds, queries, enc_out, *after)
 
 
 SPANS_STEP = 4
 
 
-def decode_kernel(carries, *refs):
+def decode_kernel(carries, split, *refs):
+    if split:
+        block_ref, refs = refs[0], refs[1:]
     own_ref, other_ref, q_ref, wk_ref, wv_ref, wo_ref = refs[:6]
-    out_ref, rows, att, ks, vs = refs[-5:]
+    rows, att, ks, vs = refs[-4:]
     for j in range(SPANS_STEP):
         for n, ref in enumerate((own_ref, other_ref)):
             at = slice((KNB * j + n) * NLEN, (KNB * j + n + 1) * NLEN)
@@ -280,48 +287,60 @@
         ).astype(BF16)
         att[s * CH : (s + 1) * CH, p * 256 : p * 256 + HD] = got[:CH, :HD]
         att[s * CH : (s + 1) * CH, p * 256 + HD : (p + 1) * 256] = got[CH:, HD:]
-    chunk = 512
-    for n in range(wo_ref.shape[1] // chunk):
-        at = slice(n * chunk, (n + 1) * chunk)
-        out_ref[:, at] = dot(att[...], wo_ref[:, at]).astype(BF16)
-
-
-def decode(first_span, own, other, carried, terms, queries, w_key, w_value, w_out):
-    tokens, width = queries.shape
+    done = att[...]
+    chunk = q_ref.shape[1]
+    if split:
+        for out_ref, first in ((refs[-6], 0), (refs[-5], 4)):
+            for j in range(4):
+                at = pl.multiple_of(block_ref[first + j] * chunk, chunk)
+                out_ref[j] = dot(done, wo_ref[:, pl.ds(at, chunk)]).astype(BF16)
+    else:
+        for n in range(wo_ref.shape[1] // chunk):
+            at = slice(n * chunk, (n + 1) * chunk)
+            refs[-5][:, at] = dot(done, wo_ref[:, at]).astype(BF16)
+
+
+def decode(first_span, own, other, queries, w_key, w_value, w_out, carried=(), blocks=None, after=()):
+    split = blocks is not None
+    width = queries.shape[1]
     count = own.shape[0]
+    tokens = count * CH
     tile = SPANS_STEP * CH
     first = first_span // SPANS_STEP
     rows = SPANS_STEP * KNB * NLEN
-    block = pl.BlockSpec((SPANS_STEP, NLEN, E), lambda i: (i, 0, 0))
-    operands = [own, other, queries, w_key, w_value, w_out, *carried]
-    specs = [
-        block,
-        block,
-        pl.BlockSpec((tile, width), lambda i: (first + i, 0)),
-        once((E, width)),
-        once((E, width)),
-        once((width, D)),
-    ] + [once((1, NLEN, E))] * len(carried)
-    aliases = {}
-    if terms is not None:
-        aliases = {len(operands): 0}
-        operands.append(terms)
-        specs.append(pl.BlockSpec(memory_space=pl.ANY))
+    block = pl.BlockSpec((SPANS_STEP, NLEN, E), lambda i, *_: (i, 0, 0))
+    if split:
+        out_shape = [jax.ShapeDtypeStruct((4, tokens, width), BF16)] * 2
+        out_specs = [pl.BlockSpec((4, tile, width), lambda i, *_: (0, i, 0))] * 2
+    else:
+        out_shape = pltpu.HBM((tokens, D), BF16)
+        out_specs = pl.BlockSpec((tile, D), lambda i, *_: (i, 0))
     return pl.pallas_call(
-        lambda *refs: decode_kernel(len(carried) > 0, *refs),
-        out_shape=jax.ShapeDtypeStruct((tokens, D), BF16),
-        grid=(count // SPANS_STEP,),
-        in_specs=specs,
-        out_specs=pl.BlockSpec((tile, D), lambda i: (first + i, 0)),
-        scratch_shapes=[
-            pltpu.VMEM((rows, E), BF16),
-            pltpu.VMEM((tile, width), BF16),
-            pltpu.VMEM((rows, width), BF16),
-            pltpu.VMEM((rows, width), BF16),
-        ],
-        input_output_aliases=aliases,
+        lambda *refs: decode_kernel(len(carried) > 0, split, *refs),
+        out_shape=out_shape,
+        grid_spec=pltpu.PrefetchScalarGridSpec(
+            num_scalar_prefetch=int(split),
+            grid=(count // SPANS_STEP,),
+            in_specs=[
+                block,
+                block,
+                pl.BlockSpec((tile, width), lambda i, *_: (first + i, 0)),
+                once((E, width)),
+                once((E, width)),
+                once((width, D)),
+            ]
+            + [once((1, NLEN, E))] * len(carried)
+            + [pl.BlockSpec(memory_space=pl.ANY)] * len(after),
+            out_specs=out_specs,
+            scratch_shapes=[
+                pltpu.VMEM((rows, E), BF16),
+                pltpu.VMEM((tile, width), BF16),
+                pltpu.VMEM((rows, width), BF16),
+                pltpu.VMEM((rows, width), BF16),
+            ],
+        ),
         compiler_params=pltpu.CompilerParams(
-            dimension_semantics=("arbitrary",), vmem_limit_bytes=40 << 20
+            dimension_semantics=("arbitrary",), vmem_limit_bytes=(60 << 20) if split else VMEM_LIMIT
         ),
         cost_estimate=pl.CostEstimate(
             flops=4 * count * KNB * NLEN * E * width + 2 * count * CH * width * D,
@@ -329,7 +348,7 @@
             transcendentals=count * CH * KNB * NLEN * (width // HD),
         ),
         name="decode",
-    )(*operands)
+    )(*([blocks] if split else []), own, other, queries, w_key, w_value, w_out, *carried, *after)
 
 
 def body(
@@ -364,6 +383,7 @@
     picked = lax.dynamic_slice_in_dim(by_owner, store_rank * per_owner, per_owner)
     sources = nbr_table[flat_ids[picked] % blocks_here]
     gathered = lax.all_gather(sources, "store", axis=0, tiled=True)
+    gathered = pltpu.with_memory_space_constraint(gathered, pltpu.HBM)
 
     pair_at = jnp.minimum(store_rank, PAIRS - 1) * 128
     weight = jnp.concatenate(
@@ -375,15 +395,15 @@
     )
     half = weight.shape[0] // 2
     a_four = jnp.stack(around(weight[:half], side, False))
-    b_four = jnp.stack(around(weight[half:], side, True))
     a_parts = around(a_four, side, True)
-    b_parts = around(b_four, side, False)
+    b_rows = jnp.broadcast_to(weight[half:][None], (seq_count, half, 256))
+    b_all = lax.all_to_all(b_rows, "seq", 0, 0, tiled=True)
     y_at, z_at = seq_rank // side, seq_rank % side
     rel = jnp.array(REL, jnp.int32)
     from_rank = (
         side * ((y_at + rel + side) % side)[:, None] + ((z_at + rel + side) % side)[None, :]
     ).reshape(-1)
-    cond = cond_rows(hidden, a_parts, b_parts, from_rank).reshape(span_count, CH, 256)
+    cond = cond_rows(hidden, a_parts, b_all, from_rank).reshape(span_count, CH, 256)
     own_lane = around_x(cond, chips)
     conds = own_lane + [swap_cores(block) for block in own_lane]
     chip, core = store_rank // 2, store_rank % 2
@@ -394,20 +414,49 @@
     mine = jnp.sum(
         jnp.where(slot[None, :] == (KNB * spans + core)[:, None], pos[None, :], 0), axis=1
     )
-    enc_q = enc_queries(mine, gathered, enc_query)
     queries = dot(hidden, w_query).astype(BF16)
+    enc_q = enc_queries(mine, gathered, enc_query, queries)
     part = span_count // 2
-    high = encode(0, part, mine, pairs, enc_q, gathered, conds, enc_out)
-    low = encode(part, part, mine, pairs, enc_q, gathered, conds, enc_out)
+    low = encode(0, part, mine, pairs, enc_q, gathered, conds, enc_out)
+    low_other = swap_cores(low)
+    carried, carried_other = (
+        lax.ppermute(
+            low[:1],
+            ("seq", "store"),
+            [
+                (i * store_count + k, (i + 1) * store_count + (k ^ flip))
+                for i in range(seq_count - 1)
+                for k in range(store_count)
+            ],
+        )
+        for flip in range(2)
+    )
+    high = encode(part, part, mine, pairs, enc_q, gathered, conds, enc_out, after=(low,))
     high_other = swap_cores(high)
-    low_other = swap_cores(low)
-    carried = lax.ppermute(low[:1], "seq", [(i, i + 1) for i in range(seq_count - 1)])
-    carried_other = swap_cores(carried)
-    terms = decode(part, high, high_other, (), None, queries, w_key, w_value, w_out)
     terms = decode(
-        0, low, low_other, (carried, carried_other), terms, queries, w_key, w_value, w_out
-    )
-    return lax.psum_scatter(terms, "store", scatter_dimension=1, tiled=True)
+        0,
+        low,
+        low_other,
+        queries,
+        w_key,
+        w_value,
+        w_out,
+        carried=(carried, carried_other),
+        after=(high,),
+    )
+    low_out = lax.psum_scatter(terms, "store", scatter_dimension=1, tiled=True)
+    kept, given = decode(
+        part, high, high_other, queries, w_key, w_value, w_out, blocks=pairs, after=(terms,)
+    )
+    taken = swap_cores(given)
+    sums = [kept[j].astype(F32) + taken[j].astype(F32) for j in range(4)]
+    high_out = sums[0]
+    for j in range(1, 4):
+        route = [
+            (2 * x + k, 2 * ((x + REL[j]) % chips) + k) for x in range(chips) for k in range(2)
+        ]
+        high_out = high_out + lax.ppermute(sums[j].astype(BF16), "store", route).astype(F32)
+    return jnp.concatenate([low_out, high_out.astype(BF16)], axis=0)
 
 
 def solution(mesh):

time: 207 us -> 203 us (0.981)
  waiting for transfers between devices: 81.5 us -> 73 us
  other arithmetic: 1.5 us -> 6.79 us
    reduce_scatter x1, waiting for transfers between devices: 51.3 us -> 0.02 us  [body(): low_out = lax.psum_scatter(terms, 'store', scatter_dimension=1, tiled=True)]
    ppermute x1 -> x5, waiting for transfers between devices: 3.14 us -> 30.5 us  [the longest x3 27.9 us: body(): lax.ppermute(sums[j].astype(BF16), 'store', route).astype(F32)]
    all_to_all x0 -> x1, starting transfers between devices: none -> 7.85 us  [body(): b_all = lax.all_to_all(b_rows, 'seq', 0, 0, tiled=True)]
    ppermute x7, waiting for transfers between devices: 0.02 us -> 7.8 us  [swap_cores(): return lax.ppermute(block, 'store', [(i, i ^ 1) for i in range(count)])]
    ppermute x12 -> x6, waiting for transfers between devices: 16 us -> 23.8 us  [around(): got.append(lax.ppermute(block, 'seq', route))]
    ppermute x12 -> x6, starting transfers between devices: 15.7 us -> 8.35 us  [around(): got.append(lax.ppermute(block, 'seq', route))]
    ppermute x7, starting transfers between devices: 13.4 us -> 8.76 us  [swap_cores(): return lax.ppermute(block, 'store', [(i, i ^ 1) for i in range(count)])]
    ppermute x1 -> x5, starting transfers between devices: 3.91 us -> 8.16 us  [the longest x2 5.06 us: body(): lax.ppermute(low[:1], ('seq', 'store'), [(i * store_count + k, (i + 1) *...]
  transfers between devices with their start and end apart: 25 -> 24, of which waited for: 11 -> 12; matrix products, arithmetic and copies ran while one was open for 4% -> 6% of each run, Pallas kernels for 14% -> 16%
where the time goes in v3:
time: 203 us; the launch traced here: 202 us
  waiting for transfers between devices  73 us (36%)
  Pallas kernels  50.4 us (25%)
  starting transfers between devices  37.3 us (18%)
  local copies, waits for them, and re-layouts  15.8 us (8%)
  between operations  13.7 us (7%)
  other arithmetic  6.79 us (3%)
  matrix products  5.46 us (3%)
    ppermute x3, waiting for transfers between devices, body(): lax.ppermute(sums[j].astype(BF16), 'store', route).astype(F32)  27.9 us
    pallas_call x2, Pallas kernels, decode(): pl.pallas_call(lambda *refs: decode_kernel(len(carried) > 0, split, *refs...  23.9 us
    ppermute x6, waiting for transfers between devices, around(): got.append(lax.ppermute(block, 'seq', route))  23.8 us
    pallas_call x2, Pallas kernels, encode(): pl.pallas_call(encode_kernel, out_shape=(pltpu.HBM if after else jax.Shap...  15.9 us
    unnamed x29, local copies, waits for them, and re-layouts  11.4 us
    ppermute x3, waiting for transfers between devices, around_x(): got.append(lax.ppermute(block, 'store', route))  10.9 us
    ppermute x7, starting transfers between devices, swap_cores(): return lax.ppermute(block, 'store', [(i, i ^ 1) for i in range(count)])  8.76 us
    ppermute x6, starting transfers between devices, around(): got.append(lax.ppermute(block, 'seq', route))  8.35 us
  transfers between devices with their start and end apart: 24, of which 12 were waited for; matrix products, arithmetic and copies ran while one was open for 6% of the time, Pallas kernels for 16%

profile of v3, /device:TPU:9, one launch (start us, length us, event | category | flops | bytes accessed | tf_op | source)
XLA Modules:
  0.0 202.4 jit_solution(12202223607918588365)
XLA Ops:
  6.5 0.9 copy.16
  7.9 0.7 broadcast_add_fusion.1
  9.3 1.6 gather_fusion.1
  10.9 0.9 constant_dynamic-slice_fusion
  11.8 1.1 broadcast_in_dim.49
  12.9 7.8 %all-to-all-start = ((bf16[16,128,256]{2,1,0:T(8,128)(2,1)}), bf16[16,128,256]{2,1,0:T(8,128)(2,1)S(1)}, u32[]{:S(2)}, u32[]{:S(2)}) async-start(bf16[16,128,256]{2,1,0:T(8,128)(2,1)} %broadcast_in_dim.49), calls=%async_computation | async-start | bytes 2097152 | tf_op jit(solution)/shard_map/all_to_all | solution.py:400
  20.8 2.8 %collective-permute-start.2 = (bf16[128,256]{1,0:T(8,128)(2,1)S(1)}, bf16[128,256]{1,0:T(8,128)(2,1)S(1)}, u32[]{:S(2)}, u32[]{:S(2)}) collective-permute-start(bf16[128,256]{1,0:T(8,128)(2,1)S(1)} %get-tuple-element.15), channel_id=1, source_target_pairs={{0,16},{8,24},{16,0},{24,8},{32,48},{40,56},{48,32},{56,40},{64,80... | collective-permute-start | bytes 196616 | tf_op jit(solution)/shard_map/ppermute | solution.py:44
  23.5 0.9 collective-permute-start.1
  25.0 8.2 %collective-permute-done.2 = bf16[128,256]{1,0:T(8,128)(2,1)S(1)} collective-permute-done((bf16[128,256]{1,0:T(8,128)(2,1)S(1)}, bf16[128,256]{1,0:T(8,128)(2,1)S(1)}, u32[]{:S(2)}, u32[]{:S(2)}) %collective-permute-start.2) | collective-permute-done | bytes 65568 | tf_op jit(solution)/shard_map/ppermute | solution.py:44
  33.2 3.5 %collective-permute-done.1 = bf16[128,256]{1,0:T(8,128)(2,1)S(1)} collective-permute-done((bf16[128,256]{1,0:T(8,128)(2,1)S(1)}, bf16[128,256]{1,0:T(8,128)(2,1)S(1)}, u32[]{:S(2)}, u32[]{:S(2)}) %collective-permute-start.1) | collective-permute-done | bytes 65568 | tf_op jit(solution)/shard_map/ppermute | solution.py:44
  36.7 0.8 collective-permute-done
  37.5 2.7 %collective-permute-start.5 = (bf16[4,128,256]{2,1,0:T(8,128)(2,1)S(1)}, bf16[4,128,256]{2,1,0:T(8,128)(2,1)S(1)}, u32[]{:S(2)}, u32[]{:S(2)}) collective-permute-start(bf16[4,128,256]{2,1,0:T(8,128)(2,1)S(1)} %pad_maximum_fusion.1.refs_0_), channel_id=1, source_target_pairs={{0,64},{8,72},{16,80},{24,88},{32,96},{40,104},{48,112},{56,120},{... | collective-permute-start | bytes 786440 | tf_op jit(solution)/shard_map/ppermute | solution.py:44
  40.2 0.9 collective-permute-start.4
  41.8 3.7 %collective-permute-done.5.refs_3_ = bf16[4,128,256]{2,1,0:T(8,128)(2,1)S(1)} collective-permute-done((bf16[4,128,256]{2,1,0:T(8,128)(2,1)S(1)}, bf16[4,128,256]{2,1,0:T(8,128)(2,1)S(1)}, u32[]{:S(2)}, u32[]{:S(2)}) %collective-permute-start.5) | collective-permute-done | bytes 262176 | tf_op jit(solution)/shard_map/ppermute | solution.py:44
  45.6 7.5 %collective-permute-done.4.refs_2_ = bf16[4,128,256]{2,1,0:T(8,128)(2,1)S(1)} collective-permute-done((bf16[4,128,256]{2,1,0:T(8,128)(2,1)S(1)}, bf16[4,128,256]{2,1,0:T(8,128)(2,1)S(1)}, u32[]{:S(2)}, u32[]{:S(2)}) %collective-permute-start.4) | collective-permute-done | bytes 262176 | tf_op jit(solution)/shard_map/ppermute | solution.py:44
  53.1 3.5 %copy-done.2 = bf16[1024,4096]{1,0:T(8,128)(2,1)S(1)} copy-done((bf16[1024,4096]{1,0:T(8,128)(2,1)S(1)}, bf16[1024,4096]{1,0:T(8,128)(2,1)}, u32[]{:S(2)}) %copy-start.2) | copy-done | bytes 8388632
  56.6 3.1 %cond_rows.1 = bf16[1024,256]{1,0:T(8,128)(2,1)S(1)} custom-call(s32[16]{0:T(128)S(1)} %add.212.src_ref, bf16[1024,4096]{1,0:T(8,128)(2,1)S(1)} %copy-done.2, bf16[4,128,256]{2,1,0:T(8,128)(2,1)S(1)} %pad_maximum_fusion.1.refs_0_, bf16[4,128,256]{2,1,0:T(8,128)(2,1)S(1)} %collective-permute-done.3.refs_1_, ...), custom_call_target="tpu_custom_call" | custom-call | flops 2147483648 | bytes 12582912 | tf_op jit(solution)/shard_map/cond_rows/pallas_call | solution.py:92
  59.7 2.7 %collective-permute-start.8 = (bf16[16,64,256]{2,1,0:T(8,128)(2,1)S(1)}, bf16[16,64,256]{2,1,0:T(8,128)(2,1)S(1)}, u32[]{:S(2)}, u32[]{:S(2)}) collective-permute-start(bf16[16,64,256]{2,1,0:T(8,128)(2,1)S(1)} %bitcast.25), channel_id=1, source_target_pairs={{0,4},{1,5},{2,6},{3,7},{4,0},{5,1},{6,2},{7,3},{8,12},{9,13},{10,... | collective-permute-start | bytes 1572872 | tf_op jit(solution)/shard_map/ppermute | solution.py:54
  62.4 0.9 collective-permute-start.7
  63.9 5.5 %convolution_convert_fusion.refs_5_.refs_2_.refs_3_ = bf16[1024,512]{1,0:T(8,128)(2,1)} fusion(bf16[1024,4096]{1,0:T(8,128)(2,1)S(1)} %copy-done.2, bf16[4096,512]{1,0:T(8,128)(2,1)S(1)} %copy-done.12), kind=kOutput, calls=%fused_computation.2 | convolution fusion | flops 4295491584 | bytes 13631488 | tf_op jit(solution)/shard_map/dot_general | solution.py:29
  69.4 1.9 collective-permute-start.9
  71.2 2.6 %collective-permute-done.8.refs_7_ = bf16[16,64,256]{2,1,0:T(8,128)(2,1)S(1)} collective-permute-done((bf16[16,64,256]{2,1,0:T(8,128)(2,1)S(1)}, bf16[16,64,256]{2,1,0:T(8,128)(2,1)S(1)}, u32[]{:S(2)}, u32[]{:S(2)}) %collective-permute-start.8) | collective-permute-done | bytes 524320 | tf_op jit(solution)/shard_map/ppermute | solution.py:54
  73.8 3.4 %collective-permute-start.12 = (bf16[16,64,256]{2,1,0:T(8,128)(2,1)S(1)}, bf16[16,64,256]{2,1,0:T(8,128)(2,1)}, u32[]{:S(2)}, u32[]{:S(2)}) collective-permute-start(bf16[16,64,256]{2,1,0:T(8,128)(2,1)S(1)} %collective-permute-done.8.refs_7_), channel_id=1, source_target_pairs={{0,1},{1,0},{2,3},{3,2},{4,5},{5,4},{6,7},{7,6},{8,9},{9,8},{10,11... | collective-permute-start | bytes 1572872 | tf_op jit(solution)/shard_map/ppermute | solution.py:60
  77.1 8.3 %collective-permute-done.7.refs_6_ = bf16[16,64,256]{2,1,0:T(8,128)(2,1)S(1)} collective-permute-done((bf16[16,64,256]{2,1,0:T(8,128)(2,1)S(1)}, bf16[16,64,256]{2,1,0:T(8,128)(2,1)S(1)}, u32[]{:S(2)}, u32[]{:S(2)}) %collective-permute-start.7) | collective-permute-done | bytes 524320 | tf_op jit(solution)/shard_map/ppermute | solution.py:54
  85.4 1.6 collective-permute-start.11
  87.3 1.5 copy-done.6
  88.8 1.2 copy-done.7
  90.1 7.5 %enc_queries.1.refs_12_ = bf16[16,128,896]{2,1,0:T(8,128)(2,1)S(1)} custom-call(s32[16]{0:T(128)S(1)} %select_reduce_fusion.1.pos_ref, bf16[32,128,896]{2,1,0:T(8,128)(2,1)} %all-gather.3.cloned.1.call-done.refs_0_.refs_1_.refs_2_.refs_3_, bf16[32,128,896]{2,1,0:T(8,128)(2,1)} %all-gather.3.cloned.1.call-done.refs_0_.refs_1_.refs_2_.refs_3_, ...), custom_call_target="tpu_custom_call" | custom-call | flops 3288334336 | bytes 10485760 | tf_op jit(solution)/shard_map/enc_queries/pallas_call | solution.py:132
  97.6 7.5 %encode.2.refs_14_.refs_0_ = bf16[8,128,896]{2,1,0:T(8,128)(2,1)S(1)} custom-call(s32[16]{0:T(128)S(1)} %select_reduce_fusion.1.pos_ref, s32[8]{0:T(128)S(1)} %pad_add_fusion.pair_ref.refs_0_, bf16[32,128,896]{2,1,0:T(8,128)(2,1)} %all-gather.3.cloned.1.call-done.refs_0_.refs_1_.refs_2_.refs_3_, ...), custom_call_target="tpu_custom_call" | custom-call | flops 2466250752 | bytes 8388608 | tf_op jit(solution)/shard_map/encode/pallas_call | solution.py:207
  105.8 2.3 %collective-permute-start.15 = (bf16[1,128,896]{2,1,0:T(8,128)(2,1)S(1)}, bf16[1,128,896]{2,1,0:T(8,128)(2,1)S(1)}, u32[]{:S(2)}, u32[]{:S(2)}) collective-permute-start(bf16[1,128,896]{2,1,0:T(8,128)(2,1)S(1)} %slice.51), channel_id=1, source_target_pairs={{0,9},{1,8},{2,11},{3,10},{4,13},{5,12},{6,15},{7,14},{8,17},{9,16... | collective-permute-start | bytes 688136 | tf_op jit(solution)/shard_map/ppermute | solution.py:423
  108.1 2.7 %collective-permute-start.14 = (bf16[1,128,896]{2,1,0:T(8,128)(2,1)S(1)}, bf16[1,128,896]{2,1,0:T(8,128)(2,1)S(1)}, u32[]{:S(2)}, u32[]{:S(2)}) collective-permute-start(bf16[1,128,896]{2,1,0:T(8,128)(2,1)S(1)} %slice.51), channel_id=1, source_target_pairs={{0,8},{1,9},{2,10},{3,11},{4,12},{5,13},{6,14},{7,15},{8,16},{9,17... | collective-permute-start | bytes 688136 | tf_op jit(solution)/shard_map/ppermute | solution.py:423
  110.8 8.4 %encode.3.refs_8_.refs_1_ = bf16[8,128,896]{2,1,0:T(8,128)(2,1)} custom-call(s32[16]{0:T(128)S(1)} %select_reduce_fusion.1.pos_ref, s32[8]{0:T(128)S(1)} %pad_add_fusion.pair_ref.refs_0_, bf16[32,128,896]{2,1,0:T(8,128)(2,1)} %all-gather.3.cloned.1.call-done.refs_0_.refs_1_.refs_2_.refs_3_, ...), custom_call_target="tpu_custom_call" | custom-call | flops 2466250752 | bytes 8388608 | tf_op jit(solution)/shard_map/encode/pallas_call | solution.py:207
  119.2 2.6 %collective-permute-done.14.refs_6_ = bf16[1,128,896]{2,1,0:T(8,128)(2,1)S(1)} collective-permute-done((bf16[1,128,896]{2,1,0:T(8,128)(2,1)S(1)}, bf16[1,128,896]{2,1,0:T(8,128)(2,1)S(1)}, u32[]{:S(2)}, u32[]{:S(2)}) %collective-permute-start.14) | collective-permute-done | bytes 229408 | tf_op jit(solution)/shard_map/ppermute | solution.py:423
  121.9 1.5 copy-done.4
  123.4 9.7 %decode.2.refs_7_ = bf16[512,4096]{1,0:T(8,128)(2,1)} custom-call(bf16[8,128,896]{2,1,0:T(8,128)(2,1)S(1)} %encode.2.refs_14_.refs_0_, bf16[8,128,896]{2,1,0:T(8,128)(2,1)S(1)} %collective-permute-done.13.refs_1_, bf16[1024,512]{1,0:T(8,128)(2,1)S(1)} %copy-done.7, bf16[896,512]{1,0:T(8,128)(2,1)S(1)} %copy-done.10, bf16[896,512]{1,0:T(8,128)(2,1)S(1)} %copy-done.11, ...), custom_call_target="tpu_custom_call" | custom-call | flops 5905580032 | bytes 12582912 | tf_op jit(solution)/shard_map/decode/pallas_call | solution.py:318
  133.1 1.5 copy-done.5
  134.5 1.0 collective-permute-start.16
  135.6 3.4 %collective-permute-done.16.refs_2_ = bf16[8,128,896]{2,1,0:T(8,128)(2,1)S(1)} collective-permute-done((bf16[8,128,896]{2,1,0:T(8,128)(2,1)S(1)}, bf16[8,128,896]{2,1,0:T(8,128)(2,1)S(1)}, u32[]{:S(2)}, u32[]{:S(2)}) %collective-permute-start.16) | collective-permute-done | bytes 1835040 | tf_op jit(solution)/shard_map/ppermute | solution.py:60
  139.0 1.3 copy-done.13
  140.2 14.2 %decode.3 = (bf16[4,512,512]{2,1,0:T(8,128)(2,1)}, bf16[4,512,512]{2,1,0:T(8,128)(2,1)}) custom-call(s32[8]{0:T(128)} %copy-done.8, bf16[8,128,896]{2,1,0:T(8,128)(2,1)} %encode.3.refs_8_.refs_1_, bf16[8,128,896]{2,1,0:T(8,128)(2,1)} %copy-done.13, bf16[1024,512]{1,0:T(8,128)(2,1)} %convolution_convert_fusion.refs_5_.refs_2_.refs_3_, ...), custom_call_target="tpu_custom_call" | custom-call | flops 5905580032 | bytes 12582912 | tf_op jit(solution)/shard_map/decode/pallas_call | solution.py:318
  154.8 4.4 %collective-permute-done.17 = bf16[4,512,512]{2,1,0:T(8,128)(2,1)S(1)} collective-permute-done((bf16[4,512,512]{2,1,0:T(8,128)(2,1)}, bf16[4,512,512]{2,1,0:T(8,128)(2,1)S(1)}, u32[]{:S(2)}, u32[]{:S(2)}) %collective-permute-start.17) | collective-permute-done | bytes 2097184 | tf_op jit(solution)/shard_map/ppermute | solution.py:60
  159.2 1.9 fusion.3
  161.0 2.0 %collective-permute-start.18 = (bf16[512,512]{1,0:T(8,128)(2,1)S(1)}, bf16[512,512]{1,0:T(8,128)(2,1)S(1)}, u32[]{:S(2)}, u32[]{:S(2)}) collective-permute-start(bf16[512,512]{1,0:T(8,128)(2,1)S(1)} %get-tuple-element.11), channel_id=1, source_target_pairs={{0,6},{1,7},{2,0},{3,1},{4,2},{5,3},{6,4},{7,5},{8,14},{9,15},{10,... | collective-permute-start | bytes 1572872 | tf_op jit(solution)/shard_map/ppermute | solution.py:458
  163.1 0.9 collective-permute-start.20
  164.1 25.4 %collective-permute-done.18 = bf16[512,512]{1,0:T(8,128)(2,1)S(1)} collective-permute-done((bf16[512,512]{1,0:T(8,128)(2,1)S(1)}, bf16[512,512]{1,0:T(8,128)(2,1)S(1)}, u32[]{:S(2)}, u32[]{:S(2)}) %collective-permute-start.18) | collective-permute-done | bytes 524320 | tf_op jit(solution)/shard_map/ppermute | solution.py:458
  189.5 2.5 %collective-permute-done.19 = bf16[512,512]{1,0:T(8,128)(2,1)S(1)} collective-permute-done((bf16[512,512]{1,0:T(8,128)(2,1)S(1)}, bf16[512,512]{1,0:T(8,128)(2,1)S(1)}, u32[]{:S(2)}, u32[]{:S(2)}) %collective-permute-start.19) | collective-permute-done | bytes 524320 | tf_op jit(solution)/shard_map/ppermute | solution.py:458
  192.0 1.4 fusion.2
  193.4 2.1 %pad_maximum_fusion = bf16[1024,512]{1,0:T(8,128)(2,1)} fusion(bf16[512,512]{1,0:T(8,128)(2,1)S(1)} %fusion.2, bf16[512,512]{1,0:T(8,128)(2,1)} %reduce-scatter.2.cloned.1.call-done), kind=kLoop, calls=%fused_computation.3 | loop fusion | flops 2097152 | bytes 2097152 | tf_op jit(solution)/shard_map/concatenate | solution.py:459
  (62 shorter events, 4.6 us)
Async XLA Ops:
  6.5 2.7 %copy-start = (bf16[8,128,896]{2,1,0:T(8,128)(2,1)S(1)}, bf16[8,128,896]{2,1,0:T(8,128)(2,1)}, u32[]{:S(2)}) copy-start(bf16[8,128,896]{2,1,0:T(8,128)(2,1)} %param.13) | copy-start | bytes 5505028
  6.5 80.7 %all-gather.3.cloned.1.call-start = ((), (), s32[]{:S(2)}) async-start(), calls=%async_computation.3 | async-start | bytes 8257536 | tf_op jit(solution)/shard_map/all_gather | solution.py:385
  12.9 40.2 %all-to-all-start = ((bf16[16,128,256]{2,1,0:T(8,128)(2,1)}), bf16[16,128,256]{2,1,0:T(8,128)(2,1)S(1)}, u32[]{:S(2)}, u32[]{:S(2)}) async-start(bf16[16,128,256]{2,1,0:T(8,128)(2,1)} %broadcast_in_dim.49), calls=%async_computation | async-start | bytes 2097152 | tf_op jit(solution)/shard_map/all_to_all | solution.py:400
  20.7 172.7 %reduce-scatter.2.cloned.1.call-start = ((), (), s32[]{:S(2)}) async-start(), calls=%async_computation.2 | async-start | bytes 4718592 | tf_op jit(solution)/shard_map/reduce_scatter | solution.py:447
  20.8 12.4 %collective-permute-start.2 = (bf16[128,256]{1,0:T(8,128)(2,1)S(1)}, bf16[128,256]{1,0:T(8,128)(2,1)S(1)}, u32[]{:S(2)}, u32[]{:S(2)}) collective-permute-start(bf16[128,256]{1,0:T(8,128)(2,1)S(1)} %get-tuple-element.15), channel_id=1, source_target_pairs={{0,16},{8,24},{16,0},{24,8},{32,48},{40,56},{48,32},{56,40},{64,80... | collective-permute-start | bytes 196616 | tf_op jit(solution)/shard_map/ppermute | solution.py:44
  23.5 13.1 %collective-permute-start.1 = (bf16[128,256]{1,0:T(8,128)(2,1)S(1)}, bf16[128,256]{1,0:T(8,128)(2,1)S(1)}, u32[]{:S(2)}, u32[]{:S(2)}) collective-permute-start(bf16[128,256]{1,0:T(8,128)(2,1)S(1)} %get-tuple-element.15), channel_id=1, source_target_pairs={{0,24},{8,0},{16,8},{24,16},{32,56},{40,32},{48,40},{56,48},{64,88... | collective-permute-start | bytes 196616 | tf_op jit(solution)/shard_map/ppermute | solution.py:44
  24.4 13.1 %collective-permute-start = (bf16[128,256]{1,0:T(8,128)(2,1)S(1)}, bf16[128,256]{1,0:T(8,128)(2,1)S(1)}, u32[]{:S(2)}, u32[]{:S(2)}) collective-permute-start(bf16[128,256]{1,0:T(8,128)(2,1)S(1)} %get-tuple-element.15), channel_id=1, source_target_pairs={{0,8},{8,16},{16,24},{24,0},{32,40},{40,48},{48,56},{56,32},{64,72... | collective-permute-start | bytes 196616 | tf_op jit(solution)/shard_map/ppermute | solution.py:44
  37.5 8.0 %collective-permute-start.5 = (bf16[4,128,256]{2,1,0:T(8,128)(2,1)S(1)}, bf16[4,128,256]{2,1,0:T(8,128)(2,1)S(1)}, u32[]{:S(2)}, u32[]{:S(2)}) collective-permute-start(bf16[4,128,256]{2,1,0:T(8,128)(2,1)S(1)} %pad_maximum_fusion.1.refs_0_), channel_id=1, source_target_pairs={{0,64},{8,72},{16,80},{24,88},{32,96},{40,104},{48,112},{56,120},{... | collective-permute-start | bytes 786440 | tf_op jit(solution)/shard_map/ppermute | solution.py:44
  40.2 12.9 %collective-permute-start.4 = (bf16[4,128,256]{2,1,0:T(8,128)(2,1)S(1)}, bf16[4,128,256]{2,1,0:T(8,128)(2,1)S(1)}, u32[]{:S(2)}, u32[]{:S(2)}) collective-permute-start(bf16[4,128,256]{2,1,0:T(8,128)(2,1)S(1)} %pad_maximum_fusion.1.refs_0_), channel_id=1, source_target_pairs={{0,96},{8,104},{16,112},{24,120},{32,0},{40,8},{48,16},{56,24},{64... | collective-permute-start | bytes 786440 | tf_op jit(solution)/shard_map/ppermute | solution.py:44
  41.1 11.9 %collective-permute-start.3 = (bf16[4,128,256]{2,1,0:T(8,128)(2,1)S(1)}, bf16[4,128,256]{2,1,0:T(8,128)(2,1)S(1)}, u32[]{:S(2)}, u32[]{:S(2)}) collective-permute-start(bf16[4,128,256]{2,1,0:T(8,128)(2,1)S(1)} %pad_maximum_fusion.1.refs_0_), channel_id=1, source_target_pairs={{0,32},{8,40},{16,48},{24,56},{32,64},{40,72},{48,80},{56,88},{64,... | collective-permute-start | bytes 786440 | tf_op jit(solution)/shard_map/ppermute | solution.py:44
  53.1 3.5 %copy-start.2 = (bf16[1024,4096]{1,0:T(8,128)(2,1)S(1)}, bf16[1024,4096]{1,0:T(8,128)(2,1)}, u32[]{:S(2)}) copy-start(bf16[1024,4096]{1,0:T(8,128)(2,1)} %hidden_ref.1) | copy-start | bytes 25165828
  56.6 7.3 %copy-start.12 = (bf16[4096,512]{1,0:T(8,128)(2,1)S(1)}, bf16[4096,512]{1,0:T(8,128)(2,1)}, u32[]{:S(2)}) copy-start(bf16[4096,512]{1,0:T(8,128)(2,1)} %param.15) | copy-start | bytes 12582916
  59.7 14.1 %collective-permute-start.8 = (bf16[16,64,256]{2,1,0:T(8,128)(2,1)S(1)}, bf16[16,64,256]{2,1,0:T(8,128)(2,1)S(1)}, u32[]{:S(2)}, u32[]{:S(2)}) collective-permute-start(bf16[16,64,256]{2,1,0:T(8,128)(2,1)S(1)} %bitcast.25), channel_id=1, source_target_pairs={{0,4},{1,5},{2,6},{3,7},{4,0},{5,1},{6,2},{7,3},{8,12},{9,13},{10,... | collective-permute-start | bytes 1572872 | tf_op jit(solution)/shard_map/ppermute | solution.py:54
  62.4 23.0 %collective-permute-start.7 = (bf16[16,64,256]{2,1,0:T(8,128)(2,1)S(1)}, bf16[16,64,256]{2,1,0:T(8,128)(2,1)S(1)}, u32[]{:S(2)}, u32[]{:S(2)}) collective-permute-start(bf16[16,64,256]{2,1,0:T(8,128)(2,1)S(1)} %bitcast.26), channel_id=1, source_target_pairs={{0,6},{1,7},{2,0},{3,1},{4,2},{5,3},{6,4},{7,5},{8,14},{9,15},{10,... | collective-permute-start | bytes 1572872 | tf_op jit(solution)/shard_map/ppermute | solution.py:54
  63.3 23.7 %collective-permute-start.6 = (bf16[16,64,256]{2,1,0:T(8,128)(2,1)S(1)}, bf16[16,64,256]{2,1,0:T(8,128)(2,1)}, u32[]{:S(2)}, u32[]{:S(2)}) collective-permute-start(bf16[16,64,256]{2,1,0:T(8,128)(2,1)S(1)} %bitcast.27), channel_id=1, source_target_pairs={{0,2},{1,3},{2,4},{3,5},{4,6},{5,7},{6,0},{7,1},{8,10},{9,11},{10,... | collective-permute-start | bytes 1572872 | tf_op jit(solution)/shard_map/ppermute | solution.py:54
  69.4 28.2 %collective-permute-start.9 = (bf16[16,64,256]{2,1,0:T(8,128)(2,1)S(1)}, bf16[16,64,256]{2,1,0:T(8,128)(2,1)}, u32[]{:S(2)}, u32[]{:S(2)}) collective-permute-start(bf16[16,64,256]{2,1,0:T(8,128)(2,1)S(1)} %bitcast.28), channel_id=1, source_target_pairs={{0,1},{1,0},{2,3},{3,2},{4,5},{5,4},{6,7},{7,6},{8,9},{9,8},{10,11... | collective-permute-start | bytes 1572872 | tf_op jit(solution)/shard_map/ppermute | solution.py:60
  73.8 23.8 %collective-permute-start.12 = (bf16[16,64,256]{2,1,0:T(8,128)(2,1)S(1)}, bf16[16,64,256]{2,1,0:T(8,128)(2,1)}, u32[]{:S(2)}, u32[]{:S(2)}) collective-permute-start(bf16[16,64,256]{2,1,0:T(8,128)(2,1)S(1)} %collective-permute-done.8.refs_7_), channel_id=1, source_target_pairs={{0,1},{1,0},{2,3},{3,2},{4,5},{5,4},{6,7},{7,6},{8,9},{9,8},{10,11... | collective-permute-start | bytes 1572872 | tf_op jit(solution)/shard_map/ppermute | solution.py:60
  85.4 12.1 %collective-permute-start.11 = (bf16[16,64,256]{2,1,0:T(8,128)(2,1)S(1)}, bf16[16,64,256]{2,1,0:T(8,128)(2,1)}, u32[]{:S(2)}, u32[]{:S(2)}) collective-permute-start(bf16[16,64,256]{2,1,0:T(8,128)(2,1)S(1)} %collective-permute-done.7.refs_6_), channel_id=1, source_target_pairs={{0,1},{1,0},{2,3},{3,2},{4,5},{5,4},{6,7},{7,6},{8,9},{9,8},{10,11... | collective-permute-start | bytes 1572872 | tf_op jit(solution)/shard_map/ppermute | solution.py:60
  87.0 10.6 %collective-permute-start.10 = (bf16[16,64,256]{2,1,0:T(8,128)(2,1)}, bf16[16,64,256]{2,1,0:T(8,128)(2,1)}, u32[]{:S(2)}, u32[]{:S(2)}) collective-permute-start(bf16[16,64,256]{2,1,0:T(8,128)(2,1)} %collective-permute-done.6.refs_5_), channel_id=1, source_target_pairs={{0,1},{1,0},{2,3},{3,2},{4,5},{5,4},{6,7},{7,6},{8,9},{9,8},{10,11... | collective-permute-start | bytes 1572872 | tf_op jit(solution)/shard_map/ppermute | solution.py:60
  87.1 23.8 %copy-start.8 = (s32[8]{0:T(128)}, s32[8]{0:T(128)S(1)}, u32[]{:S(2)}) copy-start(s32[8]{0:T(128)S(1)} %pad_add_fusion.pair_ref.refs_0_) | copy-start | bytes 100
  87.3 10.3 %copy-start.3 = (bf16[896,896]{1,0:T(8,128)(2,1)S(1)}, bf16[896,896]{1,0:T(8,128)(2,1)}, u32[]{:S(2)}) copy-start(bf16[896,896]{1,0:T(8,128)(2,1)} %refs_13_.3) | copy-start | bytes 4816900
  87.3 1.5 copy-start.6
  88.8 1.2 copy-start.7
  105.1 16.7 %collective-permute-start.13 = (bf16[8,128,896]{2,1,0:T(8,128)(2,1)S(1)}, bf16[8,128,896]{2,1,0:T(8,128)(2,1)S(1)}, u32[]{:S(2)}, u32[]{:S(2)}) collective-permute-start(bf16[8,128,896]{2,1,0:T(8,128)(2,1)S(1)} %encode.2.refs_14_.refs_0_), channel_id=1, source_target_pairs={{0,1},{1,0},{2,3},{3,2},{4,5},{5,4},{6,7},{7,6},{8,9},{9,8},{10,11... | collective-permute-start | bytes 5505032 | tf_op jit(solution)/shard_map/ppermute | solution.py:60
  105.7 16.1 %copy-start.9 = (bf16[512,4096]{1,0:T(8,128)(2,1)S(1)}, bf16[512,4096]{1,0:T(8,128)(2,1)}, u32[]{:S(2)}) copy-start(bf16[512,4096]{1,0:T(8,128)(2,1)} %refs_6_.1) | copy-start | bytes 12582916
  105.7 16.1 %copy-start.10 = (bf16[896,512]{1,0:T(8,128)(2,1)S(1)}, bf16[896,512]{1,0:T(8,128)(2,1)}, u32[]{:S(2)}) copy-start(bf16[896,512]{1,0:T(8,128)(2,1)} %refs_4_.5) | copy-start | bytes 2752516
  105.7 16.1 %copy-start.11 = (bf16[896,512]{1,0:T(8,128)(2,1)S(1)}, bf16[896,512]{1,0:T(8,128)(2,1)}, u32[]{:S(2)}) copy-start(bf16[896,512]{1,0:T(8,128)(2,1)} %refs_5_.3) | copy-start | bytes 2752516
  105.8 13.5 %collective-permute-start.15 = (bf16[1,128,896]{2,1,0:T(8,128)(2,1)S(1)}, bf16[1,128,896]{2,1,0:T(8,128)(2,1)S(1)}, u32[]{:S(2)}, u32[]{:S(2)}) collective-permute-start(bf16[1,128,896]{2,1,0:T(8,128)(2,1)S(1)} %slice.51), channel_id=1, source_target_pairs={{0,9},{1,8},{2,11},{3,10},{4,13},{5,12},{6,15},{7,14},{8,17},{9,16... | collective-permute-start | bytes 688136 | tf_op jit(solution)/shard_map/ppermute | solution.py:423
  108.1 13.8 %collective-permute-start.14 = (bf16[1,128,896]{2,1,0:T(8,128)(2,1)S(1)}, bf16[1,128,896]{2,1,0:T(8,128)(2,1)S(1)}, u32[]{:S(2)}, u32[]{:S(2)}) collective-permute-start(bf16[1,128,896]{2,1,0:T(8,128)(2,1)S(1)} %slice.51), channel_id=1, source_target_pairs={{0,8},{1,9},{2,10},{3,11},{4,12},{5,13},{6,14},{7,15},{8,16},{9,17... | collective-permute-start | bytes 688136 | tf_op jit(solution)/shard_map/ppermute | solution.py:423
  121.9 1.5 copy-start.4
  133.0 1.5 copy-start.5
  134.5 4.4 %collective-permute-start.16 = (bf16[8,128,896]{2,1,0:T(8,128)(2,1)S(1)}, bf16[8,128,896]{2,1,0:T(8,128)(2,1)S(1)}, u32[]{:S(2)}, u32[]{:S(2)}) collective-permute-start(bf16[8,128,896]{2,1,0:T(8,128)(2,1)S(1)} %copy-done.5), channel_id=1, source_target_pairs={{0,1},{1,0},{2,3},{3,2},{4,5},{5,4},{6,7},{7,6},{8,9},{9,8},{10,11... | collective-permute-start | bytes 5505032 | tf_op jit(solution)/shard_map/ppermute | solution.py:60
  139.0 1.3 copy-start.13
  154.4 4.7 %collective-permute-start.17 = (bf16[4,512,512]{2,1,0:T(8,128)(2,1)}, bf16[4,512,512]{2,1,0:T(8,128)(2,1)S(1)}, u32[]{:S(2)}, u32[]{:S(2)}) collective-permute-start(bf16[4,512,512]{2,1,0:T(8,128)(2,1)} %get-tuple-element.8), channel_id=1, source_target_pairs={{0,1},{1,0},{2,3},{3,2},{4,5},{5,4},{6,7},{7,6},{8,9},{9,8},{10,11... | collective-permute-start | bytes 6291464 | tf_op jit(solution)/shard_map/ppermute | solution.py:60
  161.0 28.5 %collective-permute-start.18 = (bf16[512,512]{1,0:T(8,128)(2,1)S(1)}, bf16[512,512]{1,0:T(8,128)(2,1)S(1)}, u32[]{:S(2)}, u32[]{:S(2)}) collective-permute-start(bf16[512,512]{1,0:T(8,128)(2,1)S(1)} %get-tuple-element.11), channel_id=1, source_target_pairs={{0,6},{1,7},{2,0},{3,1},{4,2},{5,3},{6,4},{7,5},{8,14},{9,15},{10,... | collective-permute-start | bytes 1572872 | tf_op jit(solution)/shard_map/ppermute | solution.py:458
  163.1 26.4 %collective-permute-start.20 = (bf16[512,512]{1,0:T(8,128)(2,1)S(1)}, bf16[512,512]{1,0:T(8,128)(2,1)S(1)}, u32[]{:S(2)}, u32[]{:S(2)}) collective-permute-start(bf16[512,512]{1,0:T(8,128)(2,1)S(1)} %get-tuple-element.12), channel_id=1, source_target_pairs={{0,4},{1,5},{2,6},{3,7},{4,0},{5,1},{6,2},{7,3},{8,12},{9,13},{10,... | collective-permute-start | bytes 1572872 | tf_op jit(solution)/shard_map/ppermute | solution.py:458
  164.0 31.6 %copy-start.1 = (bf16[8,128,896]{2,1,0:T(8,128)(2,1)S(1)}, bf16[8,128,896]{2,1,0:T(8,128)(2,1)}, u32[]{:S(2)}) copy-start(bf16[8,128,896]{2,1,0:T(8,128)(2,1)} %param.13) | copy-start | bytes 5505028
  164.0 28.1 %collective-permute-start.19 = (bf16[512,512]{1,0:T(8,128)(2,1)S(1)}, bf16[512,512]{1,0:T(8,128)(2,1)S(1)}, u32[]{:S(2)}, u32[]{:S(2)}) collective-permute-start(bf16[512,512]{1,0:T(8,128)(2,1)S(1)} %get-tuple-element.13), channel_id=1, source_target_pairs={{0,2},{1,3},{2,4},{3,5},{4,6},{5,7},{6,0},{7,1},{8,10},{9,11},{10,... | collective-permute-start | bytes 1572872 | tf_op jit(solution)/shard_map/ppermute | solution.py:458
Sparse Core Ops, SparseCore 0:
  11.0 47.9 all-gather.2
  133.2 43.1 reduce-scatter.1

commit v4 on v3

--- a/solution.py
+++ b/solution.py
@@ -65,40 +65,38 @@
 
 
 def cond_kernel(src_ref, hidden_ref, *refs):
-    a_refs, (b_ref, out_ref, held) = refs[:4], refs[4:]
+    parts, (out_ref, total) = refs[:4], refs[-2:]
     step = pl.program_id(0)
-    rows = hidden_ref.shape[0]
-    total = None
     for i in range(4):
-        for j in range(4):
-            rank = src_ref[4 * i + j]
-            at = pl.multiple_of(rank * 256, 256)
-            weight = jnp.concatenate([a_refs[i][j], b_ref[rank]], axis=0)
-            term = dot(hidden_ref[:, pl.ds(at, 256)], weight)
-            total = term if total is None else total + term
-    held[pl.ds(pl.multiple_of(step * rows, rows), rows), :] = total.astype(BF16)
-
-    @pl.when(step == pl.num_programs(0) - 1)
-    def _():
-        tokens = held.shape[0]
-        first = FIRST * CH
-        out_ref[: tokens - first, :] = held[first:, :]
-        out_ref[tokens - first :, :] = held[:first, :]
-
-
-def cond_rows(hidden, a_parts, b_all, ranks):
+
+        @pl.when(step == i)
+        def _():
+            terms = None if i == 0 else total[...]
+            for j in range(4):
+                at = pl.multiple_of(src_ref[4 + j] * 256, 256)
+                term = dot(hidden_ref[:, pl.ds(at, 256)], parts[i][j])
+                terms = term if terms is None else terms + term
+            if i == 3:
+                last = terms.shape[0] - CH
+                out_ref[:CH, :] = terms[last:].astype(BF16)
+                out_ref[CH:, :] = terms[:last].astype(BF16)
+            else:
+                total[...] = terms
+
+
+def cond_rows(hidden, parts, sources, after):
     tokens = hidden.shape[0]
-    tile = 512
     return pl.pallas_call(
         cond_kernel,
         out_shape=jax.ShapeDtypeStruct((tokens, 256), BF16),
         grid_spec=pltpu.PrefetchScalarGridSpec(
             num_scalar_prefetch=1,
-            grid=(tokens // tile,),
-            in_specs=[pl.BlockSpec((tile, D), lambda i, s: (i, 0))] + [once((4, 128, 256))] * 4
-            + [once(b_all.shape)],
+            grid=(4,),
+            in_specs=[pl.BlockSpec((tokens, D // 4), lambda i, s: (0, s[i]))]
+            + [once((4, 256, 256))] * 4
+            + [pl.BlockSpec(memory_space=pl.ANY)],
             out_specs=pl.BlockSpec((tokens, 256), lambda i, s: (0, 0)),
-            scratch_shapes=[pltpu.VMEM((tokens, 256), BF16)],
+            scratch_shapes=[pltpu.VMEM((tokens, 256), F32)],
         ),
         compiler_params=pltpu.CompilerParams(
             dimension_semantics=("arbitrary",), vmem_limit_bytes=VMEM_LIMIT
@@ -107,7 +105,27 @@
             flops=2 * tokens * D * 256, bytes_accessed=12 << 20, transcendentals=0
         ),
         name="cond_rows",
-    )(ranks, hidden, *a_parts, b_all)
+    )(sources, hidden, *parts, after)
+
+
+def hold_kernel(block_ref, after_ref, out_ref):
+    del after_ref
+    out_ref[...] = block_ref[...]
+
+
+def hold(block, after):
+    return pl.pallas_call(
+        hold_kernel,
+        out_shape=jax.ShapeDtypeStruct(block.shape, BF16),
+        in_specs=[
+            pl.BlockSpec(memory_space=pltpu.VMEM),
+            pl.BlockSpec(memory_space=pl.ANY),
+        ],
+        out_specs=pl.BlockSpec(memory_space=pltpu.VMEM),
+        compiler_params=pltpu.CompilerParams(vmem_limit_bytes=4 << 20),
+        cost_estimate=pl.CostEstimate(flops=0, bytes_accessed=1 << 20, transcendentals=0),
+        name="hold",
+    )(block, after)
 
 
 def enc_query_kernel(pos_ref, *refs):
@@ -123,7 +141,7 @@
         out_ref[n] = got[n * NLEN : (n + 1) * NLEN]
 
 
-def enc_queries(pos, gathered, weight, after):
+def enc_queries(pos, gathered, weight):
     count = pos.shape[0]
 
     def source(n):
@@ -135,8 +153,7 @@
         grid_spec=pltpu.PrefetchScalarGridSpec(
             num_scalar_prefetch=1,
             grid=(count // 4,),
-            in_specs=[source(n) for n in range(4)]
-            + [once((E, E)), pl.BlockSpec(memory_space=pl.ANY)],
+            in_specs=[source(n) for n in range(4)] + [once((E, E))],
             out_specs=pl.BlockSpec((4, NLEN, E), lambda i, pos: (i, 0, 0)),
         ),
         compiler_params=pltpu.CompilerParams(
@@ -146,7 +163,7 @@
             flops=2 * count * NLEN * E * E, bytes_accessed=10 << 20, transcendentals=0
         ),
         name="enc_queries",
-    )(pos, *([gathered] * 4), weight, after)
+    )(pos, *([gathered] * 4), weight)
 
 
 def encode_kernel(pos_ref, pair_ref, *refs):
@@ -197,7 +214,7 @@
         out_ref[n] = (sources[n][0].astype(F32) + rows).astype(BF16)
 
 
-def encode(base, count, pos, pairs, queries, gathered, conds, enc_out, after=()):
+def encode(base, count, pos, pairs, queries, gathered, conds, enc_out, after):
     first = base // 4
 
     def source(n):
@@ -206,7 +223,7 @@
     cond = pl.BlockSpec((4, CH, 256), lambda i, pos, pairs: (first + i, 0, 0))
     return pl.pallas_call(
         encode_kernel,
-        out_shape=(pltpu.HBM if after else jax.ShapeDtypeStruct)((count, NLEN, E), BF16),
+        out_shape=(pltpu.HBM if base > 0 else jax.ShapeDtypeStruct)((count, NLEN, E), BF16),
         grid_spec=pltpu.PrefetchScalarGridSpec(
             num_scalar_prefetch=2,
             grid=(count // 4,),
@@ -393,19 +410,16 @@
         ],
         axis=1,
     )
-    half = weight.shape[0] // 2
-    a_four = jnp.stack(around(weight[:half], side, False))
-    a_parts = around(a_four, side, True)
-    b_rows = jnp.broadcast_to(weight[half:][None], (seq_count, half, 256))
-    b_all = lax.all_to_all(b_rows, "seq", 0, 0, tiled=True)
+    row = jnp.stack(around(weight, side, False))
+    parts = around(row, side, True)
+    rel = jnp.array(REL, jnp.int32)
     y_at, z_at = seq_rank // side, seq_rank % side
-    rel = jnp.array(REL, jnp.int32)
-    from_rank = (
-        side * ((y_at + rel + side) % side)[:, None] + ((z_at + rel + side) % side)[None, :]
-    ).reshape(-1)
-    cond = cond_rows(hidden, a_parts, b_all, from_rank).reshape(span_count, CH, 256)
+    from_rank = jnp.concatenate([(y_at + rel + side) % side, (z_at + rel + side) % side])
+    hidden_far = pltpu.with_memory_space_constraint(hidden, pltpu.HBM)
+    queries = dot(hidden, w_query).astype(BF16)
+    queries = pltpu.with_memory_space_constraint(queries, pltpu.HBM)
+    cond = cond_rows(hidden_far, parts, from_rank, queries).reshape(-1, CH, 256)
     own_lane = around_x(cond, chips)
-    conds = own_lane + [swap_cores(block) for block in own_lane]
     chip, core = store_rank // 2, store_rank % 2
     lane = 2 * ((chip + rel + chips) % chips)
     pairs = jnp.concatenate([lane + core, lane + 1 - core])
@@ -414,10 +428,12 @@
     mine = jnp.sum(
         jnp.where(slot[None, :] == (KNB * spans + core)[:, None], pos[None, :], 0), axis=1
     )
-    queries = dot(hidden, w_query).astype(BF16)
-    enc_q = enc_queries(mine, gathered, enc_query, queries)
+    enc_query = pltpu.with_memory_space_constraint(enc_query, pltpu.HBM)
+    enc_q = enc_queries(mine, gathered, enc_query)
+    own_lane[1] = hold(own_lane[1], enc_q)
+    conds = own_lane + [swap_cores(block) for block in own_lane]
     part = span_count // 2
-    low = encode(0, part, mine, pairs, enc_q, gathered, conds, enc_out)
+    low = encode(0, part, mine, pairs, enc_q, gathered, conds, enc_out, ())
     low_other = swap_cores(low)
     carried, carried_other = (
         lax.ppermute(
@@ -431,7 +447,7 @@
         )
         for flip in range(2)
     )
-    high = encode(part, part, mine, pairs, enc_q, gathered, conds, enc_out, after=(low,))
+    high = encode(part, part, mine, pairs, enc_q, gathered, conds, enc_out, (low,))
     high_other = swap_cores(high)
     terms = decode(
         0,

time: 203 us -> 201 us (level)
  starting transfers between devices: 37.3 us -> 27.1 us
  local copies, waits for them, and re-layouts: 15.8 us -> 8.4 us
  waiting for transfers between devices: 73 us -> 79.2 us
  Pallas kernels: 50.4 us -> 55.3 us
  matrix products: 5.46 us -> 10.2 us
    all_to_all x1 -> x0, starting transfers between devices: 7.85 us -> none  [body(): b_all = lax.all_to_all(b_rows, 'seq', 0, 0, tiled=True)]
    ppermute x3, waiting for transfers between devices: 10.9 us -> 17.7 us  [around_x(): got.append(lax.ppermute(block, 'store', route))]
    unnamed x29 -> x21, local copies, waits for them, and re-layouts: 11.4 us -> 5.11 us
    dot_general x1, matrix products: 5.46 us -> 10.2 us  [dot(): return jnp.dot(a, b, preferred_element_type=F32)]
    ppermute x6, waiting for transfers between devices: 23.8 us -> 20.3 us  [around(): got.append(lax.ppermute(block, 'seq', route))]
    pallas_call x1, Pallas kernels: 3.14 us -> 6.2 us  [cond_rows(): pl.pallas_call(cond_kernel, out_shape=jax.ShapeDtypeStruct((tokens, 256),...]
    ppermute x7, starting transfers between devices: 8.76 us -> 6.64 us  [swap_cores(): return lax.ppermute(block, 'store', [(i, i ^ 1) for i in range(count)])]
    pallas_call x2 -> x3, Pallas kernels: 15.9 us -> 16.6 us  [the longest x2 15.4 us: encode(): pl.pallas_call(encode_kernel, out_shape=(pltpu.HBM if base > 0 else jax.S...]
  transfers between devices with their start and end apart: 24 -> 23, of which waited for: 12 -> 12; matrix products, arithmetic and copies ran while one was open for 6% -> 7% of each run, Pallas kernels for 16% -> 19%
where the time goes in v4:
time: 201 us
  waiting for transfers between devices  79.2 us (39%)
  Pallas kernels  55.3 us (28%)
  starting transfers between devices  27.1 us (13%)
  between operations  13.7 us (7%)
  matrix products  10.2 us (5%)
  local copies, waits for them, and re-layouts  8.4 us (4%)
  other arithmetic  6.79 us (3%)
    ppermute x3, waiting for transfers between devices, body(): lax.ppermute(sums[j].astype(BF16), 'store', route).astype(F32)  27.5 us
    pallas_call x2, Pallas kernels, decode(): pl.pallas_call(lambda *refs: decode_kernel(len(carried) > 0, split, *refs...  24.4 us
    ppermute x6, waiting for transfers between devices, around(): got.append(lax.ppermute(block, 'seq', route))  20.3 us
    ppermute x3, waiting for transfers between devices, around_x(): got.append(lax.ppermute(block, 'store', route))  17.7 us
    pallas_call x2, Pallas kernels, encode(): pl.pallas_call(encode_kernel, out_shape=(pltpu.HBM if base > 0 else jax.S...  15.4 us
    dot_general x1, matrix products, dot(): return jnp.dot(a, b, preferred_element_type=F32)  10.2 us
    ppermute x7, waiting for transfers between devices, swap_cores(): return lax.ppermute(block, 'store', [(i, i ^ 1) for i in range(count)])  9.3 us
    ppermute x6, starting transfers between devices, around(): got.append(lax.ppermute(block, 'seq', route))  8.69 us
  transfers between devices with their start and end apart: 23, of which 12 were waited for; matrix products, arithmetic and copies ran while one was open for 7% of the time, Pallas kernels for 19%

profile of v4, /device:TPU:9, one launch (start us, length us, event | category | flops | bytes accessed | tf_op | source)
XLA Modules:
  0.0 200.7 jit_solution(8414012763144307703)
XLA Ops:
  6.5 0.9 copy.16
  7.9 0.7 broadcast_add_fusion
  8.6 0.6 gather_fusion
  9.3 1.7 gather_fusion.1
  11.0 0.9 constant_dynamic-slice_fusion
  11.9 3.8 %collective-permute-start.1 = (bf16[256,256]{1,0:T(8,128)(2,1)S(1)}, bf16[256,256]{1,0:T(8,128)(2,1)S(1)}, u32[]{:S(2)}, u32[]{:S(2)}) collective-permute-start(bf16[256,256]{1,0:T(8,128)(2,1)S(1)} %get-tuple-element.15), channel_id=1, source_target_pairs={{0,24},{8,0},{16,8},{24,16},{32,56},{40,32},{48,40},{56,48},{64,88... | collective-permute-start | bytes 393224 | tf_op jit(solution)/shard_map/ppermute | solution.py:44
  15.8 1.3 collective-permute-start.2
  17.1 0.9 collective-permute-done.1
  17.9 6.5 %collective-permute-done = bf16[256,256]{1,0:T(8,128)(2,1)S(1)} collective-permute-done((bf16[256,256]{1,0:T(8,128)(2,1)S(1)}, bf16[256,256]{1,0:T(8,128)(2,1)S(1)}, u32[]{:S(2)}, u32[]{:S(2)}) %collective-permute-start) | collective-permute-done | bytes 131104 | tf_op jit(solution)/shard_map/ppermute | solution.py:44
  24.5 2.1 %collective-permute-start.5 = (bf16[4,256,256]{2,1,0:T(8,128)(2,1)S(1)}, bf16[4,256,256]{2,1,0:T(8,128)(2,1)S(1)}, u32[]{:S(2)}, u32[]{:S(2)}) collective-permute-start(bf16[4,256,256]{2,1,0:T(8,128)(2,1)S(1)} %pad_maximum_fusion.1.refs_0_), channel_id=1, source_target_pairs={{0,64},{8,72},{16,80},{24,88},{32,96},{40,104},{48,112},{56,120},{... | collective-permute-start | bytes 1572872 | tf_op jit(solution)/shard_map/ppermute | solution.py:44
  26.6 1.1 collective-permute-start.4
  27.6 0.4 collective-permute-start.3
  28.0 10.2 %convolution_convert_fusion.refs_4_.refs_2_.refs_3_ = bf16[1024,512]{1,0:T(8,128)(2,1)} fusion(bf16[1024,4096]{1,0:T(8,128)(2,1)} %hidden_ref.1, bf16[4096,512]{1,0:T(8,128)(2,1)} %param.15), kind=kOutput, calls=%fused_computation.2 | convolution fusion | flops 4295491584 | bytes 13631488 | tf_op jit(solution)/shard_map/dot_general | solution.py:29
  38.3 12.9 %collective-permute-done.4.refs_2_ = bf16[4,256,256]{2,1,0:T(8,128)(2,1)S(1)} collective-permute-done((bf16[4,256,256]{2,1,0:T(8,128)(2,1)S(1)}, bf16[4,256,256]{2,1,0:T(8,128)(2,1)S(1)}, u32[]{:S(2)}, u32[]{:S(2)}) %collective-permute-start.4) | collective-permute-done | bytes 524320 | tf_op jit(solution)/shard_map/ppermute | solution.py:44
  51.2 6.2 %cond_rows.1 = bf16[1024,256]{1,0:T(8,128)(2,1)S(1)} custom-call(s32[8]{0:T(128)S(1)} %pad_add_fusion.1.src_ref, bf16[1024,4096]{1,0:T(8,128)(2,1)} %hidden_ref.1, bf16[4,256,256]{2,1,0:T(8,128)(2,1)S(1)} %pad_maximum_fusion.1.refs_0_, bf16[4,256,256]{2,1,0:T(8,128)(2,1)S(1)} %collective-permute-done.3.refs_1_, ...), custom_call_target="tpu_custom_call" | custom-call | flops 2147483648 | bytes 12582912 | tf_op jit(solution)/shard_map/cond_rows/pallas_call | solution.py:89
  57.4 2.8 %collective-permute-start.8 = (bf16[16,64,256]{2,1,0:T(8,128)(2,1)S(1)}, bf16[16,64,256]{2,1,0:T(8,128)(2,1)S(1)}, u32[]{:S(2)}, u32[]{:S(2)}) collective-permute-start(bf16[16,64,256]{2,1,0:T(8,128)(2,1)S(1)} %bitcast.26), channel_id=1, source_target_pairs={{0,4},{1,5},{2,6},{3,7},{4,0},{5,1},{6,2},{7,3},{8,12},{9,13},{10,... | collective-permute-start | bytes 1572872 | tf_op jit(solution)/shard_map/ppermute | solution.py:54
  60.2 0.9 collective-permute-start.7
  61.1 0.6 collective-permute-start.6
  61.9 1.5 collective-permute-start.9
  63.3 8.7 %collective-permute-done.8.refs_7_ = bf16[16,64,256]{2,1,0:T(8,128)(2,1)S(1)} collective-permute-done((bf16[16,64,256]{2,1,0:T(8,128)(2,1)S(1)}, bf16[16,64,256]{2,1,0:T(8,128)(2,1)S(1)}, u32[]{:S(2)}, u32[]{:S(2)}) %collective-permute-start.8) | collective-permute-done | bytes 524320 | tf_op jit(solution)/shard_map/ppermute | solution.py:54
  72.0 2.4 %collective-permute-start.12 = (bf16[16,64,256]{2,1,0:T(8,128)(2,1)S(1)}, bf16[16,64,256]{2,1,0:T(8,128)(2,1)S(1)}, u32[]{:S(2)}, u32[]{:S(2)}) collective-permute-start(bf16[16,64,256]{2,1,0:T(8,128)(2,1)S(1)} %collective-permute-done.8.refs_7_), channel_id=1, source_target_pairs={{0,1},{1,0},{2,3},{3,2},{4,5},{5,4},{6,7},{7,6},{8,9},{9,8},{10,11... | collective-permute-start | bytes 1572872 | tf_op jit(solution)/shard_map/ppermute | solution.py:60
  74.4 9.0 %collective-permute-done.7.refs_6_ = bf16[16,64,256]{2,1,0:T(8,128)(2,1)S(1)} collective-permute-done((bf16[16,64,256]{2,1,0:T(8,128)(2,1)S(1)}, bf16[16,64,256]{2,1,0:T(8,128)(2,1)S(1)}, u32[]{:S(2)}, u32[]{:S(2)}) %collective-permute-start.7) | collective-permute-done | bytes 524320 | tf_op jit(solution)/shard_map/ppermute | solution.py:54
  83.4 1.3 collective-permute-start.11
  84.7 8.1 %enc_queries.1.after_ref.refs_12_ = bf16[16,128,896]{2,1,0:T(8,128)(2,1)S(1)} custom-call(s32[16]{0:T(128)S(1)} %select_reduce_fusion.1.pos_ref, bf16[32,128,896]{2,1,0:T(8,128)(2,1)} %all-gather.3.cloned.1.call-done.refs_0_.refs_1_.refs_2_.refs_3_, bf16[32,128,896]{2,1,0:T(8,128)(2,1)} %all-gather.3.cloned.1.call-done.refs_0_.refs_1_.refs_2_.refs_3_, ...), custom_call_target="tpu_custom_call" | custom-call | flops 3288334336 | bytes 10485760 | tf_op jit(solution)/shard_map/enc_queries/pallas_call | solution.py:150
  92.8 1.2 hold.1.refs_5_
  94.4 1.8 collective-permute-done.10.refs_9_
  96.2 7.3 %encode.2.refs_14_.refs_0_ = bf16[8,128,896]{2,1,0:T(8,128)(2,1)S(1)} custom-call(s32[16]{0:T(128)S(1)} %select_reduce_fusion.1.pos_ref, s32[8]{0:T(128)S(1)} %pad_add_fusion.pair_ref.refs_0_, bf16[32,128,896]{2,1,0:T(8,128)(2,1)} %all-gather.3.cloned.1.call-done.refs_0_.refs_1_.refs_2_.refs_3_, ...), custom_call_target="tpu_custom_call" | custom-call | flops 2466250752 | bytes 8388608 | tf_op jit(solution)/shard_map/encode/pallas_call | solution.py:224
  103.7 2.3 %collective-permute-start.15 = (bf16[1,128,896]{2,1,0:T(8,128)(2,1)S(1)}, bf16[1,128,896]{2,1,0:T(8,128)(2,1)S(1)}, u32[]{:S(2)}, u32[]{:S(2)}) collective-permute-start(bf16[1,128,896]{2,1,0:T(8,128)(2,1)S(1)} %slice.41), channel_id=1, source_target_pairs={{0,9},{1,8},{2,11},{3,10},{4,13},{5,12},{6,15},{7,14},{8,17},{9,16... | collective-permute-start | bytes 688136 | tf_op jit(solution)/shard_map/ppermute | solution.py:439
  106.1 1.9 collective-permute-start.14
  108.0 8.2 %encode.3.refs_8_.refs_1_ = bf16[8,128,896]{2,1,0:T(8,128)(2,1)} custom-call(s32[16]{0:T(128)S(1)} %select_reduce_fusion.1.pos_ref, s32[8]{0:T(128)S(1)} %pad_add_fusion.pair_ref.refs_0_, bf16[32,128,896]{2,1,0:T(8,128)(2,1)} %all-gather.3.cloned.1.call-done.refs_0_.refs_1_.refs_2_.refs_3_, ...), custom_call_target="tpu_custom_call" | custom-call | flops 2466250752 | bytes 8388608 | tf_op jit(solution)/shard_map/encode/pallas_call | solution.py:224
  116.2 4.3 %collective-permute-done.14.refs_6_ = bf16[1,128,896]{2,1,0:T(8,128)(2,1)S(1)} collective-permute-done((bf16[1,128,896]{2,1,0:T(8,128)(2,1)S(1)}, bf16[1,128,896]{2,1,0:T(8,128)(2,1)S(1)}, u32[]{:S(2)}, u32[]{:S(2)}) %collective-permute-start.14) | collective-permute-done | bytes 229408 | tf_op jit(solution)/shard_map/ppermute | solution.py:439
  120.5 1.5 copy-done.3
  122.0 10.6 %decode.2.refs_7_ = bf16[512,4096]{1,0:T(8,128)(2,1)} custom-call(bf16[8,128,896]{2,1,0:T(8,128)(2,1)S(1)} %encode.2.refs_14_.refs_0_, bf16[8,128,896]{2,1,0:T(8,128)(2,1)S(1)} %collective-permute-done.13.refs_1_, bf16[1024,512]{1,0:T(8,128)(2,1)} %convolution_convert_fusion.refs_4_.refs_2_.refs_3_, bf16[896,512]{1,0:T(8,128)(2,1)S(1)} %copy-done.7, ...), custom_call_target="tpu_custom_call" | custom-call | flops 5905580032 | bytes 12582912 | tf_op jit(solution)/shard_map/decode/pallas_call | solution.py:335
  132.6 1.5 copy-done.4
  134.1 0.7 collective-permute-start.16
  134.8 3.4 %collective-permute-done.16.refs_2_ = bf16[8,128,896]{2,1,0:T(8,128)(2,1)S(1)} collective-permute-done((bf16[8,128,896]{2,1,0:T(8,128)(2,1)S(1)}, bf16[8,128,896]{2,1,0:T(8,128)(2,1)S(1)}, u32[]{:S(2)}, u32[]{:S(2)}) %collective-permute-start.16) | collective-permute-done | bytes 1835040 | tf_op jit(solution)/shard_map/ppermute | solution.py:60
  138.2 1.2 copy-done.9
  139.4 13.8 %decode.3 = (bf16[4,512,512]{2,1,0:T(8,128)(2,1)}, bf16[4,512,512]{2,1,0:T(8,128)(2,1)}) custom-call(s32[8]{0:T(128)} %copy-done.5, bf16[8,128,896]{2,1,0:T(8,128)(2,1)} %encode.3.refs_8_.refs_1_, bf16[8,128,896]{2,1,0:T(8,128)(2,1)} %copy-done.9, bf16[1024,512]{1,0:T(8,128)(2,1)} %convolution_convert_fusion.refs_4_.refs_2_.refs_3_, ...), custom_call_target="tpu_custom_call" | custom-call | flops 5905580032 | bytes 12582912 | tf_op jit(solution)/shard_map/decode/pallas_call | solution.py:335
  153.3 0.4 collective-permute-start.17
  153.6 4.1 %collective-permute-done.17 = bf16[4,512,512]{2,1,0:T(8,128)(2,1)S(1)} collective-permute-done((bf16[4,512,512]{2,1,0:T(8,128)(2,1)}, bf16[4,512,512]{2,1,0:T(8,128)(2,1)S(1)}, u32[]{:S(2)}, u32[]{:S(2)}) %collective-permute-start.17) | collective-permute-done | bytes 2097184 | tf_op jit(solution)/shard_map/ppermute | solution.py:60
  157.7 1.8 fusion.3
  159.6 2.4 %collective-permute-start.18 = (bf16[512,512]{1,0:T(8,128)(2,1)S(1)}, bf16[512,512]{1,0:T(8,128)(2,1)S(1)}, u32[]{:S(2)}, u32[]{:S(2)}) collective-permute-start(bf16[512,512]{1,0:T(8,128)(2,1)S(1)} %get-tuple-element.11), channel_id=1, source_target_pairs={{0,6},{1,7},{2,0},{3,1},{4,2},{5,3},{6,4},{7,5},{8,14},{9,15},{10,... | collective-permute-start | bytes 1572872 | tf_op jit(solution)/shard_map/ppermute | solution.py:474
  162.0 0.5 collective-permute-start.20
  162.8 14.4 %collective-permute-done.18 = bf16[512,512]{1,0:T(8,128)(2,1)S(1)} collective-permute-done((bf16[512,512]{1,0:T(8,128)(2,1)S(1)}, bf16[512,512]{1,0:T(8,128)(2,1)S(1)}, u32[]{:S(2)}, u32[]{:S(2)}) %collective-permute-start.18) | collective-permute-done | bytes 524320 | tf_op jit(solution)/shard_map/ppermute | solution.py:474
  177.2 1.6 collective-permute-done.20
  178.9 11.5 %collective-permute-done.19 = bf16[512,512]{1,0:T(8,128)(2,1)S(1)} collective-permute-done((bf16[512,512]{1,0:T(8,128)(2,1)S(1)}, bf16[512,512]{1,0:T(8,128)(2,1)S(1)}, u32[]{:S(2)}, u32[]{:S(2)}) %collective-permute-start.19) | collective-permute-done | bytes 524320 | tf_op jit(solution)/shard_map/ppermute | solution.py:474
  190.3 1.4 fusion.2
  191.7 2.1 %pad_maximum_fusion = bf16[1024,512]{1,0:T(8,128)(2,1)} fusion(bf16[512,512]{1,0:T(8,128)(2,1)S(1)} %fusion.2, bf16[512,512]{1,0:T(8,128)(2,1)} %reduce-scatter.2.cloned.1.call-done), kind=kLoop, calls=%fused_computation.3 | loop fusion | flops 2097152 | bytes 2097152 | tf_op jit(solution)/shard_map/concatenate | solution.py:475
  (51 shorter events, 1.8 us)
Async XLA Ops:
  6.5 2.7 %copy-start = (bf16[8,128,896]{2,1,0:T(8,128)(2,1)S(1)}, bf16[8,128,896]{2,1,0:T(8,128)(2,1)}, u32[]{:S(2)}) copy-start(bf16[8,128,896]{2,1,0:T(8,128)(2,1)} %param.13) | copy-start | bytes 5505028
  6.5 78.1 %all-gather.3.cloned.1.call-start = ((), (), s32[]{:S(2)}) async-start(), calls=%async_computation.2 | async-start | bytes 8257536 | tf_op jit(solution)/shard_map/all_gather | solution.py:402
  11.0 180.8 %reduce-scatter.2.cloned.1.call-start = ((), (), s32[]{:S(2)}) async-start(), calls=%async_computation.1 | async-start | bytes 4718592 | tf_op jit(solution)/shard_map/reduce_scatter | solution.py:463
  11.9 6.0 %collective-permute-start.1 = (bf16[256,256]{1,0:T(8,128)(2,1)S(1)}, bf16[256,256]{1,0:T(8,128)(2,1)S(1)}, u32[]{:S(2)}, u32[]{:S(2)}) collective-permute-start(bf16[256,256]{1,0:T(8,128)(2,1)S(1)} %get-tuple-element.15), channel_id=1, source_target_pairs={{0,24},{8,0},{16,8},{24,16},{32,56},{40,32},{48,40},{56,48},{64,88... | collective-permute-start | bytes 393224 | tf_op jit(solution)/shard_map/ppermute | solution.py:44
  15.8 8.6 %collective-permute-start = (bf16[256,256]{1,0:T(8,128)(2,1)S(1)}, bf16[256,256]{1,0:T(8,128)(2,1)S(1)}, u32[]{:S(2)}, u32[]{:S(2)}) collective-permute-start(bf16[256,256]{1,0:T(8,128)(2,1)S(1)} %get-tuple-element.15), channel_id=1, source_target_pairs={{0,8},{8,16},{16,24},{24,0},{32,40},{40,48},{48,56},{56,32},{64,72... | collective-permute-start | bytes 393224 | tf_op jit(solution)/shard_map/ppermute | solution.py:44
  15.8 8.6 %collective-permute-start.2 = (bf16[256,256]{1,0:T(8,128)(2,1)S(1)}, bf16[256,256]{1,0:T(8,128)(2,1)S(1)}, u32[]{:S(2)}, u32[]{:S(2)}) collective-permute-start(bf16[256,256]{1,0:T(8,128)(2,1)S(1)} %get-tuple-element.15), channel_id=1, source_target_pairs={{0,16},{8,24},{16,0},{24,8},{32,48},{40,56},{48,32},{56,40},{64,80... | collective-permute-start | bytes 393224 | tf_op jit(solution)/shard_map/ppermute | solution.py:44
  24.5 13.8 %collective-permute-start.5 = (bf16[4,256,256]{2,1,0:T(8,128)(2,1)S(1)}, bf16[4,256,256]{2,1,0:T(8,128)(2,1)S(1)}, u32[]{:S(2)}, u32[]{:S(2)}) collective-permute-start(bf16[4,256,256]{2,1,0:T(8,128)(2,1)S(1)} %pad_maximum_fusion.1.refs_0_), channel_id=1, source_target_pairs={{0,64},{8,72},{16,80},{24,88},{32,96},{40,104},{48,112},{56,120},{... | collective-permute-start | bytes 1572872 | tf_op jit(solution)/shard_map/ppermute | solution.py:44
  26.6 24.7 %collective-permute-start.4 = (bf16[4,256,256]{2,1,0:T(8,128)(2,1)S(1)}, bf16[4,256,256]{2,1,0:T(8,128)(2,1)S(1)}, u32[]{:S(2)}, u32[]{:S(2)}) collective-permute-start(bf16[4,256,256]{2,1,0:T(8,128)(2,1)S(1)} %pad_maximum_fusion.1.refs_0_), channel_id=1, source_target_pairs={{0,96},{8,104},{16,112},{24,120},{32,0},{40,8},{48,16},{56,24},{64... | collective-permute-start | bytes 1572872 | tf_op jit(solution)/shard_map/ppermute | solution.py:44
  27.6 23.6 %collective-permute-start.3 = (bf16[4,256,256]{2,1,0:T(8,128)(2,1)S(1)}, bf16[4,256,256]{2,1,0:T(8,128)(2,1)S(1)}, u32[]{:S(2)}, u32[]{:S(2)}) collective-permute-start(bf16[4,256,256]{2,1,0:T(8,128)(2,1)S(1)} %pad_maximum_fusion.1.refs_0_), channel_id=1, source_target_pairs={{0,32},{8,40},{16,48},{24,56},{32,64},{40,72},{48,80},{56,88},{64,... | collective-permute-start | bytes 1572872 | tf_op jit(solution)/shard_map/ppermute | solution.py:44
  57.4 14.6 %collective-permute-start.8 = (bf16[16,64,256]{2,1,0:T(8,128)(2,1)S(1)}, bf16[16,64,256]{2,1,0:T(8,128)(2,1)S(1)}, u32[]{:S(2)}, u32[]{:S(2)}) collective-permute-start(bf16[16,64,256]{2,1,0:T(8,128)(2,1)S(1)} %bitcast.26), channel_id=1, source_target_pairs={{0,4},{1,5},{2,6},{3,7},{4,0},{5,1},{6,2},{7,3},{8,12},{9,13},{10,... | collective-permute-start | bytes 1572872 | tf_op jit(solution)/shard_map/ppermute | solution.py:54
  60.2 23.2 %collective-permute-start.7 = (bf16[16,64,256]{2,1,0:T(8,128)(2,1)S(1)}, bf16[16,64,256]{2,1,0:T(8,128)(2,1)S(1)}, u32[]{:S(2)}, u32[]{:S(2)}) collective-permute-start(bf16[16,64,256]{2,1,0:T(8,128)(2,1)S(1)} %bitcast.27), channel_id=1, source_target_pairs={{0,6},{1,7},{2,0},{3,1},{4,2},{5,3},{6,4},{7,5},{8,14},{9,15},{10,... | collective-permute-start | bytes 1572872 | tf_op jit(solution)/shard_map/ppermute | solution.py:54
  61.1 31.7 %collective-permute-start.6 = (bf16[16,64,256]{2,1,0:T(8,128)(2,1)S(1)}, bf16[16,64,256]{2,1,0:T(8,128)(2,1)}, u32[]{:S(2)}, u32[]{:S(2)}) collective-permute-start(bf16[16,64,256]{2,1,0:T(8,128)(2,1)S(1)} %bitcast.28), channel_id=1, source_target_pairs={{0,2},{1,3},{2,4},{3,5},{4,6},{5,7},{6,0},{7,1},{8,10},{9,11},{10,... | collective-permute-start | bytes 1572872 | tf_op jit(solution)/shard_map/ppermute | solution.py:54
  61.9 32.5 %collective-permute-start.9 = (bf16[16,64,256]{2,1,0:T(8,128)(2,1)S(1)}, bf16[16,64,256]{2,1,0:T(8,128)(2,1)S(1)}, u32[]{:S(2)}, u32[]{:S(2)}) collective-permute-start(bf16[16,64,256]{2,1,0:T(8,128)(2,1)S(1)} %bitcast.29), channel_id=1, source_target_pairs={{0,1},{1,0},{2,3},{3,2},{4,5},{5,4},{6,7},{7,6},{8,9},{9,8},{10,11... | collective-permute-start | bytes 1572872 | tf_op jit(solution)/shard_map/ppermute | solution.py:60
  72.0 22.3 %collective-permute-start.12 = (bf16[16,64,256]{2,1,0:T(8,128)(2,1)S(1)}, bf16[16,64,256]{2,1,0:T(8,128)(2,1)S(1)}, u32[]{:S(2)}, u32[]{:S(2)}) collective-permute-start(bf16[16,64,256]{2,1,0:T(8,128)(2,1)S(1)} %collective-permute-done.8.refs_7_), channel_id=1, source_target_pairs={{0,1},{1,0},{2,3},{3,2},{4,5},{5,4},{6,7},{7,6},{8,9},{9,8},{10,11... | collective-permute-start | bytes 1572872 | tf_op jit(solution)/shard_map/ppermute | solution.py:60
  83.4 11.0 %collective-permute-start.11 = (bf16[16,64,256]{2,1,0:T(8,128)(2,1)S(1)}, bf16[16,64,256]{2,1,0:T(8,128)(2,1)S(1)}, u32[]{:S(2)}, u32[]{:S(2)}) collective-permute-start(bf16[16,64,256]{2,1,0:T(8,128)(2,1)S(1)} %collective-permute-done.7.refs_6_), channel_id=1, source_target_pairs={{0,1},{1,0},{2,3},{3,2},{4,5},{5,4},{6,7},{7,6},{8,9},{9,8},{10,11... | collective-permute-start | bytes 1572872 | tf_op jit(solution)/shard_map/ppermute | solution.py:60
  92.8 3.4 %copy-start.2 = (bf16[896,896]{1,0:T(8,128)(2,1)S(1)}, bf16[896,896]{1,0:T(8,128)(2,1)}, u32[]{:S(2)}) copy-start(bf16[896,896]{1,0:T(8,128)(2,1)} %refs_13_.3) | copy-start | bytes 4816900
  94.0 2.2 %collective-permute-start.10 = (bf16[16,64,256]{2,1,0:T(8,128)(2,1)S(1)}, bf16[16,64,256]{2,1,0:T(8,128)(2,1)S(1)}, u32[]{:S(2)}, u32[]{:S(2)}) collective-permute-start(bf16[16,64,256]{2,1,0:T(8,128)(2,1)S(1)} %hold.1.refs_5_), channel_id=1, source_target_pairs={{0,1},{1,0},{2,3},{3,2},{4,5},{5,4},{6,7},{7,6},{8,9},{9,8},{10,11... | collective-permute-start | bytes 1572872 | tf_op jit(solution)/shard_map/ppermute | solution.py:60
  94.4 13.6 %copy-start.5 = (s32[8]{0:T(128)}, s32[8]{0:T(128)S(1)}, u32[]{:S(2)}) copy-start(s32[8]{0:T(128)S(1)} %pad_add_fusion.pair_ref.refs_0_) | copy-start | bytes 100
  103.5 17.0 %collective-permute-start.13 = (bf16[8,128,896]{2,1,0:T(8,128)(2,1)S(1)}, bf16[8,128,896]{2,1,0:T(8,128)(2,1)S(1)}, u32[]{:S(2)}, u32[]{:S(2)}) collective-permute-start(bf16[8,128,896]{2,1,0:T(8,128)(2,1)S(1)} %encode.2.refs_14_.refs_0_), channel_id=1, source_target_pairs={{0,1},{1,0},{2,3},{3,2},{4,5},{5,4},{6,7},{7,6},{8,9},{9,8},{10,11... | collective-permute-start | bytes 5505032 | tf_op jit(solution)/shard_map/ppermute | solution.py:60
  103.7 16.8 %copy-start.6 = (bf16[512,4096]{1,0:T(8,128)(2,1)S(1)}, bf16[512,4096]{1,0:T(8,128)(2,1)}, u32[]{:S(2)}) copy-start(bf16[512,4096]{1,0:T(8,128)(2,1)} %refs_6_.1) | copy-start | bytes 12582916
  103.7 16.8 %copy-start.7 = (bf16[896,512]{1,0:T(8,128)(2,1)S(1)}, bf16[896,512]{1,0:T(8,128)(2,1)}, u32[]{:S(2)}) copy-start(bf16[896,512]{1,0:T(8,128)(2,1)} %refs_4_.5) | copy-start | bytes 2752516
  103.7 16.8 %copy-start.8 = (bf16[896,512]{1,0:T(8,128)(2,1)S(1)}, bf16[896,512]{1,0:T(8,128)(2,1)}, u32[]{:S(2)}) copy-start(bf16[896,512]{1,0:T(8,128)(2,1)} %refs_5_.3) | copy-start | bytes 2752516
  103.7 12.4 %collective-permute-start.15 = (bf16[1,128,896]{2,1,0:T(8,128)(2,1)S(1)}, bf16[1,128,896]{2,1,0:T(8,128)(2,1)S(1)}, u32[]{:S(2)}, u32[]{:S(2)}) collective-permute-start(bf16[1,128,896]{2,1,0:T(8,128)(2,1)S(1)} %slice.41), channel_id=1, source_target_pairs={{0,9},{1,8},{2,11},{3,10},{4,13},{5,12},{6,15},{7,14},{8,17},{9,16... | collective-permute-start | bytes 688136 | tf_op jit(solution)/shard_map/ppermute | solution.py:439
  106.1 14.4 %collective-permute-start.14 = (bf16[1,128,896]{2,1,0:T(8,128)(2,1)S(1)}, bf16[1,128,896]{2,1,0:T(8,128)(2,1)S(1)}, u32[]{:S(2)}, u32[]{:S(2)}) collective-permute-start(bf16[1,128,896]{2,1,0:T(8,128)(2,1)S(1)} %slice.41), channel_id=1, source_target_pairs={{0,8},{1,9},{2,10},{3,11},{4,12},{5,13},{6,14},{7,15},{8,16},{9,17... | collective-permute-start | bytes 688136 | tf_op jit(solution)/shard_map/ppermute | solution.py:439
  120.5 1.5 copy-start.3
  132.6 1.5 copy-start.4
  134.1 4.1 %collective-permute-start.16 = (bf16[8,128,896]{2,1,0:T(8,128)(2,1)S(1)}, bf16[8,128,896]{2,1,0:T(8,128)(2,1)S(1)}, u32[]{:S(2)}, u32[]{:S(2)}) collective-permute-start(bf16[8,128,896]{2,1,0:T(8,128)(2,1)S(1)} %copy-done.4), channel_id=1, source_target_pairs={{0,1},{1,0},{2,3},{3,2},{4,5},{5,4},{6,7},{7,6},{8,9},{9,8},{10,11... | collective-permute-start | bytes 5505032 | tf_op jit(solution)/shard_map/ppermute | solution.py:60
  138.2 1.2 copy-start.9
  153.3 4.5 %collective-permute-start.17 = (bf16[4,512,512]{2,1,0:T(8,128)(2,1)}, bf16[4,512,512]{2,1,0:T(8,128)(2,1)S(1)}, u32[]{:S(2)}, u32[]{:S(2)}) collective-permute-start(bf16[4,512,512]{2,1,0:T(8,128)(2,1)} %get-tuple-element.8), channel_id=1, source_target_pairs={{0,1},{1,0},{2,3},{3,2},{4,5},{5,4},{6,7},{7,6},{8,9},{9,8},{10,11... | collective-permute-start | bytes 6291464 | tf_op jit(solution)/shard_map/ppermute | solution.py:60
  159.6 17.7 %collective-permute-start.18 = (bf16[512,512]{1,0:T(8,128)(2,1)S(1)}, bf16[512,512]{1,0:T(8,128)(2,1)S(1)}, u32[]{:S(2)}, u32[]{:S(2)}) collective-permute-start(bf16[512,512]{1,0:T(8,128)(2,1)S(1)} %get-tuple-element.11), channel_id=1, source_target_pairs={{0,6},{1,7},{2,0},{3,1},{4,2},{5,3},{6,4},{7,5},{8,14},{9,15},{10,... | collective-permute-start | bytes 1572872 | tf_op jit(solution)/shard_map/ppermute | solution.py:474
  162.0 16.9 %collective-permute-start.20 = (bf16[512,512]{1,0:T(8,128)(2,1)S(1)}, bf16[512,512]{1,0:T(8,128)(2,1)S(1)}, u32[]{:S(2)}, u32[]{:S(2)}) collective-permute-start(bf16[512,512]{1,0:T(8,128)(2,1)S(1)} %get-tuple-element.12), channel_id=1, source_target_pairs={{0,4},{1,5},{2,6},{3,7},{4,0},{5,1},{6,2},{7,3},{8,12},{9,13},{10,... | collective-permute-start | bytes 1572872 | tf_op jit(solution)/shard_map/ppermute | solution.py:474
  162.5 31.3 %copy-start.1 = (bf16[8,128,896]{2,1,0:T(8,128)(2,1)S(1)}, bf16[8,128,896]{2,1,0:T(8,128)(2,1)}, u32[]{:S(2)}) copy-start(bf16[8,128,896]{2,1,0:T(8,128)(2,1)} %param.13) | copy-start | bytes 5505028
  162.5 27.8 %collective-permute-start.19 = (bf16[512,512]{1,0:T(8,128)(2,1)S(1)}, bf16[512,512]{1,0:T(8,128)(2,1)S(1)}, u32[]{:S(2)}, u32[]{:S(2)}) collective-permute-start(bf16[512,512]{1,0:T(8,128)(2,1)S(1)} %get-tuple-element.13), channel_id=1, source_target_pairs={{0,2},{1,3},{2,4},{3,5},{4,6},{5,7},{6,0},{7,1},{8,10},{9,11},{10,... | collective-permute-start | bytes 1572872 | tf_op jit(solution)/shard_map/ppermute | solution.py:474
Sparse Core Ops, SparseCore 0:
  11.1 47.9 all-gather.2
  132.7 42.1 reduce-scatter.1

commit v5 on v4

--- a/solution.py
+++ b/solution.py
@@ -60,12 +60,28 @@
     return lax.ppermute(block, "store", [(i, i ^ 1) for i in range(count)])
 
 
+def core_sums(kept, given):
+    taken = swap_cores(given)
+    sums = [kept[j].astype(F32) + taken[j].astype(F32) for j in range(4)]
+    return sums[:1] + [block.astype(BF16) for block in sums[1:]]
+
+
+def sum_over_x(sums, chips):
+    total = sums[0]
+    for j in range(1, 4):
+        route = [
+            (2 * x + core, 2 * ((x + REL[j]) % chips) + core) for x in range(chips) for core in range(2)
+        ]
+        total = total + lax.ppermute(sums[j], "store", route).astype(F32)
+    return total
+
+
 def once(shape):
     return pl.BlockSpec(shape, lambda *_: (0,) * len(shape), pipeline_mode=pl.Buffered(1))
 
 
 def cond_kernel(src_ref, hidden_ref, *refs):
-    parts, (out_ref, total) = refs[:4], refs[-2:]
+    a_refs, b_refs, (out_ref, total) = refs[:4], refs[4:8], refs[-2:]
     step = pl.program_id(0)
     for i in range(4):
 
@@ -74,7 +90,8 @@
             terms = None if i == 0 else total[...]
             for j in range(4):
                 at = pl.multiple_of(src_ref[4 + j] * 256, 256)
-                term = dot(hidden_ref[:, pl.ds(at, 256)], parts[i][j])
+                weight = jnp.concatenate([a_refs[i][j], b_refs[j][i]], axis=0)
+                term = dot(hidden_ref[:, pl.ds(at, 256)], weight)
                 terms = term if terms is None else terms + term
             if i == 3:
                 last = terms.shape[0] - CH
@@ -93,7 +110,7 @@
             num_scalar_prefetch=1,
             grid=(4,),
             in_specs=[pl.BlockSpec((tokens, D // 4), lambda i, s: (0, s[i]))]
-            + [once((4, 256, 256))] * 4
+            + [once((4, 128, 256))] * 8
             + [pl.BlockSpec(memory_space=pl.ANY)],
             out_specs=pl.BlockSpec((tokens, 256), lambda i, s: (0, 0)),
             scratch_shapes=[pltpu.VMEM((tokens, 256), F32)],
@@ -108,24 +125,44 @@
     )(sources, hidden, *parts, after)
 
 
-def hold_kernel(block_ref, after_ref, out_ref):
-    del after_ref
-    out_ref[...] = block_ref[...]
-
-
-def hold(block, after):
+def hold_kernel(*refs):
+    count = len(refs) // 2
+    for source, target in zip(refs[:count], refs[count + 1 :]):
+        target[...] = source[...]
+
+
+def hold(blocks, after):
+    count = len(blocks)
+    vmem = pl.BlockSpec(memory_space=pltpu.VMEM)
     return pl.pallas_call(
         hold_kernel,
-        out_shape=jax.ShapeDtypeStruct(block.shape, BF16),
-        in_specs=[
-            pl.BlockSpec(memory_space=pltpu.VMEM),
-            pl.BlockSpec(memory_space=pl.ANY),
-        ],
-        out_specs=pl.BlockSpec(memory_space=pltpu.VMEM),
-        compiler_params=pltpu.CompilerParams(vmem_limit_bytes=4 << 20),
+        out_shape=[jax.ShapeDtypeStruct(block.shape, BF16) for block in blocks],
+        in_specs=[vmem] * count + [pl.BlockSpec(memory_space=pl.ANY)],
+        out_specs=[vmem] * count,
+        compiler_params=pltpu.CompilerParams(vmem_limit_bytes=8 << 20),
         cost_estimate=pl.CostEstimate(flops=0, bytes_accessed=1 << 20, transcendentals=0),
         name="hold",
-    )(block, after)
+    )(*blocks, after)
+
+
+def stack_kernel(*refs):
+    for j in range(4):
+        refs[8][j] = refs[j][...]
+        refs[9][j] = refs[4 + j][...]
+
+
+def stack_fours(a, b):
+    vmem = pl.BlockSpec(memory_space=pltpu.VMEM)
+    shape = jax.ShapeDtypeStruct((4, *a[0].shape), BF16)
+    return pl.pallas_call(
+        stack_kernel,
+        out_shape=[shape, shape],
+        in_specs=[vmem] * 8,
+        out_specs=[vmem] * 2,
+        compiler_params=pltpu.CompilerParams(vmem_limit_bytes=8 << 20),
+        cost_estimate=pl.CostEstimate(flops=0, bytes_accessed=1 << 20, transcendentals=0),
+        name="stack_fours",
+    )(*a, *b)
 
 
 def enc_query_kernel(pos_ref, *refs):
@@ -223,7 +260,7 @@
     cond = pl.BlockSpec((4, CH, 256), lambda i, pos, pairs: (first + i, 0, 0))
     return pl.pallas_call(
         encode_kernel,
-        out_shape=(pltpu.HBM if base > 0 else jax.ShapeDtypeStruct)((count, NLEN, E), BF16),
+        out_shape=jax.ShapeDtypeStruct((count, NLEN, E), BF16),
         grid_spec=pltpu.PrefetchScalarGridSpec(
             num_scalar_prefetch=2,
             grid=(count // 4,),
@@ -250,9 +287,7 @@
 SPANS_STEP = 4
 
 
-def decode_kernel(carries, split, *refs):
-    if split:
-        block_ref, refs = refs[0], refs[1:]
+def decode_kernel(carries, block_ref, *refs):
     own_ref, other_ref, q_ref, wk_ref, wv_ref, wo_ref = refs[:6]
     rows, att, ks, vs = refs[-4:]
     for j in range(SPANS_STEP):
@@ -306,19 +341,13 @@
         att[s * CH : (s + 1) * CH, p * 256 + HD : (p + 1) * 256] = got[CH:, HD:]
     done = att[...]
     chunk = q_ref.shape[1]
-    if split:
-        for out_ref, first in ((refs[-6], 0), (refs[-5], 4)):
-            for j in range(4):
-                at = pl.multiple_of(block_ref[first + j] * chunk, chunk)
-                out_ref[j] = dot(done, wo_ref[:, pl.ds(at, chunk)]).astype(BF16)
-    else:
-        for n in range(wo_ref.shape[1] // chunk):
-            at = slice(n * chunk, (n + 1) * chunk)
-            refs[-5][:, at] = dot(done, wo_ref[:, at]).astype(BF16)
-
-
-def decode(first_span, own, other, queries, w_key, w_value, w_out, carried=(), blocks=None, after=()):
-    split = blocks is not None
+    for out_ref, first in ((refs[-6], 0), (refs[-5], 4)):
+        for j in range(4):
+            at = pl.multiple_of(block_ref[first + j] * chunk, chunk)
+            out_ref[j] = dot(done, wo_ref[:, pl.ds(at, chunk)]).astype(BF16)
+
+
+def decode(first_span, own, other, queries, w_key, w_value, w_out, blocks, carried=(), after=()):
     width = queries.shape[1]
     count = own.shape[0]
     tokens = count * CH
@@ -326,17 +355,13 @@
     first = first_span // SPANS_STEP
     rows = SPANS_STEP * KNB * NLEN
     block = pl.BlockSpec((SPANS_STEP, NLEN, E), lambda i, *_: (i, 0, 0))
-    if split:
-        out_shape = [jax.ShapeDtypeStruct((4, tokens, width), BF16)] * 2
-        out_specs = [pl.BlockSpec((4, tile, width), lambda i, *_: (0, i, 0))] * 2
-    else:
-        out_shape = pltpu.HBM((tokens, D), BF16)
-        out_specs = pl.BlockSpec((tile, D), lambda i, *_: (i, 0))
+    out_shape = [jax.ShapeDtypeStruct((4, tokens, width), BF16)] * 2
+    out_specs = [pl.BlockSpec((4, tile, width), lambda i, *_: (0, i, 0))] * 2
     return pl.pallas_call(
-        lambda *refs: decode_kernel(len(carried) > 0, split, *refs),
+        lambda *refs: decode_kernel(len(carried) > 0, *refs),
         out_shape=out_shape,
         grid_spec=pltpu.PrefetchScalarGridSpec(
-            num_scalar_prefetch=int(split),
+            num_scalar_prefetch=1,
             grid=(count // SPANS_STEP,),
             in_specs=[
                 block,
@@ -357,7 +382,7 @@
             ],
         ),
         compiler_params=pltpu.CompilerParams(
-            dimension_semantics=("arbitrary",), vmem_limit_bytes=(60 << 20) if split else VMEM_LIMIT
+            dimension_semantics=("arbitrary",), vmem_limit_bytes=VMEM_LIMIT
         ),
         cost_estimate=pl.CostEstimate(
             flops=4 * count * KNB * NLEN * E * width + 2 * count * CH * width * D,
@@ -365,7 +390,7 @@
             transcendentals=count * CH * KNB * NLEN * (width // HD),
         ),
         name="decode",
-    )(*([blocks] if split else []), own, other, queries, w_key, w_value, w_out, *carried, *after)
+    )(blocks, own, other, queries, w_key, w_value, w_out, *carried, *after)
 
 
 def body(
@@ -410,8 +435,11 @@
         ],
         axis=1,
     )
-    row = jnp.stack(around(weight, side, False))
-    parts = around(row, side, True)
+    half = weight.shape[0] // 2
+    a_four, b_four = stack_fours(
+        around(weight[:half], side, False), around(weight[half:], side, True)
+    )
+    parts = around(a_four, side, True) + around(b_four, side, False)
     rel = jnp.array(REL, jnp.int32)
     y_at, z_at = seq_rank // side, seq_rank % side
     from_rank = jnp.concatenate([(y_at + rel + side) % side, (z_at + rel + side) % side])
@@ -430,7 +458,7 @@
     )
     enc_query = pltpu.with_memory_space_constraint(enc_query, pltpu.HBM)
     enc_q = enc_queries(mine, gathered, enc_query)
-    own_lane[1] = hold(own_lane[1], enc_q)
+    own_lane[1:] = hold(own_lane[1:], enc_q)
     conds = own_lane + [swap_cores(block) for block in own_lane]
     part = span_count // 2
     low = encode(0, part, mine, pairs, enc_q, gathered, conds, enc_out, ())
@@ -449,7 +477,7 @@
     )
     high = encode(part, part, mine, pairs, enc_q, gathered, conds, enc_out, (low,))
     high_other = swap_cores(high)
-    terms = decode(
+    low_terms = decode(
         0,
         low,
         low_other,
@@ -457,22 +485,17 @@
         w_key,
         w_value,
         w_out,
+        pairs,
         carried=(carried, carried_other),
         after=(high,),
     )
-    low_out = lax.psum_scatter(terms, "store", scatter_dimension=1, tiled=True)
-    kept, given = decode(
-        part, high, high_other, queries, w_key, w_value, w_out, blocks=pairs, after=(terms,)
-    )
-    taken = swap_cores(given)
-    sums = [kept[j].astype(F32) + taken[j].astype(F32) for j in range(4)]
-    high_out = sums[0]
-    for j in range(1, 4):
-        route = [
-            (2 * x + k, 2 * ((x + REL[j]) % chips) + k) for x in range(chips) for k in range(2)
-        ]
-        high_out = high_out + lax.ppermute(sums[j].astype(BF16), "store", route).astype(F32)
-    return jnp.concatenate([low_out, high_out.astype(BF16)], axis=0)
+    low_sums = core_sums(*low_terms)
+    low_out = sum_over_x(low_sums, chips)
+    high_terms = decode(
+        part, high, high_other, queries, w_key, w_value, w_out, pairs, after=low_sums[1:]
+    )
+    high_out = sum_over_x(core_sums(*high_terms), chips)
+    return jnp.concatenate([low_out, high_out], axis=0).astype(BF16)
 
 
 def solution(mesh):

time: 201 us -> 197 us (0.980)
  starting transfers between devices: 27.1 us -> 45.9 us
  waiting for transfers between devices: 79.2 us -> 65.9 us
  Pallas kernels: 55.3 us -> 49 us
  other arithmetic: 6.79 us -> 4.06 us
    ppermute x3, waiting for transfers between devices: 17.7 us -> 0.01 us  [around_x(): got.append(lax.ppermute(block, 'store', route))]
    ppermute x6 -> x12, waiting for transfers between devices: 20.3 us -> 4.29 us  [around(): got.append(lax.ppermute(block, 'seq', route))]
    all_gather x1, waiting for transfers between devices: 0.01 us -> 12.4 us  [body(): gathered = lax.all_gather(sources, 'store', axis=0, tiled=True)]
    ppermute x3 -> x6, waiting for transfers between devices: 27.5 us -> 39.7 us  [sum_over_x(): total = total + lax.ppermute(sums[j], 'store', route).astype(F32)]
    pallas_call x5 -> x6, Pallas kernels: 41 us -> 34.6 us  [the longest x2 20 us: decode(): pl.pallas_call(lambda *refs: decode_kernel(len(carried) > 0, *refs), out_...]
    ppermute x6 -> x12, starting transfers between devices: 8.69 us -> 15.1 us  [around(): got.append(lax.ppermute(block, 'seq', route))]
    ppermute x3 -> x6, starting transfers between devices: 3.23 us -> 8.58 us  [sum_over_x(): total = total + lax.ppermute(sums[j], 'store', route).astype(F32)]
    ppermute x7 -> x8, starting transfers between devices: 6.64 us -> 10.5 us  [swap_cores(): return lax.ppermute(block, 'store', [(i, i ^ 1) for i in range(count)])]
  transfers between devices with their start and end apart: 23 -> 32, of which waited for: 12 -> 16; matrix products, arithmetic and copies ran while one was open for 7% -> 7% of each run, Pallas kernels for 19% -> 11%
where the time goes in v5:
time: 197 us; the launch traced here: 195 us
  waiting for transfers between devices  65.9 us (33%)
  Pallas kernels  49 us (25%)
  starting transfers between devices  45.9 us (23%)
  between operations  13.7 us (7%)
  matrix products  10.2 us (5%)
  local copies, waits for them, and re-layouts  6.42 us (3%)
  other arithmetic  4.06 us (2%)
    ppermute x6, waiting for transfers between devices, sum_over_x(): total = total + lax.ppermute(sums[j], 'store', route).astype(F32)  39.7 us
    pallas_call x2, Pallas kernels, decode(): pl.pallas_call(lambda *refs: decode_kernel(len(carried) > 0, *refs), out_...  20 us
    ppermute x12, starting transfers between devices, around(): got.append(lax.ppermute(block, 'seq', route))  15.1 us
    pallas_call x2, Pallas kernels, encode(): pl.pallas_call(encode_kernel, out_shape=jax.ShapeDtypeStruct((count, NLEN...  14.5 us
    all_gather x1, waiting for transfers between devices, body(): gathered = lax.all_gather(sources, 'store', axis=0, tiled=True)  12.4 us
    ppermute x8, starting transfers between devices, swap_cores(): return lax.ppermute(block, 'store', [(i, i ^ 1) for i in range(count)])  10.5 us
    dot_general x1, matrix products, dot(): return jnp.dot(a, b, preferred_element_type=F32)  10.2 us
    ppermute x6, starting transfers between devices, sum_over_x(): total = total + lax.ppermute(sums[j], 'store', route).astype(F32)  8.58 us
  transfers between devices with their start and end apart: 32, of which 16 were waited for; matrix products, arithmetic and copies ran while one was open for 7% of the time, Pallas kernels for 11%

profile of v5, /device:TPU:9, one launch (start us, length us, event | category | flops | bytes accessed | tf_op | source)
XLA Modules:
  0.0 195.2 jit_solution(4604083067455850291)
XLA Ops:
  6.5 0.9 copy.16
  7.9 0.7 broadcast_add_fusion
  8.6 0.6 gather_fusion
  9.3 1.7 gather_fusion.1
  11.0 0.9 constant_dynamic-slice_fusion
  11.9 2.1 %collective-permute-start.5 = (bf16[128,256]{1,0:T(8,128)(2,1)S(1)}, bf16[128,256]{1,0:T(8,128)(2,1)S(1)}, u32[]{:S(2)}, u32[]{:S(2)}) collective-permute-start(bf16[128,256]{1,0:T(8,128)(2,1)S(1)} %get-tuple-element.31.refs_4_), channel_id=1, source_target_pairs={{0,64},{8,72},{16,80},{24,88},{32,96},{40,104},{48,112},{56,120},{... | collective-permute-start | bytes 196616 | tf_op jit(solution)/shard_map/ppermute | solution.py:44
  14.0 1.1 collective-permute-start.4
  15.5 3.6 %collective-permute-start.2 = (bf16[128,256]{1,0:T(8,128)(2,1)S(1)}, bf16[128,256]{1,0:T(8,128)(2,1)S(1)}, u32[]{:S(2)}, u32[]{:S(2)}) collective-permute-start(bf16[128,256]{1,0:T(8,128)(2,1)S(1)} %get-tuple-element.32.refs_0_), channel_id=1, source_target_pairs={{0,16},{8,24},{16,0},{24,8},{32,48},{40,56},{48,32},{56,40},{64,80... | collective-permute-start | bytes 196616 | tf_op jit(solution)/shard_map/ppermute | solution.py:44
  19.5 1.0 collective-permute-start
  20.7 1.8 collective-permute-done.1.refs_2_
  22.5 1.4 collective-permute-done.refs_1_
  23.9 2.2 %collective-permute-start.8 = (bf16[4,128,256]{2,1,0:T(8,128)(2,1)S(1)}, bf16[4,128,256]{2,1,0:T(8,128)(2,1)S(1)}, u32[]{:S(2)}, u32[]{:S(2)}) collective-permute-start(bf16[4,128,256]{2,1,0:T(8,128)(2,1)S(1)} %get-tuple-element.14.refs_0_), channel_id=1, source_target_pairs={{0,64},{8,72},{16,80},{24,88},{32,96},{40,104},{48,112},{56,120},{... | collective-permute-start | bytes 786440 | tf_op jit(solution)/shard_map/ppermute | solution.py:44
  26.1 1.5 collective-permute-start.6
  27.6 1.2 collective-permute-start.11
  28.8 1.4 collective-permute-start.10
  30.1 1.0 collective-permute-done.8.refs_3_
  31.3 10.2 %convolution_convert_fusion.refs_8_.refs_3_ = bf16[1024,512]{1,0:T(8,128)(2,1)} fusion(bf16[1024,4096]{1,0:T(8,128)(2,1)} %hidden_ref.1, bf16[4096,512]{1,0:T(8,128)(2,1)} %param.15), kind=kOutput, calls=%fused_computation.2 | convolution fusion | flops 4295491584 | bytes 13631488 | tf_op jit(solution)/shard_map/dot_general | solution.py:29
  41.6 6.3 %cond_rows.1 = bf16[1024,256]{1,0:T(8,128)(2,1)S(1)} custom-call(s32[8]{0:T(128)S(1)} %pad_add_fusion.1.src_ref, bf16[1024,4096]{1,0:T(8,128)(2,1)} %hidden_ref.1, bf16[4,128,256]{2,1,0:T(8,128)(2,1)S(1)} %get-tuple-element.14.refs_0_, bf16[4,128,256]{2,1,0:T(8,128)(2,1)S(1)} %collective-permute-done.6.refs_1_, ...), custom_call_target="tpu_custom_call" | custom-call | flops 2147483648 | bytes 12582912 | tf_op jit(solution)/shard_map/cond_rows/pallas_call | solution.py:106
  47.8 2.5 %collective-permute-start.14 = (bf16[16,64,256]{2,1,0:T(8,128)(2,1)S(1)}, bf16[16,64,256]{2,1,0:T(8,128)(2,1)S(1)}, u32[]{:S(2)}, u32[]{:S(2)}) collective-permute-start(bf16[16,64,256]{2,1,0:T(8,128)(2,1)S(1)} %bitcast.35), channel_id=1, source_target_pairs={{0,4},{1,5},{2,6},{3,7},{4,0},{5,1},{6,2},{7,3},{8,12},{9,13},{10,... | collective-permute-start | bytes 1572872 | tf_op jit(solution)/shard_map/ppermute | solution.py:54
  50.4 0.9 collective-permute-start.13
  52.0 7.7 %collective-permute-start.15 = (bf16[16,64,256]{2,1,0:T(8,128)(2,1)S(1)}, bf16[16,64,256]{2,1,0:T(8,128)(2,1)S(1)}, u32[]{:S(2)}, u32[]{:S(2)}) collective-permute-start(bf16[16,64,256]{2,1,0:T(8,128)(2,1)S(1)} %bitcast.38), channel_id=1, source_target_pairs={{0,1},{1,0},{2,3},{3,2},{4,5},{5,4},{6,7},{7,6},{8,9},{9,8},{10,11... | collective-permute-start | bytes 1572872 | tf_op jit(solution)/shard_map/ppermute | solution.py:60
  59.7 12.4 %all-gather.3.cloned.1.call-done.refs_0_.refs_1_.refs_2_.refs_3_ = bf16[32,128,896]{2,1,0:T(8,128)(2,1)} async-done(((bf16[4,128,896]{2,1,0:T(8,128)(2,1)}), bf16[32,128,896]{2,1,0:T(8,128)(2,1)}) %all-gather.3.cloned.1.call-update) | async-done | bytes 7340048 | tf_op jit(solution)/shard_map/all_gather | solution.py:427
  72.1 8.1 %enc_queries.1.refs_3_.refs_12_ = bf16[16,128,896]{2,1,0:T(8,128)(2,1)S(1)} custom-call(s32[16]{0:T(128)S(1)} %select_reduce_fusion.1.pos_ref, bf16[32,128,896]{2,1,0:T(8,128)(2,1)} %all-gather.3.cloned.1.call-done.refs_0_.refs_1_.refs_2_.refs_3_, bf16[32,128,896]{2,1,0:T(8,128)(2,1)} %all-gather.3.cloned.1.call-done.refs_0_.refs_1_.refs_2_.refs_3_, ...), custom_call_target="tpu_custom_call" | custom-call | flops 3288334336 | bytes 10485760 | tf_op jit(solution)/shard_map/enc_queries/pallas_call | solution.py:187
  81.3 1.1 collective-permute-done.16.refs_9_
  82.4 0.7 collective-permute-done.17.refs_10_
  83.1 0.7 collective-permute-done.18.refs_11_
  83.9 7.3 %encode.2.refs_14_.refs_1_ = bf16[8,128,896]{2,1,0:T(8,128)(2,1)S(1)} custom-call(s32[16]{0:T(128)S(1)} %select_reduce_fusion.1.pos_ref, s32[8]{0:T(128)S(1)} %pad_add_fusion.pair_ref.refs_0_, bf16[32,128,896]{2,1,0:T(8,128)(2,1)} %all-gather.3.cloned.1.call-done.refs_0_.refs_1_.refs_2_.refs_3_, ...), custom_call_target="tpu_custom_call" | custom-call | flops 2466250752 | bytes 8388608 | tf_op jit(solution)/shard_map/encode/pallas_call | solution.py:261
  91.5 4.2 %collective-permute-start.21 = (bf16[1,128,896]{2,1,0:T(8,128)(2,1)S(1)}, bf16[1,128,896]{2,1,0:T(8,128)(2,1)S(1)}, u32[]{:S(2)}, u32[]{:S(2)}) collective-permute-start(bf16[1,128,896]{2,1,0:T(8,128)(2,1)S(1)} %slice.83), channel_id=1, source_target_pairs={{0,9},{1,8},{2,11},{3,10},{4,13},{5,12},{6,15},{7,14},{8,17},{9,16... | collective-permute-start | bytes 688136 | tf_op jit(solution)/shard_map/ppermute | solution.py:467
  95.8 3.6 %collective-permute-start.20 = (bf16[1,128,896]{2,1,0:T(8,128)(2,1)S(1)}, bf16[1,128,896]{2,1,0:T(8,128)(2,1)S(1)}, u32[]{:S(2)}, u32[]{:S(2)}) collective-permute-start(bf16[1,128,896]{2,1,0:T(8,128)(2,1)S(1)} %slice.83), channel_id=1, source_target_pairs={{0,8},{1,9},{2,10},{3,11},{4,12},{5,13},{6,14},{7,15},{8,16},{9,17... | collective-permute-start | bytes 688136 | tf_op jit(solution)/shard_map/ppermute | solution.py:467
  99.4 7.3 %encode.3.refs_9_.refs_1_ = bf16[8,128,896]{2,1,0:T(8,128)(2,1)S(1)} custom-call(s32[16]{0:T(128)S(1)} %select_reduce_fusion.1.pos_ref, s32[8]{0:T(128)S(1)} %pad_add_fusion.pair_ref.refs_0_, bf16[32,128,896]{2,1,0:T(8,128)(2,1)} %all-gather.3.cloned.1.call-done.refs_0_.refs_1_.refs_2_.refs_3_, ...), custom_call_target="tpu_custom_call" | custom-call | flops 2466250752 | bytes 8388608 | tf_op jit(solution)/shard_map/encode/pallas_call | solution.py:261
  106.7 1.3 collective-permute-done.20.refs_7_
  108.1 2.2 %copy-done.3 = bf16[512,4096]{1,0:T(8,128)(2,1)S(1)} copy-done((bf16[512,4096]{1,0:T(8,128)(2,1)S(1)}, bf16[512,4096]{1,0:T(8,128)(2,1)}, u32[]{:S(2)}) %copy-start.3) | copy-done | bytes 4194328
  110.2 10.1 %decode.2 = (bf16[4,512,512]{2,1,0:T(8,128)(2,1)S(1)}, bf16[4,512,512]{2,1,0:T(8,128)(2,1)S(1)}) custom-call(s32[8]{0:T(128)S(1)} %pad_add_fusion.pair_ref.refs_0_, bf16[8,128,896]{2,1,0:T(8,128)(2,1)S(1)} %encode.2.refs_14_.refs_1_, bf16[8,128,896]{2,1,0:T(8,128)(2,1)S(1)} %collective-permute-done.19.refs_2_, ...), custom_call_target="tpu_custom_call" | custom-call | flops 5905580032 | bytes 12582912 | tf_op jit(solution)/shard_map/decode/pallas_call | solution.py:360
  120.4 0.8 collective-permute-start.22
  121.5 3.5 %collective-permute-done.22 = bf16[4,512,512]{2,1,0:T(8,128)(2,1)S(1)} collective-permute-done((bf16[4,512,512]{2,1,0:T(8,128)(2,1)S(1)}, bf16[4,512,512]{2,1,0:T(8,128)(2,1)S(1)}, u32[]{:S(2)}, u32[]{:S(2)}) %collective-permute-start.22) | collective-permute-done | bytes 2097184 | tf_op jit(solution)/shard_map/ppermute | solution.py:60
  125.4 2.2 %collective-permute-done.26.refs_2_ = bf16[8,128,896]{2,1,0:T(8,128)(2,1)S(1)} collective-permute-done((bf16[8,128,896]{2,1,0:T(8,128)(2,1)S(1)}, bf16[8,128,896]{2,1,0:T(8,128)(2,1)S(1)}, u32[]{:S(2)}, u32[]{:S(2)}) %collective-permute-start.26) | collective-permute-done | bytes 1835040 | tf_op jit(solution)/shard_map/ppermute | solution.py:60
  127.6 9.8 %decode.3 = (bf16[4,512,512]{2,1,0:T(8,128)(2,1)S(1)}, bf16[4,512,512]{2,1,0:T(8,128)(2,1)S(1)}) custom-call(s32[8]{0:T(128)S(1)} %pad_add_fusion.pair_ref.refs_0_, bf16[8,128,896]{2,1,0:T(8,128)(2,1)S(1)} %encode.3.refs_9_.refs_1_, bf16[8,128,896]{2,1,0:T(8,128)(2,1)S(1)} %collective-permute-done.26.refs_2_, ...), custom_call_target="tpu_custom_call" | custom-call | flops 5905580032 | bytes 12582912 | tf_op jit(solution)/shard_map/decode/pallas_call | solution.py:360
  137.9 1.1 collective-permute-start.25
  139.4 2.4 %collective-permute-start.23 = (bf16[512,512]{1,0:T(8,128)(2,1)S(1)}, bf16[512,512]{1,0:T(8,128)(2,1)S(1)}, u32[]{:S(2)}, u32[]{:S(2)}) collective-permute-start(bf16[512,512]{1,0:T(8,128)(2,1)S(1)} %get-tuple-element.30.refs_7_), channel_id=1, source_target_pairs={{0,6},{1,7},{2,0},{3,1},{4,2},{5,3},{6,4},{7,5},{8,14},{9,15},{10,... | collective-permute-start | bytes 1572872 | tf_op jit(solution)/shard_map/ppermute | solution.py:75
  142.2 1.5 collective-permute-start.28
  143.8 1.7 collective-permute-start.30
  145.5 7.4 %collective-permute-done.25 = bf16[512,512]{1,0:T(8,128)(2,1)S(1)} collective-permute-done((bf16[512,512]{1,0:T(8,128)(2,1)S(1)}, bf16[512,512]{1,0:T(8,128)(2,1)S(1)}, u32[]{:S(2)}, u32[]{:S(2)}) %collective-permute-start.25) | collective-permute-done | bytes 524320 | tf_op jit(solution)/shard_map/ppermute | solution.py:75
  152.9 1.5 collective-permute-start.29
  154.3 10.6 %collective-permute-done.24 = bf16[512,512]{1,0:T(8,128)(2,1)S(1)} collective-permute-done((bf16[512,512]{1,0:T(8,128)(2,1)S(1)}, bf16[512,512]{1,0:T(8,128)(2,1)S(1)}, u32[]{:S(2)}, u32[]{:S(2)}) %collective-permute-start.24) | collective-permute-done | bytes 524320 | tf_op jit(solution)/shard_map/ppermute | solution.py:75
  165.3 8.8 %collective-permute-done.28 = bf16[512,512]{1,0:T(8,128)(2,1)S(1)} collective-permute-done((bf16[512,512]{1,0:T(8,128)(2,1)S(1)}, bf16[512,512]{1,0:T(8,128)(2,1)S(1)}, u32[]{:S(2)}, u32[]{:S(2)}) %collective-permute-start.28) | collective-permute-done | bytes 524320 | tf_op jit(solution)/shard_map/ppermute | solution.py:75
  174.1 1.3 collective-permute-done.30
  175.4 11.6 %collective-permute-done.29 = bf16[512,512]{1,0:T(8,128)(2,1)S(1)} collective-permute-done((bf16[512,512]{1,0:T(8,128)(2,1)S(1)}, bf16[512,512]{1,0:T(8,128)(2,1)S(1)}, u32[]{:S(2)}, u32[]{:S(2)}) %collective-permute-start.29) | collective-permute-done | bytes 524320 | tf_op jit(solution)/shard_map/ppermute | solution.py:75
  187.3 1.0 pad_maximum_fusion
  (64 shorter events, 6.7 us)
Async XLA Ops:
  6.5 2.7 %copy-start = (bf16[8,128,896]{2,1,0:T(8,128)(2,1)S(1)}, bf16[8,128,896]{2,1,0:T(8,128)(2,1)}, u32[]{:S(2)}) copy-start(bf16[8,128,896]{2,1,0:T(8,128)(2,1)} %param.13) | copy-start | bytes 5505028
  6.5 65.6 %all-gather.3.cloned.1.call-start = ((), (), s32[]{:S(2)}) async-start(), calls=%async_computation | async-start | bytes 8257536 | tf_op jit(solution)/shard_map/all_gather | solution.py:427
  11.9 7.6 %collective-permute-start.5 = (bf16[128,256]{1,0:T(8,128)(2,1)S(1)}, bf16[128,256]{1,0:T(8,128)(2,1)S(1)}, u32[]{:S(2)}, u32[]{:S(2)}) collective-permute-start(bf16[128,256]{1,0:T(8,128)(2,1)S(1)} %get-tuple-element.31.refs_4_), channel_id=1, source_target_pairs={{0,64},{8,72},{16,80},{24,88},{32,96},{40,104},{48,112},{56,120},{... | collective-permute-start | bytes 196616 | tf_op jit(solution)/shard_map/ppermute | solution.py:44
  14.0 6.5 %collective-permute-start.4 = (bf16[128,256]{1,0:T(8,128)(2,1)S(1)}, bf16[128,256]{1,0:T(8,128)(2,1)S(1)}, u32[]{:S(2)}, u32[]{:S(2)}) collective-permute-start(bf16[128,256]{1,0:T(8,128)(2,1)S(1)} %get-tuple-element.31.refs_4_), channel_id=1, source_target_pairs={{0,96},{8,104},{16,112},{24,120},{32,0},{40,8},{48,16},{56,24},{64... | collective-permute-start | bytes 196616 | tf_op jit(solution)/shard_map/ppermute | solution.py:44
  15.1 5.5 %collective-permute-start.3 = (bf16[128,256]{1,0:T(8,128)(2,1)S(1)}, bf16[128,256]{1,0:T(8,128)(2,1)S(1)}, u32[]{:S(2)}, u32[]{:S(2)}) collective-permute-start(bf16[128,256]{1,0:T(8,128)(2,1)S(1)} %get-tuple-element.31.refs_4_), channel_id=1, source_target_pairs={{0,32},{8,40},{16,48},{24,56},{32,64},{40,72},{48,80},{56,88},{64,... | collective-permute-start | bytes 196616 | tf_op jit(solution)/shard_map/ppermute | solution.py:44
  15.5 5.2 %collective-permute-start.2 = (bf16[128,256]{1,0:T(8,128)(2,1)S(1)}, bf16[128,256]{1,0:T(8,128)(2,1)S(1)}, u32[]{:S(2)}, u32[]{:S(2)}) collective-permute-start(bf16[128,256]{1,0:T(8,128)(2,1)S(1)} %get-tuple-element.32.refs_0_), channel_id=1, source_target_pairs={{0,16},{8,24},{16,0},{24,8},{32,48},{40,56},{48,32},{56,40},{64,80... | collective-permute-start | bytes 196616 | tf_op jit(solution)/shard_map/ppermute | solution.py:44
  19.1 3.4 %collective-permute-start.1 = (bf16[128,256]{1,0:T(8,128)(2,1)S(1)}, bf16[128,256]{1,0:T(8,128)(2,1)S(1)}, u32[]{:S(2)}, u32[]{:S(2)}) collective-permute-start(bf16[128,256]{1,0:T(8,128)(2,1)S(1)} %get-tuple-element.32.refs_0_), channel_id=1, source_target_pairs={{0,24},{8,0},{16,8},{24,16},{32,56},{40,32},{48,40},{56,48},{64,88... | collective-permute-start | bytes 196616 | tf_op jit(solution)/shard_map/ppermute | solution.py:44
  19.5 4.3 %collective-permute-start = (bf16[128,256]{1,0:T(8,128)(2,1)S(1)}, bf16[128,256]{1,0:T(8,128)(2,1)S(1)}, u32[]{:S(2)}, u32[]{:S(2)}) collective-permute-start(bf16[128,256]{1,0:T(8,128)(2,1)S(1)} %get-tuple-element.32.refs_0_), channel_id=1, source_target_pairs={{0,8},{8,16},{16,24},{24,0},{32,40},{40,48},{48,56},{56,32},{64,72... | collective-permute-start | bytes 196616 | tf_op jit(solution)/shard_map/ppermute | solution.py:44
  23.9 7.2 %collective-permute-start.8 = (bf16[4,128,256]{2,1,0:T(8,128)(2,1)S(1)}, bf16[4,128,256]{2,1,0:T(8,128)(2,1)S(1)}, u32[]{:S(2)}, u32[]{:S(2)}) collective-permute-start(bf16[4,128,256]{2,1,0:T(8,128)(2,1)S(1)} %get-tuple-element.14.refs_0_), channel_id=1, source_target_pairs={{0,64},{8,72},{16,80},{24,88},{32,96},{40,104},{48,112},{56,120},{... | collective-permute-start | bytes 786440 | tf_op jit(solution)/shard_map/ppermute | solution.py:44
  26.1 15.4 %collective-permute-start.7 = (bf16[4,128,256]{2,1,0:T(8,128)(2,1)S(1)}, bf16[4,128,256]{2,1,0:T(8,128)(2,1)S(1)}, u32[]{:S(2)}, u32[]{:S(2)}) collective-permute-start(bf16[4,128,256]{2,1,0:T(8,128)(2,1)S(1)} %get-tuple-element.14.refs_0_), channel_id=1, source_target_pairs={{0,96},{8,104},{16,112},{24,120},{32,0},{40,8},{48,16},{56,24},{64... | collective-permute-start | bytes 786440 | tf_op jit(solution)/shard_map/ppermute | solution.py:44
  26.1 15.4 %collective-permute-start.6 = (bf16[4,128,256]{2,1,0:T(8,128)(2,1)S(1)}, bf16[4,128,256]{2,1,0:T(8,128)(2,1)S(1)}, u32[]{:S(2)}, u32[]{:S(2)}) collective-permute-start(bf16[4,128,256]{2,1,0:T(8,128)(2,1)S(1)} %get-tuple-element.14.refs_0_), channel_id=1, source_target_pairs={{0,32},{8,40},{16,48},{24,56},{32,64},{40,72},{48,80},{56,88},{64,... | collective-permute-start | bytes 786440 | tf_op jit(solution)/shard_map/ppermute | solution.py:44
  27.6 14.0 %collective-permute-start.11 = (bf16[4,128,256]{2,1,0:T(8,128)(2,1)S(1)}, bf16[4,128,256]{2,1,0:T(8,128)(2,1)S(1)}, u32[]{:S(2)}, u32[]{:S(2)}) collective-permute-start(bf16[4,128,256]{2,1,0:T(8,128)(2,1)S(1)} %get-tuple-element.15.refs_4_), channel_id=1, source_target_pairs={{0,16},{8,24},{16,0},{24,8},{32,48},{40,56},{48,32},{56,40},{64,80... | collective-permute-start | bytes 786440 | tf_op jit(solution)/shard_map/ppermute | solution.py:44
  28.8 12.8 %collective-permute-start.10 = (bf16[4,128,256]{2,1,0:T(8,128)(2,1)S(1)}, bf16[4,128,256]{2,1,0:T(8,128)(2,1)S(1)}, u32[]{:S(2)}, u32[]{:S(2)}) collective-permute-start(bf16[4,128,256]{2,1,0:T(8,128)(2,1)S(1)} %get-tuple-element.15.refs_4_), channel_id=1, source_target_pairs={{0,24},{8,0},{16,8},{24,16},{32,56},{40,32},{48,40},{56,48},{64,88... | collective-permute-start | bytes 786440 | tf_op jit(solution)/shard_map/ppermute | solution.py:44
  31.1 10.5 %collective-permute-start.9 = (bf16[4,128,256]{2,1,0:T(8,128)(2,1)S(1)}, bf16[4,128,256]{2,1,0:T(8,128)(2,1)S(1)}, u32[]{:S(2)}, u32[]{:S(2)}) collective-permute-start(bf16[4,128,256]{2,1,0:T(8,128)(2,1)S(1)} %get-tuple-element.15.refs_4_), channel_id=1, source_target_pairs={{0,8},{8,16},{16,24},{24,0},{32,40},{40,48},{48,56},{56,32},{64,72... | collective-permute-start | bytes 786440 | tf_op jit(solution)/shard_map/ppermute | solution.py:44
  47.8 32.4 %collective-permute-start.14 = (bf16[16,64,256]{2,1,0:T(8,128)(2,1)S(1)}, bf16[16,64,256]{2,1,0:T(8,128)(2,1)S(1)}, u32[]{:S(2)}, u32[]{:S(2)}) collective-permute-start(bf16[16,64,256]{2,1,0:T(8,128)(2,1)S(1)} %bitcast.35), channel_id=1, source_target_pairs={{0,4},{1,5},{2,6},{3,7},{4,0},{5,1},{6,2},{7,3},{8,12},{9,13},{10,... | collective-permute-start | bytes 1572872 | tf_op jit(solution)/shard_map/ppermute | solution.py:54
  50.4 29.9 %collective-permute-start.13 = (bf16[16,64,256]{2,1,0:T(8,128)(2,1)S(1)}, bf16[16,64,256]{2,1,0:T(8,128)(2,1)S(1)}, u32[]{:S(2)}, u32[]{:S(2)}) collective-permute-start(bf16[16,64,256]{2,1,0:T(8,128)(2,1)S(1)} %bitcast.36), channel_id=1, source_target_pairs={{0,6},{1,7},{2,0},{3,1},{4,2},{5,3},{6,4},{7,5},{8,14},{9,15},{10,... | collective-permute-start | bytes 1572872 | tf_op jit(solution)/shard_map/ppermute | solution.py:54
  51.2 29.0 %collective-permute-start.12 = (bf16[16,64,256]{2,1,0:T(8,128)(2,1)S(1)}, bf16[16,64,256]{2,1,0:T(8,128)(2,1)S(1)}, u32[]{:S(2)}, u32[]{:S(2)}) collective-permute-start(bf16[16,64,256]{2,1,0:T(8,128)(2,1)S(1)} %bitcast.37), channel_id=1, source_target_pairs={{0,2},{1,3},{2,4},{3,5},{4,6},{5,7},{6,0},{7,1},{8,10},{9,11},{10,... | collective-permute-start | bytes 1572872 | tf_op jit(solution)/shard_map/ppermute | solution.py:54
  52.0 29.3 %collective-permute-start.15 = (bf16[16,64,256]{2,1,0:T(8,128)(2,1)S(1)}, bf16[16,64,256]{2,1,0:T(8,128)(2,1)S(1)}, u32[]{:S(2)}, u32[]{:S(2)}) collective-permute-start(bf16[16,64,256]{2,1,0:T(8,128)(2,1)S(1)} %bitcast.38), channel_id=1, source_target_pairs={{0,1},{1,0},{2,3},{3,2},{4,5},{5,4},{6,7},{7,6},{8,9},{9,8},{10,11... | collective-permute-start | bytes 1572872 | tf_op jit(solution)/shard_map/ppermute | solution.py:60
  80.2 3.6 %copy-start.2 = (bf16[896,896]{1,0:T(8,128)(2,1)S(1)}, bf16[896,896]{1,0:T(8,128)(2,1)}, u32[]{:S(2)}) copy-start(bf16[896,896]{1,0:T(8,128)(2,1)} %refs_13_.3) | copy-start | bytes 4816900
  80.4 2.0 %collective-permute-start.16 = (bf16[16,64,256]{2,1,0:T(8,128)(2,1)S(1)}, bf16[16,64,256]{2,1,0:T(8,128)(2,1)S(1)}, u32[]{:S(2)}, u32[]{:S(2)}) collective-permute-start(bf16[16,64,256]{2,1,0:T(8,128)(2,1)S(1)} %get-tuple-element.16.refs_5_), channel_id=1, source_target_pairs={{0,1},{1,0},{2,3},{3,2},{4,5},{5,4},{6,7},{7,6},{8,9},{9,8},{10,11... | collective-permute-start | bytes 1572872 | tf_op jit(solution)/shard_map/ppermute | solution.py:60
  80.7 2.4 %collective-permute-start.17 = (bf16[16,64,256]{2,1,0:T(8,128)(2,1)S(1)}, bf16[16,64,256]{2,1,0:T(8,128)(2,1)S(1)}, u32[]{:S(2)}, u32[]{:S(2)}) collective-permute-start(bf16[16,64,256]{2,1,0:T(8,128)(2,1)S(1)} %get-tuple-element.17.refs_6_), channel_id=1, source_target_pairs={{0,1},{1,0},{2,3},{3,2},{4,5},{5,4},{6,7},{7,6},{8,9},{9,8},{10,11... | collective-permute-start | bytes 1572872 | tf_op jit(solution)/shard_map/ppermute | solution.py:60
  81.0 2.9 %collective-permute-start.18 = (bf16[16,64,256]{2,1,0:T(8,128)(2,1)S(1)}, bf16[16,64,256]{2,1,0:T(8,128)(2,1)S(1)}, u32[]{:S(2)}, u32[]{:S(2)}) collective-permute-start(bf16[16,64,256]{2,1,0:T(8,128)(2,1)S(1)} %get-tuple-element.18.refs_7_), channel_id=1, source_target_pairs={{0,1},{1,0},{2,3},{3,2},{4,5},{5,4},{6,7},{7,6},{8,9},{9,8},{10,11... | collective-permute-start | bytes 1572872 | tf_op jit(solution)/shard_map/ppermute | solution.py:60
  91.2 16.9 %collective-permute-start.19 = (bf16[8,128,896]{2,1,0:T(8,128)(2,1)S(1)}, bf16[8,128,896]{2,1,0:T(8,128)(2,1)S(1)}, u32[]{:S(2)}, u32[]{:S(2)}) collective-permute-start(bf16[8,128,896]{2,1,0:T(8,128)(2,1)S(1)} %encode.2.refs_14_.refs_1_), channel_id=1, source_target_pairs={{0,1},{1,0},{2,3},{3,2},{4,5},{5,4},{6,7},{7,6},{8,9},{9,8},{10,11... | collective-permute-start | bytes 5505032 | tf_op jit(solution)/shard_map/ppermute | solution.py:60
  91.5 16.5 %copy-start.5 = (bf16[896,512]{1,0:T(8,128)(2,1)S(1)}, bf16[896,512]{1,0:T(8,128)(2,1)}, u32[]{:S(2)}) copy-start(bf16[896,512]{1,0:T(8,128)(2,1)} %refs_4_.5) | copy-start | bytes 2752516
  91.5 16.5 %copy-start.6 = (bf16[896,512]{1,0:T(8,128)(2,1)S(1)}, bf16[896,512]{1,0:T(8,128)(2,1)}, u32[]{:S(2)}) copy-start(bf16[896,512]{1,0:T(8,128)(2,1)} %refs_5_.3) | copy-start | bytes 2752516
  91.5 15.2 %collective-permute-start.21 = (bf16[1,128,896]{2,1,0:T(8,128)(2,1)S(1)}, bf16[1,128,896]{2,1,0:T(8,128)(2,1)S(1)}, u32[]{:S(2)}, u32[]{:S(2)}) collective-permute-start(bf16[1,128,896]{2,1,0:T(8,128)(2,1)S(1)} %slice.83), channel_id=1, source_target_pairs={{0,9},{1,8},{2,11},{3,10},{4,13},{5,12},{6,15},{7,14},{8,17},{9,16... | collective-permute-start | bytes 688136 | tf_op jit(solution)/shard_map/ppermute | solution.py:467
  95.8 12.2 %collective-permute-start.20 = (bf16[1,128,896]{2,1,0:T(8,128)(2,1)S(1)}, bf16[1,128,896]{2,1,0:T(8,128)(2,1)S(1)}, u32[]{:S(2)}, u32[]{:S(2)}) collective-permute-start(bf16[1,128,896]{2,1,0:T(8,128)(2,1)S(1)} %slice.83), channel_id=1, source_target_pairs={{0,8},{1,9},{2,10},{3,11},{4,12},{5,13},{6,14},{7,15},{8,16},{9,17... | collective-permute-start | bytes 688136 | tf_op jit(solution)/shard_map/ppermute | solution.py:467
  108.0 2.2 %copy-start.3 = (bf16[512,4096]{1,0:T(8,128)(2,1)S(1)}, bf16[512,4096]{1,0:T(8,128)(2,1)}, u32[]{:S(2)}) copy-start(bf16[512,4096]{1,0:T(8,128)(2,1)} %refs_6_.3) | copy-start | bytes 12582916
  120.4 4.6 %collective-permute-start.22 = (bf16[4,512,512]{2,1,0:T(8,128)(2,1)S(1)}, bf16[4,512,512]{2,1,0:T(8,128)(2,1)S(1)}, u32[]{:S(2)}, u32[]{:S(2)}) collective-permute-start(bf16[4,512,512]{2,1,0:T(8,128)(2,1)S(1)} %get-tuple-element.20), channel_id=1, source_target_pairs={{0,1},{1,0},{2,3},{3,2},{4,5},{5,4},{6,7},{7,6},{8,9},{9,8},{10,11... | collective-permute-start | bytes 6291464 | tf_op jit(solution)/shard_map/ppermute | solution.py:60
  121.2 6.4 %collective-permute-start.26 = (bf16[8,128,896]{2,1,0:T(8,128)(2,1)S(1)}, bf16[8,128,896]{2,1,0:T(8,128)(2,1)S(1)}, u32[]{:S(2)}, u32[]{:S(2)}) collective-permute-start(bf16[8,128,896]{2,1,0:T(8,128)(2,1)S(1)} %encode.3.refs_9_.refs_1_), channel_id=1, source_target_pairs={{0,1},{1,0},{2,3},{3,2},{4,5},{5,4},{6,7},{7,6},{8,9},{9,8},{10,11... | collective-permute-start | bytes 5505032 | tf_op jit(solution)/shard_map/ppermute | solution.py:60
  125.0 2.6 %copy-start.4 = (bf16[512,4096]{1,0:T(8,128)(2,1)S(1)}, bf16[512,4096]{1,0:T(8,128)(2,1)}, u32[]{:S(2)}) copy-start(bf16[512,4096]{1,0:T(8,128)(2,1)} %refs_6_.3) | copy-start | bytes 12582916
  137.5 4.3 %collective-permute-start.27 = (bf16[4,512,512]{2,1,0:T(8,128)(2,1)S(1)}, bf16[4,512,512]{2,1,0:T(8,128)(2,1)S(1)}, u32[]{:S(2)}, u32[]{:S(2)}) collective-permute-start(bf16[4,512,512]{2,1,0:T(8,128)(2,1)S(1)} %get-tuple-element.22), channel_id=1, source_target_pairs={{0,1},{1,0},{2,3},{3,2},{4,5},{5,4},{6,7},{7,6},{8,9},{9,8},{10,11... | collective-permute-start | bytes 6291464 | tf_op jit(solution)/shard_map/ppermute | solution.py:60
  137.9 14.9 %collective-permute-start.25 = (bf16[512,512]{1,0:T(8,128)(2,1)S(1)}, bf16[512,512]{1,0:T(8,128)(2,1)S(1)}, u32[]{:S(2)}, u32[]{:S(2)}) collective-permute-start(bf16[512,512]{1,0:T(8,128)(2,1)S(1)} %get-tuple-element.28.refs_9_), channel_id=1, source_target_pairs={{0,4},{1,5},{2,6},{3,7},{4,0},{5,1},{6,2},{7,3},{8,12},{9,13},{10,... | collective-permute-start | bytes 1572872 | tf_op jit(solution)/shard_map/ppermute | solution.py:75
  139.0 25.9 %collective-permute-start.24 = (bf16[512,512]{1,0:T(8,128)(2,1)S(1)}, bf16[512,512]{1,0:T(8,128)(2,1)S(1)}, u32[]{:S(2)}, u32[]{:S(2)}) collective-permute-start(bf16[512,512]{1,0:T(8,128)(2,1)S(1)} %get-tuple-element.29.refs_8_), channel_id=1, source_target_pairs={{0,2},{1,3},{2,4},{3,5},{4,6},{5,7},{6,0},{7,1},{8,10},{9,11},{10,... | collective-permute-start | bytes 1572872 | tf_op jit(solution)/shard_map/ppermute | solution.py:75
  139.4 25.6 %collective-permute-start.23 = (bf16[512,512]{1,0:T(8,128)(2,1)S(1)}, bf16[512,512]{1,0:T(8,128)(2,1)S(1)}, u32[]{:S(2)}, u32[]{:S(2)}) collective-permute-start(bf16[512,512]{1,0:T(8,128)(2,1)S(1)} %get-tuple-element.30.refs_7_), channel_id=1, source_target_pairs={{0,6},{1,7},{2,0},{3,1},{4,2},{5,3},{6,4},{7,5},{8,14},{9,15},{10,... | collective-permute-start | bytes 1572872 | tf_op jit(solution)/shard_map/ppermute | solution.py:75
  142.2 31.8 %collective-permute-start.28 = (bf16[512,512]{1,0:T(8,128)(2,1)S(1)}, bf16[512,512]{1,0:T(8,128)(2,1)S(1)}, u32[]{:S(2)}, u32[]{:S(2)}) collective-permute-start(bf16[512,512]{1,0:T(8,128)(2,1)S(1)} %get-tuple-element.25), channel_id=1, source_target_pairs={{0,6},{1,7},{2,0},{3,1},{4,2},{5,3},{6,4},{7,5},{8,14},{9,15},{10,... | collective-permute-start | bytes 1572872 | tf_op jit(solution)/shard_map/ppermute | solution.py:75
  143.8 31.6 %collective-permute-start.30 = (bf16[512,512]{1,0:T(8,128)(2,1)S(1)}, bf16[512,512]{1,0:T(8,128)(2,1)S(1)}, u32[]{:S(2)}, u32[]{:S(2)}) collective-permute-start(bf16[512,512]{1,0:T(8,128)(2,1)S(1)} %get-tuple-element.26), channel_id=1, source_target_pairs={{0,4},{1,5},{2,6},{3,7},{4,0},{5,1},{6,2},{7,3},{8,12},{9,13},{10,... | collective-permute-start | bytes 1572872 | tf_op jit(solution)/shard_map/ppermute | solution.py:75
  152.9 34.1 %collective-permute-start.29 = (bf16[512,512]{1,0:T(8,128)(2,1)S(1)}, bf16[512,512]{1,0:T(8,128)(2,1)S(1)}, u32[]{:S(2)}, u32[]{:S(2)}) collective-permute-start(bf16[512,512]{1,0:T(8,128)(2,1)S(1)} %get-tuple-element.27), channel_id=1, source_target_pairs={{0,2},{1,3},{2,4},{3,5},{4,6},{5,7},{6,0},{7,1},{8,10},{9,11},{10,... | collective-permute-start | bytes 1572872 | tf_op jit(solution)/shard_map/ppermute | solution.py:75
  165.0 23.4 %copy-start.1 = (bf16[8,128,896]{2,1,0:T(8,128)(2,1)S(1)}, bf16[8,128,896]{2,1,0:T(8,128)(2,1)}, u32[]{:S(2)}) copy-start(bf16[8,128,896]{2,1,0:T(8,128)(2,1)} %param.13) | copy-start | bytes 5505028
Sparse Core Ops, SparseCore 0:
  11.1 60.9 all-gather.2

commit v6 on v5

--- a/solution.py
+++ b/solution.py
@@ -60,20 +60,36 @@
     return lax.ppermute(block, "store", [(i, i ^ 1) for i in range(count)])
 
 
-def core_sums(kept, given):
-    taken = swap_cores(given)
-    sums = [kept[j].astype(F32) + taken[j].astype(F32) for j in range(4)]
-    return sums[:1] + [block.astype(BF16) for block in sums[1:]]
-
-
-def sum_over_x(sums, chips):
-    total = sums[0]
+def add_kernel(kept_ref, taken_ref, *refs):
+    for j, out_ref in enumerate(refs[-4:]):
+        total = kept_ref[j].astype(F32) + taken_ref[j].astype(F32)
+        out_ref[...] = total.astype(out_ref.dtype)
+
+
+def core_sums(kept, taken, after):
+    vmem = pl.BlockSpec(memory_space=pltpu.VMEM)
+    shape = kept.shape[1:]
+    return pl.pallas_call(
+        add_kernel,
+        out_shape=[jax.ShapeDtypeStruct(shape, F32)] + [jax.ShapeDtypeStruct(shape, BF16)] * 3,
+        in_specs=[vmem] * 2 + [pl.BlockSpec(memory_space=pl.ANY)] * len(after),
+        out_specs=[vmem] * 4,
+        compiler_params=pltpu.CompilerParams(vmem_limit_bytes=8 << 20),
+        cost_estimate=pl.CostEstimate(flops=1 << 19, bytes_accessed=4 << 20, transcendentals=0),
+        name="core_sums",
+    )(kept, taken, *after)
+
+
+def send_over_x(sums, chips):
+    got = []
     for j in range(1, 4):
         route = [
-            (2 * x + core, 2 * ((x + REL[j]) % chips) + core) for x in range(chips) for core in range(2)
+            (2 * x + core, 2 * ((x + REL[j]) % chips) + core)
+            for x in range(chips)
+            for core in range(2)
         ]
-        total = total + lax.ppermute(sums[j], "store", route).astype(F32)
-    return total
+        got.append(lax.ppermute(sums[j], "store", route))
+    return got
 
 
 def once(shape):
@@ -341,39 +357,37 @@
         att[s * CH : (s + 1) * CH, p * 256 + HD : (p + 1) * 256] = got[CH:, HD:]
     done = att[...]
     chunk = q_ref.shape[1]
-    for out_ref, first in ((refs[-6], 0), (refs[-5], 4)):
-        for j in range(4):
+
+    @pl.loop(0, 4)
+    def _(j):
+        for out_ref, first in ((refs[-6], 0), (refs[-5], 4)):
             at = pl.multiple_of(block_ref[first + j] * chunk, chunk)
             out_ref[j] = dot(done, wo_ref[:, pl.ds(at, chunk)]).astype(BF16)
 
 
-def decode(first_span, own, other, queries, w_key, w_value, w_out, blocks, carried=(), after=()):
+def decode(step, own, other, queries, w_key, w_value, w_out, blocks, carried, after):
     width = queries.shape[1]
-    count = own.shape[0]
-    tokens = count * CH
     tile = SPANS_STEP * CH
-    first = first_span // SPANS_STEP
+    part = step % (own.shape[0] // SPANS_STEP)
     rows = SPANS_STEP * KNB * NLEN
-    block = pl.BlockSpec((SPANS_STEP, NLEN, E), lambda i, *_: (i, 0, 0))
-    out_shape = [jax.ShapeDtypeStruct((4, tokens, width), BF16)] * 2
-    out_specs = [pl.BlockSpec((4, tile, width), lambda i, *_: (0, i, 0))] * 2
+    block = pl.BlockSpec((SPANS_STEP, NLEN, E), lambda i, *_: (part, 0, 0))
     return pl.pallas_call(
         lambda *refs: decode_kernel(len(carried) > 0, *refs),
-        out_shape=out_shape,
+        out_shape=[jax.ShapeDtypeStruct((4, tile, width), BF16)] * 2,
         grid_spec=pltpu.PrefetchScalarGridSpec(
             num_scalar_prefetch=1,
-            grid=(count // SPANS_STEP,),
+            grid=(1,),
             in_specs=[
                 block,
                 block,
-                pl.BlockSpec((tile, width), lambda i, *_: (first + i, 0)),
+                pl.BlockSpec((tile, width), lambda i, *_: (step, 0)),
                 once((E, width)),
                 once((E, width)),
                 once((width, D)),
             ]
             + [once((1, NLEN, E))] * len(carried)
             + [pl.BlockSpec(memory_space=pl.ANY)] * len(after),
-            out_specs=out_specs,
+            out_specs=[once((4, tile, width))] * 2,
             scratch_shapes=[
                 pltpu.VMEM((rows, E), BF16),
                 pltpu.VMEM((tile, width), BF16),
@@ -385,9 +399,9 @@
             dimension_semantics=("arbitrary",), vmem_limit_bytes=VMEM_LIMIT
         ),
         cost_estimate=pl.CostEstimate(
-            flops=4 * count * KNB * NLEN * E * width + 2 * count * CH * width * D,
-            bytes_accessed=12 << 20,
-            transcendentals=count * CH * KNB * NLEN * (width // HD),
+            flops=4 * SPANS_STEP * KNB * NLEN * E * width + 2 * tile * width * D,
+            bytes_accessed=6 << 20,
+            transcendentals=tile * KNB * NLEN * (width // HD),
         ),
         name="decode",
     )(blocks, own, other, queries, w_key, w_value, w_out, *carried, *after)
@@ -477,25 +491,31 @@
     )
     high = encode(part, part, mine, pairs, enc_q, gathered, conds, enc_out, (low,))
     high_other = swap_cores(high)
-    low_terms = decode(
-        0,
-        low,
-        low_other,
-        queries,
-        w_key,
-        w_value,
-        w_out,
-        pairs,
-        carried=(carried, carried_other),
-        after=(high,),
-    )
-    low_sums = core_sums(*low_terms)
-    low_out = sum_over_x(low_sums, chips)
-    high_terms = decode(
-        part, high, high_other, queries, w_key, w_value, w_out, pairs, after=low_sums[1:]
-    )
-    high_out = sum_over_x(core_sums(*high_terms), chips)
-    return jnp.concatenate([low_out, high_out], axis=0).astype(BF16)
+    weights = (queries, w_key, w_value, w_out, pairs)
+    kept, given, taken, sums, got = ([None] * 4 for _ in range(5))
+    kept[0], given[0] = decode(0, low, low_other, *weights, (carried, carried_other), (high,))
+    taken[0] = swap_cores(given[0])
+    kept[1], given[1] = decode(1, low, low_other, *weights, (), (kept[0],))
+    taken[1] = swap_cores(given[1])
+    sums[0] = core_sums(kept[0], taken[0], (kept[1],))
+    got[0] = send_over_x(sums[0], chips)
+    kept[2], given[2] = decode(2, high, high_other, *weights, (), sums[0][1:])
+    taken[2] = swap_cores(given[2])
+    sums[1] = core_sums(kept[1], taken[1], (kept[2],))
+    got[1] = send_over_x(sums[1], chips)
+    kept[3], given[3] = decode(3, high, high_other, *weights, (), (*sums[1][1:], *got[0]))
+    taken[3] = swap_cores(given[3])
+    sums[2] = core_sums(kept[2], taken[2], (kept[3],))
+    got[2] = send_over_x(sums[2], chips)
+    sums[3] = core_sums(kept[3], taken[3], (*sums[2][1:], *got[1][:1]))
+    got[3] = send_over_x(sums[3], chips)
+    outs = []
+    for k in range(4):
+        total = sums[k][0]
+        for block in got[k]:
+            total = total + block.astype(F32)
+        outs.append(total.astype(BF16))
+    return jnp.concatenate(outs, axis=0)
 
 
 def solution(mesh):

time: 197 us -> 201 us (1.020)
  waiting for transfers between devices: 65.9 us -> 60 us
  Pallas kernels: 49 us -> 54.8 us
  starting transfers between devices: 45.9 us -> 51 us
    ppermute x6 -> x12, waiting for transfers between devices: 39.7 us -> 32.2 us  [send_over_x(): got.append(lax.ppermute(sums[j], 'store', route))]
    ppermute x2, waiting for transfers between devices: 1.32 us -> 8.55 us  [body(): lax.ppermute(low[:1], ('seq', 'store'), [(i * store_count + k, (i + 1) *...]
    ppermute x8 -> x10, waiting for transfers between devices: 8.21 us -> 2.58 us  [swap_cores(): return lax.ppermute(block, 'store', [(i, i ^ 1) for i in range(count)])]
    pallas_call x2 -> x4, Pallas kernels: 20 us -> 24.5 us  [decode(): pl.pallas_call(lambda *refs: decode_kernel(len(carried) > 0, *refs), out_...]
    ppermute x6 -> x12, starting transfers between devices: 8.58 us -> 11.4 us  [send_over_x(): got.append(lax.ppermute(sums[j], 'store', route))]
    ppermute x8 -> x10, starting transfers between devices: 10.5 us -> 12.8 us  [swap_cores(): return lax.ppermute(block, 'store', [(i, i ^ 1) for i in range(count)])]
  transfers between devices with their start and end apart: 32 -> 40, of which waited for: 16 -> 19; matrix products, arithmetic and copies ran while one was open for 7% -> 6% of each run, Pallas kernels for 11% -> 24%
where the time goes in v6:
time: 201 us; the launch traced here: 199 us
  waiting for transfers between devices  60 us (30%)
  Pallas kernels  54.8 us (27%)
  starting transfers between devices  51 us (25%)
  between operations  13.7 us (7%)
  matrix products  10.2 us (5%)
  local copies, waits for them, and re-layouts  6.18 us (3%)
  other arithmetic  3.06 us (2%)
    ppermute x12, waiting for transfers between devices, send_over_x(): got.append(lax.ppermute(sums[j], 'store', route))  32.2 us
    pallas_call x4, Pallas kernels, decode(): pl.pallas_call(lambda *refs: decode_kernel(len(carried) > 0, *refs), out_...  24.5 us
    ppermute x12, starting transfers between devices, around(): got.append(lax.ppermute(block, 'seq', route))  15.1 us
    pallas_call x2, Pallas kernels, encode(): pl.pallas_call(encode_kernel, out_shape=jax.ShapeDtypeStruct((count, NLEN...  14.8 us
    ppermute x10, starting transfers between devices, swap_cores(): return lax.ppermute(block, 'store', [(i, i ^ 1) for i in range(count)])  12.8 us
    all_gather x1, waiting for transfers between devices, body(): gathered = lax.all_gather(sources, 'store', axis=0, tiled=True)  12.4 us
    ppermute x12, starting transfers between devices, send_over_x(): got.append(lax.ppermute(sums[j], 'store', route))  11.4 us
    dot_general x1, matrix products, dot(): return jnp.dot(a, b, preferred_element_type=F32)  10.2 us
  transfers between devices with their start and end apart: 40, of which 19 were waited for; matrix products, arithmetic and copies ran while one was open for 6% of the time, Pallas kernels for 24%

profile of v6, /device:TPU:9, one launch (start us, length us, event | category | flops | bytes accessed | tf_op | source)
XLA Modules:
  0.0 199.0 jit_solution(14588524352524432174)
XLA Ops:
  9.3 1.6 gather_fusion.1
  11.9 2.1 %collective-permute-start.5 = (bf16[128,256]{1,0:T(8,128)(2,1)S(1)}, bf16[128,256]{1,0:T(8,128)(2,1)S(1)}, u32[]{:S(2)}, u32[]{:S(2)}) collective-permute-start(bf16[128,256]{1,0:T(8,128)(2,1)S(1)} %get-tuple-element.65.refs_4_), channel_id=1, source_target_pairs={{0,64},{8,72},{16,80},{24,88},{32,96},{40,104},{48,112},{56,120},{... | collective-permute-start | bytes 196616 | tf_op jit(solution)/shard_map/ppermute | solution.py:44
  14.0 1.1 collective-permute-start.4
  15.4 3.6 %collective-permute-start.2 = (bf16[128,256]{1,0:T(8,128)(2,1)S(1)}, bf16[128,256]{1,0:T(8,128)(2,1)S(1)}, u32[]{:S(2)}, u32[]{:S(2)}) collective-permute-start(bf16[128,256]{1,0:T(8,128)(2,1)S(1)} %get-tuple-element.66.refs_0_), channel_id=1, source_target_pairs={{0,16},{8,24},{16,0},{24,8},{32,48},{40,56},{48,32},{56,40},{64,80... | collective-permute-start | bytes 196616 | tf_op jit(solution)/shard_map/ppermute | solution.py:44
  19.5 1.0 collective-permute-start
  20.7 1.8 collective-permute-done.1.refs_2_
  22.4 1.4 collective-permute-done.refs_1_
  23.8 2.2 %collective-permute-start.8 = (bf16[4,128,256]{2,1,0:T(8,128)(2,1)S(1)}, bf16[4,128,256]{2,1,0:T(8,128)(2,1)S(1)}, u32[]{:S(2)}, u32[]{:S(2)}) collective-permute-start(bf16[4,128,256]{2,1,0:T(8,128)(2,1)S(1)} %get-tuple-element.34.refs_0_), channel_id=1, source_target_pairs={{0,64},{8,72},{16,80},{24,88},{32,96},{40,104},{48,112},{56,120},{... | collective-permute-start | bytes 786440 | tf_op jit(solution)/shard_map/ppermute | solution.py:44
  26.1 1.5 collective-permute-start.6
  27.5 1.2 collective-permute-start.11
  28.7 1.4 collective-permute-start.10
  31.2 10.2 %convolution_convert_fusion.refs_8_.refs_3_ = bf16[1024,512]{1,0:T(8,128)(2,1)} fusion(bf16[1024,4096]{1,0:T(8,128)(2,1)} %hidden_ref.1, bf16[4096,512]{1,0:T(8,128)(2,1)} %param.15), kind=kOutput, calls=%fused_computation.2 | convolution fusion | flops 4295491584 | bytes 13631488 | tf_op jit(solution)/shard_map/dot_general | solution.py:29
  41.5 6.3 %cond_rows.1 = bf16[1024,256]{1,0:T(8,128)(2,1)S(1)} custom-call(s32[8]{0:T(128)S(1)} %pad_add_fusion.1.src_ref, bf16[1024,4096]{1,0:T(8,128)(2,1)} %hidden_ref.1, bf16[4,128,256]{2,1,0:T(8,128)(2,1)S(1)} %get-tuple-element.34.refs_0_, bf16[4,128,256]{2,1,0:T(8,128)(2,1)S(1)} %collective-permute-done.6.refs_1_, ...), custom_call_target="tpu_custom_call" | custom-call | flops 2147483648 | bytes 12582912 | tf_op jit(solution)/shard_map/cond_rows/pallas_call | solution.py:122
  47.8 2.5 %collective-permute-start.14 = (bf16[16,64,256]{2,1,0:T(8,128)(2,1)S(1)}, bf16[16,64,256]{2,1,0:T(8,128)(2,1)S(1)}, u32[]{:S(2)}, u32[]{:S(2)}) collective-permute-start(bf16[16,64,256]{2,1,0:T(8,128)(2,1)S(1)} %bitcast.7), channel_id=1, source_target_pairs={{0,4},{1,5},{2,6},{3,7},{4,0},{5,1},{6,2},{7,3},{8,12},{9,13},{10,... | collective-permute-start | bytes 1572872 | tf_op jit(solution)/shard_map/ppermute | solution.py:54
  52.0 7.7 %collective-permute-start.15 = (bf16[16,64,256]{2,1,0:T(8,128)(2,1)S(1)}, bf16[16,64,256]{2,1,0:T(8,128)(2,1)S(1)}, u32[]{:S(2)}, u32[]{:S(2)}) collective-permute-start(bf16[16,64,256]{2,1,0:T(8,128)(2,1)S(1)} %bitcast.10), channel_id=1, source_target_pairs={{0,1},{1,0},{2,3},{3,2},{4,5},{5,4},{6,7},{7,6},{8,9},{9,8},{10,11... | collective-permute-start | bytes 1572872 | tf_op jit(solution)/shard_map/ppermute | solution.py:60
  59.7 12.4 %all-gather.3.cloned.1.call-done.refs_0_.refs_1_.refs_2_.refs_3_ = bf16[32,128,896]{2,1,0:T(8,128)(2,1)} async-done(((bf16[4,128,896]{2,1,0:T(8,128)(2,1)}), bf16[32,128,896]{2,1,0:T(8,128)(2,1)}) %all-gather.3.cloned.1.call-update) | async-done | bytes 7340048 | tf_op jit(solution)/shard_map/all_gather | solution.py:441
  72.1 8.1 %enc_queries.1.refs_3_.refs_12_ = bf16[16,128,896]{2,1,0:T(8,128)(2,1)S(1)} custom-call(s32[16]{0:T(128)S(1)} %select_reduce_fusion.1.pos_ref, bf16[32,128,896]{2,1,0:T(8,128)(2,1)} %all-gather.3.cloned.1.call-done.refs_0_.refs_1_.refs_2_.refs_3_, bf16[32,128,896]{2,1,0:T(8,128)(2,1)} %all-gather.3.cloned.1.call-done.refs_0_.refs_1_.refs_2_.refs_3_, ...), custom_call_target="tpu_custom_call" | custom-call | flops 3288334336 | bytes 10485760 | tf_op jit(solution)/shard_map/enc_queries/pallas_call | solution.py:203
  81.3 1.1 collective-permute-done.16.refs_9_
  83.8 7.3 %encode.2.refs_14_.refs_1_ = bf16[8,128,896]{2,1,0:T(8,128)(2,1)S(1)} custom-call(s32[16]{0:T(128)S(1)} %select_reduce_fusion.1.pos_ref, s32[8]{0:T(128)S(1)} %pad_add_fusion.pair_ref.refs_0_, bf16[32,128,896]{2,1,0:T(8,128)(2,1)} %all-gather.3.cloned.1.call-done.refs_0_.refs_1_.refs_2_.refs_3_, ...), custom_call_target="tpu_custom_call" | custom-call | flops 2466250752 | bytes 8388608 | tf_op jit(solution)/shard_map/encode/pallas_call | solution.py:277
  92.2 1.2 copy-done.7
  93.4 7.5 %encode.3.refs_9_.refs_1_ = bf16[8,128,896]{2,1,0:T(8,128)(2,1)S(1)} custom-call(s32[16]{0:T(128)S(1)} %select_reduce_fusion.1.pos_ref, s32[8]{0:T(128)S(1)} %pad_add_fusion.pair_ref.refs_0_, bf16[32,128,896]{2,1,0:T(8,128)(2,1)} %all-gather.3.cloned.1.call-done.refs_0_.refs_1_.refs_2_.refs_3_, ...), custom_call_target="tpu_custom_call" | custom-call | flops 2466250752 | bytes 8388608 | tf_op jit(solution)/shard_map/encode/pallas_call | solution.py:277
  101.2 4.1 %collective-permute-start.21 = (bf16[1,128,896]{2,1,0:T(8,128)(2,1)S(1)}, bf16[1,128,896]{2,1,0:T(8,128)(2,1)S(1)}, u32[]{:S(2)}, u32[]{:S(2)}) collective-permute-start(bf16[1,128,896]{2,1,0:T(8,128)(2,1)S(1)} %slice.19), channel_id=1, source_target_pairs={{0,9},{1,8},{2,11},{3,10},{4,13},{5,12},{6,15},{7,14},{8,17},{9,16... | collective-permute-start | bytes 688136 | tf_op jit(solution)/shard_map/ppermute | solution.py:481
  105.4 3.6 %collective-permute-start.20 = (bf16[1,128,896]{2,1,0:T(8,128)(2,1)S(1)}, bf16[1,128,896]{2,1,0:T(8,128)(2,1)S(1)}, u32[]{:S(2)}, u32[]{:S(2)}) collective-permute-start(bf16[1,128,896]{2,1,0:T(8,128)(2,1)S(1)} %slice.19), channel_id=1, source_target_pairs={{0,8},{1,9},{2,10},{3,11},{4,12},{5,13},{6,14},{7,15},{8,16},{9,17... | collective-permute-start | bytes 688136 | tf_op jit(solution)/shard_map/ppermute | solution.py:481
  109.0 4.1 %collective-permute-done.21.refs_8_ = bf16[1,128,896]{2,1,0:T(8,128)(2,1)S(1)} collective-permute-done((bf16[1,128,896]{2,1,0:T(8,128)(2,1)S(1)}, bf16[1,128,896]{2,1,0:T(8,128)(2,1)S(1)}, u32[]{:S(2)}, u32[]{:S(2)}) %collective-permute-start.21) | collective-permute-done | bytes 229408 | tf_op jit(solution)/shard_map/ppermute | solution.py:481
  113.1 4.5 %collective-permute-done.20.refs_7_ = bf16[1,128,896]{2,1,0:T(8,128)(2,1)S(1)} collective-permute-done((bf16[1,128,896]{2,1,0:T(8,128)(2,1)S(1)}, bf16[1,128,896]{2,1,0:T(8,128)(2,1)S(1)}, u32[]{:S(2)}, u32[]{:S(2)}) %collective-permute-start.20) | collective-permute-done | bytes 229408 | tf_op jit(solution)/shard_map/ppermute | solution.py:481
  117.6 6.1 %decode.4 = (bf16[4,256,512]{2,1,0:T(8,128)(2,1)S(1)}, bf16[4,256,512]{2,1,0:T(8,128)(2,1)S(1)}) custom-call(s32[8]{0:T(128)S(1)} %pad_add_fusion.pair_ref.refs_0_, bf16[8,128,896]{2,1,0:T(8,128)(2,1)S(1)} %encode.2.refs_14_.refs_1_, bf16[8,128,896]{2,1,0:T(8,128)(2,1)S(1)} %collective-permute-done.19.refs_2_, ...), custom_call_target="tpu_custom_call" | custom-call | flops 2952790016 | bytes 6291456 | tf_op jit(solution)/shard_map/decode/pallas_call | solution.py:374
  123.7 1.1 collective-permute-start.22
  124.8 6.1 %decode.5 = (bf16[4,256,512]{2,1,0:T(8,128)(2,1)S(1)}, bf16[4,256,512]{2,1,0:T(8,128)(2,1)S(1)}) custom-call(s32[8]{0:T(128)S(1)} %pad_add_fusion.pair_ref.refs_0_, bf16[8,128,896]{2,1,0:T(8,128)(2,1)S(1)} %encode.2.refs_14_.refs_1_, bf16[8,128,896]{2,1,0:T(8,128)(2,1)S(1)} %collective-permute-done.19.refs_2_, ...), custom_call_target="tpu_custom_call" | custom-call | flops 2952790016 | bytes 6291456 | tf_op jit(solution)/shard_map/decode/pallas_call | solution.py:374
  131.7 1.2 collective-permute-start.24
  132.9 1.7 collective-permute-start.25
  134.6 6.1 %decode.6 = (bf16[4,256,512]{2,1,0:T(8,128)(2,1)S(1)}, bf16[4,256,512]{2,1,0:T(8,128)(2,1)S(1)}) custom-call(s32[8]{0:T(128)S(1)} %pad_add_fusion.pair_ref.refs_0_, bf16[8,128,896]{2,1,0:T(8,128)(2,1)S(1)} %encode.3.refs_9_.refs_1_, bf16[8,128,896]{2,1,0:T(8,128)(2,1)S(1)} %collective-permute-done.27.refs_2_, ...), custom_call_target="tpu_custom_call" | custom-call | flops 2952790016 | bytes 6291456 | tf_op jit(solution)/shard_map/decode/pallas_call | solution.py:374
  140.8 1.1 collective-permute-start.31
  142.1 4.0 %collective-permute-done.25.refs_12_ = bf16[256,512]{1,0:T(8,128)(2,1)S(1)} collective-permute-done((bf16[256,512]{1,0:T(8,128)(2,1)S(1)}, bf16[256,512]{1,0:T(8,128)(2,1)S(1)}, u32[]{:S(2)}, u32[]{:S(2)}) %collective-permute-start.25) | collective-permute-done | bytes 262176 | tf_op jit(solution)/shard_map/ppermute | solution.py:91
  146.2 6.1 %decode.7 = (bf16[4,256,512]{2,1,0:T(8,128)(2,1)S(1)}, bf16[4,256,512]{2,1,0:T(8,128)(2,1)S(1)}) custom-call(s32[8]{0:T(128)S(1)} %pad_add_fusion.pair_ref.refs_0_, bf16[8,128,896]{2,1,0:T(8,128)(2,1)S(1)} %encode.3.refs_9_.refs_1_, bf16[8,128,896]{2,1,0:T(8,128)(2,1)S(1)} %collective-permute-done.27.refs_2_, ...), custom_call_target="tpu_custom_call" | custom-call | flops 2952790016 | bytes 6291456 | tf_op jit(solution)/shard_map/decode/pallas_call | solution.py:374
  152.3 1.4 collective-permute-start.35
  155.2 1.5 collective-permute-start.30
  158.1 3.5 %collective-permute-done.28.refs_3_ = bf16[256,512]{1,0:T(8,128)(2,1)S(1)} collective-permute-done((bf16[256,512]{1,0:T(8,128)(2,1)S(1)}, bf16[256,512]{1,0:T(8,128)(2,1)S(1)}, u32[]{:S(2)}, u32[]{:S(2)}) %collective-permute-start.28) | collective-permute-done | bytes 262176 | tf_op jit(solution)/shard_map/ppermute | solution.py:91
  161.6 1.8 collective-permute-done.29
  163.4 1.2 collective-permute-start.34
  164.6 3.8 %collective-permute-done.30 = bf16[256,512]{1,0:T(8,128)(2,1)S(1)} collective-permute-done((bf16[256,512]{1,0:T(8,128)(2,1)S(1)}, bf16[256,512]{1,0:T(8,128)(2,1)S(1)}, u32[]{:S(2)}, u32[]{:S(2)}) %collective-permute-start.30) | collective-permute-done | bytes 262176 | tf_op jit(solution)/shard_map/ppermute | solution.py:91
  168.8 1.3 collective-permute-start.36
  170.4 2.5 %collective-permute-done.32 = bf16[256,512]{1,0:T(8,128)(2,1)S(1)} collective-permute-done((bf16[256,512]{1,0:T(8,128)(2,1)S(1)}, bf16[256,512]{1,0:T(8,128)(2,1)S(1)}, u32[]{:S(2)}, u32[]{:S(2)}) %collective-permute-start.32) | collective-permute-done | bytes 262176 | tf_op jit(solution)/shard_map/ppermute | solution.py:91
  172.9 1.5 collective-permute-start.38
  174.3 5.5 %collective-permute-done.33 = bf16[256,512]{1,0:T(8,128)(2,1)S(1)} collective-permute-done((bf16[256,512]{1,0:T(8,128)(2,1)S(1)}, bf16[256,512]{1,0:T(8,128)(2,1)S(1)}, u32[]{:S(2)}, u32[]{:S(2)}) %collective-permute-start.33) | collective-permute-done | bytes 262176 | tf_op jit(solution)/shard_map/ppermute | solution.py:91
  180.0 4.2 %collective-permute-done.36 = bf16[256,512]{1,0:T(8,128)(2,1)S(1)} collective-permute-done((bf16[256,512]{1,0:T(8,128)(2,1)S(1)}, bf16[256,512]{1,0:T(8,128)(2,1)S(1)}, u32[]{:S(2)}, u32[]{:S(2)}) %collective-permute-start.36) | collective-permute-done | bytes 262176 | tf_op jit(solution)/shard_map/ppermute | solution.py:91
  184.2 2.8 %collective-permute-done.37 = bf16[256,512]{1,0:T(8,128)(2,1)S(1)} collective-permute-done((bf16[256,512]{1,0:T(8,128)(2,1)S(1)}, bf16[256,512]{1,0:T(8,128)(2,1)S(1)}, u32[]{:S(2)}, u32[]{:S(2)}) %collective-permute-start.37) | collective-permute-done | bytes 262176 | tf_op jit(solution)/shard_map/ppermute | solution.py:91
  186.9 4.0 %collective-permute-done.38 = bf16[256,512]{1,0:T(8,128)(2,1)S(1)} collective-permute-done((bf16[256,512]{1,0:T(8,128)(2,1)S(1)}, bf16[256,512]{1,0:T(8,128)(2,1)S(1)}, u32[]{:S(2)}, u32[]{:S(2)}) %collective-permute-start.38) | collective-permute-done | bytes 262176 | tf_op jit(solution)/shard_map/ppermute | solution.py:91
  191.1 1.0 pad_maximum_fusion
  (88 shorter events, 16.3 us)
Async XLA Ops:
  6.5 2.7 %copy-start = (bf16[8,128,896]{2,1,0:T(8,128)(2,1)S(1)}, bf16[8,128,896]{2,1,0:T(8,128)(2,1)}, u32[]{:S(2)}) copy-start(bf16[8,128,896]{2,1,0:T(8,128)(2,1)} %param.13) | copy-start | bytes 5505028
  6.5 65.5 %all-gather.3.cloned.1.call-start = ((), (), s32[]{:S(2)}) async-start(), calls=%async_computation | async-start | bytes 8257536 | tf_op jit(solution)/shard_map/all_gather | solution.py:441
  11.9 7.6 %collective-permute-start.5 = (bf16[128,256]{1,0:T(8,128)(2,1)S(1)}, bf16[128,256]{1,0:T(8,128)(2,1)S(1)}, u32[]{:S(2)}, u32[]{:S(2)}) collective-permute-start(bf16[128,256]{1,0:T(8,128)(2,1)S(1)} %get-tuple-element.65.refs_4_), channel_id=1, source_target_pairs={{0,64},{8,72},{16,80},{24,88},{32,96},{40,104},{48,112},{56,120},{... | collective-permute-start | bytes 196616 | tf_op jit(solution)/shard_map/ppermute | solution.py:44
  14.0 6.5 %collective-permute-start.4 = (bf16[128,256]{1,0:T(8,128)(2,1)S(1)}, bf16[128,256]{1,0:T(8,128)(2,1)S(1)}, u32[]{:S(2)}, u32[]{:S(2)}) collective-permute-start(bf16[128,256]{1,0:T(8,128)(2,1)S(1)} %get-tuple-element.65.refs_4_), channel_id=1, source_target_pairs={{0,96},{8,104},{16,112},{24,120},{32,0},{40,8},{48,16},{56,24},{64... | collective-permute-start | bytes 196616 | tf_op jit(solution)/shard_map/ppermute | solution.py:44
  15.0 5.5 %collective-permute-start.3 = (bf16[128,256]{1,0:T(8,128)(2,1)S(1)}, bf16[128,256]{1,0:T(8,128)(2,1)S(1)}, u32[]{:S(2)}, u32[]{:S(2)}) collective-permute-start(bf16[128,256]{1,0:T(8,128)(2,1)S(1)} %get-tuple-element.65.refs_4_), channel_id=1, source_target_pairs={{0,32},{8,40},{16,48},{24,56},{32,64},{40,72},{48,80},{56,88},{64,... | collective-permute-start | bytes 196616 | tf_op jit(solution)/shard_map/ppermute | solution.py:44
  15.4 5.2 %collective-permute-start.2 = (bf16[128,256]{1,0:T(8,128)(2,1)S(1)}, bf16[128,256]{1,0:T(8,128)(2,1)S(1)}, u32[]{:S(2)}, u32[]{:S(2)}) collective-permute-start(bf16[128,256]{1,0:T(8,128)(2,1)S(1)} %get-tuple-element.66.refs_0_), channel_id=1, source_target_pairs={{0,16},{8,24},{16,0},{24,8},{32,48},{40,56},{48,32},{56,40},{64,80... | collective-permute-start | bytes 196616 | tf_op jit(solution)/shard_map/ppermute | solution.py:44
  19.0 3.4 %collective-permute-start.1 = (bf16[128,256]{1,0:T(8,128)(2,1)S(1)}, bf16[128,256]{1,0:T(8,128)(2,1)S(1)}, u32[]{:S(2)}, u32[]{:S(2)}) collective-permute-start(bf16[128,256]{1,0:T(8,128)(2,1)S(1)} %get-tuple-element.66.refs_0_), channel_id=1, source_target_pairs={{0,24},{8,0},{16,8},{24,16},{32,56},{40,32},{48,40},{56,48},{64,88... | collective-permute-start | bytes 196616 | tf_op jit(solution)/shard_map/ppermute | solution.py:44
  19.5 4.3 %collective-permute-start = (bf16[128,256]{1,0:T(8,128)(2,1)S(1)}, bf16[128,256]{1,0:T(8,128)(2,1)S(1)}, u32[]{:S(2)}, u32[]{:S(2)}) collective-permute-start(bf16[128,256]{1,0:T(8,128)(2,1)S(1)} %get-tuple-element.66.refs_0_), channel_id=1, source_target_pairs={{0,8},{8,16},{16,24},{24,0},{32,40},{40,48},{48,56},{56,32},{64,72... | collective-permute-start | bytes 196616 | tf_op jit(solution)/shard_map/ppermute | solution.py:44
  23.8 7.2 %collective-permute-start.8 = (bf16[4,128,256]{2,1,0:T(8,128)(2,1)S(1)}, bf16[4,128,256]{2,1,0:T(8,128)(2,1)S(1)}, u32[]{:S(2)}, u32[]{:S(2)}) collective-permute-start(bf16[4,128,256]{2,1,0:T(8,128)(2,1)S(1)} %get-tuple-element.34.refs_0_), channel_id=1, source_target_pairs={{0,64},{8,72},{16,80},{24,88},{32,96},{40,104},{48,112},{56,120},{... | collective-permute-start | bytes 786440 | tf_op jit(solution)/shard_map/ppermute | solution.py:44
  26.1 15.4 %collective-permute-start.7 = (bf16[4,128,256]{2,1,0:T(8,128)(2,1)S(1)}, bf16[4,128,256]{2,1,0:T(8,128)(2,1)S(1)}, u32[]{:S(2)}, u32[]{:S(2)}) collective-permute-start(bf16[4,128,256]{2,1,0:T(8,128)(2,1)S(1)} %get-tuple-element.34.refs_0_), channel_id=1, source_target_pairs={{0,96},{8,104},{16,112},{24,120},{32,0},{40,8},{48,16},{56,24},{64... | collective-permute-start | bytes 786440 | tf_op jit(solution)/shard_map/ppermute | solution.py:44
  26.1 15.4 %collective-permute-start.6 = (bf16[4,128,256]{2,1,0:T(8,128)(2,1)S(1)}, bf16[4,128,256]{2,1,0:T(8,128)(2,1)S(1)}, u32[]{:S(2)}, u32[]{:S(2)}) collective-permute-start(bf16[4,128,256]{2,1,0:T(8,128)(2,1)S(1)} %get-tuple-element.34.refs_0_), channel_id=1, source_target_pairs={{0,32},{8,40},{16,48},{24,56},{32,64},{40,72},{48,80},{56,88},{64,... | collective-permute-start | bytes 786440 | tf_op jit(solution)/shard_map/ppermute | solution.py:44
  27.5 14.0 %collective-permute-start.11 = (bf16[4,128,256]{2,1,0:T(8,128)(2,1)S(1)}, bf16[4,128,256]{2,1,0:T(8,128)(2,1)S(1)}, u32[]{:S(2)}, u32[]{:S(2)}) collective-permute-start(bf16[4,128,256]{2,1,0:T(8,128)(2,1)S(1)} %get-tuple-element.35.refs_4_), channel_id=1, source_target_pairs={{0,16},{8,24},{16,0},{24,8},{32,48},{40,56},{48,32},{56,40},{64,80... | collective-permute-start | bytes 786440 | tf_op jit(solution)/shard_map/ppermute | solution.py:44
  28.7 12.8 %collective-permute-start.10 = (bf16[4,128,256]{2,1,0:T(8,128)(2,1)S(1)}, bf16[4,128,256]{2,1,0:T(8,128)(2,1)S(1)}, u32[]{:S(2)}, u32[]{:S(2)}) collective-permute-start(bf16[4,128,256]{2,1,0:T(8,128)(2,1)S(1)} %get-tuple-element.35.refs_4_), channel_id=1, source_target_pairs={{0,24},{8,0},{16,8},{24,16},{32,56},{40,32},{48,40},{56,48},{64,88... | collective-permute-start | bytes 786440 | tf_op jit(solution)/shard_map/ppermute | solution.py:44
  31.1 10.5 %collective-permute-start.9 = (bf16[4,128,256]{2,1,0:T(8,128)(2,1)S(1)}, bf16[4,128,256]{2,1,0:T(8,128)(2,1)S(1)}, u32[]{:S(2)}, u32[]{:S(2)}) collective-permute-start(bf16[4,128,256]{2,1,0:T(8,128)(2,1)S(1)} %get-tuple-element.35.refs_4_), channel_id=1, source_target_pairs={{0,8},{8,16},{16,24},{24,0},{32,40},{40,48},{48,56},{56,32},{64,72... | collective-permute-start | bytes 786440 | tf_op jit(solution)/shard_map/ppermute | solution.py:44
  47.8 32.4 %collective-permute-start.14 = (bf16[16,64,256]{2,1,0:T(8,128)(2,1)S(1)}, bf16[16,64,256]{2,1,0:T(8,128)(2,1)S(1)}, u32[]{:S(2)}, u32[]{:S(2)}) collective-permute-start(bf16[16,64,256]{2,1,0:T(8,128)(2,1)S(1)} %bitcast.7), channel_id=1, source_target_pairs={{0,4},{1,5},{2,6},{3,7},{4,0},{5,1},{6,2},{7,3},{8,12},{9,13},{10,... | collective-permute-start | bytes 1572872 | tf_op jit(solution)/shard_map/ppermute | solution.py:54
  50.3 29.9 %collective-permute-start.13 = (bf16[16,64,256]{2,1,0:T(8,128)(2,1)S(1)}, bf16[16,64,256]{2,1,0:T(8,128)(2,1)S(1)}, u32[]{:S(2)}, u32[]{:S(2)}) collective-permute-start(bf16[16,64,256]{2,1,0:T(8,128)(2,1)S(1)} %bitcast.8), channel_id=1, source_target_pairs={{0,6},{1,7},{2,0},{3,1},{4,2},{5,3},{6,4},{7,5},{8,14},{9,15},{10,... | collective-permute-start | bytes 1572872 | tf_op jit(solution)/shard_map/ppermute | solution.py:54
  51.2 29.0 %collective-permute-start.12 = (bf16[16,64,256]{2,1,0:T(8,128)(2,1)S(1)}, bf16[16,64,256]{2,1,0:T(8,128)(2,1)S(1)}, u32[]{:S(2)}, u32[]{:S(2)}) collective-permute-start(bf16[16,64,256]{2,1,0:T(8,128)(2,1)S(1)} %bitcast.9), channel_id=1, source_target_pairs={{0,2},{1,3},{2,4},{3,5},{4,6},{5,7},{6,0},{7,1},{8,10},{9,11},{10,... | collective-permute-start | bytes 1572872 | tf_op jit(solution)/shard_map/ppermute | solution.py:54
  52.0 29.3 %collective-permute-start.15 = (bf16[16,64,256]{2,1,0:T(8,128)(2,1)S(1)}, bf16[16,64,256]{2,1,0:T(8,128)(2,1)S(1)}, u32[]{:S(2)}, u32[]{:S(2)}) collective-permute-start(bf16[16,64,256]{2,1,0:T(8,128)(2,1)S(1)} %bitcast.10), channel_id=1, source_target_pairs={{0,1},{1,0},{2,3},{3,2},{4,5},{5,4},{6,7},{7,6},{8,9},{9,8},{10,11... | collective-permute-start | bytes 1572872 | tf_op jit(solution)/shard_map/ppermute | solution.py:60
  80.2 3.6 %copy-start.5 = (bf16[896,896]{1,0:T(8,128)(2,1)S(1)}, bf16[896,896]{1,0:T(8,128)(2,1)}, u32[]{:S(2)}) copy-start(bf16[896,896]{1,0:T(8,128)(2,1)} %refs_13_.3) | copy-start | bytes 4816900
  80.3 2.0 %collective-permute-start.16 = (bf16[16,64,256]{2,1,0:T(8,128)(2,1)S(1)}, bf16[16,64,256]{2,1,0:T(8,128)(2,1)S(1)}, u32[]{:S(2)}, u32[]{:S(2)}) collective-permute-start(bf16[16,64,256]{2,1,0:T(8,128)(2,1)S(1)} %get-tuple-element.36.refs_5_), channel_id=1, source_target_pairs={{0,1},{1,0},{2,3},{3,2},{4,5},{5,4},{6,7},{7,6},{8,9},{9,8},{10,11... | collective-permute-start | bytes 1572872 | tf_op jit(solution)/shard_map/ppermute | solution.py:60
  80.7 2.4 %collective-permute-start.17 = (bf16[16,64,256]{2,1,0:T(8,128)(2,1)S(1)}, bf16[16,64,256]{2,1,0:T(8,128)(2,1)S(1)}, u32[]{:S(2)}, u32[]{:S(2)}) collective-permute-start(bf16[16,64,256]{2,1,0:T(8,128)(2,1)S(1)} %get-tuple-element.37.refs_6_), channel_id=1, source_target_pairs={{0,1},{1,0},{2,3},{3,2},{4,5},{5,4},{6,7},{7,6},{8,9},{9,8},{10,11... | collective-permute-start | bytes 1572872 | tf_op jit(solution)/shard_map/ppermute | solution.py:60
  80.9 2.9 %collective-permute-start.18 = (bf16[16,64,256]{2,1,0:T(8,128)(2,1)S(1)}, bf16[16,64,256]{2,1,0:T(8,128)(2,1)S(1)}, u32[]{:S(2)}, u32[]{:S(2)}) collective-permute-start(bf16[16,64,256]{2,1,0:T(8,128)(2,1)S(1)} %get-tuple-element.38.refs_7_), channel_id=1, source_target_pairs={{0,1},{1,0},{2,3},{3,2},{4,5},{5,4},{6,7},{7,6},{8,9},{9,8},{10,11... | collective-permute-start | bytes 1572872 | tf_op jit(solution)/shard_map/ppermute | solution.py:60
  91.1 0.8 copy-start.6
  91.9 25.6 %copy-start.3 = (bf16[896,512]{1,0:T(8,128)(2,1)S(1)}, bf16[896,512]{1,0:T(8,128)(2,1)}, u32[]{:S(2)}) copy-start(bf16[896,512]{1,0:T(8,128)(2,1)} %refs_4_.9) | copy-start | bytes 2752516
  91.9 25.6 %copy-start.4 = (bf16[896,512]{1,0:T(8,128)(2,1)S(1)}, bf16[896,512]{1,0:T(8,128)(2,1)}, u32[]{:S(2)}) copy-start(bf16[896,512]{1,0:T(8,128)(2,1)} %refs_5_.7) | copy-start | bytes 2752516
  91.9 25.6 %collective-permute-start.19 = (bf16[8,128,896]{2,1,0:T(8,128)(2,1)S(1)}, bf16[8,128,896]{2,1,0:T(8,128)(2,1)S(1)}, u32[]{:S(2)}, u32[]{:S(2)}) collective-permute-start(bf16[8,128,896]{2,1,0:T(8,128)(2,1)S(1)} %encode.2.refs_14_.refs_1_), channel_id=1, source_target_pairs={{0,1},{1,0},{2,3},{3,2},{4,5},{5,4},{6,7},{7,6},{8,9},{9,8},{10,11... | collective-permute-start | bytes 5505032 | tf_op jit(solution)/shard_map/ppermute | solution.py:60
  92.2 1.2 copy-start.7
  93.4 24.2 %copy-start.2 = (bf16[512,4096]{1,0:T(8,128)(2,1)S(1)}, bf16[512,4096]{1,0:T(8,128)(2,1)}, u32[]{:S(2)}) copy-start(bf16[512,4096]{1,0:T(8,128)(2,1)} %refs_6_.7) | copy-start | bytes 12582916
  100.9 33.7 %collective-permute-start.27 = (bf16[8,128,896]{2,1,0:T(8,128)(2,1)S(1)}, bf16[8,128,896]{2,1,0:T(8,128)(2,1)S(1)}, u32[]{:S(2)}, u32[]{:S(2)}) collective-permute-start(bf16[8,128,896]{2,1,0:T(8,128)(2,1)S(1)} %encode.3.refs_9_.refs_1_), channel_id=1, source_target_pairs={{0,1},{1,0},{2,3},{3,2},{4,5},{5,4},{6,7},{7,6},{8,9},{9,8},{10,11... | collective-permute-start | bytes 5505032 | tf_op jit(solution)/shard_map/ppermute | solution.py:60
  101.2 11.8 %collective-permute-start.21 = (bf16[1,128,896]{2,1,0:T(8,128)(2,1)S(1)}, bf16[1,128,896]{2,1,0:T(8,128)(2,1)S(1)}, u32[]{:S(2)}, u32[]{:S(2)}) collective-permute-start(bf16[1,128,896]{2,1,0:T(8,128)(2,1)S(1)} %slice.19), channel_id=1, source_target_pairs={{0,9},{1,8},{2,11},{3,10},{4,13},{5,12},{6,15},{7,14},{8,17},{9,16... | collective-permute-start | bytes 688136 | tf_op jit(solution)/shard_map/ppermute | solution.py:481
  105.4 12.2 %collective-permute-start.20 = (bf16[1,128,896]{2,1,0:T(8,128)(2,1)S(1)}, bf16[1,128,896]{2,1,0:T(8,128)(2,1)S(1)}, u32[]{:S(2)}, u32[]{:S(2)}) collective-permute-start(bf16[1,128,896]{2,1,0:T(8,128)(2,1)S(1)} %slice.19), channel_id=1, source_target_pairs={{0,8},{1,9},{2,10},{3,11},{4,12},{5,13},{6,14},{7,15},{8,16},{9,17... | collective-permute-start | bytes 688136 | tf_op jit(solution)/shard_map/ppermute | solution.py:481
  123.7 7.3 %collective-permute-start.22 = (bf16[4,256,512]{2,1,0:T(8,128)(2,1)S(1)}, bf16[4,256,512]{2,1,0:T(8,128)(2,1)S(1)}, u32[]{:S(2)}, u32[]{:S(2)}) collective-permute-start(bf16[4,256,512]{2,1,0:T(8,128)(2,1)S(1)} %get-tuple-element.40), channel_id=1, source_target_pairs={{0,1},{1,0},{2,3},{3,2},{4,5},{5,4},{6,7},{7,6},{8,9},{9,8},{10,11... | collective-permute-start | bytes 3145736 | tf_op jit(solution)/shard_map/ppermute | solution.py:60
  130.9 10.9 %collective-permute-start.26 = (bf16[4,256,512]{2,1,0:T(8,128)(2,1)S(1)}, bf16[4,256,512]{2,1,0:T(8,128)(2,1)S(1)}, u32[]{:S(2)}, u32[]{:S(2)}) collective-permute-start(bf16[4,256,512]{2,1,0:T(8,128)(2,1)S(1)} %get-tuple-element.46), channel_id=1, source_target_pairs={{0,1},{1,0},{2,3},{3,2},{4,5},{5,4},{6,7},{7,6},{8,9},{9,8},{10,11... | collective-permute-start | bytes 3145736 | tf_op jit(solution)/shard_map/ppermute | solution.py:60
  131.3 10.8 %collective-permute-start.23 = (bf16[256,512]{1,0:T(8,128)(2,1)S(1)}, bf16[256,512]{1,0:T(8,128)(2,1)S(1)}, u32[]{:S(2)}, u32[]{:S(2)}) collective-permute-start(bf16[256,512]{1,0:T(8,128)(2,1)S(1)} %get-tuple-element.43.refs_7_), channel_id=1, source_target_pairs={{0,6},{1,7},{2,0},{3,1},{4,2},{5,3},{6,4},{7,5},{8,14},{9,15},{10,... | collective-permute-start | bytes 786440 | tf_op jit(solution)/shard_map/ppermute | solution.py:91
  131.7 10.4 %collective-permute-start.24 = (bf16[256,512]{1,0:T(8,128)(2,1)S(1)}, bf16[256,512]{1,0:T(8,128)(2,1)S(1)}, u32[]{:S(2)}, u32[]{:S(2)}) collective-permute-start(bf16[256,512]{1,0:T(8,128)(2,1)S(1)} %get-tuple-element.44.refs_8_), channel_id=1, source_target_pairs={{0,2},{1,3},{2,4},{3,5},{4,6},{5,7},{6,0},{7,1},{8,10},{9,11},{10,... | collective-permute-start | bytes 786440 | tf_op jit(solution)/shard_map/ppermute | solution.py:91
  132.9 13.3 %collective-permute-start.25 = (bf16[256,512]{1,0:T(8,128)(2,1)S(1)}, bf16[256,512]{1,0:T(8,128)(2,1)S(1)}, u32[]{:S(2)}, u32[]{:S(2)}) collective-permute-start(bf16[256,512]{1,0:T(8,128)(2,1)S(1)} %get-tuple-element.45.refs_9_), channel_id=1, source_target_pairs={{0,4},{1,5},{2,6},{3,7},{4,0},{5,1},{6,2},{7,3},{8,12},{9,13},{10,... | collective-permute-start | bytes 786440 | tf_op jit(solution)/shard_map/ppermute | solution.py:91
  140.8 16.0 %collective-permute-start.31 = (bf16[4,256,512]{2,1,0:T(8,128)(2,1)S(1)}, bf16[4,256,512]{2,1,0:T(8,128)(2,1)S(1)}, u32[]{:S(2)}, u32[]{:S(2)}) collective-permute-start(bf16[4,256,512]{2,1,0:T(8,128)(2,1)S(1)} %get-tuple-element.52), channel_id=1, source_target_pairs={{0,1},{1,0},{2,3},{3,2},{4,5},{5,4},{6,7},{7,6},{8,9},{9,8},{10,11... | collective-permute-start | bytes 3145736 | tf_op jit(solution)/shard_map/ppermute | solution.py:60
  152.3 16.3 %collective-permute-start.35 = (bf16[4,256,512]{2,1,0:T(8,128)(2,1)S(1)}, bf16[4,256,512]{2,1,0:T(8,128)(2,1)S(1)}, u32[]{:S(2)}, u32[]{:S(2)}) collective-permute-start(bf16[4,256,512]{2,1,0:T(8,128)(2,1)S(1)} %get-tuple-element.58), channel_id=1, source_target_pairs={{0,1},{1,0},{2,3},{3,2},{4,5},{5,4},{6,7},{7,6},{8,9},{9,8},{10,11... | collective-permute-start | bytes 3145736 | tf_op jit(solution)/shard_map/ppermute | solution.py:60
  153.7 7.9 %collective-permute-start.28 = (bf16[256,512]{1,0:T(8,128)(2,1)S(1)}, bf16[256,512]{1,0:T(8,128)(2,1)S(1)}, u32[]{:S(2)}, u32[]{:S(2)}) collective-permute-start(bf16[256,512]{1,0:T(8,128)(2,1)S(1)} %get-tuple-element.49.refs_7_), channel_id=1, source_target_pairs={{0,6},{1,7},{2,0},{3,1},{4,2},{5,3},{6,4},{7,5},{8,14},{9,15},{10,... | collective-permute-start | bytes 786440 | tf_op jit(solution)/shard_map/ppermute | solution.py:91
  154.3 9.1 %collective-permute-start.29 = (bf16[256,512]{1,0:T(8,128)(2,1)S(1)}, bf16[256,512]{1,0:T(8,128)(2,1)S(1)}, u32[]{:S(2)}, u32[]{:S(2)}) collective-permute-start(bf16[256,512]{1,0:T(8,128)(2,1)S(1)} %get-tuple-element.50.refs_8_), channel_id=1, source_target_pairs={{0,2},{1,3},{2,4},{3,5},{4,6},{5,7},{6,0},{7,1},{8,10},{9,11},{10,... | collective-permute-start | bytes 786440 | tf_op jit(solution)/shard_map/ppermute | solution.py:91
  155.2 13.2 %collective-permute-start.30 = (bf16[256,512]{1,0:T(8,128)(2,1)S(1)}, bf16[256,512]{1,0:T(8,128)(2,1)S(1)}, u32[]{:S(2)}, u32[]{:S(2)}) collective-permute-start(bf16[256,512]{1,0:T(8,128)(2,1)S(1)} %get-tuple-element.51.refs_9_), channel_id=1, source_target_pairs={{0,4},{1,5},{2,6},{3,7},{4,0},{5,1},{6,2},{7,3},{8,12},{9,13},{10,... | collective-permute-start | bytes 786440 | tf_op jit(solution)/shard_map/ppermute | solution.py:91
  157.1 15.8 %collective-permute-start.32 = (bf16[256,512]{1,0:T(8,128)(2,1)S(1)}, bf16[256,512]{1,0:T(8,128)(2,1)S(1)}, u32[]{:S(2)}, u32[]{:S(2)}) collective-permute-start(bf16[256,512]{1,0:T(8,128)(2,1)S(1)} %get-tuple-element.55.refs_0_), channel_id=1, source_target_pairs={{0,6},{1,7},{2,0},{3,1},{4,2},{5,3},{6,4},{7,5},{8,14},{9,15},{10,... | collective-permute-start | bytes 786440 | tf_op jit(solution)/shard_map/ppermute | solution.py:91
  161.6 18.2 %collective-permute-start.33 = (bf16[256,512]{1,0:T(8,128)(2,1)S(1)}, bf16[256,512]{1,0:T(8,128)(2,1)S(1)}, u32[]{:S(2)}, u32[]{:S(2)}) collective-permute-start(bf16[256,512]{1,0:T(8,128)(2,1)S(1)} %get-tuple-element.56.refs_1_), channel_id=1, source_target_pairs={{0,2},{1,3},{2,4},{3,5},{4,6},{5,7},{6,0},{7,1},{8,10},{9,11},{10,... | collective-permute-start | bytes 786440 | tf_op jit(solution)/shard_map/ppermute | solution.py:91
  163.4 16.4 %collective-permute-start.34 = (bf16[256,512]{1,0:T(8,128)(2,1)S(1)}, bf16[256,512]{1,0:T(8,128)(2,1)S(1)}, u32[]{:S(2)}, u32[]{:S(2)}) collective-permute-start(bf16[256,512]{1,0:T(8,128)(2,1)S(1)} %get-tuple-element.57.refs_2_), channel_id=1, source_target_pairs={{0,4},{1,5},{2,6},{3,7},{4,0},{5,1},{6,2},{7,3},{8,12},{9,13},{10,... | collective-permute-start | bytes 786440 | tf_op jit(solution)/shard_map/ppermute | solution.py:91
  168.8 15.3 %collective-permute-start.36 = (bf16[256,512]{1,0:T(8,128)(2,1)S(1)}, bf16[256,512]{1,0:T(8,128)(2,1)S(1)}, u32[]{:S(2)}, u32[]{:S(2)}) collective-permute-start(bf16[256,512]{1,0:T(8,128)(2,1)S(1)} %get-tuple-element.60), channel_id=1, source_target_pairs={{0,6},{1,7},{2,0},{3,1},{4,2},{5,3},{6,4},{7,5},{8,14},{9,15},{10,... | collective-permute-start | bytes 786440 | tf_op jit(solution)/shard_map/ppermute | solution.py:91
  170.1 16.8 %collective-permute-start.37 = (bf16[256,512]{1,0:T(8,128)(2,1)S(1)}, bf16[256,512]{1,0:T(8,128)(2,1)S(1)}, u32[]{:S(2)}, u32[]{:S(2)}) collective-permute-start(bf16[256,512]{1,0:T(8,128)(2,1)S(1)} %get-tuple-element.61), channel_id=1, source_target_pairs={{0,2},{1,3},{2,4},{3,5},{4,6},{5,7},{6,0},{7,1},{8,10},{9,11},{10,... | collective-permute-start | bytes 786440 | tf_op jit(solution)/shard_map/ppermute | solution.py:91
  172.9 18.1 %collective-permute-start.38 = (bf16[256,512]{1,0:T(8,128)(2,1)S(1)}, bf16[256,512]{1,0:T(8,128)(2,1)S(1)}, u32[]{:S(2)}, u32[]{:S(2)}) collective-permute-start(bf16[256,512]{1,0:T(8,128)(2,1)S(1)} %get-tuple-element.62), channel_id=1, source_target_pairs={{0,4},{1,5},{2,6},{3,7},{4,0},{5,1},{6,2},{7,3},{8,12},{9,13},{10,... | collective-permute-start | bytes 786440 | tf_op jit(solution)/shard_map/ppermute | solution.py:91
  179.8 12.3 %copy-start.1 = (bf16[8,128,896]{2,1,0:T(8,128)(2,1)S(1)}, bf16[8,128,896]{2,1,0:T(8,128)(2,1)}, u32[]{:S(2)}) copy-start(bf16[8,128,896]{2,1,0:T(8,128)(2,1)} %param.13) | copy-start | bytes 5505028
Sparse Core Ops, SparseCore 0:
  11.1 60.9 all-gather.2

commit v7 on v6

--- a/solution.py
+++ b/solution.py
@@ -22,7 +22,7 @@
 F32 = jnp.float32
 BF16 = jnp.bfloat16
 REL = (0, -1, 1, 2)
-FIRST = 15
+FIRST = 7
 
 
 def dot(a, b):
@@ -110,9 +110,9 @@
                 term = dot(hidden_ref[:, pl.ds(at, 256)], weight)
                 terms = term if terms is None else terms + term
             if i == 3:
-                last = terms.shape[0] - CH
-                out_ref[:CH, :] = terms[last:].astype(BF16)
-                out_ref[CH:, :] = terms[:last].astype(BF16)
+                first = FIRST * CH
+                out_ref[: terms.shape[0] - first, :] = terms[first:].astype(BF16)
+                out_ref[terms.shape[0] - first :, :] = terms[:first].astype(BF16)
             else:
                 total[...] = terms
 
@@ -303,7 +303,9 @@
 SPANS_STEP = 4
 
 
-def decode_kernel(carries, block_ref, *refs):
+def decode_kernel(carries, split, *refs):
+    if split:
+        block_ref, refs = refs[0], refs[1:]
     own_ref, other_ref, q_ref, wk_ref, wv_ref, wo_ref = refs[:6]
     rows, att, ks, vs = refs[-4:]
     for j in range(SPANS_STEP):
@@ -358,36 +360,52 @@
     done = att[...]
     chunk = q_ref.shape[1]
 
-    @pl.loop(0, 4)
-    def _(j):
-        for out_ref, first in ((refs[-6], 0), (refs[-5], 4)):
-            at = pl.multiple_of(block_ref[first + j] * chunk, chunk)
-            out_ref[j] = dot(done, wo_ref[:, pl.ds(at, chunk)]).astype(BF16)
-
-
-def decode(step, own, other, queries, w_key, w_value, w_out, blocks, carried, after):
+    if split:
+
+        @pl.loop(0, 4)
+        def _(j):
+            for out_ref, first in ((refs[-6], 0), (refs[-5], 4)):
+                at = pl.multiple_of(block_ref[first + j] * chunk, chunk)
+                out_ref[j] = dot(done, wo_ref[:, pl.ds(at, chunk)]).astype(BF16)
+
+    else:
+
+        @pl.loop(0, wo_ref.shape[1] // chunk)
+        def _(j):
+            at = pl.ds(pl.multiple_of(j * chunk, chunk), chunk)
+            refs[-5][:, at] = dot(done, wo_ref[:, at]).astype(BF16)
+
+
+def decode(first, steps, own, other, queries, w_key, w_value, w_out, blocks, carried, after):
+    split = blocks is not None
     width = queries.shape[1]
     tile = SPANS_STEP * CH
-    part = step % (own.shape[0] // SPANS_STEP)
+    part = first % (own.shape[0] // SPANS_STEP)
     rows = SPANS_STEP * KNB * NLEN
-    block = pl.BlockSpec((SPANS_STEP, NLEN, E), lambda i, *_: (part, 0, 0))
-    return pl.pallas_call(
-        lambda *refs: decode_kernel(len(carried) > 0, *refs),
-        out_shape=[jax.ShapeDtypeStruct((4, tile, width), BF16)] * 2,
+    block = pl.BlockSpec((SPANS_STEP, NLEN, E), lambda i, *_: (part + i, 0, 0))
+    if split:
+        out_shape = [jax.ShapeDtypeStruct((4, steps * tile, width), BF16)] * 2
+        out_specs = [pl.BlockSpec((4, tile, width), lambda i, *_: (0, i, 0))] * 2
+    else:
+        out_shape = pltpu.HBM((steps * tile, D), BF16)
+        out_specs = pl.BlockSpec((tile, D), lambda i, *_: (i, 0))
+    return pl.pallas_call(
+        lambda *refs: decode_kernel(len(carried) > 0, split, *refs),
+        out_shape=out_shape,
         grid_spec=pltpu.PrefetchScalarGridSpec(
-            num_scalar_prefetch=1,
-            grid=(1,),
+            num_scalar_prefetch=int(split),
+            grid=(steps,),
             in_specs=[
                 block,
                 block,
-                pl.BlockSpec((tile, width), lambda i, *_: (step, 0)),
+                pl.BlockSpec((tile, width), lambda i, *_: (first + i, 0)),
                 once((E, width)),
                 once((E, width)),
                 once((width, D)),
             ]
             + [once((1, NLEN, E))] * len(carried)
-            + [pl.BlockSpec(memory_space=pl.ANY)] * len(after),
-            out_specs=[once((4, tile, width))] * 2,
+            + [pl.BlockSpec(memory_space=pltpu.HBM if split else pl.ANY)],
+            out_specs=out_specs,
             scratch_shapes=[
                 pltpu.VMEM((rows, E), BF16),
                 pltpu.VMEM((tile, width), BF16),
@@ -396,15 +414,16 @@
             ],
         ),
         compiler_params=pltpu.CompilerParams(
-            dimension_semantics=("arbitrary",), vmem_limit_bytes=VMEM_LIMIT
+            dimension_semantics=("arbitrary",),
+            vmem_limit_bytes=(60 << 20) if split else VMEM_LIMIT,
         ),
         cost_estimate=pl.CostEstimate(
-            flops=4 * SPANS_STEP * KNB * NLEN * E * width + 2 * tile * width * D,
+            flops=steps * (4 * SPANS_STEP * KNB * NLEN * E * width + 2 * tile * width * D),
             bytes_accessed=6 << 20,
-            transcendentals=tile * KNB * NLEN * (width // HD),
+            transcendentals=steps * tile * KNB * NLEN * (width // HD),
         ),
         name="decode",
-    )(blocks, own, other, queries, w_key, w_value, w_out, *carried, *after)
+    )(*([blocks] if split else []), own, other, queries, w_key, w_value, w_out, *carried, after)
 
 
 def body(
@@ -475,9 +494,11 @@
     own_lane[1:] = hold(own_lane[1:], enc_q)
     conds = own_lane + [swap_cores(block) for block in own_lane]
     part = span_count // 2
-    low = encode(0, part, mine, pairs, enc_q, gathered, conds, enc_out, ())
+    high = encode(0, part, mine, pairs, enc_q, gathered, conds, enc_out, ())
+    high_other = swap_cores(high)
+    low = encode(part, part, mine, pairs, enc_q, gathered, conds, enc_out, (high,))
     low_other = swap_cores(low)
-    carried, carried_other = (
+    carried = tuple(
         lax.ppermute(
             low[:1],
             ("seq", "store"),
@@ -489,33 +510,24 @@
         )
         for flip in range(2)
     )
-    high = encode(part, part, mine, pairs, enc_q, gathered, conds, enc_out, (low,))
-    high_other = swap_cores(high)
-    weights = (queries, w_key, w_value, w_out, pairs)
-    kept, given, taken, sums, got = ([None] * 4 for _ in range(5))
-    kept[0], given[0] = decode(0, low, low_other, *weights, (carried, carried_other), (high,))
-    taken[0] = swap_cores(given[0])
-    kept[1], given[1] = decode(1, low, low_other, *weights, (), (kept[0],))
-    taken[1] = swap_cores(given[1])
-    sums[0] = core_sums(kept[0], taken[0], (kept[1],))
-    got[0] = send_over_x(sums[0], chips)
-    kept[2], given[2] = decode(2, high, high_other, *weights, (), sums[0][1:])
-    taken[2] = swap_cores(given[2])
-    sums[1] = core_sums(kept[1], taken[1], (kept[2],))
-    got[1] = send_over_x(sums[1], chips)
-    kept[3], given[3] = decode(3, high, high_other, *weights, (), (*sums[1][1:], *got[0]))
-    taken[3] = swap_cores(given[3])
-    sums[2] = core_sums(kept[2], taken[2], (kept[3],))
-    got[2] = send_over_x(sums[2], chips)
-    sums[3] = core_sums(kept[3], taken[3], (*sums[2][1:], *got[1][:1]))
-    got[3] = send_over_x(sums[3], chips)
+    weights = (queries, w_key, w_value, w_out)
+    terms = decode(2, 2, high, high_other, *weights, None, (), low)
+    high_out = lax.psum_scatter(terms, "store", scatter_dimension=1, tiled=True)
+    kept_1, given_1 = decode(1, 1, low, low_other, *weights, pairs, (), terms)
+    taken_1 = swap_cores(given_1)
+    kept_0, given_0 = decode(0, 1, low, low_other, *weights, pairs, carried, kept_1)
+    taken_0 = swap_cores(given_0)
+    sums_1 = core_sums(kept_1, taken_1, (kept_0,))
+    got_1 = send_over_x(sums_1, chips)
+    sums_0 = core_sums(kept_0, taken_0, sums_1[1:])
+    got_0 = send_over_x(sums_0, chips)
     outs = []
-    for k in range(4):
-        total = sums[k][0]
-        for block in got[k]:
+    for sums, got in ((sums_0, got_0), (sums_1, got_1)):
+        total = sums[0]
+        for block in got:
             total = total + block.astype(F32)
         outs.append(total.astype(BF16))
-    return jnp.concatenate(outs, axis=0)
+    return jnp.concatenate([*outs, high_out], axis=0)
 
 
 def solution(mesh):

time: 201 us -> 184 us (0.915)
  waiting for transfers between devices: 60 us -> 42.6 us
  starting transfers between devices: 51 us -> 42.1 us
  Pallas kernels: 54.8 us -> 63.2 us
    ppermute x12 -> x6, waiting for transfers between devices: 32.2 us -> 22 us  [send_over_x(): got.append(lax.ppermute(sums[j], 'store', route))]
    pallas_call x4 -> x3, Pallas kernels: 24.5 us -> 33.7 us  [decode(): pl.pallas_call(lambda *refs: decode_kernel(len(carried) > 0, split, *refs...]
    ppermute x2, waiting for transfers between devices: 8.55 us -> 0.01 us  [body(): lax.ppermute(low[:1], ('seq', 'store'), [(i * store_count + k, (i + 1) *...]
    ppermute x12 -> x6, starting transfers between devices: 11.4 us -> 5.45 us  [send_over_x(): got.append(lax.ppermute(sums[j], 'store', route))]
    ppermute x10 -> x8, starting transfers between devices: 12.8 us -> 9.79 us  [swap_cores(): return lax.ppermute(block, 'store', [(i, i ^ 1) for i in range(count)])]
    unnamed x17 -> x29, local copies, waits for them, and re-layouts: 2.91 us -> 4.15 us
  transfers between devices with their start and end apart: 40 -> 33, of which waited for: 19 -> 13; matrix products, arithmetic and copies ran while one was open for 6% -> 6% of each run, Pallas kernels for 24% -> 23%
where the time goes in v7:
time: 184 us; the launch traced here: 183 us
  Pallas kernels  63.2 us (34%)
  waiting for transfers between devices  42.6 us (23%)
  starting transfers between devices  42.1 us (23%)
  between operations  13.8 us (8%)
  matrix products  10.2 us (6%)
  local copies, waits for them, and re-layouts  7.44 us (4%)
  other arithmetic  3.79 us (2%)
    pallas_call x3, Pallas kernels, decode(): pl.pallas_call(lambda *refs: decode_kernel(len(carried) > 0, split, *refs...  33.7 us
    ppermute x6, waiting for transfers between devices, send_over_x(): got.append(lax.ppermute(sums[j], 'store', route))  22 us
    ppermute x12, starting transfers between devices, around(): got.append(lax.ppermute(block, 'seq', route))  15.1 us
    pallas_call x2, Pallas kernels, encode(): pl.pallas_call(encode_kernel, out_shape=jax.ShapeDtypeStruct((count, NLEN...  14.5 us
    all_gather x1, waiting for transfers between devices, body(): gathered = lax.all_gather(sources, 'store', axis=0, tiled=True)  12.3 us
    dot_general x1, matrix products, dot(): return jnp.dot(a, b, preferred_element_type=F32)  10.2 us
    ppermute x8, starting transfers between devices, swap_cores(): return lax.ppermute(block, 'store', [(i, i ^ 1) for i in range(count)])  9.79 us
    pallas_call x1, Pallas kernels, enc_queries(): pl.pallas_call(enc_query_kernel, out_shape=jax.ShapeDtypeStruct((count, N...  8.1 us
  transfers between devices with their start and end apart: 33, of which 13 were waited for; matrix products, arithmetic and copies ran while one was open for 6% of the time, Pallas kernels for 23%

profile of v7, /device:TPU:9, one launch (start us, length us, event | category | flops | bytes accessed | tf_op | source)
XLA Modules:
  0.0 183.1 jit_solution(13769705752467057935)
XLA Ops:
  6.5 0.9 copy.16
  7.9 0.7 broadcast_add_fusion
  8.6 0.6 gather_fusion
  9.3 1.7 gather_fusion.1
  11.0 0.9 constant_dynamic-slice_fusion
  11.9 2.1 %collective-permute-start.5 = (bf16[128,256]{1,0:T(8,128)(2,1)S(1)}, bf16[128,256]{1,0:T(8,128)(2,1)S(1)}, u32[]{:S(2)}, u32[]{:S(2)}) collective-permute-start(bf16[128,256]{1,0:T(8,128)(2,1)S(1)} %get-tuple-element.41.refs_4_), channel_id=1, source_target_pairs={{0,64},{8,72},{16,80},{24,88},{32,96},{40,104},{48,112},{56,120},{... | collective-permute-start | bytes 196616 | tf_op jit(solution)/shard_map/ppermute | solution.py:44
  14.0 1.1 collective-permute-start.4
  15.5 3.6 %collective-permute-start.2 = (bf16[128,256]{1,0:T(8,128)(2,1)S(1)}, bf16[128,256]{1,0:T(8,128)(2,1)S(1)}, u32[]{:S(2)}, u32[]{:S(2)}) collective-permute-start(bf16[128,256]{1,0:T(8,128)(2,1)S(1)} %get-tuple-element.42.refs_0_), channel_id=1, source_target_pairs={{0,16},{8,24},{16,0},{24,8},{32,48},{40,56},{48,32},{56,40},{64,80... | collective-permute-start | bytes 196616 | tf_op jit(solution)/shard_map/ppermute | solution.py:44
  19.1 0.4 collective-permute-start.1
  19.5 1.0 collective-permute-start
  20.7 1.8 collective-permute-done.1.refs_2_
  22.5 1.4 collective-permute-done.refs_1_
  23.9 2.2 %collective-permute-start.8 = (bf16[4,128,256]{2,1,0:T(8,128)(2,1)S(1)}, bf16[4,128,256]{2,1,0:T(8,128)(2,1)S(1)}, u32[]{:S(2)}, u32[]{:S(2)}) collective-permute-start(bf16[4,128,256]{2,1,0:T(8,128)(2,1)S(1)} %get-tuple-element.22.refs_0_), channel_id=1, source_target_pairs={{0,64},{8,72},{16,80},{24,88},{32,96},{40,104},{48,112},{56,120},{... | collective-permute-start | bytes 786440 | tf_op jit(solution)/shard_map/ppermute | solution.py:44
  26.1 1.5 collective-permute-start.6
  27.6 1.2 collective-permute-start.11
  28.8 1.4 collective-permute-start.10
  30.2 1.0 collective-permute-done.8.refs_3_
  31.3 10.2 %convolution_convert_fusion.refs_8_.refs_2_.refs_3_ = bf16[1024,512]{1,0:T(8,128)(2,1)} fusion(bf16[1024,4096]{1,0:T(8,128)(2,1)} %hidden_ref.1, bf16[4096,512]{1,0:T(8,128)(2,1)} %param.15), kind=kOutput, calls=%fused_computation.2 | convolution fusion | flops 4295491584 | bytes 13631488 | tf_op jit(solution)/shard_map/dot_general | solution.py:29
  41.6 6.3 %cond_rows.1 = bf16[1024,256]{1,0:T(8,128)(2,1)S(1)} custom-call(s32[8]{0:T(128)S(1)} %pad_add_fusion.1.src_ref, bf16[1024,4096]{1,0:T(8,128)(2,1)} %hidden_ref.1, bf16[4,128,256]{2,1,0:T(8,128)(2,1)S(1)} %get-tuple-element.22.refs_0_, bf16[4,128,256]{2,1,0:T(8,128)(2,1)S(1)} %collective-permute-done.6.refs_1_, ...), custom_call_target="tpu_custom_call" | custom-call | flops 2147483648 | bytes 12582912 | tf_op jit(solution)/shard_map/cond_rows/pallas_call | solution.py:122
  47.9 2.5 %collective-permute-start.14 = (bf16[16,64,256]{2,1,0:T(8,128)(2,1)S(1)}, bf16[16,64,256]{2,1,0:T(8,128)(2,1)S(1)}, u32[]{:S(2)}, u32[]{:S(2)}) collective-permute-start(bf16[16,64,256]{2,1,0:T(8,128)(2,1)S(1)} %bitcast.7), channel_id=1, source_target_pairs={{0,4},{1,5},{2,6},{3,7},{4,0},{5,1},{6,2},{7,3},{8,12},{9,13},{10,... | collective-permute-start | bytes 1572872 | tf_op jit(solution)/shard_map/ppermute | solution.py:54
  50.4 0.9 collective-permute-start.13
  51.3 0.6 collective-permute-start.12
  52.0 7.7 %collective-permute-start.15 = (bf16[16,64,256]{2,1,0:T(8,128)(2,1)S(1)}, bf16[16,64,256]{2,1,0:T(8,128)(2,1)S(1)}, u32[]{:S(2)}, u32[]{:S(2)}) collective-permute-start(bf16[16,64,256]{2,1,0:T(8,128)(2,1)S(1)} %bitcast.10), channel_id=1, source_target_pairs={{0,1},{1,0},{2,3},{3,2},{4,5},{5,4},{6,7},{7,6},{8,9},{9,8},{10,11... | collective-permute-start | bytes 1572872 | tf_op jit(solution)/shard_map/ppermute | solution.py:60
  59.7 12.3 %all-gather.3.cloned.1.call-done.refs_0_.refs_1_.refs_2_.refs_3_ = bf16[32,128,896]{2,1,0:T(8,128)(2,1)} async-done(((bf16[4,128,896]{2,1,0:T(8,128)(2,1)}), bf16[32,128,896]{2,1,0:T(8,128)(2,1)}) %all-gather.3.cloned.1.call-update) | async-done | bytes 7340048 | tf_op jit(solution)/shard_map/all_gather | solution.py:460
  72.0 8.1 %enc_queries.1.refs_3_.refs_12_ = bf16[16,128,896]{2,1,0:T(8,128)(2,1)S(1)} custom-call(s32[16]{0:T(128)S(1)} %select_reduce_fusion.1.pos_ref, bf16[32,128,896]{2,1,0:T(8,128)(2,1)} %all-gather.3.cloned.1.call-done.refs_0_.refs_1_.refs_2_.refs_3_, bf16[32,128,896]{2,1,0:T(8,128)(2,1)} %all-gather.3.cloned.1.call-done.refs_0_.refs_1_.refs_2_.refs_3_, ...), custom_call_target="tpu_custom_call" | custom-call | flops 3288334336 | bytes 10485760 | tf_op jit(solution)/shard_map/enc_queries/pallas_call | solution.py:203
  81.2 1.1 collective-permute-done.16.refs_9_
  82.3 0.7 collective-permute-done.17.refs_10_
  83.0 0.7 collective-permute-done.18.refs_11_
  83.8 7.3 %encode.2.refs_14_.refs_0_ = bf16[8,128,896]{2,1,0:T(8,128)(2,1)S(1)} custom-call(s32[16]{0:T(128)S(1)} %select_reduce_fusion.1.pos_ref, s32[8]{0:T(128)S(1)} %pad_add_fusion.pair_ref.refs_0_, bf16[32,128,896]{2,1,0:T(8,128)(2,1)} %all-gather.3.cloned.1.call-done.refs_0_.refs_1_.refs_2_.refs_3_, ...), custom_call_target="tpu_custom_call" | custom-call | flops 2466250752 | bytes 8388608 | tf_op jit(solution)/shard_map/encode/pallas_call | solution.py:277
  91.4 1.2 copy-done.10
  92.7 7.3 %encode.3.refs_6_.refs_1_ = bf16[8,128,896]{2,1,0:T(8,128)(2,1)S(1)} custom-call(s32[16]{0:T(128)S(1)} %select_reduce_fusion.1.pos_ref, s32[8]{0:T(128)S(1)} %pad_add_fusion.pair_ref.refs_0_, bf16[32,128,896]{2,1,0:T(8,128)(2,1)} %all-gather.3.cloned.1.call-done.refs_0_.refs_1_.refs_2_.refs_3_, ...), custom_call_target="tpu_custom_call" | custom-call | flops 2466250752 | bytes 8388608 | tf_op jit(solution)/shard_map/encode/pallas_call | solution.py:277
  100.0 13.2 %decode.3.refs_7_ = bf16[512,4096]{1,0:T(8,128)(2,1)} custom-call(bf16[8,128,896]{2,1,0:T(8,128)(2,1)S(1)} %encode.2.refs_14_.refs_0_, bf16[8,128,896]{2,1,0:T(8,128)(2,1)S(1)} %collective-permute-done.22.refs_1_, bf16[1024,512]{1,0:T(8,128)(2,1)} %convolution_convert_fusion.refs_8_.refs_2_.refs_3_, bf16[896,512]{1,0:T(8,128)(2,1)S(1)} %copy-done.7, ...), custom_call_target="tpu_custom_call" | custom-call | flops 5905580032 | bytes 6291456 | tf_op jit(solution)/shard_map/decode/pallas_call | solution.py:392
  113.6 4.1 %collective-permute-start.21 = (bf16[1,128,896]{2,1,0:T(8,128)(2,1)S(1)}, bf16[1,128,896]{2,1,0:T(8,128)(2,1)S(1)}, u32[]{:S(2)}, u32[]{:S(2)}) collective-permute-start(bf16[1,128,896]{2,1,0:T(8,128)(2,1)S(1)} %slice.19), channel_id=1, source_target_pairs={{0,9},{1,8},{2,11},{3,10},{4,13},{5,12},{6,15},{7,14},{8,17},{9,16... | collective-permute-start | bytes 688136 | tf_op jit(solution)/shard_map/ppermute | solution.py:502
  117.7 3.6 %collective-permute-start.20 = (bf16[1,128,896]{2,1,0:T(8,128)(2,1)S(1)}, bf16[1,128,896]{2,1,0:T(8,128)(2,1)S(1)}, u32[]{:S(2)}, u32[]{:S(2)}) collective-permute-start(bf16[1,128,896]{2,1,0:T(8,128)(2,1)S(1)} %slice.19), channel_id=1, source_target_pairs={{0,8},{1,9},{2,10},{3,11},{4,12},{5,13},{6,14},{7,15},{8,16},{9,17... | collective-permute-start | bytes 688136 | tf_op jit(solution)/shard_map/ppermute | solution.py:502
  121.3 10.3 %decode.4 = (bf16[4,256,512]{2,1,0:T(8,128)(2,1)}, bf16[4,256,512]{2,1,0:T(8,128)(2,1)}) custom-call(s32[8]{0:T(128)} %copy-done.11, bf16[8,128,896]{2,1,0:T(8,128)(2,1)} %copy-done.2, bf16[8,128,896]{2,1,0:T(8,128)(2,1)} %collective-permute-done.19.refs_2_, bf16[1024,512]{1,0:T(8,128)(2,1)} %convolution_convert_fusion.refs_8_.refs_2_.refs_3_, ...), custom_call_target="tpu_custom_call" | custom-call | flops 2952790016 | bytes 6291456 | tf_op jit(solution)/shard_map/decode/pallas_call | solution.py:392
  131.7 0.6 collective-permute-start.24
  132.3 0.7 copy-done.12
  133.0 10.2 %decode.5 = (bf16[4,256,512]{2,1,0:T(8,128)(2,1)}, bf16[4,256,512]{2,1,0:T(8,128)(2,1)}) custom-call(s32[8]{0:T(128)} %copy-done.11, bf16[8,128,896]{2,1,0:T(8,128)(2,1)} %copy-done.2, bf16[8,128,896]{2,1,0:T(8,128)(2,1)} %collective-permute-done.19.refs_2_, bf16[1024,512]{1,0:T(8,128)(2,1)} %convolution_convert_fusion.refs_8_.refs_2_.refs_3_, ...), custom_call_target="tpu_custom_call" | custom-call | flops 2952790016 | bytes 6291456 | tf_op jit(solution)/shard_map/decode/pallas_call | solution.py:392
  143.3 1.2 copy-done.6
  144.7 1.4 collective-permute-done.23.taken_ref
  146.4 1.6 collective-permute-start.26
  148.0 1.7 collective-permute-start.27
  149.7 2.1 %collective-permute-start.28 = (bf16[256,512]{1,0:T(8,128)(2,1)S(1)}, bf16[256,512]{1,0:T(8,128)(2,1)S(1)}, u32[]{:S(2)}, u32[]{:S(2)}) collective-permute-start(bf16[256,512]{1,0:T(8,128)(2,1)S(1)} %get-tuple-element.31.refs_0_), channel_id=1, source_target_pairs={{0,6},{1,7},{2,0},{3,1},{4,2},{5,3},{6,4},{7,5},{8,14},{9,15},{10,... | collective-permute-start | bytes 786440 | tf_op jit(solution)/shard_map/ppermute | solution.py:91
  151.8 8.4 %collective-permute-done.25 = bf16[256,512]{1,0:T(8,128)(2,1)S(1)} collective-permute-done((bf16[256,512]{1,0:T(8,128)(2,1)S(1)}, bf16[256,512]{1,0:T(8,128)(2,1)S(1)}, u32[]{:S(2)}, u32[]{:S(2)}) %collective-permute-start.25) | collective-permute-done | bytes 262176 | tf_op jit(solution)/shard_map/ppermute | solution.py:91
  160.2 2.5 %collective-permute-done.26 = bf16[256,512]{1,0:T(8,128)(2,1)S(1)} collective-permute-done((bf16[256,512]{1,0:T(8,128)(2,1)S(1)}, bf16[256,512]{1,0:T(8,128)(2,1)S(1)}, u32[]{:S(2)}, u32[]{:S(2)}) %collective-permute-start.26) | collective-permute-done | bytes 262176 | tf_op jit(solution)/shard_map/ppermute | solution.py:91
  162.8 8.6 %collective-permute-done.28 = bf16[256,512]{1,0:T(8,128)(2,1)S(1)} collective-permute-done((bf16[256,512]{1,0:T(8,128)(2,1)S(1)}, bf16[256,512]{1,0:T(8,128)(2,1)S(1)}, u32[]{:S(2)}, u32[]{:S(2)}) %collective-permute-start.28) | collective-permute-done | bytes 262176 | tf_op jit(solution)/shard_map/ppermute | solution.py:91
  171.4 2.6 %collective-permute-done.29 = bf16[256,512]{1,0:T(8,128)(2,1)S(1)} collective-permute-done((bf16[256,512]{1,0:T(8,128)(2,1)S(1)}, bf16[256,512]{1,0:T(8,128)(2,1)S(1)}, u32[]{:S(2)}, u32[]{:S(2)}) %collective-permute-start.29) | collective-permute-done | bytes 262176 | tf_op jit(solution)/shard_map/ppermute | solution.py:91
  174.2 2.1 %pad_maximum_fusion = bf16[1024,512]{1,0:T(8,128)(2,1)} fusion(bf16[512,512]{1,0:T(8,128)(2,1)} %reduce-scatter.2.cloned.1.call-done, bf16[256,512]{1,0:T(8,128)(2,1)S(1)} %add_convert_fusion, bf16[256,512]{1,0:T(8,128)(2,1)S(1)} %add_convert_fusion.1), kind=kLoop, calls=%fused_computation.3 | loop fusion | flops 3145728 | bytes 2097152 | tf_op jit(solution)/shard_map/concatenate | solution.py:530
  (82 shorter events, 4.3 us)
Async XLA Ops:
  6.5 2.7 %copy-start = (bf16[8,128,896]{2,1,0:T(8,128)(2,1)S(1)}, bf16[8,128,896]{2,1,0:T(8,128)(2,1)}, u32[]{:S(2)}) copy-start(bf16[8,128,896]{2,1,0:T(8,128)(2,1)} %param.13) | copy-start | bytes 5505028
  6.5 65.5 %all-gather.3.cloned.1.call-start = ((), (), s32[]{:S(2)}) async-start(), calls=%async_computation.2 | async-start | bytes 8257536 | tf_op jit(solution)/shard_map/all_gather | solution.py:460
  11.0 163.2 %reduce-scatter.2.cloned.1.call-start = ((), (), s32[]{:S(2)}) async-start(), calls=%async_computation.1 | async-start | bytes 4718592 | tf_op jit(solution)/shard_map/reduce_scatter | solution.py:515
  11.9 7.6 %collective-permute-start.5 = (bf16[128,256]{1,0:T(8,128)(2,1)S(1)}, bf16[128,256]{1,0:T(8,128)(2,1)S(1)}, u32[]{:S(2)}, u32[]{:S(2)}) collective-permute-start(bf16[128,256]{1,0:T(8,128)(2,1)S(1)} %get-tuple-element.41.refs_4_), channel_id=1, source_target_pairs={{0,64},{8,72},{16,80},{24,88},{32,96},{40,104},{48,112},{56,120},{... | collective-permute-start | bytes 196616 | tf_op jit(solution)/shard_map/ppermute | solution.py:44
  14.0 6.5 %collective-permute-start.4 = (bf16[128,256]{1,0:T(8,128)(2,1)S(1)}, bf16[128,256]{1,0:T(8,128)(2,1)S(1)}, u32[]{:S(2)}, u32[]{:S(2)}) collective-permute-start(bf16[128,256]{1,0:T(8,128)(2,1)S(1)} %get-tuple-element.41.refs_4_), channel_id=1, source_target_pairs={{0,96},{8,104},{16,112},{24,120},{32,0},{40,8},{48,16},{56,24},{64... | collective-permute-start | bytes 196616 | tf_op jit(solution)/shard_map/ppermute | solution.py:44
  15.1 5.5 %collective-permute-start.3 = (bf16[128,256]{1,0:T(8,128)(2,1)S(1)}, bf16[128,256]{1,0:T(8,128)(2,1)S(1)}, u32[]{:S(2)}, u32[]{:S(2)}) collective-permute-start(bf16[128,256]{1,0:T(8,128)(2,1)S(1)} %get-tuple-element.41.refs_4_), channel_id=1, source_target_pairs={{0,32},{8,40},{16,48},{24,56},{32,64},{40,72},{48,80},{56,88},{64,... | collective-permute-start | bytes 196616 | tf_op jit(solution)/shard_map/ppermute | solution.py:44
  15.5 5.2 %collective-permute-start.2 = (bf16[128,256]{1,0:T(8,128)(2,1)S(1)}, bf16[128,256]{1,0:T(8,128)(2,1)S(1)}, u32[]{:S(2)}, u32[]{:S(2)}) collective-permute-start(bf16[128,256]{1,0:T(8,128)(2,1)S(1)} %get-tuple-element.42.refs_0_), channel_id=1, source_target_pairs={{0,16},{8,24},{16,0},{24,8},{32,48},{40,56},{48,32},{56,40},{64,80... | collective-permute-start | bytes 196616 | tf_op jit(solution)/shard_map/ppermute | solution.py:44
  19.1 3.4 %collective-permute-start.1 = (bf16[128,256]{1,0:T(8,128)(2,1)S(1)}, bf16[128,256]{1,0:T(8,128)(2,1)S(1)}, u32[]{:S(2)}, u32[]{:S(2)}) collective-permute-start(bf16[128,256]{1,0:T(8,128)(2,1)S(1)} %get-tuple-element.42.refs_0_), channel_id=1, source_target_pairs={{0,24},{8,0},{16,8},{24,16},{32,56},{40,32},{48,40},{56,48},{64,88... | collective-permute-start | bytes 196616 | tf_op jit(solution)/shard_map/ppermute | solution.py:44
  19.5 4.3 %collective-permute-start = (bf16[128,256]{1,0:T(8,128)(2,1)S(1)}, bf16[128,256]{1,0:T(8,128)(2,1)S(1)}, u32[]{:S(2)}, u32[]{:S(2)}) collective-permute-start(bf16[128,256]{1,0:T(8,128)(2,1)S(1)} %get-tuple-element.42.refs_0_), channel_id=1, source_target_pairs={{0,8},{8,16},{16,24},{24,0},{32,40},{40,48},{48,56},{56,32},{64,72... | collective-permute-start | bytes 196616 | tf_op jit(solution)/shard_map/ppermute | solution.py:44
  23.9 7.2 %collective-permute-start.8 = (bf16[4,128,256]{2,1,0:T(8,128)(2,1)S(1)}, bf16[4,128,256]{2,1,0:T(8,128)(2,1)S(1)}, u32[]{:S(2)}, u32[]{:S(2)}) collective-permute-start(bf16[4,128,256]{2,1,0:T(8,128)(2,1)S(1)} %get-tuple-element.22.refs_0_), channel_id=1, source_target_pairs={{0,64},{8,72},{16,80},{24,88},{32,96},{40,104},{48,112},{56,120},{... | collective-permute-start | bytes 786440 | tf_op jit(solution)/shard_map/ppermute | solution.py:44
  26.1 15.4 %collective-permute-start.7 = (bf16[4,128,256]{2,1,0:T(8,128)(2,1)S(1)}, bf16[4,128,256]{2,1,0:T(8,128)(2,1)S(1)}, u32[]{:S(2)}, u32[]{:S(2)}) collective-permute-start(bf16[4,128,256]{2,1,0:T(8,128)(2,1)S(1)} %get-tuple-element.22.refs_0_), channel_id=1, source_target_pairs={{0,96},{8,104},{16,112},{24,120},{32,0},{40,8},{48,16},{56,24},{64... | collective-permute-start | bytes 786440 | tf_op jit(solution)/shard_map/ppermute | solution.py:44
  26.1 15.4 %collective-permute-start.6 = (bf16[4,128,256]{2,1,0:T(8,128)(2,1)S(1)}, bf16[4,128,256]{2,1,0:T(8,128)(2,1)S(1)}, u32[]{:S(2)}, u32[]{:S(2)}) collective-permute-start(bf16[4,128,256]{2,1,0:T(8,128)(2,1)S(1)} %get-tuple-element.22.refs_0_), channel_id=1, source_target_pairs={{0,32},{8,40},{16,48},{24,56},{32,64},{40,72},{48,80},{56,88},{64,... | collective-permute-start | bytes 786440 | tf_op jit(solution)/shard_map/ppermute | solution.py:44
  27.6 14.0 %collective-permute-start.11 = (bf16[4,128,256]{2,1,0:T(8,128)(2,1)S(1)}, bf16[4,128,256]{2,1,0:T(8,128)(2,1)S(1)}, u32[]{:S(2)}, u32[]{:S(2)}) collective-permute-start(bf16[4,128,256]{2,1,0:T(8,128)(2,1)S(1)} %get-tuple-element.23.refs_4_), channel_id=1, source_target_pairs={{0,16},{8,24},{16,0},{24,8},{32,48},{40,56},{48,32},{56,40},{64,80... | collective-permute-start | bytes 786440 | tf_op jit(solution)/shard_map/ppermute | solution.py:44
  28.8 12.8 %collective-permute-start.10 = (bf16[4,128,256]{2,1,0:T(8,128)(2,1)S(1)}, bf16[4,128,256]{2,1,0:T(8,128)(2,1)S(1)}, u32[]{:S(2)}, u32[]{:S(2)}) collective-permute-start(bf16[4,128,256]{2,1,0:T(8,128)(2,1)S(1)} %get-tuple-element.23.refs_4_), channel_id=1, source_target_pairs={{0,24},{8,0},{16,8},{24,16},{32,56},{40,32},{48,40},{56,48},{64,88... | collective-permute-start | bytes 786440 | tf_op jit(solution)/shard_map/ppermute | solution.py:44
  31.1 10.5 %collective-permute-start.9 = (bf16[4,128,256]{2,1,0:T(8,128)(2,1)S(1)}, bf16[4,128,256]{2,1,0:T(8,128)(2,1)S(1)}, u32[]{:S(2)}, u32[]{:S(2)}) collective-permute-start(bf16[4,128,256]{2,1,0:T(8,128)(2,1)S(1)} %get-tuple-element.23.refs_4_), channel_id=1, source_target_pairs={{0,8},{8,16},{16,24},{24,0},{32,40},{40,48},{48,56},{56,32},{64,72... | collective-permute-start | bytes 786440 | tf_op jit(solution)/shard_map/ppermute | solution.py:44
  47.9 32.3 %collective-permute-start.14 = (bf16[16,64,256]{2,1,0:T(8,128)(2,1)S(1)}, bf16[16,64,256]{2,1,0:T(8,128)(2,1)S(1)}, u32[]{:S(2)}, u32[]{:S(2)}) collective-permute-start(bf16[16,64,256]{2,1,0:T(8,128)(2,1)S(1)} %bitcast.7), channel_id=1, source_target_pairs={{0,4},{1,5},{2,6},{3,7},{4,0},{5,1},{6,2},{7,3},{8,12},{9,13},{10,... | collective-permute-start | bytes 1572872 | tf_op jit(solution)/shard_map/ppermute | solution.py:54
  50.4 29.8 %collective-permute-start.13 = (bf16[16,64,256]{2,1,0:T(8,128)(2,1)S(1)}, bf16[16,64,256]{2,1,0:T(8,128)(2,1)S(1)}, u32[]{:S(2)}, u32[]{:S(2)}) collective-permute-start(bf16[16,64,256]{2,1,0:T(8,128)(2,1)S(1)} %bitcast.8), channel_id=1, source_target_pairs={{0,6},{1,7},{2,0},{3,1},{4,2},{5,3},{6,4},{7,5},{8,14},{9,15},{10,... | collective-permute-start | bytes 1572872 | tf_op jit(solution)/shard_map/ppermute | solution.py:54
  51.3 28.9 %collective-permute-start.12 = (bf16[16,64,256]{2,1,0:T(8,128)(2,1)S(1)}, bf16[16,64,256]{2,1,0:T(8,128)(2,1)S(1)}, u32[]{:S(2)}, u32[]{:S(2)}) collective-permute-start(bf16[16,64,256]{2,1,0:T(8,128)(2,1)S(1)} %bitcast.9), channel_id=1, source_target_pairs={{0,2},{1,3},{2,4},{3,5},{4,6},{5,7},{6,0},{7,1},{8,10},{9,11},{10,... | collective-permute-start | bytes 1572872 | tf_op jit(solution)/shard_map/ppermute | solution.py:54
  52.0 29.2 %collective-permute-start.15 = (bf16[16,64,256]{2,1,0:T(8,128)(2,1)S(1)}, bf16[16,64,256]{2,1,0:T(8,128)(2,1)S(1)}, u32[]{:S(2)}, u32[]{:S(2)}) collective-permute-start(bf16[16,64,256]{2,1,0:T(8,128)(2,1)S(1)} %bitcast.10), channel_id=1, source_target_pairs={{0,1},{1,0},{2,3},{3,2},{4,5},{5,4},{6,7},{7,6},{8,9},{9,8},{10,11... | collective-permute-start | bytes 1572872 | tf_op jit(solution)/shard_map/ppermute | solution.py:60
  80.1 3.6 %copy-start.4 = (bf16[896,896]{1,0:T(8,128)(2,1)S(1)}, bf16[896,896]{1,0:T(8,128)(2,1)}, u32[]{:S(2)}) copy-start(bf16[896,896]{1,0:T(8,128)(2,1)} %refs_13_.3) | copy-start | bytes 4816900
  80.3 2.0 %collective-permute-start.16 = (bf16[16,64,256]{2,1,0:T(8,128)(2,1)S(1)}, bf16[16,64,256]{2,1,0:T(8,128)(2,1)S(1)}, u32[]{:S(2)}, u32[]{:S(2)}) collective-permute-start(bf16[16,64,256]{2,1,0:T(8,128)(2,1)S(1)} %get-tuple-element.24.refs_5_), channel_id=1, source_target_pairs={{0,1},{1,0},{2,3},{3,2},{4,5},{5,4},{6,7},{7,6},{8,9},{9,8},{10,11... | collective-permute-start | bytes 1572872 | tf_op jit(solution)/shard_map/ppermute | solution.py:60
  80.6 2.4 %collective-permute-start.17 = (bf16[16,64,256]{2,1,0:T(8,128)(2,1)S(1)}, bf16[16,64,256]{2,1,0:T(8,128)(2,1)S(1)}, u32[]{:S(2)}, u32[]{:S(2)}) collective-permute-start(bf16[16,64,256]{2,1,0:T(8,128)(2,1)S(1)} %get-tuple-element.25.refs_6_), channel_id=1, source_target_pairs={{0,1},{1,0},{2,3},{3,2},{4,5},{5,4},{6,7},{7,6},{8,9},{9,8},{10,11... | collective-permute-start | bytes 1572872 | tf_op jit(solution)/shard_map/ppermute | solution.py:60
  80.9 2.9 %collective-permute-start.18 = (bf16[16,64,256]{2,1,0:T(8,128)(2,1)S(1)}, bf16[16,64,256]{2,1,0:T(8,128)(2,1)S(1)}, u32[]{:S(2)}, u32[]{:S(2)}) collective-permute-start(bf16[16,64,256]{2,1,0:T(8,128)(2,1)S(1)} %get-tuple-element.26.refs_7_), channel_id=1, source_target_pairs={{0,1},{1,0},{2,3},{3,2},{4,5},{5,4},{6,7},{7,6},{8,9},{9,8},{10,11... | collective-permute-start | bytes 1572872 | tf_op jit(solution)/shard_map/ppermute | solution.py:60
  81.2 10.2 %copy-start.11 = (s32[8]{0:T(128)}, s32[8]{0:T(128)S(1)}, u32[]{:S(2)}) copy-start(s32[8]{0:T(128)S(1)} %pad_add_fusion.pair_ref.refs_0_) | copy-start | bytes 100
  81.2 9.8 %copy-start.9 = (bf16[16,64,256]{2,1,0:T(8,128)(2,1)}, bf16[16,64,256]{2,1,0:T(8,128)(2,1)S(1)}, u32[]{:S(2)}) copy-start(bf16[16,64,256]{2,1,0:T(8,128)(2,1)S(1)} %collective-permute-done.15.refs_8_) | copy-start | bytes 1572868
  91.1 8.9 %copy-start.3 = (bf16[512,4096]{1,0:T(8,128)(2,1)S(1)}, bf16[512,4096]{1,0:T(8,128)(2,1)}, u32[]{:S(2)}) copy-start(bf16[512,4096]{1,0:T(8,128)(2,1)} %refs_6_.3) | copy-start | bytes 12582916
  91.1 8.9 %copy-start.7 = (bf16[896,512]{1,0:T(8,128)(2,1)S(1)}, bf16[896,512]{1,0:T(8,128)(2,1)}, u32[]{:S(2)}) copy-start(bf16[896,512]{1,0:T(8,128)(2,1)} %refs_4_.7) | copy-start | bytes 2752516
  91.1 8.9 %copy-start.8 = (bf16[896,512]{1,0:T(8,128)(2,1)S(1)}, bf16[896,512]{1,0:T(8,128)(2,1)}, u32[]{:S(2)}) copy-start(bf16[896,512]{1,0:T(8,128)(2,1)} %refs_5_.5) | copy-start | bytes 2752516
  91.1 8.8 %collective-permute-start.22 = (bf16[8,128,896]{2,1,0:T(8,128)(2,1)S(1)}, bf16[8,128,896]{2,1,0:T(8,128)(2,1)S(1)}, u32[]{:S(2)}, u32[]{:S(2)}) collective-permute-start(bf16[8,128,896]{2,1,0:T(8,128)(2,1)S(1)} %encode.2.refs_14_.refs_0_), channel_id=1, source_target_pairs={{0,1},{1,0},{2,3},{3,2},{4,5},{5,4},{6,7},{7,6},{8,9},{9,8},{10,11... | collective-permute-start | bytes 5505032 | tf_op jit(solution)/shard_map/ppermute | solution.py:60
  91.4 1.2 copy-start.10
  99.9 13.6 %copy-start.2 = (bf16[8,128,896]{2,1,0:T(8,128)(2,1)}, bf16[8,128,896]{2,1,0:T(8,128)(2,1)S(1)}, u32[]{:S(2)}) copy-start(bf16[8,128,896]{2,1,0:T(8,128)(2,1)S(1)} %encode.3.refs_6_.refs_1_) | copy-start | bytes 5505028
  113.2 8.1 %collective-permute-start.19 = (bf16[8,128,896]{2,1,0:T(8,128)(2,1)S(1)}, bf16[8,128,896]{2,1,0:T(8,128)(2,1)}, u32[]{:S(2)}, u32[]{:S(2)}) collective-permute-start(bf16[8,128,896]{2,1,0:T(8,128)(2,1)S(1)} %encode.3.refs_6_.refs_1_), channel_id=1, source_target_pairs={{0,1},{1,0},{2,3},{3,2},{4,5},{5,4},{6,7},{7,6},{8,9},{9,8},{10,11... | collective-permute-start | bytes 5505032 | tf_op jit(solution)/shard_map/ppermute | solution.py:60
  113.6 18.7 %collective-permute-start.21 = (bf16[1,128,896]{2,1,0:T(8,128)(2,1)S(1)}, bf16[1,128,896]{2,1,0:T(8,128)(2,1)S(1)}, u32[]{:S(2)}, u32[]{:S(2)}) collective-permute-start(bf16[1,128,896]{2,1,0:T(8,128)(2,1)S(1)} %slice.19), channel_id=1, source_target_pairs={{0,9},{1,8},{2,11},{3,10},{4,13},{5,12},{6,15},{7,14},{8,17},{9,16... | collective-permute-start | bytes 688136 | tf_op jit(solution)/shard_map/ppermute | solution.py:502
  117.7 14.6 %collective-permute-start.20 = (bf16[1,128,896]{2,1,0:T(8,128)(2,1)S(1)}, bf16[1,128,896]{2,1,0:T(8,128)(2,1)S(1)}, u32[]{:S(2)}, u32[]{:S(2)}) collective-permute-start(bf16[1,128,896]{2,1,0:T(8,128)(2,1)S(1)} %slice.19), channel_id=1, source_target_pairs={{0,8},{1,9},{2,10},{3,11},{4,12},{5,13},{6,14},{7,15},{8,16},{9,17... | collective-permute-start | bytes 688136 | tf_op jit(solution)/shard_map/ppermute | solution.py:502
  131.7 11.5 %collective-permute-start.24 = (bf16[4,256,512]{2,1,0:T(8,128)(2,1)}, bf16[4,256,512]{2,1,0:T(8,128)(2,1)S(1)}, u32[]{:S(2)}, u32[]{:S(2)}) collective-permute-start(bf16[4,256,512]{2,1,0:T(8,128)(2,1)} %get-tuple-element.30), channel_id=1, source_target_pairs={{0,1},{1,0},{2,3},{3,2},{4,5},{5,4},{6,7},{7,6},{8,9},{9,8},{10,11... | collective-permute-start | bytes 3145736 | tf_op jit(solution)/shard_map/ppermute | solution.py:60
  132.3 0.7 copy-start.12
  132.3 0.8 copy-start.13
  133.0 10.2 %copy-start.5 = (bf16[4,256,512]{2,1,0:T(8,128)(2,1)S(1)}, bf16[4,256,512]{2,1,0:T(8,128)(2,1)}, u32[]{:S(2)}) copy-start(bf16[4,256,512]{2,1,0:T(8,128)(2,1)} %get-tuple-element.27.refs_9_.kept_ref) | copy-start | bytes 3145732
  143.2 2.9 %collective-permute-start.23 = (bf16[4,256,512]{2,1,0:T(8,128)(2,1)}, bf16[4,256,512]{2,1,0:T(8,128)(2,1)S(1)}, u32[]{:S(2)}, u32[]{:S(2)}) collective-permute-start(bf16[4,256,512]{2,1,0:T(8,128)(2,1)} %get-tuple-element.29), channel_id=1, source_target_pairs={{0,1},{1,0},{2,3},{3,2},{4,5},{5,4},{6,7},{7,6},{8,9},{9,8},{10,11... | collective-permute-start | bytes 3145736 | tf_op jit(solution)/shard_map/ppermute | solution.py:60
  143.2 1.2 copy-start.6
  146.4 13.8 %collective-permute-start.25 = (bf16[256,512]{1,0:T(8,128)(2,1)S(1)}, bf16[256,512]{1,0:T(8,128)(2,1)S(1)}, u32[]{:S(2)}, u32[]{:S(2)}) collective-permute-start(bf16[256,512]{1,0:T(8,128)(2,1)S(1)} %get-tuple-element.35), channel_id=1, source_target_pairs={{0,6},{1,7},{2,0},{3,1},{4,2},{5,3},{6,4},{7,5},{8,14},{9,15},{10,... | collective-permute-start | bytes 786440 | tf_op jit(solution)/shard_map/ppermute | solution.py:91
  146.4 16.2 %collective-permute-start.26 = (bf16[256,512]{1,0:T(8,128)(2,1)S(1)}, bf16[256,512]{1,0:T(8,128)(2,1)S(1)}, u32[]{:S(2)}, u32[]{:S(2)}) collective-permute-start(bf16[256,512]{1,0:T(8,128)(2,1)S(1)} %get-tuple-element.36), channel_id=1, source_target_pairs={{0,2},{1,3},{2,4},{3,5},{4,6},{5,7},{6,0},{7,1},{8,10},{9,11},{10,... | collective-permute-start | bytes 786440 | tf_op jit(solution)/shard_map/ppermute | solution.py:91
  148.0 14.7 %collective-permute-start.27 = (bf16[256,512]{1,0:T(8,128)(2,1)S(1)}, bf16[256,512]{1,0:T(8,128)(2,1)S(1)}, u32[]{:S(2)}, u32[]{:S(2)}) collective-permute-start(bf16[256,512]{1,0:T(8,128)(2,1)S(1)} %get-tuple-element.37), channel_id=1, source_target_pairs={{0,4},{1,5},{2,6},{3,7},{4,0},{5,1},{6,2},{7,3},{8,12},{9,13},{10,... | collective-permute-start | bytes 786440 | tf_op jit(solution)/shard_map/ppermute | solution.py:91
  149.7 21.7 %collective-permute-start.28 = (bf16[256,512]{1,0:T(8,128)(2,1)S(1)}, bf16[256,512]{1,0:T(8,128)(2,1)S(1)}, u32[]{:S(2)}, u32[]{:S(2)}) collective-permute-start(bf16[256,512]{1,0:T(8,128)(2,1)S(1)} %get-tuple-element.31.refs_0_), channel_id=1, source_target_pairs={{0,6},{1,7},{2,0},{3,1},{4,2},{5,3},{6,4},{7,5},{8,14},{9,15},{10,... | collective-permute-start | bytes 786440 | tf_op jit(solution)/shard_map/ppermute | solution.py:91
  151.8 22.2 %collective-permute-start.29 = (bf16[256,512]{1,0:T(8,128)(2,1)S(1)}, bf16[256,512]{1,0:T(8,128)(2,1)S(1)}, u32[]{:S(2)}, u32[]{:S(2)}) collective-permute-start(bf16[256,512]{1,0:T(8,128)(2,1)S(1)} %get-tuple-element.32.refs_1_), channel_id=1, source_target_pairs={{0,2},{1,3},{2,4},{3,5},{4,6},{5,7},{6,0},{7,1},{8,10},{9,11},{10,... | collective-permute-start | bytes 786440 | tf_op jit(solution)/shard_map/ppermute | solution.py:91
  160.2 13.8 %collective-permute-start.30 = (bf16[256,512]{1,0:T(8,128)(2,1)S(1)}, bf16[256,512]{1,0:T(8,128)(2,1)S(1)}, u32[]{:S(2)}, u32[]{:S(2)}) collective-permute-start(bf16[256,512]{1,0:T(8,128)(2,1)S(1)} %get-tuple-element.33.refs_2_), channel_id=1, source_target_pairs={{0,4},{1,5},{2,6},{3,7},{4,0},{5,1},{6,2},{7,3},{8,12},{9,13},{10,... | collective-permute-start | bytes 786440 | tf_op jit(solution)/shard_map/ppermute | solution.py:91
  162.7 13.6 %copy-start.1 = (bf16[8,128,896]{2,1,0:T(8,128)(2,1)S(1)}, bf16[8,128,896]{2,1,0:T(8,128)(2,1)}, u32[]{:S(2)}) copy-start(bf16[8,128,896]{2,1,0:T(8,128)(2,1)} %param.13) | copy-start | bytes 5505028
Sparse Core Ops, SparseCore 0:
  11.1 60.9 all-gather.2
  113.3 36.4 reduce-scatter.1

commit v8 on v7

--- a/solution.py
+++ b/solution.py
@@ -307,7 +307,15 @@
     if split:
         block_ref, refs = refs[0], refs[1:]
     own_ref, other_ref, q_ref, wk_ref, wv_ref, wo_ref = refs[:6]
-    rows, att, ks, vs = refs[-4:]
+    if split:
+        outs, (rows, att, ks, vs, wv_here, wo_here, sems) = refs[-9:-7], refs[-7:]
+        load_value = pltpu.make_async_copy(wv_ref, wv_here, sems.at[0])
+        load_out = pltpu.make_async_copy(wo_ref, wo_here, sems.at[1])
+        load_value.start()
+        load_out.start()
+        wv_ref, wo_ref = wv_here, wo_here
+    else:
+        outs, (rows, att, ks, vs) = refs[-5:-4], refs[-4:]
     for j in range(SPANS_STEP):
         for n, ref in enumerate((own_ref, other_ref)):
             at = slice((KNB * j + n) * NLEN, (KNB * j + n + 1) * NLEN)
@@ -347,6 +355,8 @@
     for score in scores:
         grown = jnp.exp(score - jnp.max(score, axis=0, keepdims=True))
         weights.append((grown * (1.0 / jnp.sum(grown, axis=0, keepdims=True))).astype(BF16))
+    if split:
+        load_value.wait()
     vs[...] = dot(block, wv_ref[...]).astype(BF16)
     for weight, (s, p) in zip(weights, units):
         got = lax.dot_general(
@@ -361,19 +371,15 @@
     chunk = q_ref.shape[1]
 
     if split:
-
-        @pl.loop(0, 4)
-        def _(j):
-            for out_ref, first in ((refs[-6], 0), (refs[-5], 4)):
+        load_out.wait()
+        for out_ref, first in ((outs[0], 0), (outs[1], 4)):
+            for j in range(4):
                 at = pl.multiple_of(block_ref[first + j] * chunk, chunk)
                 out_ref[j] = dot(done, wo_ref[:, pl.ds(at, chunk)]).astype(BF16)
-
     else:
-
-        @pl.loop(0, wo_ref.shape[1] // chunk)
-        def _(j):
-            at = pl.ds(pl.multiple_of(j * chunk, chunk), chunk)
-            refs[-5][:, at] = dot(done, wo_ref[:, at]).astype(BF16)
+        for j in range(wo_ref.shape[1] // chunk):
+            at = slice(j * chunk, (j + 1) * chunk)
+            outs[0][:, at] = dot(done, wo_ref[:, at]).astype(BF16)
 
 
 def decode(first, steps, own, other, queries, w_key, w_value, w_out, blocks, carried, after):
@@ -383,7 +389,15 @@
     part = first % (own.shape[0] // SPANS_STEP)
     rows = SPANS_STEP * KNB * NLEN
     block = pl.BlockSpec((SPANS_STEP, NLEN, E), lambda i, *_: (part + i, 0, 0))
+    far = pl.BlockSpec(memory_space=pltpu.HBM)
+    scratch = []
     if split:
+        assert steps == 1
+        scratch = [
+            pltpu.VMEM((E, width), BF16),
+            pltpu.VMEM((width, D), BF16),
+            pltpu.SemaphoreType.DMA((2,)),
+        ]
         out_shape = [jax.ShapeDtypeStruct((4, steps * tile, width), BF16)] * 2
         out_specs = [pl.BlockSpec((4, tile, width), lambda i, *_: (0, i, 0))] * 2
     else:
@@ -400,18 +414,19 @@
                 block,
                 pl.BlockSpec((tile, width), lambda i, *_: (first + i, 0)),
                 once((E, width)),
-                once((E, width)),
-                once((width, D)),
+                far if split else once((E, width)),
+                far if split else once((width, D)),
             ]
             + [once((1, NLEN, E))] * len(carried)
-            + [pl.BlockSpec(memory_space=pltpu.HBM if split else pl.ANY)],
+            + [far if split else pl.BlockSpec(memory_space=pl.ANY)],
             out_specs=out_specs,
             scratch_shapes=[
                 pltpu.VMEM((rows, E), BF16),
                 pltpu.VMEM((tile, width), BF16),
                 pltpu.VMEM((rows, width), BF16),
                 pltpu.VMEM((rows, width), BF16),
-            ],
+            ]
+            + scratch,
         ),
         compiler_params=pltpu.CompilerParams(
             dimension_semantics=("arbitrary",),

time: 184 us -> 180 us (0.978)
  Pallas kernels: 63.2 us -> 56.2 us
  starting transfers between devices: 42.1 us -> 44.2 us
    pallas_call x3, Pallas kernels: 33.7 us -> 26.7 us  [decode(): pl.pallas_call(lambda *refs: decode_kernel(len(carried) > 0, split, *refs...]
  transfers between devices with their start and end apart: 33 -> 33, of which waited for: 13 -> 13; matrix products, arithmetic and copies ran while one was open for 6% -> 7% of each run, Pallas kernels for 23% -> 21%
where the time goes in v8:
time: 180 us; the launch traced here: 178 us
  Pallas kernels  56.2 us (31%)
  starting transfers between devices  44.2 us (25%)
  waiting for transfers between devices  42.8 us (24%)
  between operations  13.7 us (8%)
  matrix products  10.2 us (6%)
  local copies, waits for them, and re-layouts  7.46 us (4%)
  other arithmetic  3.79 us (2%)
    pallas_call x3, Pallas kernels, decode(): pl.pallas_call(lambda *refs: decode_kernel(len(carried) > 0, split, *refs...  26.7 us
    ppermute x6, waiting for transfers between devices, send_over_x(): got.append(lax.ppermute(sums[j], 'store', route))  22.4 us
    ppermute x12, starting transfers between devices, around(): got.append(lax.ppermute(block, 'seq', route))  15.1 us
    pallas_call x2, Pallas kernels, encode(): pl.pallas_call(encode_kernel, out_shape=jax.ShapeDtypeStruct((count, NLEN...  14.5 us
    all_gather x1, waiting for transfers between devices, body(): gathered = lax.all_gather(sources, 'store', axis=0, tiled=True)  12.3 us
    ppermute x8, starting transfers between devices, swap_cores(): return lax.ppermute(block, 'store', [(i, i ^ 1) for i in range(count)])  10.4 us
    dot_general x1, matrix products, dot(): return jnp.dot(a, b, preferred_element_type=F32)  10.2 us
    pallas_call x1, Pallas kernels, enc_queries(): pl.pallas_call(enc_query_kernel, out_shape=jax.ShapeDtypeStruct((count, N...  8.1 us
  transfers between devices with their start and end apart: 33, of which 13 were waited for; matrix products, arithmetic and copies ran while one was open for 7% of the time, Pallas kernels for 21%

profile of v8, /device:TPU:9, one launch (start us, length us, event | category | flops | bytes accessed | tf_op | source)
XLA Modules:
  0.0 178.5 jit_solution(744749609882206092)
XLA Ops:
  6.5 0.9 copy.16
  7.9 0.7 broadcast_add_fusion
  8.6 0.6 gather_fusion
  9.3 1.7 gather_fusion.1
  11.0 0.9 constant_dynamic-slice_fusion
  11.9 2.1 %collective-permute-start.5 = (bf16[128,256]{1,0:T(8,128)(2,1)S(1)}, bf16[128,256]{1,0:T(8,128)(2,1)S(1)}, u32[]{:S(2)}, u32[]{:S(2)}) collective-permute-start(bf16[128,256]{1,0:T(8,128)(2,1)S(1)} %get-tuple-element.41.refs_4_), channel_id=1, source_target_pairs={{0,64},{8,72},{16,80},{24,88},{32,96},{40,104},{48,112},{56,120},{... | collective-permute-start | bytes 196616 | tf_op jit(solution)/shard_map/ppermute | solution.py:44
  14.0 1.1 collective-permute-start.4
  15.5 3.6 %collective-permute-start.2 = (bf16[128,256]{1,0:T(8,128)(2,1)S(1)}, bf16[128,256]{1,0:T(8,128)(2,1)S(1)}, u32[]{:S(2)}, u32[]{:S(2)}) collective-permute-start(bf16[128,256]{1,0:T(8,128)(2,1)S(1)} %get-tuple-element.42.refs_0_), channel_id=1, source_target_pairs={{0,16},{8,24},{16,0},{24,8},{32,48},{40,56},{48,32},{56,40},{64,80... | collective-permute-start | bytes 196616 | tf_op jit(solution)/shard_map/ppermute | solution.py:44
  19.5 1.0 collective-permute-start
  20.7 1.8 collective-permute-done.1.refs_2_
  22.5 1.4 collective-permute-done.refs_1_
  23.9 2.2 %collective-permute-start.8 = (bf16[4,128,256]{2,1,0:T(8,128)(2,1)S(1)}, bf16[4,128,256]{2,1,0:T(8,128)(2,1)S(1)}, u32[]{:S(2)}, u32[]{:S(2)}) collective-permute-start(bf16[4,128,256]{2,1,0:T(8,128)(2,1)S(1)} %get-tuple-element.22.refs_0_), channel_id=1, source_target_pairs={{0,64},{8,72},{16,80},{24,88},{32,96},{40,104},{48,112},{56,120},{... | collective-permute-start | bytes 786440 | tf_op jit(solution)/shard_map/ppermute | solution.py:44
  26.1 1.5 collective-permute-start.6
  27.6 1.2 collective-permute-start.11
  28.8 1.4 collective-permute-start.10
  30.2 1.0 collective-permute-done.8.refs_3_
  31.3 10.2 %convolution_convert_fusion.refs_8_.refs_2_.refs_3_ = bf16[1024,512]{1,0:T(8,128)(2,1)} fusion(bf16[1024,4096]{1,0:T(8,128)(2,1)} %hidden_ref.1, bf16[4096,512]{1,0:T(8,128)(2,1)} %param.15), kind=kOutput, calls=%fused_computation.2 | convolution fusion | flops 4295491584 | bytes 13631488 | tf_op jit(solution)/shard_map/dot_general | solution.py:29
  41.6 6.3 %cond_rows.1 = bf16[1024,256]{1,0:T(8,128)(2,1)S(1)} custom-call(s32[8]{0:T(128)S(1)} %pad_add_fusion.1.src_ref, bf16[1024,4096]{1,0:T(8,128)(2,1)} %hidden_ref.1, bf16[4,128,256]{2,1,0:T(8,128)(2,1)S(1)} %get-tuple-element.22.refs_0_, bf16[4,128,256]{2,1,0:T(8,128)(2,1)S(1)} %collective-permute-done.6.refs_1_, ...), custom_call_target="tpu_custom_call" | custom-call | flops 2147483648 | bytes 12582912 | tf_op jit(solution)/shard_map/cond_rows/pallas_call | solution.py:122
  47.9 2.5 %collective-permute-start.14 = (bf16[16,64,256]{2,1,0:T(8,128)(2,1)S(1)}, bf16[16,64,256]{2,1,0:T(8,128)(2,1)S(1)}, u32[]{:S(2)}, u32[]{:S(2)}) collective-permute-start(bf16[16,64,256]{2,1,0:T(8,128)(2,1)S(1)} %bitcast.7), channel_id=1, source_target_pairs={{0,4},{1,5},{2,6},{3,7},{4,0},{5,1},{6,2},{7,3},{8,12},{9,13},{10,... | collective-permute-start | bytes 1572872 | tf_op jit(solution)/shard_map/ppermute | solution.py:54
  50.4 0.9 collective-permute-start.13
  51.3 0.6 collective-permute-start.12
  52.0 7.7 %collective-permute-start.15 = (bf16[16,64,256]{2,1,0:T(8,128)(2,1)S(1)}, bf16[16,64,256]{2,1,0:T(8,128)(2,1)S(1)}, u32[]{:S(2)}, u32[]{:S(2)}) collective-permute-start(bf16[16,64,256]{2,1,0:T(8,128)(2,1)S(1)} %bitcast.10), channel_id=1, source_target_pairs={{0,1},{1,0},{2,3},{3,2},{4,5},{5,4},{6,7},{7,6},{8,9},{9,8},{10,11... | collective-permute-start | bytes 1572872 | tf_op jit(solution)/shard_map/ppermute | solution.py:60
  59.7 12.3 %all-gather.3.cloned.1.call-done.refs_0_.refs_1_.refs_2_.refs_3_ = bf16[32,128,896]{2,1,0:T(8,128)(2,1)} async-done(((bf16[4,128,896]{2,1,0:T(8,128)(2,1)}), bf16[32,128,896]{2,1,0:T(8,128)(2,1)}) %all-gather.3.cloned.1.call-update) | async-done | bytes 7340048 | tf_op jit(solution)/shard_map/all_gather | solution.py:475
  72.0 8.1 %enc_queries.1.refs_3_.refs_12_ = bf16[16,128,896]{2,1,0:T(8,128)(2,1)S(1)} custom-call(s32[16]{0:T(128)S(1)} %select_reduce_fusion.1.pos_ref, bf16[32,128,896]{2,1,0:T(8,128)(2,1)} %all-gather.3.cloned.1.call-done.refs_0_.refs_1_.refs_2_.refs_3_, bf16[32,128,896]{2,1,0:T(8,128)(2,1)} %all-gather.3.cloned.1.call-done.refs_0_.refs_1_.refs_2_.refs_3_, ...), custom_call_target="tpu_custom_call" | custom-call | flops 3288334336 | bytes 10485760 | tf_op jit(solution)/shard_map/enc_queries/pallas_call | solution.py:203
  81.2 1.1 collective-permute-done.16.refs_9_
  82.3 0.7 collective-permute-done.17.refs_10_
  83.0 0.7 collective-permute-done.18.refs_11_
  83.8 7.3 %encode.2.refs_14_.refs_0_ = bf16[8,128,896]{2,1,0:T(8,128)(2,1)S(1)} custom-call(s32[16]{0:T(128)S(1)} %select_reduce_fusion.1.pos_ref, s32[8]{0:T(128)S(1)} %pad_add_fusion.pair_ref.refs_0_, bf16[32,128,896]{2,1,0:T(8,128)(2,1)} %all-gather.3.cloned.1.call-done.refs_0_.refs_1_.refs_2_.refs_3_, ...), custom_call_target="tpu_custom_call" | custom-call | flops 2466250752 | bytes 8388608 | tf_op jit(solution)/shard_map/encode/pallas_call | solution.py:277
  91.4 1.2 copy-done.10
  92.7 7.3 %encode.3.refs_6_.refs_1_ = bf16[8,128,896]{2,1,0:T(8,128)(2,1)S(1)} custom-call(s32[16]{0:T(128)S(1)} %select_reduce_fusion.1.pos_ref, s32[8]{0:T(128)S(1)} %pad_add_fusion.pair_ref.refs_0_, bf16[32,128,896]{2,1,0:T(8,128)(2,1)} %all-gather.3.cloned.1.call-done.refs_0_.refs_1_.refs_2_.refs_3_, ...), custom_call_target="tpu_custom_call" | custom-call | flops 2466250752 | bytes 8388608 | tf_op jit(solution)/shard_map/encode/pallas_call | solution.py:277
  100.0 10.6 %decode.3.refs_7_ = bf16[512,4096]{1,0:T(8,128)(2,1)} custom-call(bf16[8,128,896]{2,1,0:T(8,128)(2,1)S(1)} %encode.2.refs_14_.refs_0_, bf16[8,128,896]{2,1,0:T(8,128)(2,1)S(1)} %collective-permute-done.22.refs_1_, bf16[1024,512]{1,0:T(8,128)(2,1)} %convolution_convert_fusion.refs_8_.refs_2_.refs_3_, bf16[896,512]{1,0:T(8,128)(2,1)S(1)} %copy-done.7, ...), custom_call_target="tpu_custom_call" | custom-call | flops 5905580032 | bytes 6291456 | tf_op jit(solution)/shard_map/decode/pallas_call | solution.py:406
  111.0 4.1 %collective-permute-start.21 = (bf16[1,128,896]{2,1,0:T(8,128)(2,1)S(1)}, bf16[1,128,896]{2,1,0:T(8,128)(2,1)S(1)}, u32[]{:S(2)}, u32[]{:S(2)}) collective-permute-start(bf16[1,128,896]{2,1,0:T(8,128)(2,1)S(1)} %slice.19), channel_id=1, source_target_pairs={{0,9},{1,8},{2,11},{3,10},{4,13},{5,12},{6,15},{7,14},{8,17},{9,16... | collective-permute-start | bytes 688136 | tf_op jit(solution)/shard_map/ppermute | solution.py:517
  115.1 3.9 %collective-permute-start.20 = (bf16[1,128,896]{2,1,0:T(8,128)(2,1)S(1)}, bf16[1,128,896]{2,1,0:T(8,128)(2,1)S(1)}, u32[]{:S(2)}, u32[]{:S(2)}) collective-permute-start(bf16[1,128,896]{2,1,0:T(8,128)(2,1)S(1)} %slice.19), channel_id=1, source_target_pairs={{0,8},{1,9},{2,10},{3,11},{4,12},{5,13},{6,14},{7,15},{8,16},{9,17... | collective-permute-start | bytes 688136 | tf_op jit(solution)/shard_map/ppermute | solution.py:517
  119.0 7.9 %decode.4 = (bf16[4,256,512]{2,1,0:T(8,128)(2,1)}, bf16[4,256,512]{2,1,0:T(8,128)(2,1)}) custom-call(s32[8]{0:T(128)} %copy-done.11, bf16[8,128,896]{2,1,0:T(8,128)(2,1)} %copy-done.2, bf16[8,128,896]{2,1,0:T(8,128)(2,1)} %collective-permute-done.19.refs_2_, bf16[1024,512]{1,0:T(8,128)(2,1)} %convolution_convert_fusion.refs_8_.refs_2_.refs_3_, ...), custom_call_target="tpu_custom_call" | custom-call | flops 2952790016 | bytes 6291456 | tf_op jit(solution)/shard_map/decode/pallas_call | solution.py:406
  126.9 0.8 collective-permute-start.24
  127.8 0.7 copy-done.12
  128.6 8.2 %decode.5 = (bf16[4,256,512]{2,1,0:T(8,128)(2,1)}, bf16[4,256,512]{2,1,0:T(8,128)(2,1)}) custom-call(s32[8]{0:T(128)} %copy-done.11, bf16[8,128,896]{2,1,0:T(8,128)(2,1)} %copy-done.2, bf16[8,128,896]{2,1,0:T(8,128)(2,1)} %collective-permute-done.19.refs_2_, bf16[1024,512]{1,0:T(8,128)(2,1)} %convolution_convert_fusion.refs_8_.refs_2_.refs_3_, ...), custom_call_target="tpu_custom_call" | custom-call | flops 2952790016 | bytes 6291456 | tf_op jit(solution)/shard_map/decode/pallas_call | solution.py:406
  137.1 1.2 copy-done.6
  138.6 1.2 collective-permute-done.23.taken_ref
  140.4 1.3 collective-permute-start.26
  141.7 1.7 collective-permute-start.27
  143.4 2.1 %collective-permute-start.28 = (bf16[256,512]{1,0:T(8,128)(2,1)S(1)}, bf16[256,512]{1,0:T(8,128)(2,1)S(1)}, u32[]{:S(2)}, u32[]{:S(2)}) collective-permute-start(bf16[256,512]{1,0:T(8,128)(2,1)S(1)} %get-tuple-element.31.refs_0_), channel_id=1, source_target_pairs={{0,6},{1,7},{2,0},{3,1},{4,2},{5,3},{6,4},{7,5},{8,14},{9,15},{10,... | collective-permute-start | bytes 786440 | tf_op jit(solution)/shard_map/ppermute | solution.py:91
  145.4 5.3 %collective-permute-done.25 = bf16[256,512]{1,0:T(8,128)(2,1)S(1)} collective-permute-done((bf16[256,512]{1,0:T(8,128)(2,1)S(1)}, bf16[256,512]{1,0:T(8,128)(2,1)S(1)}, u32[]{:S(2)}, u32[]{:S(2)}) %collective-permute-start.25) | collective-permute-done | bytes 262176 | tf_op jit(solution)/shard_map/ppermute | solution.py:91
  150.7 1.3 collective-permute-start.30
  152.1 6.0 %collective-permute-done.27 = bf16[256,512]{1,0:T(8,128)(2,1)S(1)} collective-permute-done((bf16[256,512]{1,0:T(8,128)(2,1)S(1)}, bf16[256,512]{1,0:T(8,128)(2,1)S(1)}, u32[]{:S(2)}, u32[]{:S(2)}) %collective-permute-start.27) | collective-permute-done | bytes 262176 | tf_op jit(solution)/shard_map/ppermute | solution.py:91
  158.2 9.9 %collective-permute-done.28 = bf16[256,512]{1,0:T(8,128)(2,1)S(1)} collective-permute-done((bf16[256,512]{1,0:T(8,128)(2,1)S(1)}, bf16[256,512]{1,0:T(8,128)(2,1)S(1)}, u32[]{:S(2)}, u32[]{:S(2)}) %collective-permute-start.28) | collective-permute-done | bytes 262176 | tf_op jit(solution)/shard_map/ppermute | solution.py:91
  168.1 1.2 collective-permute-done.30
  169.5 2.1 %pad_maximum_fusion = bf16[1024,512]{1,0:T(8,128)(2,1)} fusion(bf16[512,512]{1,0:T(8,128)(2,1)} %reduce-scatter.2.cloned.1.call-done, bf16[256,512]{1,0:T(8,128)(2,1)S(1)} %add_convert_fusion, bf16[256,512]{1,0:T(8,128)(2,1)S(1)} %add_convert_fusion.1), kind=kLoop, calls=%fused_computation.3 | loop fusion | flops 3145728 | bytes 2097152 | tf_op jit(solution)/shard_map/concatenate | solution.py:545
  (82 shorter events, 5.4 us)
Async XLA Ops:
  6.5 2.7 %copy-start = (bf16[8,128,896]{2,1,0:T(8,128)(2,1)S(1)}, bf16[8,128,896]{2,1,0:T(8,128)(2,1)}, u32[]{:S(2)}) copy-start(bf16[8,128,896]{2,1,0:T(8,128)(2,1)} %param.13) | copy-start | bytes 5505028
  6.5 65.5 %all-gather.3.cloned.1.call-start = ((), (), s32[]{:S(2)}) async-start(), calls=%async_computation.2 | async-start | bytes 8257536 | tf_op jit(solution)/shard_map/all_gather | solution.py:475
  11.0 158.6 %reduce-scatter.2.cloned.1.call-start = ((), (), s32[]{:S(2)}) async-start(), calls=%async_computation.1 | async-start | bytes 4718592 | tf_op jit(solution)/shard_map/reduce_scatter | solution.py:530
  11.9 7.6 %collective-permute-start.5 = (bf16[128,256]{1,0:T(8,128)(2,1)S(1)}, bf16[128,256]{1,0:T(8,128)(2,1)S(1)}, u32[]{:S(2)}, u32[]{:S(2)}) collective-permute-start(bf16[128,256]{1,0:T(8,128)(2,1)S(1)} %get-tuple-element.41.refs_4_), channel_id=1, source_target_pairs={{0,64},{8,72},{16,80},{24,88},{32,96},{40,104},{48,112},{56,120},{... | collective-permute-start | bytes 196616 | tf_op jit(solution)/shard_map/ppermute | solution.py:44
  14.0 6.5 %collective-permute-start.4 = (bf16[128,256]{1,0:T(8,128)(2,1)S(1)}, bf16[128,256]{1,0:T(8,128)(2,1)S(1)}, u32[]{:S(2)}, u32[]{:S(2)}) collective-permute-start(bf16[128,256]{1,0:T(8,128)(2,1)S(1)} %get-tuple-element.41.refs_4_), channel_id=1, source_target_pairs={{0,96},{8,104},{16,112},{24,120},{32,0},{40,8},{48,16},{56,24},{64... | collective-permute-start | bytes 196616 | tf_op jit(solution)/shard_map/ppermute | solution.py:44
  15.1 5.5 %collective-permute-start.3 = (bf16[128,256]{1,0:T(8,128)(2,1)S(1)}, bf16[128,256]{1,0:T(8,128)(2,1)S(1)}, u32[]{:S(2)}, u32[]{:S(2)}) collective-permute-start(bf16[128,256]{1,0:T(8,128)(2,1)S(1)} %get-tuple-element.41.refs_4_), channel_id=1, source_target_pairs={{0,32},{8,40},{16,48},{24,56},{32,64},{40,72},{48,80},{56,88},{64,... | collective-permute-start | bytes 196616 | tf_op jit(solution)/shard_map/ppermute | solution.py:44
  15.5 5.2 %collective-permute-start.2 = (bf16[128,256]{1,0:T(8,128)(2,1)S(1)}, bf16[128,256]{1,0:T(8,128)(2,1)S(1)}, u32[]{:S(2)}, u32[]{:S(2)}) collective-permute-start(bf16[128,256]{1,0:T(8,128)(2,1)S(1)} %get-tuple-element.42.refs_0_), channel_id=1, source_target_pairs={{0,16},{8,24},{16,0},{24,8},{32,48},{40,56},{48,32},{56,40},{64,80... | collective-permute-start | bytes 196616 | tf_op jit(solution)/shard_map/ppermute | solution.py:44
  19.1 3.4 %collective-permute-start.1 = (bf16[128,256]{1,0:T(8,128)(2,1)S(1)}, bf16[128,256]{1,0:T(8,128)(2,1)S(1)}, u32[]{:S(2)}, u32[]{:S(2)}) collective-permute-start(bf16[128,256]{1,0:T(8,128)(2,1)S(1)} %get-tuple-element.42.refs_0_), channel_id=1, source_target_pairs={{0,24},{8,0},{16,8},{24,16},{32,56},{40,32},{48,40},{56,48},{64,88... | collective-permute-start | bytes 196616 | tf_op jit(solution)/shard_map/ppermute | solution.py:44
  19.5 4.3 %collective-permute-start = (bf16[128,256]{1,0:T(8,128)(2,1)S(1)}, bf16[128,256]{1,0:T(8,128)(2,1)S(1)}, u32[]{:S(2)}, u32[]{:S(2)}) collective-permute-start(bf16[128,256]{1,0:T(8,128)(2,1)S(1)} %get-tuple-element.42.refs_0_), channel_id=1, source_target_pairs={{0,8},{8,16},{16,24},{24,0},{32,40},{40,48},{48,56},{56,32},{64,72... | collective-permute-start | bytes 196616 | tf_op jit(solution)/shard_map/ppermute | solution.py:44
  23.9 7.2 %collective-permute-start.8 = (bf16[4,128,256]{2,1,0:T(8,128)(2,1)S(1)}, bf16[4,128,256]{2,1,0:T(8,128)(2,1)S(1)}, u32[]{:S(2)}, u32[]{:S(2)}) collective-permute-start(bf16[4,128,256]{2,1,0:T(8,128)(2,1)S(1)} %get-tuple-element.22.refs_0_), channel_id=1, source_target_pairs={{0,64},{8,72},{16,80},{24,88},{32,96},{40,104},{48,112},{56,120},{... | collective-permute-start | bytes 786440 | tf_op jit(solution)/shard_map/ppermute | solution.py:44
  26.1 15.4 %collective-permute-start.7 = (bf16[4,128,256]{2,1,0:T(8,128)(2,1)S(1)}, bf16[4,128,256]{2,1,0:T(8,128)(2,1)S(1)}, u32[]{:S(2)}, u32[]{:S(2)}) collective-permute-start(bf16[4,128,256]{2,1,0:T(8,128)(2,1)S(1)} %get-tuple-element.22.refs_0_), channel_id=1, source_target_pairs={{0,96},{8,104},{16,112},{24,120},{32,0},{40,8},{48,16},{56,24},{64... | collective-permute-start | bytes 786440 | tf_op jit(solution)/shard_map/ppermute | solution.py:44
  26.1 15.4 %collective-permute-start.6 = (bf16[4,128,256]{2,1,0:T(8,128)(2,1)S(1)}, bf16[4,128,256]{2,1,0:T(8,128)(2,1)S(1)}, u32[]{:S(2)}, u32[]{:S(2)}) collective-permute-start(bf16[4,128,256]{2,1,0:T(8,128)(2,1)S(1)} %get-tuple-element.22.refs_0_), channel_id=1, source_target_pairs={{0,32},{8,40},{16,48},{24,56},{32,64},{40,72},{48,80},{56,88},{64,... | collective-permute-start | bytes 786440 | tf_op jit(solution)/shard_map/ppermute | solution.py:44
  27.6 14.0 %collective-permute-start.11 = (bf16[4,128,256]{2,1,0:T(8,128)(2,1)S(1)}, bf16[4,128,256]{2,1,0:T(8,128)(2,1)S(1)}, u32[]{:S(2)}, u32[]{:S(2)}) collective-permute-start(bf16[4,128,256]{2,1,0:T(8,128)(2,1)S(1)} %get-tuple-element.23.refs_4_), channel_id=1, source_target_pairs={{0,16},{8,24},{16,0},{24,8},{32,48},{40,56},{48,32},{56,40},{64,80... | collective-permute-start | bytes 786440 | tf_op jit(solution)/shard_map/ppermute | solution.py:44
  28.8 12.8 %collective-permute-start.10 = (bf16[4,128,256]{2,1,0:T(8,128)(2,1)S(1)}, bf16[4,128,256]{2,1,0:T(8,128)(2,1)S(1)}, u32[]{:S(2)}, u32[]{:S(2)}) collective-permute-start(bf16[4,128,256]{2,1,0:T(8,128)(2,1)S(1)} %get-tuple-element.23.refs_4_), channel_id=1, source_target_pairs={{0,24},{8,0},{16,8},{24,16},{32,56},{40,32},{48,40},{56,48},{64,88... | collective-permute-start | bytes 786440 | tf_op jit(solution)/shard_map/ppermute | solution.py:44
  31.1 10.5 %collective-permute-start.9 = (bf16[4,128,256]{2,1,0:T(8,128)(2,1)S(1)}, bf16[4,128,256]{2,1,0:T(8,128)(2,1)S(1)}, u32[]{:S(2)}, u32[]{:S(2)}) collective-permute-start(bf16[4,128,256]{2,1,0:T(8,128)(2,1)S(1)} %get-tuple-element.23.refs_4_), channel_id=1, source_target_pairs={{0,8},{8,16},{16,24},{24,0},{32,40},{40,48},{48,56},{56,32},{64,72... | collective-permute-start | bytes 786440 | tf_op jit(solution)/shard_map/ppermute | solution.py:44
  47.9 32.3 %collective-permute-start.14 = (bf16[16,64,256]{2,1,0:T(8,128)(2,1)S(1)}, bf16[16,64,256]{2,1,0:T(8,128)(2,1)S(1)}, u32[]{:S(2)}, u32[]{:S(2)}) collective-permute-start(bf16[16,64,256]{2,1,0:T(8,128)(2,1)S(1)} %bitcast.7), channel_id=1, source_target_pairs={{0,4},{1,5},{2,6},{3,7},{4,0},{5,1},{6,2},{7,3},{8,12},{9,13},{10,... | collective-permute-start | bytes 1572872 | tf_op jit(solution)/shard_map/ppermute | solution.py:54
  50.4 29.8 %collective-permute-start.13 = (bf16[16,64,256]{2,1,0:T(8,128)(2,1)S(1)}, bf16[16,64,256]{2,1,0:T(8,128)(2,1)S(1)}, u32[]{:S(2)}, u32[]{:S(2)}) collective-permute-start(bf16[16,64,256]{2,1,0:T(8,128)(2,1)S(1)} %bitcast.8), channel_id=1, source_target_pairs={{0,6},{1,7},{2,0},{3,1},{4,2},{5,3},{6,4},{7,5},{8,14},{9,15},{10,... | collective-permute-start | bytes 1572872 | tf_op jit(solution)/shard_map/ppermute | solution.py:54
  51.3 28.9 %collective-permute-start.12 = (bf16[16,64,256]{2,1,0:T(8,128)(2,1)S(1)}, bf16[16,64,256]{2,1,0:T(8,128)(2,1)S(1)}, u32[]{:S(2)}, u32[]{:S(2)}) collective-permute-start(bf16[16,64,256]{2,1,0:T(8,128)(2,1)S(1)} %bitcast.9), channel_id=1, source_target_pairs={{0,2},{1,3},{2,4},{3,5},{4,6},{5,7},{6,0},{7,1},{8,10},{9,11},{10,... | collective-permute-start | bytes 1572872 | tf_op jit(solution)/shard_map/ppermute | solution.py:54
  52.0 29.2 %collective-permute-start.15 = (bf16[16,64,256]{2,1,0:T(8,128)(2,1)S(1)}, bf16[16,64,256]{2,1,0:T(8,128)(2,1)S(1)}, u32[]{:S(2)}, u32[]{:S(2)}) collective-permute-start(bf16[16,64,256]{2,1,0:T(8,128)(2,1)S(1)} %bitcast.10), channel_id=1, source_target_pairs={{0,1},{1,0},{2,3},{3,2},{4,5},{5,4},{6,7},{7,6},{8,9},{9,8},{10,11... | collective-permute-start | bytes 1572872 | tf_op jit(solution)/shard_map/ppermute | solution.py:60
  80.1 3.6 %copy-start.4 = (bf16[896,896]{1,0:T(8,128)(2,1)S(1)}, bf16[896,896]{1,0:T(8,128)(2,1)}, u32[]{:S(2)}) copy-start(bf16[896,896]{1,0:T(8,128)(2,1)} %refs_13_.3) | copy-start | bytes 4816900
  80.3 2.0 %collective-permute-start.16 = (bf16[16,64,256]{2,1,0:T(8,128)(2,1)S(1)}, bf16[16,64,256]{2,1,0:T(8,128)(2,1)S(1)}, u32[]{:S(2)}, u32[]{:S(2)}) collective-permute-start(bf16[16,64,256]{2,1,0:T(8,128)(2,1)S(1)} %get-tuple-element.24.refs_5_), channel_id=1, source_target_pairs={{0,1},{1,0},{2,3},{3,2},{4,5},{5,4},{6,7},{7,6},{8,9},{9,8},{10,11... | collective-permute-start | bytes 1572872 | tf_op jit(solution)/shard_map/ppermute | solution.py:60
  80.6 2.4 %collective-permute-start.17 = (bf16[16,64,256]{2,1,0:T(8,128)(2,1)S(1)}, bf16[16,64,256]{2,1,0:T(8,128)(2,1)S(1)}, u32[]{:S(2)}, u32[]{:S(2)}) collective-permute-start(bf16[16,64,256]{2,1,0:T(8,128)(2,1)S(1)} %get-tuple-element.25.refs_6_), channel_id=1, source_target_pairs={{0,1},{1,0},{2,3},{3,2},{4,5},{5,4},{6,7},{7,6},{8,9},{9,8},{10,11... | collective-permute-start | bytes 1572872 | tf_op jit(solution)/shard_map/ppermute | solution.py:60
  80.9 2.9 %collective-permute-start.18 = (bf16[16,64,256]{2,1,0:T(8,128)(2,1)S(1)}, bf16[16,64,256]{2,1,0:T(8,128)(2,1)S(1)}, u32[]{:S(2)}, u32[]{:S(2)}) collective-permute-start(bf16[16,64,256]{2,1,0:T(8,128)(2,1)S(1)} %get-tuple-element.26.refs_7_), channel_id=1, source_target_pairs={{0,1},{1,0},{2,3},{3,2},{4,5},{5,4},{6,7},{7,6},{8,9},{9,8},{10,11... | collective-permute-start | bytes 1572872 | tf_op jit(solution)/shard_map/ppermute | solution.py:60
  81.2 10.2 %copy-start.11 = (s32[8]{0:T(128)}, s32[8]{0:T(128)S(1)}, u32[]{:S(2)}) copy-start(s32[8]{0:T(128)S(1)} %pad_add_fusion.pair_ref.refs_0_) | copy-start | bytes 100
  81.2 9.8 %copy-start.9 = (bf16[16,64,256]{2,1,0:T(8,128)(2,1)}, bf16[16,64,256]{2,1,0:T(8,128)(2,1)S(1)}, u32[]{:S(2)}) copy-start(bf16[16,64,256]{2,1,0:T(8,128)(2,1)S(1)} %collective-permute-done.15.refs_8_) | copy-start | bytes 1572868
  91.1 8.9 %copy-start.3 = (bf16[512,4096]{1,0:T(8,128)(2,1)S(1)}, bf16[512,4096]{1,0:T(8,128)(2,1)}, u32[]{:S(2)}) copy-start(bf16[512,4096]{1,0:T(8,128)(2,1)} %refs_6_.3) | copy-start | bytes 12582916
  91.1 8.9 %copy-start.7 = (bf16[896,512]{1,0:T(8,128)(2,1)S(1)}, bf16[896,512]{1,0:T(8,128)(2,1)}, u32[]{:S(2)}) copy-start(bf16[896,512]{1,0:T(8,128)(2,1)} %refs_4_.7) | copy-start | bytes 2752516
  91.1 8.9 %copy-start.8 = (bf16[896,512]{1,0:T(8,128)(2,1)S(1)}, bf16[896,512]{1,0:T(8,128)(2,1)}, u32[]{:S(2)}) copy-start(bf16[896,512]{1,0:T(8,128)(2,1)} %refs_5_.5) | copy-start | bytes 2752516
  91.1 8.8 %collective-permute-start.22 = (bf16[8,128,896]{2,1,0:T(8,128)(2,1)S(1)}, bf16[8,128,896]{2,1,0:T(8,128)(2,1)S(1)}, u32[]{:S(2)}, u32[]{:S(2)}) collective-permute-start(bf16[8,128,896]{2,1,0:T(8,128)(2,1)S(1)} %encode.2.refs_14_.refs_0_), channel_id=1, source_target_pairs={{0,1},{1,0},{2,3},{3,2},{4,5},{5,4},{6,7},{7,6},{8,9},{9,8},{10,11... | collective-permute-start | bytes 5505032 | tf_op jit(solution)/shard_map/ppermute | solution.py:60
  91.4 1.2 copy-start.10
  99.9 11.1 %copy-start.2 = (bf16[8,128,896]{2,1,0:T(8,128)(2,1)}, bf16[8,128,896]{2,1,0:T(8,128)(2,1)S(1)}, u32[]{:S(2)}) copy-start(bf16[8,128,896]{2,1,0:T(8,128)(2,1)S(1)} %encode.3.refs_6_.refs_1_) | copy-start | bytes 5505028
  110.6 8.4 %collective-permute-start.19 = (bf16[8,128,896]{2,1,0:T(8,128)(2,1)S(1)}, bf16[8,128,896]{2,1,0:T(8,128)(2,1)}, u32[]{:S(2)}, u32[]{:S(2)}) collective-permute-start(bf16[8,128,896]{2,1,0:T(8,128)(2,1)S(1)} %encode.3.refs_6_.refs_1_), channel_id=1, source_target_pairs={{0,1},{1,0},{2,3},{3,2},{4,5},{5,4},{6,7},{7,6},{8,9},{9,8},{10,11... | collective-permute-start | bytes 5505032 | tf_op jit(solution)/shard_map/ppermute | solution.py:60
  111.0 16.8 %collective-permute-start.21 = (bf16[1,128,896]{2,1,0:T(8,128)(2,1)S(1)}, bf16[1,128,896]{2,1,0:T(8,128)(2,1)S(1)}, u32[]{:S(2)}, u32[]{:S(2)}) collective-permute-start(bf16[1,128,896]{2,1,0:T(8,128)(2,1)S(1)} %slice.19), channel_id=1, source_target_pairs={{0,9},{1,8},{2,11},{3,10},{4,13},{5,12},{6,15},{7,14},{8,17},{9,16... | collective-permute-start | bytes 688136 | tf_op jit(solution)/shard_map/ppermute | solution.py:517
  115.1 12.6 %collective-permute-start.20 = (bf16[1,128,896]{2,1,0:T(8,128)(2,1)S(1)}, bf16[1,128,896]{2,1,0:T(8,128)(2,1)S(1)}, u32[]{:S(2)}, u32[]{:S(2)}) collective-permute-start(bf16[1,128,896]{2,1,0:T(8,128)(2,1)S(1)} %slice.19), channel_id=1, source_target_pairs={{0,8},{1,9},{2,10},{3,11},{4,12},{5,13},{6,14},{7,15},{8,16},{9,17... | collective-permute-start | bytes 688136 | tf_op jit(solution)/shard_map/ppermute | solution.py:517
  126.9 10.2 %collective-permute-start.24 = (bf16[4,256,512]{2,1,0:T(8,128)(2,1)}, bf16[4,256,512]{2,1,0:T(8,128)(2,1)S(1)}, u32[]{:S(2)}, u32[]{:S(2)}) collective-permute-start(bf16[4,256,512]{2,1,0:T(8,128)(2,1)} %get-tuple-element.30), channel_id=1, source_target_pairs={{0,1},{1,0},{2,3},{3,2},{4,5},{5,4},{6,7},{7,6},{8,9},{9,8},{10,11... | collective-permute-start | bytes 3145736 | tf_op jit(solution)/shard_map/ppermute | solution.py:60
  127.8 0.7 copy-start.12
  127.8 0.8 copy-start.13
  128.6 8.5 %copy-start.5 = (bf16[4,256,512]{2,1,0:T(8,128)(2,1)S(1)}, bf16[4,256,512]{2,1,0:T(8,128)(2,1)}, u32[]{:S(2)}) copy-start(bf16[4,256,512]{2,1,0:T(8,128)(2,1)} %get-tuple-element.27.refs_9_.kept_ref) | copy-start | bytes 3145732
  136.7 3.0 %collective-permute-start.23 = (bf16[4,256,512]{2,1,0:T(8,128)(2,1)}, bf16[4,256,512]{2,1,0:T(8,128)(2,1)S(1)}, u32[]{:S(2)}, u32[]{:S(2)}) collective-permute-start(bf16[4,256,512]{2,1,0:T(8,128)(2,1)} %get-tuple-element.29), channel_id=1, source_target_pairs={{0,1},{1,0},{2,3},{3,2},{4,5},{5,4},{6,7},{7,6},{8,9},{9,8},{10,11... | collective-permute-start | bytes 3145736 | tf_op jit(solution)/shard_map/ppermute | solution.py:60
  137.1 1.2 copy-start.6
  140.0 10.8 %collective-permute-start.25 = (bf16[256,512]{1,0:T(8,128)(2,1)S(1)}, bf16[256,512]{1,0:T(8,128)(2,1)S(1)}, u32[]{:S(2)}, u32[]{:S(2)}) collective-permute-start(bf16[256,512]{1,0:T(8,128)(2,1)S(1)} %get-tuple-element.35), channel_id=1, source_target_pairs={{0,6},{1,7},{2,0},{3,1},{4,2},{5,3},{6,4},{7,5},{8,14},{9,15},{10,... | collective-permute-start | bytes 786440 | tf_op jit(solution)/shard_map/ppermute | solution.py:91
  140.4 11.7 %collective-permute-start.26 = (bf16[256,512]{1,0:T(8,128)(2,1)S(1)}, bf16[256,512]{1,0:T(8,128)(2,1)S(1)}, u32[]{:S(2)}, u32[]{:S(2)}) collective-permute-start(bf16[256,512]{1,0:T(8,128)(2,1)S(1)} %get-tuple-element.36), channel_id=1, source_target_pairs={{0,2},{1,3},{2,4},{3,5},{4,6},{5,7},{6,0},{7,1},{8,10},{9,11},{10,... | collective-permute-start | bytes 786440 | tf_op jit(solution)/shard_map/ppermute | solution.py:91
  141.7 16.4 %collective-permute-start.27 = (bf16[256,512]{1,0:T(8,128)(2,1)S(1)}, bf16[256,512]{1,0:T(8,128)(2,1)S(1)}, u32[]{:S(2)}, u32[]{:S(2)}) collective-permute-start(bf16[256,512]{1,0:T(8,128)(2,1)S(1)} %get-tuple-element.37), channel_id=1, source_target_pairs={{0,4},{1,5},{2,6},{3,7},{4,0},{5,1},{6,2},{7,3},{8,12},{9,13},{10,... | collective-permute-start | bytes 786440 | tf_op jit(solution)/shard_map/ppermute | solution.py:91
  143.4 24.8 %collective-permute-start.28 = (bf16[256,512]{1,0:T(8,128)(2,1)S(1)}, bf16[256,512]{1,0:T(8,128)(2,1)S(1)}, u32[]{:S(2)}, u32[]{:S(2)}) collective-permute-start(bf16[256,512]{1,0:T(8,128)(2,1)S(1)} %get-tuple-element.31.refs_0_), channel_id=1, source_target_pairs={{0,6},{1,7},{2,0},{3,1},{4,2},{5,3},{6,4},{7,5},{8,14},{9,15},{10,... | collective-permute-start | bytes 786440 | tf_op jit(solution)/shard_map/ppermute | solution.py:91
  145.4 22.7 %collective-permute-start.29 = (bf16[256,512]{1,0:T(8,128)(2,1)S(1)}, bf16[256,512]{1,0:T(8,128)(2,1)S(1)}, u32[]{:S(2)}, u32[]{:S(2)}) collective-permute-start(bf16[256,512]{1,0:T(8,128)(2,1)S(1)} %get-tuple-element.32.refs_1_), channel_id=1, source_target_pairs={{0,2},{1,3},{2,4},{3,5},{4,6},{5,7},{6,0},{7,1},{8,10},{9,11},{10,... | collective-permute-start | bytes 786440 | tf_op jit(solution)/shard_map/ppermute | solution.py:91
  150.7 18.6 %collective-permute-start.30 = (bf16[256,512]{1,0:T(8,128)(2,1)S(1)}, bf16[256,512]{1,0:T(8,128)(2,1)S(1)}, u32[]{:S(2)}, u32[]{:S(2)}) collective-permute-start(bf16[256,512]{1,0:T(8,128)(2,1)S(1)} %get-tuple-element.33.refs_2_), channel_id=1, source_target_pairs={{0,4},{1,5},{2,6},{3,7},{4,0},{5,1},{6,2},{7,3},{8,12},{9,13},{10,... | collective-permute-start | bytes 786440 | tf_op jit(solution)/shard_map/ppermute | solution.py:91
  158.1 13.5 %copy-start.1 = (bf16[8,128,896]{2,1,0:T(8,128)(2,1)S(1)}, bf16[8,128,896]{2,1,0:T(8,128)(2,1)}, u32[]{:S(2)}) copy-start(bf16[8,128,896]{2,1,0:T(8,128)(2,1)} %param.13) | copy-start | bytes 5505028
Sparse Core Ops, SparseCore 0:
  11.1 60.9 all-gather.2
  110.8 40.8 reduce-scatter.1

commit v9 on v8

--- a/solution.py
+++ b/solution.py
@@ -430,7 +430,7 @@
         ),
         compiler_params=pltpu.CompilerParams(
             dimension_semantics=("arbitrary",),
-            vmem_limit_bytes=(60 << 20) if split else VMEM_LIMIT,
+            vmem_limit_bytes=(46 << 20) if split else VMEM_LIMIT,
         ),
         cost_estimate=pl.CostEstimate(
             flops=steps * (4 * SPANS_STEP * KNB * NLEN * E * width + 2 * tile * width * D),
@@ -525,8 +525,13 @@
         )
         for flip in range(2)
     )
-    weights = (queries, w_key, w_value, w_out)
-    terms = decode(2, 2, high, high_other, *weights, None, (), low)
+    terms = decode(2, 2, high, high_other, queries, w_key, w_value, w_out, None, (), low)
+    weights = (
+        queries,
+        w_key,
+        pltpu.with_memory_space_constraint(w_value, pltpu.HBM),
+        pltpu.with_memory_space_constraint(w_out, pltpu.HBM),
+    )
     high_out = lax.psum_scatter(terms, "store", scatter_dimension=1, tiled=True)
     kept_1, given_1 = decode(1, 1, low, low_other, *weights, pairs, (), terms)
     taken_1 = swap_cores(given_1)

time: 180 us -> 180 us (level)
  waiting for transfers between devices: 42.8 us -> 47.2 us
  Pallas kernels: 56.2 us -> 52.9 us
  local copies, waits for them, and re-layouts: 7.46 us -> 5.46 us
    pallas_call x3, Pallas kernels: 26.7 us -> 23.4 us  [decode(): pl.pallas_call(lambda *refs: decode_kernel(len(carried) > 0, split, *refs...]
    ppermute x6, waiting for transfers between devices: 22.4 us -> 24.8 us  [send_over_x(): got.append(lax.ppermute(sums[j], 'store', route))]
    unnamed x29 -> x17, local copies, waits for them, and re-layouts: 4.18 us -> 2.15 us
  transfers between devices with their start and end apart: 33 -> 33, of which waited for: 13 -> 16; matrix products, arithmetic and copies ran while one was open for 7% -> 7% of each run, Pallas kernels for 21% -> 20%
where the time goes in v9:
time: 180 us; the launch traced here: 178 us
  Pallas kernels  52.9 us (29%)
  waiting for transfers between devices  47.2 us (26%)
  starting transfers between devices  44.4 us (25%)
  between operations  13.7 us (8%)
  matrix products  10.2 us (6%)
  local copies, waits for them, and re-layouts  5.46 us (3%)
  other arithmetic  3.79 us (2%)
    ppermute x6, waiting for transfers between devices, send_over_x(): got.append(lax.ppermute(sums[j], 'store', route))  24.8 us
    pallas_call x3, Pallas kernels, decode(): pl.pallas_call(lambda *refs: decode_kernel(len(carried) > 0, split, *refs...  23.4 us
    ppermute x12, starting transfers between devices, around(): got.append(lax.ppermute(block, 'seq', route))  15.1 us
    pallas_call x2, Pallas kernels, encode(): pl.pallas_call(encode_kernel, out_shape=jax.ShapeDtypeStruct((count, NLEN...  14.5 us
    all_gather x1, waiting for transfers between devices, body(): gathered = lax.all_gather(sources, 'store', axis=0, tiled=True)  12.3 us
    ppermute x8, starting transfers between devices, swap_cores(): return lax.ppermute(block, 'store', [(i, i ^ 1) for i in range(count)])  10.7 us
    dot_general x1, matrix products, dot(): return jnp.dot(a, b, preferred_element_type=F32)  10.2 us
    pallas_call x1, Pallas kernels, enc_queries(): pl.pallas_call(enc_query_kernel, out_shape=jax.ShapeDtypeStruct((count, N...  8.1 us
  transfers between devices with their start and end apart: 33, of which 16 were waited for; matrix products, arithmetic and copies ran while one was open for 7% of the time, Pallas kernels for 20%

profile of v9, /device:TPU:9, one launch (start us, length us, event | category | flops | bytes accessed | tf_op | source)
XLA Modules:
  0.0 177.7 jit_solution(7985619858997952231)
XLA Ops:
  6.5 0.9 copy.16
  7.9 0.7 broadcast_add_fusion
  8.6 0.6 gather_fusion
  9.3 1.7 gather_fusion.1
  11.0 0.9 constant_dynamic-slice_fusion
  12.0 2.1 %collective-permute-start.5 = (bf16[128,256]{1,0:T(8,128)(2,1)S(1)}, bf16[128,256]{1,0:T(8,128)(2,1)S(1)}, u32[]{:S(2)}, u32[]{:S(2)}) collective-permute-start(bf16[128,256]{1,0:T(8,128)(2,1)S(1)} %get-tuple-element.41.refs_4_), channel_id=1, source_target_pairs={{0,64},{8,72},{16,80},{24,88},{32,96},{40,104},{48,112},{56,120},{... | collective-permute-start | bytes 196616 | tf_op jit(solution)/shard_map/ppermute | solution.py:44
  14.0 1.1 collective-permute-start.4
  15.5 3.6 %collective-permute-start.2 = (bf16[128,256]{1,0:T(8,128)(2,1)S(1)}, bf16[128,256]{1,0:T(8,128)(2,1)S(1)}, u32[]{:S(2)}, u32[]{:S(2)}) collective-permute-start(bf16[128,256]{1,0:T(8,128)(2,1)S(1)} %get-tuple-element.42.refs_0_), channel_id=1, source_target_pairs={{0,16},{8,24},{16,0},{24,8},{32,48},{40,56},{48,32},{56,40},{64,80... | collective-permute-start | bytes 196616 | tf_op jit(solution)/shard_map/ppermute | solution.py:44
  19.5 1.0 collective-permute-start
  20.8 1.8 collective-permute-done.1.refs_2_
  22.5 1.4 collective-permute-done.refs_1_
  23.9 2.2 %collective-permute-start.8 = (bf16[4,128,256]{2,1,0:T(8,128)(2,1)S(1)}, bf16[4,128,256]{2,1,0:T(8,128)(2,1)S(1)}, u32[]{:S(2)}, u32[]{:S(2)}) collective-permute-start(bf16[4,128,256]{2,1,0:T(8,128)(2,1)S(1)} %get-tuple-element.22.refs_0_), channel_id=1, source_target_pairs={{0,64},{8,72},{16,80},{24,88},{32,96},{40,104},{48,112},{56,120},{... | collective-permute-start | bytes 786440 | tf_op jit(solution)/shard_map/ppermute | solution.py:44
  26.2 1.5 collective-permute-start.6
  27.6 1.2 collective-permute-start.11
  28.8 1.4 collective-permute-start.10
  30.2 1.0 collective-permute-done.8.refs_3_
  31.3 10.2 %convolution_convert_fusion.refs_8_.refs_2_.refs_3_ = bf16[1024,512]{1,0:T(8,128)(2,1)} fusion(bf16[1024,4096]{1,0:T(8,128)(2,1)} %hidden_ref.1, bf16[4096,512]{1,0:T(8,128)(2,1)} %param.15), kind=kOutput, calls=%fused_computation.2 | convolution fusion | flops 4295491584 | bytes 13631488 | tf_op jit(solution)/shard_map/dot_general | solution.py:29
  41.6 6.3 %cond_rows.1 = bf16[1024,256]{1,0:T(8,128)(2,1)S(1)} custom-call(s32[8]{0:T(128)S(1)} %pad_add_fusion.1.src_ref, bf16[1024,4096]{1,0:T(8,128)(2,1)} %hidden_ref.1, bf16[4,128,256]{2,1,0:T(8,128)(2,1)S(1)} %get-tuple-element.22.refs_0_, bf16[4,128,256]{2,1,0:T(8,128)(2,1)S(1)} %collective-permute-done.6.refs_1_, ...), custom_call_target="tpu_custom_call" | custom-call | flops 2147483648 | bytes 12582912 | tf_op jit(solution)/shard_map/cond_rows/pallas_call | solution.py:122
  47.9 2.5 %collective-permute-start.14 = (bf16[16,64,256]{2,1,0:T(8,128)(2,1)S(1)}, bf16[16,64,256]{2,1,0:T(8,128)(2,1)S(1)}, u32[]{:S(2)}, u32[]{:S(2)}) collective-permute-start(bf16[16,64,256]{2,1,0:T(8,128)(2,1)S(1)} %bitcast.7), channel_id=1, source_target_pairs={{0,4},{1,5},{2,6},{3,7},{4,0},{5,1},{6,2},{7,3},{8,12},{9,13},{10,... | collective-permute-start | bytes 1572872 | tf_op jit(solution)/shard_map/ppermute | solution.py:54
  50.4 0.9 collective-permute-start.13
  52.1 7.7 %collective-permute-start.15 = (bf16[16,64,256]{2,1,0:T(8,128)(2,1)S(1)}, bf16[16,64,256]{2,1,0:T(8,128)(2,1)S(1)}, u32[]{:S(2)}, u32[]{:S(2)}) collective-permute-start(bf16[16,64,256]{2,1,0:T(8,128)(2,1)S(1)} %bitcast.10), channel_id=1, source_target_pairs={{0,1},{1,0},{2,3},{3,2},{4,5},{5,4},{6,7},{7,6},{8,9},{9,8},{10,11... | collective-permute-start | bytes 1572872 | tf_op jit(solution)/shard_map/ppermute | solution.py:60
  59.8 12.3 %all-gather.3.cloned.1.call-done.refs_0_.refs_1_.refs_2_.refs_3_ = bf16[32,128,896]{2,1,0:T(8,128)(2,1)} async-done(((bf16[4,128,896]{2,1,0:T(8,128)(2,1)}), bf16[32,128,896]{2,1,0:T(8,128)(2,1)}) %all-gather.3.cloned.1.call-update) | async-done | bytes 7340048 | tf_op jit(solution)/shard_map/all_gather | solution.py:475
  72.0 8.1 %enc_queries.1.refs_3_.refs_12_ = bf16[16,128,896]{2,1,0:T(8,128)(2,1)S(1)} custom-call(s32[16]{0:T(128)S(1)} %select_reduce_fusion.1.pos_ref, bf16[32,128,896]{2,1,0:T(8,128)(2,1)} %all-gather.3.cloned.1.call-done.refs_0_.refs_1_.refs_2_.refs_3_, bf16[32,128,896]{2,1,0:T(8,128)(2,1)} %all-gather.3.cloned.1.call-done.refs_0_.refs_1_.refs_2_.refs_3_, ...), custom_call_target="tpu_custom_call" | custom-call | flops 3288334336 | bytes 10485760 | tf_op jit(solution)/shard_map/enc_queries/pallas_call | solution.py:203
  81.2 1.1 collective-permute-done.16.refs_9_
  82.3 0.7 collective-permute-done.17.refs_10_
  83.0 0.7 collective-permute-done.18.refs_11_
  83.8 7.3 %encode.2.refs_14_.refs_0_ = bf16[8,128,896]{2,1,0:T(8,128)(2,1)S(1)} custom-call(s32[16]{0:T(128)S(1)} %select_reduce_fusion.1.pos_ref, s32[8]{0:T(128)S(1)} %pad_add_fusion.pair_ref.refs_0_, bf16[32,128,896]{2,1,0:T(8,128)(2,1)} %all-gather.3.cloned.1.call-done.refs_0_.refs_1_.refs_2_.refs_3_, ...), custom_call_target="tpu_custom_call" | custom-call | flops 2466250752 | bytes 8388608 | tf_op jit(solution)/shard_map/encode/pallas_call | solution.py:277
  91.4 1.2 copy-done.7
  92.7 7.3 %encode.3.refs_6_.refs_1_ = bf16[8,128,896]{2,1,0:T(8,128)(2,1)S(1)} custom-call(s32[16]{0:T(128)S(1)} %select_reduce_fusion.1.pos_ref, s32[8]{0:T(128)S(1)} %pad_add_fusion.pair_ref.refs_0_, bf16[32,128,896]{2,1,0:T(8,128)(2,1)} %all-gather.3.cloned.1.call-done.refs_0_.refs_1_.refs_2_.refs_3_, ...), custom_call_target="tpu_custom_call" | custom-call | flops 2466250752 | bytes 8388608 | tf_op jit(solution)/shard_map/encode/pallas_call | solution.py:277
  100.0 10.4 %decode.3.refs_7_ = bf16[512,4096]{1,0:T(8,128)(2,1)} custom-call(bf16[8,128,896]{2,1,0:T(8,128)(2,1)S(1)} %encode.2.refs_14_.refs_0_, bf16[8,128,896]{2,1,0:T(8,128)(2,1)S(1)} %collective-permute-done.22.refs_1_, bf16[1024,512]{1,0:T(8,128)(2,1)} %convolution_convert_fusion.refs_8_.refs_2_.refs_3_, bf16[896,512]{1,0:T(8,128)(2,1)S(1)} %copy-done.4, ...), custom_call_target="tpu_custom_call" | custom-call | flops 5905580032 | bytes 6291456 | tf_op jit(solution)/shard_map/decode/pallas_call | solution.py:406
  110.8 4.1 %collective-permute-start.21 = (bf16[1,128,896]{2,1,0:T(8,128)(2,1)S(1)}, bf16[1,128,896]{2,1,0:T(8,128)(2,1)S(1)}, u32[]{:S(2)}, u32[]{:S(2)}) collective-permute-start(bf16[1,128,896]{2,1,0:T(8,128)(2,1)S(1)} %slice.19), channel_id=1, source_target_pairs={{0,9},{1,8},{2,11},{3,10},{4,13},{5,12},{6,15},{7,14},{8,17},{9,16... | collective-permute-start | bytes 688136 | tf_op jit(solution)/shard_map/ppermute | solution.py:517
  114.9 3.8 %collective-permute-start.20 = (bf16[1,128,896]{2,1,0:T(8,128)(2,1)S(1)}, bf16[1,128,896]{2,1,0:T(8,128)(2,1)S(1)}, u32[]{:S(2)}, u32[]{:S(2)}) collective-permute-start(bf16[1,128,896]{2,1,0:T(8,128)(2,1)S(1)} %slice.19), channel_id=1, source_target_pairs={{0,8},{1,9},{2,10},{3,11},{4,12},{5,13},{6,14},{7,15},{8,16},{9,17... | collective-permute-start | bytes 688136 | tf_op jit(solution)/shard_map/ppermute | solution.py:517
  118.8 6.5 %decode.4 = (bf16[4,256,512]{2,1,0:T(8,128)(2,1)S(1)}, bf16[4,256,512]{2,1,0:T(8,128)(2,1)S(1)}) custom-call(s32[8]{0:T(128)S(1)} %pad_add_fusion.pair_ref.refs_0_, bf16[8,128,896]{2,1,0:T(8,128)(2,1)S(1)} %encode.3.refs_6_.refs_1_, bf16[8,128,896]{2,1,0:T(8,128)(2,1)S(1)} %collective-permute-done.19.refs_2_, ...), custom_call_target="tpu_custom_call" | custom-call | flops 2952790016 | bytes 6291456 | tf_op jit(solution)/shard_map/decode/pallas_call | solution.py:406
  125.3 0.6 collective-permute-start.24
  125.9 1.2 collective-permute-done.20.refs_7_
  127.1 6.5 %decode.5 = (bf16[4,256,512]{2,1,0:T(8,128)(2,1)S(1)}, bf16[4,256,512]{2,1,0:T(8,128)(2,1)S(1)}) custom-call(s32[8]{0:T(128)S(1)} %pad_add_fusion.pair_ref.refs_0_, bf16[8,128,896]{2,1,0:T(8,128)(2,1)S(1)} %encode.3.refs_6_.refs_1_, bf16[8,128,896]{2,1,0:T(8,128)(2,1)S(1)} %collective-permute-done.19.refs_2_, ...), custom_call_target="tpu_custom_call" | custom-call | flops 2952790016 | bytes 6291456 | tf_op jit(solution)/shard_map/decode/pallas_call | solution.py:406
  133.6 0.8 collective-permute-start.23
  134.7 2.0 %collective-permute-done.23.taken_ref = bf16[4,256,512]{2,1,0:T(8,128)(2,1)S(1)} collective-permute-done((bf16[4,256,512]{2,1,0:T(8,128)(2,1)S(1)}, bf16[4,256,512]{2,1,0:T(8,128)(2,1)S(1)}, u32[]{:S(2)}, u32[]{:S(2)}) %collective-permute-start.23) | collective-permute-done | bytes 1048608 | tf_op jit(solution)/shard_map/ppermute | solution.py:60
  137.5 1.1 collective-permute-start.26
  138.6 1.7 collective-permute-start.27
  140.3 2.1 %collective-permute-start.28 = (bf16[256,512]{1,0:T(8,128)(2,1)S(1)}, bf16[256,512]{1,0:T(8,128)(2,1)S(1)}, u32[]{:S(2)}, u32[]{:S(2)}) collective-permute-start(bf16[256,512]{1,0:T(8,128)(2,1)S(1)} %get-tuple-element.31.refs_0_), channel_id=1, source_target_pairs={{0,6},{1,7},{2,0},{3,1},{4,2},{5,3},{6,4},{7,5},{8,14},{9,15},{10,... | collective-permute-start | bytes 786440 | tf_op jit(solution)/shard_map/ppermute | solution.py:91
  142.3 5.5 %collective-permute-done.25 = bf16[256,512]{1,0:T(8,128)(2,1)S(1)} collective-permute-done((bf16[256,512]{1,0:T(8,128)(2,1)S(1)}, bf16[256,512]{1,0:T(8,128)(2,1)S(1)}, u32[]{:S(2)}, u32[]{:S(2)}) %collective-permute-start.25) | collective-permute-done | bytes 262176 | tf_op jit(solution)/shard_map/ppermute | solution.py:91
  147.8 1.3 collective-permute-start.30
  149.2 8.1 %collective-permute-done.27 = bf16[256,512]{1,0:T(8,128)(2,1)S(1)} collective-permute-done((bf16[256,512]{1,0:T(8,128)(2,1)S(1)}, bf16[256,512]{1,0:T(8,128)(2,1)S(1)}, u32[]{:S(2)}, u32[]{:S(2)}) %collective-permute-start.27) | collective-permute-done | bytes 262176 | tf_op jit(solution)/shard_map/ppermute | solution.py:91
  157.4 4.1 %collective-permute-done.28 = bf16[256,512]{1,0:T(8,128)(2,1)S(1)} collective-permute-done((bf16[256,512]{1,0:T(8,128)(2,1)S(1)}, bf16[256,512]{1,0:T(8,128)(2,1)S(1)}, u32[]{:S(2)}, u32[]{:S(2)}) %collective-permute-start.28) | collective-permute-done | bytes 262176 | tf_op jit(solution)/shard_map/ppermute | solution.py:91
  161.5 2.0 %collective-permute-done.29 = bf16[256,512]{1,0:T(8,128)(2,1)S(1)} collective-permute-done((bf16[256,512]{1,0:T(8,128)(2,1)S(1)}, bf16[256,512]{1,0:T(8,128)(2,1)S(1)}, u32[]{:S(2)}, u32[]{:S(2)}) %collective-permute-start.29) | collective-permute-done | bytes 262176 | tf_op jit(solution)/shard_map/ppermute | solution.py:91
  163.5 5.0 %collective-permute-done.30 = bf16[256,512]{1,0:T(8,128)(2,1)S(1)} collective-permute-done((bf16[256,512]{1,0:T(8,128)(2,1)S(1)}, bf16[256,512]{1,0:T(8,128)(2,1)S(1)}, u32[]{:S(2)}, u32[]{:S(2)}) %collective-permute-start.30) | collective-permute-done | bytes 262176 | tf_op jit(solution)/shard_map/ppermute | solution.py:91
  168.7 2.1 %pad_maximum_fusion = bf16[1024,512]{1,0:T(8,128)(2,1)} fusion(bf16[512,512]{1,0:T(8,128)(2,1)} %reduce-scatter.2.cloned.1.call-done, bf16[256,512]{1,0:T(8,128)(2,1)S(1)} %add_convert_fusion, bf16[256,512]{1,0:T(8,128)(2,1)S(1)} %add_convert_fusion.1), kind=kLoop, calls=%fused_computation.3 | loop fusion | flops 3145728 | bytes 2097152 | tf_op jit(solution)/shard_map/concatenate | solution.py:550
  (70 shorter events, 5.8 us)
Async XLA Ops:
  6.5 2.7 %copy-start = (bf16[8,128,896]{2,1,0:T(8,128)(2,1)S(1)}, bf16[8,128,896]{2,1,0:T(8,128)(2,1)}, u32[]{:S(2)}) copy-start(bf16[8,128,896]{2,1,0:T(8,128)(2,1)} %param.13) | copy-start | bytes 5505028
  6.5 65.5 %all-gather.3.cloned.1.call-start = ((), (), s32[]{:S(2)}) async-start(), calls=%async_computation.2 | async-start | bytes 8257536 | tf_op jit(solution)/shard_map/all_gather | solution.py:475
  11.0 157.7 %reduce-scatter.2.cloned.1.call-start = ((), (), s32[]{:S(2)}) async-start(), calls=%async_computation.1 | async-start | bytes 4718592 | tf_op jit(solution)/shard_map/reduce_scatter | solution.py:535
  12.0 7.6 %collective-permute-start.5 = (bf16[128,256]{1,0:T(8,128)(2,1)S(1)}, bf16[128,256]{1,0:T(8,128)(2,1)S(1)}, u32[]{:S(2)}, u32[]{:S(2)}) collective-permute-start(bf16[128,256]{1,0:T(8,128)(2,1)S(1)} %get-tuple-element.41.refs_4_), channel_id=1, source_target_pairs={{0,64},{8,72},{16,80},{24,88},{32,96},{40,104},{48,112},{56,120},{... | collective-permute-start | bytes 196616 | tf_op jit(solution)/shard_map/ppermute | solution.py:44
  14.0 6.5 %collective-permute-start.4 = (bf16[128,256]{1,0:T(8,128)(2,1)S(1)}, bf16[128,256]{1,0:T(8,128)(2,1)S(1)}, u32[]{:S(2)}, u32[]{:S(2)}) collective-permute-start(bf16[128,256]{1,0:T(8,128)(2,1)S(1)} %get-tuple-element.41.refs_4_), channel_id=1, source_target_pairs={{0,96},{8,104},{16,112},{24,120},{32,0},{40,8},{48,16},{56,24},{64... | collective-permute-start | bytes 196616 | tf_op jit(solution)/shard_map/ppermute | solution.py:44
  15.1 5.5 %collective-permute-start.3 = (bf16[128,256]{1,0:T(8,128)(2,1)S(1)}, bf16[128,256]{1,0:T(8,128)(2,1)S(1)}, u32[]{:S(2)}, u32[]{:S(2)}) collective-permute-start(bf16[128,256]{1,0:T(8,128)(2,1)S(1)} %get-tuple-element.41.refs_4_), channel_id=1, source_target_pairs={{0,32},{8,40},{16,48},{24,56},{32,64},{40,72},{48,80},{56,88},{64,... | collective-permute-start | bytes 196616 | tf_op jit(solution)/shard_map/ppermute | solution.py:44
  15.5 5.2 %collective-permute-start.2 = (bf16[128,256]{1,0:T(8,128)(2,1)S(1)}, bf16[128,256]{1,0:T(8,128)(2,1)S(1)}, u32[]{:S(2)}, u32[]{:S(2)}) collective-permute-start(bf16[128,256]{1,0:T(8,128)(2,1)S(1)} %get-tuple-element.42.refs_0_), channel_id=1, source_target_pairs={{0,16},{8,24},{16,0},{24,8},{32,48},{40,56},{48,32},{56,40},{64,80... | collective-permute-start | bytes 196616 | tf_op jit(solution)/shard_map/ppermute | solution.py:44
  19.1 3.4 %collective-permute-start.1 = (bf16[128,256]{1,0:T(8,128)(2,1)S(1)}, bf16[128,256]{1,0:T(8,128)(2,1)S(1)}, u32[]{:S(2)}, u32[]{:S(2)}) collective-permute-start(bf16[128,256]{1,0:T(8,128)(2,1)S(1)} %get-tuple-element.42.refs_0_), channel_id=1, source_target_pairs={{0,24},{8,0},{16,8},{24,16},{32,56},{40,32},{48,40},{56,48},{64,88... | collective-permute-start | bytes 196616 | tf_op jit(solution)/shard_map/ppermute | solution.py:44
  19.5 4.3 %collective-permute-start = (bf16[128,256]{1,0:T(8,128)(2,1)S(1)}, bf16[128,256]{1,0:T(8,128)(2,1)S(1)}, u32[]{:S(2)}, u32[]{:S(2)}) collective-permute-start(bf16[128,256]{1,0:T(8,128)(2,1)S(1)} %get-tuple-element.42.refs_0_), channel_id=1, source_target_pairs={{0,8},{8,16},{16,24},{24,0},{32,40},{40,48},{48,56},{56,32},{64,72... | collective-permute-start | bytes 196616 | tf_op jit(solution)/shard_map/ppermute | solution.py:44
  23.9 7.2 %collective-permute-start.8 = (bf16[4,128,256]{2,1,0:T(8,128)(2,1)S(1)}, bf16[4,128,256]{2,1,0:T(8,128)(2,1)S(1)}, u32[]{:S(2)}, u32[]{:S(2)}) collective-permute-start(bf16[4,128,256]{2,1,0:T(8,128)(2,1)S(1)} %get-tuple-element.22.refs_0_), channel_id=1, source_target_pairs={{0,64},{8,72},{16,80},{24,88},{32,96},{40,104},{48,112},{56,120},{... | collective-permute-start | bytes 786440 | tf_op jit(solution)/shard_map/ppermute | solution.py:44
  26.2 15.4 %collective-permute-start.7 = (bf16[4,128,256]{2,1,0:T(8,128)(2,1)S(1)}, bf16[4,128,256]{2,1,0:T(8,128)(2,1)S(1)}, u32[]{:S(2)}, u32[]{:S(2)}) collective-permute-start(bf16[4,128,256]{2,1,0:T(8,128)(2,1)S(1)} %get-tuple-element.22.refs_0_), channel_id=1, source_target_pairs={{0,96},{8,104},{16,112},{24,120},{32,0},{40,8},{48,16},{56,24},{64... | collective-permute-start | bytes 786440 | tf_op jit(solution)/shard_map/ppermute | solution.py:44
  26.2 15.4 %collective-permute-start.6 = (bf16[4,128,256]{2,1,0:T(8,128)(2,1)S(1)}, bf16[4,128,256]{2,1,0:T(8,128)(2,1)S(1)}, u32[]{:S(2)}, u32[]{:S(2)}) collective-permute-start(bf16[4,128,256]{2,1,0:T(8,128)(2,1)S(1)} %get-tuple-element.22.refs_0_), channel_id=1, source_target_pairs={{0,32},{8,40},{16,48},{24,56},{32,64},{40,72},{48,80},{56,88},{64,... | collective-permute-start | bytes 786440 | tf_op jit(solution)/shard_map/ppermute | solution.py:44
  27.6 14.0 %collective-permute-start.11 = (bf16[4,128,256]{2,1,0:T(8,128)(2,1)S(1)}, bf16[4,128,256]{2,1,0:T(8,128)(2,1)S(1)}, u32[]{:S(2)}, u32[]{:S(2)}) collective-permute-start(bf16[4,128,256]{2,1,0:T(8,128)(2,1)S(1)} %get-tuple-element.23.refs_4_), channel_id=1, source_target_pairs={{0,16},{8,24},{16,0},{24,8},{32,48},{40,56},{48,32},{56,40},{64,80... | collective-permute-start | bytes 786440 | tf_op jit(solution)/shard_map/ppermute | solution.py:44
  28.8 12.8 %collective-permute-start.10 = (bf16[4,128,256]{2,1,0:T(8,128)(2,1)S(1)}, bf16[4,128,256]{2,1,0:T(8,128)(2,1)S(1)}, u32[]{:S(2)}, u32[]{:S(2)}) collective-permute-start(bf16[4,128,256]{2,1,0:T(8,128)(2,1)S(1)} %get-tuple-element.23.refs_4_), channel_id=1, source_target_pairs={{0,24},{8,0},{16,8},{24,16},{32,56},{40,32},{48,40},{56,48},{64,88... | collective-permute-start | bytes 786440 | tf_op jit(solution)/shard_map/ppermute | solution.py:44
  31.2 10.5 %collective-permute-start.9 = (bf16[4,128,256]{2,1,0:T(8,128)(2,1)S(1)}, bf16[4,128,256]{2,1,0:T(8,128)(2,1)S(1)}, u32[]{:S(2)}, u32[]{:S(2)}) collective-permute-start(bf16[4,128,256]{2,1,0:T(8,128)(2,1)S(1)} %get-tuple-element.23.refs_4_), channel_id=1, source_target_pairs={{0,8},{8,16},{16,24},{24,0},{32,40},{40,48},{48,56},{56,32},{64,72... | collective-permute-start | bytes 786440 | tf_op jit(solution)/shard_map/ppermute | solution.py:44
  47.9 32.2 %collective-permute-start.14 = (bf16[16,64,256]{2,1,0:T(8,128)(2,1)S(1)}, bf16[16,64,256]{2,1,0:T(8,128)(2,1)S(1)}, u32[]{:S(2)}, u32[]{:S(2)}) collective-permute-start(bf16[16,64,256]{2,1,0:T(8,128)(2,1)S(1)} %bitcast.7), channel_id=1, source_target_pairs={{0,4},{1,5},{2,6},{3,7},{4,0},{5,1},{6,2},{7,3},{8,12},{9,13},{10,... | collective-permute-start | bytes 1572872 | tf_op jit(solution)/shard_map/ppermute | solution.py:54
  50.4 29.8 %collective-permute-start.13 = (bf16[16,64,256]{2,1,0:T(8,128)(2,1)S(1)}, bf16[16,64,256]{2,1,0:T(8,128)(2,1)S(1)}, u32[]{:S(2)}, u32[]{:S(2)}) collective-permute-start(bf16[16,64,256]{2,1,0:T(8,128)(2,1)S(1)} %bitcast.8), channel_id=1, source_target_pairs={{0,6},{1,7},{2,0},{3,1},{4,2},{5,3},{6,4},{7,5},{8,14},{9,15},{10,... | collective-permute-start | bytes 1572872 | tf_op jit(solution)/shard_map/ppermute | solution.py:54
  51.3 28.9 %collective-permute-start.12 = (bf16[16,64,256]{2,1,0:T(8,128)(2,1)S(1)}, bf16[16,64,256]{2,1,0:T(8,128)(2,1)S(1)}, u32[]{:S(2)}, u32[]{:S(2)}) collective-permute-start(bf16[16,64,256]{2,1,0:T(8,128)(2,1)S(1)} %bitcast.9), channel_id=1, source_target_pairs={{0,2},{1,3},{2,4},{3,5},{4,6},{5,7},{6,0},{7,1},{8,10},{9,11},{10,... | collective-permute-start | bytes 1572872 | tf_op jit(solution)/shard_map/ppermute | solution.py:54
  52.1 29.2 %collective-permute-start.15 = (bf16[16,64,256]{2,1,0:T(8,128)(2,1)S(1)}, bf16[16,64,256]{2,1,0:T(8,128)(2,1)S(1)}, u32[]{:S(2)}, u32[]{:S(2)}) collective-permute-start(bf16[16,64,256]{2,1,0:T(8,128)(2,1)S(1)} %bitcast.10), channel_id=1, source_target_pairs={{0,1},{1,0},{2,3},{3,2},{4,5},{5,4},{6,7},{7,6},{8,9},{9,8},{10,11... | collective-permute-start | bytes 1572872 | tf_op jit(solution)/shard_map/ppermute | solution.py:60
  80.1 3.6 %copy-start.3 = (bf16[896,896]{1,0:T(8,128)(2,1)S(1)}, bf16[896,896]{1,0:T(8,128)(2,1)}, u32[]{:S(2)}) copy-start(bf16[896,896]{1,0:T(8,128)(2,1)} %refs_13_.3) | copy-start | bytes 4816900
  80.3 2.0 %collective-permute-start.16 = (bf16[16,64,256]{2,1,0:T(8,128)(2,1)S(1)}, bf16[16,64,256]{2,1,0:T(8,128)(2,1)S(1)}, u32[]{:S(2)}, u32[]{:S(2)}) collective-permute-start(bf16[16,64,256]{2,1,0:T(8,128)(2,1)S(1)} %get-tuple-element.24.refs_5_), channel_id=1, source_target_pairs={{0,1},{1,0},{2,3},{3,2},{4,5},{5,4},{6,7},{7,6},{8,9},{9,8},{10,11... | collective-permute-start | bytes 1572872 | tf_op jit(solution)/shard_map/ppermute | solution.py:60
  80.6 2.4 %collective-permute-start.17 = (bf16[16,64,256]{2,1,0:T(8,128)(2,1)S(1)}, bf16[16,64,256]{2,1,0:T(8,128)(2,1)S(1)}, u32[]{:S(2)}, u32[]{:S(2)}) collective-permute-start(bf16[16,64,256]{2,1,0:T(8,128)(2,1)S(1)} %get-tuple-element.25.refs_6_), channel_id=1, source_target_pairs={{0,1},{1,0},{2,3},{3,2},{4,5},{5,4},{6,7},{7,6},{8,9},{9,8},{10,11... | collective-permute-start | bytes 1572872 | tf_op jit(solution)/shard_map/ppermute | solution.py:60
  80.9 2.9 %collective-permute-start.18 = (bf16[16,64,256]{2,1,0:T(8,128)(2,1)S(1)}, bf16[16,64,256]{2,1,0:T(8,128)(2,1)S(1)}, u32[]{:S(2)}, u32[]{:S(2)}) collective-permute-start(bf16[16,64,256]{2,1,0:T(8,128)(2,1)S(1)} %get-tuple-element.26.refs_7_), channel_id=1, source_target_pairs={{0,1},{1,0},{2,3},{3,2},{4,5},{5,4},{6,7},{7,6},{8,9},{9,8},{10,11... | collective-permute-start | bytes 1572872 | tf_op jit(solution)/shard_map/ppermute | solution.py:60
  81.2 9.8 %copy-start.6 = (bf16[16,64,256]{2,1,0:T(8,128)(2,1)}, bf16[16,64,256]{2,1,0:T(8,128)(2,1)S(1)}, u32[]{:S(2)}) copy-start(bf16[16,64,256]{2,1,0:T(8,128)(2,1)S(1)} %collective-permute-done.15.refs_8_) | copy-start | bytes 1572868
  91.1 8.9 %copy-start.2 = (bf16[512,4096]{1,0:T(8,128)(2,1)S(1)}, bf16[512,4096]{1,0:T(8,128)(2,1)}, u32[]{:S(2)}) copy-start(bf16[512,4096]{1,0:T(8,128)(2,1)} %refs_6_.3) | copy-start | bytes 12582916
  91.1 8.9 %copy-start.4 = (bf16[896,512]{1,0:T(8,128)(2,1)S(1)}, bf16[896,512]{1,0:T(8,128)(2,1)}, u32[]{:S(2)}) copy-start(bf16[896,512]{1,0:T(8,128)(2,1)} %refs_4_.7) | copy-start | bytes 2752516
  91.1 8.9 %copy-start.5 = (bf16[896,512]{1,0:T(8,128)(2,1)S(1)}, bf16[896,512]{1,0:T(8,128)(2,1)}, u32[]{:S(2)}) copy-start(bf16[896,512]{1,0:T(8,128)(2,1)} %refs_5_.5) | copy-start | bytes 2752516
  91.1 8.8 %collective-permute-start.22 = (bf16[8,128,896]{2,1,0:T(8,128)(2,1)S(1)}, bf16[8,128,896]{2,1,0:T(8,128)(2,1)S(1)}, u32[]{:S(2)}, u32[]{:S(2)}) collective-permute-start(bf16[8,128,896]{2,1,0:T(8,128)(2,1)S(1)} %encode.2.refs_14_.refs_0_), channel_id=1, source_target_pairs={{0,1},{1,0},{2,3},{3,2},{4,5},{5,4},{6,7},{7,6},{8,9},{9,8},{10,11... | collective-permute-start | bytes 5505032 | tf_op jit(solution)/shard_map/ppermute | solution.py:60
  91.4 1.2 copy-start.7
  110.4 8.4 %collective-permute-start.19 = (bf16[8,128,896]{2,1,0:T(8,128)(2,1)S(1)}, bf16[8,128,896]{2,1,0:T(8,128)(2,1)S(1)}, u32[]{:S(2)}, u32[]{:S(2)}) collective-permute-start(bf16[8,128,896]{2,1,0:T(8,128)(2,1)S(1)} %encode.3.refs_6_.refs_1_), channel_id=1, source_target_pairs={{0,1},{1,0},{2,3},{3,2},{4,5},{5,4},{6,7},{7,6},{8,9},{9,8},{10,11... | collective-permute-start | bytes 5505032 | tf_op jit(solution)/shard_map/ppermute | solution.py:60
  110.8 15.1 %collective-permute-start.21 = (bf16[1,128,896]{2,1,0:T(8,128)(2,1)S(1)}, bf16[1,128,896]{2,1,0:T(8,128)(2,1)S(1)}, u32[]{:S(2)}, u32[]{:S(2)}) collective-permute-start(bf16[1,128,896]{2,1,0:T(8,128)(2,1)S(1)} %slice.19), channel_id=1, source_target_pairs={{0,9},{1,8},{2,11},{3,10},{4,13},{5,12},{6,15},{7,14},{8,17},{9,16... | collective-permute-start | bytes 688136 | tf_op jit(solution)/shard_map/ppermute | solution.py:517
  114.9 12.2 %collective-permute-start.20 = (bf16[1,128,896]{2,1,0:T(8,128)(2,1)S(1)}, bf16[1,128,896]{2,1,0:T(8,128)(2,1)S(1)}, u32[]{:S(2)}, u32[]{:S(2)}) collective-permute-start(bf16[1,128,896]{2,1,0:T(8,128)(2,1)S(1)} %slice.19), channel_id=1, source_target_pairs={{0,8},{1,9},{2,10},{3,11},{4,12},{5,13},{6,14},{7,15},{8,16},{9,17... | collective-permute-start | bytes 688136 | tf_op jit(solution)/shard_map/ppermute | solution.py:517
  125.3 9.1 %collective-permute-start.24 = (bf16[4,256,512]{2,1,0:T(8,128)(2,1)S(1)}, bf16[4,256,512]{2,1,0:T(8,128)(2,1)S(1)}, u32[]{:S(2)}, u32[]{:S(2)}) collective-permute-start(bf16[4,256,512]{2,1,0:T(8,128)(2,1)S(1)} %get-tuple-element.30), channel_id=1, source_target_pairs={{0,1},{1,0},{2,3},{3,2},{4,5},{5,4},{6,7},{7,6},{8,9},{9,8},{10,11... | collective-permute-start | bytes 3145736 | tf_op jit(solution)/shard_map/ppermute | solution.py:60
  133.6 3.1 %collective-permute-start.23 = (bf16[4,256,512]{2,1,0:T(8,128)(2,1)S(1)}, bf16[4,256,512]{2,1,0:T(8,128)(2,1)S(1)}, u32[]{:S(2)}, u32[]{:S(2)}) collective-permute-start(bf16[4,256,512]{2,1,0:T(8,128)(2,1)S(1)} %get-tuple-element.29), channel_id=1, source_target_pairs={{0,1},{1,0},{2,3},{3,2},{4,5},{5,4},{6,7},{7,6},{8,9},{9,8},{10,11... | collective-permute-start | bytes 3145736 | tf_op jit(solution)/shard_map/ppermute | solution.py:60
  136.9 10.9 %collective-permute-start.25 = (bf16[256,512]{1,0:T(8,128)(2,1)S(1)}, bf16[256,512]{1,0:T(8,128)(2,1)S(1)}, u32[]{:S(2)}, u32[]{:S(2)}) collective-permute-start(bf16[256,512]{1,0:T(8,128)(2,1)S(1)} %get-tuple-element.35), channel_id=1, source_target_pairs={{0,6},{1,7},{2,0},{3,1},{4,2},{5,3},{6,4},{7,5},{8,14},{9,15},{10,... | collective-permute-start | bytes 786440 | tf_op jit(solution)/shard_map/ppermute | solution.py:91
  137.5 11.8 %collective-permute-start.26 = (bf16[256,512]{1,0:T(8,128)(2,1)S(1)}, bf16[256,512]{1,0:T(8,128)(2,1)S(1)}, u32[]{:S(2)}, u32[]{:S(2)}) collective-permute-start(bf16[256,512]{1,0:T(8,128)(2,1)S(1)} %get-tuple-element.36), channel_id=1, source_target_pairs={{0,2},{1,3},{2,4},{3,5},{4,6},{5,7},{6,0},{7,1},{8,10},{9,11},{10,... | collective-permute-start | bytes 786440 | tf_op jit(solution)/shard_map/ppermute | solution.py:91
  138.6 18.7 %collective-permute-start.27 = (bf16[256,512]{1,0:T(8,128)(2,1)S(1)}, bf16[256,512]{1,0:T(8,128)(2,1)S(1)}, u32[]{:S(2)}, u32[]{:S(2)}) collective-permute-start(bf16[256,512]{1,0:T(8,128)(2,1)S(1)} %get-tuple-element.37), channel_id=1, source_target_pairs={{0,4},{1,5},{2,6},{3,7},{4,0},{5,1},{6,2},{7,3},{8,12},{9,13},{10,... | collective-permute-start | bytes 786440 | tf_op jit(solution)/shard_map/ppermute | solution.py:91
  140.3 21.3 %collective-permute-start.28 = (bf16[256,512]{1,0:T(8,128)(2,1)S(1)}, bf16[256,512]{1,0:T(8,128)(2,1)S(1)}, u32[]{:S(2)}, u32[]{:S(2)}) collective-permute-start(bf16[256,512]{1,0:T(8,128)(2,1)S(1)} %get-tuple-element.31.refs_0_), channel_id=1, source_target_pairs={{0,6},{1,7},{2,0},{3,1},{4,2},{5,3},{6,4},{7,5},{8,14},{9,15},{10,... | collective-permute-start | bytes 786440 | tf_op jit(solution)/shard_map/ppermute | solution.py:91
  142.3 21.2 %collective-permute-start.29 = (bf16[256,512]{1,0:T(8,128)(2,1)S(1)}, bf16[256,512]{1,0:T(8,128)(2,1)S(1)}, u32[]{:S(2)}, u32[]{:S(2)}) collective-permute-start(bf16[256,512]{1,0:T(8,128)(2,1)S(1)} %get-tuple-element.32.refs_1_), channel_id=1, source_target_pairs={{0,2},{1,3},{2,4},{3,5},{4,6},{5,7},{6,0},{7,1},{8,10},{9,11},{10,... | collective-permute-start | bytes 786440 | tf_op jit(solution)/shard_map/ppermute | solution.py:91
  147.8 20.8 %collective-permute-start.30 = (bf16[256,512]{1,0:T(8,128)(2,1)S(1)}, bf16[256,512]{1,0:T(8,128)(2,1)S(1)}, u32[]{:S(2)}, u32[]{:S(2)}) collective-permute-start(bf16[256,512]{1,0:T(8,128)(2,1)S(1)} %get-tuple-element.33.refs_2_), channel_id=1, source_target_pairs={{0,4},{1,5},{2,6},{3,7},{4,0},{5,1},{6,2},{7,3},{8,12},{9,13},{10,... | collective-permute-start | bytes 786440 | tf_op jit(solution)/shard_map/ppermute | solution.py:91
  157.3 13.5 %copy-start.1 = (bf16[8,128,896]{2,1,0:T(8,128)(2,1)S(1)}, bf16[8,128,896]{2,1,0:T(8,128)(2,1)}, u32[]{:S(2)}) copy-start(bf16[8,128,896]{2,1,0:T(8,128)(2,1)} %param.13) | copy-start | bytes 5505028
Sparse Core Ops, SparseCore 0:
  11.1 60.8 all-gather.2
  110.5 47.1 reduce-scatter.1

commit v10 on v9

--- a/solution.py
+++ b/solution.py
@@ -508,6 +508,7 @@
     enc_q = enc_queries(mine, gathered, enc_query)
     own_lane[1:] = hold(own_lane[1:], enc_q)
     conds = own_lane + [swap_cores(block) for block in own_lane]
+    conds[4] = pltpu.with_memory_space_constraint(conds[4], pltpu.HBM)
     part = span_count // 2
     high = encode(0, part, mine, pairs, enc_q, gathered, conds, enc_out, ())
     high_other = swap_cores(high)

time: 180 us -> 179 us (level)
  no operation moved by 1% of the time
where the time goes in v10:
time: 179 us; the launch traced here: 177 us
  Pallas kernels  53.4 us (30%)
  waiting for transfers between devices  47.2 us (26%)
  starting transfers between devices  44.4 us (25%)
  between operations  13.7 us (8%)
  matrix products  10.2 us (6%)
  local copies, waits for them, and re-layouts  4.24 us (2%)
  other arithmetic  3.79 us (2%)
    ppermute x6, waiting for transfers between devices, send_over_x(): got.append(lax.ppermute(sums[j], 'store', route))  24.7 us
    pallas_call x3, Pallas kernels, decode(): pl.pallas_call(lambda *refs: decode_kernel(len(carried) > 0, split, *refs...  23.4 us
    ppermute x12, starting transfers between devices, around(): got.append(lax.ppermute(block, 'seq', route))  15.1 us
    pallas_call x2, Pallas kernels, encode(): pl.pallas_call(encode_kernel, out_shape=jax.ShapeDtypeStruct((count, NLEN...  15.1 us
    all_gather x1, waiting for transfers between devices, body(): gathered = lax.all_gather(sources, 'store', axis=0, tiled=True)  12.3 us
    ppermute x8, starting transfers between devices, swap_cores(): return lax.ppermute(block, 'store', [(i, i ^ 1) for i in range(count)])  10.7 us
    dot_general x1, matrix products, dot(): return jnp.dot(a, b, preferred_element_type=F32)  10.2 us
    pallas_call x1, Pallas kernels, enc_queries(): pl.pallas_call(enc_query_kernel, out_shape=jax.ShapeDtypeStruct((count, N...  8.1 us
  transfers between devices with their start and end apart: 33, of which 16 were waited for; matrix products, arithmetic and copies ran while one was open for 7% of the time, Pallas kernels for 20%

profile of v10, /device:TPU:9, one launch (start us, length us, event | category | flops | bytes accessed | tf_op | source)
XLA Modules:
  0.0 176.9 jit_solution(4927096840509412316)
XLA Ops:
  6.5 0.9 copy.16
  7.9 0.7 broadcast_add_fusion
  8.6 0.6 gather_fusion
  9.3 1.7 gather_fusion.1
  11.0 0.9 constant_dynamic-slice_fusion
  12.0 2.1 %collective-permute-start.5 = (bf16[128,256]{1,0:T(8,128)(2,1)S(1)}, bf16[128,256]{1,0:T(8,128)(2,1)S(1)}, u32[]{:S(2)}, u32[]{:S(2)}) collective-permute-start(bf16[128,256]{1,0:T(8,128)(2,1)S(1)} %get-tuple-element.41.refs_4_), channel_id=1, source_target_pairs={{0,64},{8,72},{16,80},{24,88},{32,96},{40,104},{48,112},{56,120},{... | collective-permute-start | bytes 196616 | tf_op jit(solution)/shard_map/ppermute | solution.py:44
  14.1 1.1 collective-permute-start.4
  15.5 3.6 %collective-permute-start.2 = (bf16[128,256]{1,0:T(8,128)(2,1)S(1)}, bf16[128,256]{1,0:T(8,128)(2,1)S(1)}, u32[]{:S(2)}, u32[]{:S(2)}) collective-permute-start(bf16[128,256]{1,0:T(8,128)(2,1)S(1)} %get-tuple-element.42.refs_0_), channel_id=1, source_target_pairs={{0,16},{8,24},{16,0},{24,8},{32,48},{40,56},{48,32},{56,40},{64,80... | collective-permute-start | bytes 196616 | tf_op jit(solution)/shard_map/ppermute | solution.py:44
  19.6 1.0 collective-permute-start
  20.8 1.8 collective-permute-done.1.refs_2_
  22.5 1.4 collective-permute-done.refs_1_
  23.9 2.2 %collective-permute-start.8 = (bf16[4,128,256]{2,1,0:T(8,128)(2,1)S(1)}, bf16[4,128,256]{2,1,0:T(8,128)(2,1)S(1)}, u32[]{:S(2)}, u32[]{:S(2)}) collective-permute-start(bf16[4,128,256]{2,1,0:T(8,128)(2,1)S(1)} %get-tuple-element.22.refs_0_), channel_id=1, source_target_pairs={{0,64},{8,72},{16,80},{24,88},{32,96},{40,104},{48,112},{56,120},{... | collective-permute-start | bytes 786440 | tf_op jit(solution)/shard_map/ppermute | solution.py:44
  26.2 1.5 collective-permute-start.6
  27.6 1.2 collective-permute-start.11
  28.8 1.4 collective-permute-start.10
  30.2 1.0 collective-permute-done.8.refs_3_
  31.3 10.2 %convolution_convert_fusion.refs_8_.refs_2_.refs_3_ = bf16[1024,512]{1,0:T(8,128)(2,1)} fusion(bf16[1024,4096]{1,0:T(8,128)(2,1)} %hidden_ref.1, bf16[4096,512]{1,0:T(8,128)(2,1)} %param.15), kind=kOutput, calls=%fused_computation.2 | convolution fusion | flops 4295491584 | bytes 13631488 | tf_op jit(solution)/shard_map/dot_general | solution.py:29
  41.6 6.3 %cond_rows.1 = bf16[1024,256]{1,0:T(8,128)(2,1)S(1)} custom-call(s32[8]{0:T(128)S(1)} %pad_add_fusion.1.src_ref, bf16[1024,4096]{1,0:T(8,128)(2,1)} %hidden_ref.1, bf16[4,128,256]{2,1,0:T(8,128)(2,1)S(1)} %get-tuple-element.22.refs_0_, bf16[4,128,256]{2,1,0:T(8,128)(2,1)S(1)} %collective-permute-done.6.refs_1_, ...), custom_call_target="tpu_custom_call" | custom-call | flops 2147483648 | bytes 12582912 | tf_op jit(solution)/shard_map/cond_rows/pallas_call | solution.py:122
  47.9 2.5 %collective-permute-start.14 = (bf16[16,64,256]{2,1,0:T(8,128)(2,1)S(1)}, bf16[16,64,256]{2,1,0:T(8,128)(2,1)S(1)}, u32[]{:S(2)}, u32[]{:S(2)}) collective-permute-start(bf16[16,64,256]{2,1,0:T(8,128)(2,1)S(1)} %bitcast.7), channel_id=1, source_target_pairs={{0,4},{1,5},{2,6},{3,7},{4,0},{5,1},{6,2},{7,3},{8,12},{9,13},{10,... | collective-permute-start | bytes 1572872 | tf_op jit(solution)/shard_map/ppermute | solution.py:54
  50.4 0.9 collective-permute-start.13
  51.3 0.6 collective-permute-start.12
  52.1 7.7 %collective-permute-start.15 = (bf16[16,64,256]{2,1,0:T(8,128)(2,1)S(1)}, bf16[16,64,256]{2,1,0:T(8,128)(2,1)S(1)}, u32[]{:S(2)}, u32[]{:S(2)}) collective-permute-start(bf16[16,64,256]{2,1,0:T(8,128)(2,1)S(1)} %bitcast.10), channel_id=1, source_target_pairs={{0,1},{1,0},{2,3},{3,2},{4,5},{5,4},{6,7},{7,6},{8,9},{9,8},{10,11... | collective-permute-start | bytes 1572872 | tf_op jit(solution)/shard_map/ppermute | solution.py:60
  59.8 12.3 %all-gather.3.cloned.1.call-done.refs_0_.refs_1_.refs_2_.refs_3_ = bf16[32,128,896]{2,1,0:T(8,128)(2,1)} async-done(((bf16[4,128,896]{2,1,0:T(8,128)(2,1)}), bf16[32,128,896]{2,1,0:T(8,128)(2,1)}) %all-gather.3.cloned.1.call-update) | async-done | bytes 7340048 | tf_op jit(solution)/shard_map/all_gather | solution.py:475
  72.1 8.1 %enc_queries.1.refs_3_.refs_12_ = bf16[16,128,896]{2,1,0:T(8,128)(2,1)S(1)} custom-call(s32[16]{0:T(128)S(1)} %select_reduce_fusion.1.pos_ref, bf16[32,128,896]{2,1,0:T(8,128)(2,1)} %all-gather.3.cloned.1.call-done.refs_0_.refs_1_.refs_2_.refs_3_, bf16[32,128,896]{2,1,0:T(8,128)(2,1)} %all-gather.3.cloned.1.call-done.refs_0_.refs_1_.refs_2_.refs_3_, ...), custom_call_target="tpu_custom_call" | custom-call | flops 3288334336 | bytes 10485760 | tf_op jit(solution)/shard_map/enc_queries/pallas_call | solution.py:203
  81.3 1.1 collective-permute-done.16.refs_9_
  82.3 0.7 collective-permute-done.17.refs_10_
  83.1 0.7 collective-permute-done.18.refs_11_
  83.8 7.3 %encode.2.refs_14_.refs_0_ = bf16[8,128,896]{2,1,0:T(8,128)(2,1)S(1)} custom-call(s32[16]{0:T(128)S(1)} %select_reduce_fusion.1.pos_ref, s32[8]{0:T(128)S(1)} %pad_add_fusion.pair_ref.refs_0_, bf16[32,128,896]{2,1,0:T(8,128)(2,1)} %all-gather.3.cloned.1.call-done.refs_0_.refs_1_.refs_2_.refs_3_, ...), custom_call_target="tpu_custom_call" | custom-call | flops 2466250752 | bytes 8388608 | tf_op jit(solution)/shard_map/encode/pallas_call | solution.py:277
  91.5 7.7 %encode.3.refs_6_.refs_1_ = bf16[8,128,896]{2,1,0:T(8,128)(2,1)S(1)} custom-call(s32[16]{0:T(128)S(1)} %select_reduce_fusion.1.pos_ref, s32[8]{0:T(128)S(1)} %pad_add_fusion.pair_ref.refs_0_, bf16[32,128,896]{2,1,0:T(8,128)(2,1)} %all-gather.3.cloned.1.call-done.refs_0_.refs_1_.refs_2_.refs_3_, ...), custom_call_target="tpu_custom_call" | custom-call | flops 2466250752 | bytes 8388608 | tf_op jit(solution)/shard_map/encode/pallas_call | solution.py:277
  99.3 10.4 %decode.3.refs_7_ = bf16[512,4096]{1,0:T(8,128)(2,1)} custom-call(bf16[8,128,896]{2,1,0:T(8,128)(2,1)S(1)} %encode.2.refs_14_.refs_0_, bf16[8,128,896]{2,1,0:T(8,128)(2,1)S(1)} %collective-permute-done.22.refs_1_, bf16[1024,512]{1,0:T(8,128)(2,1)} %convolution_convert_fusion.refs_8_.refs_2_.refs_3_, bf16[896,512]{1,0:T(8,128)(2,1)S(1)} %copy-done.4, ...), custom_call_target="tpu_custom_call" | custom-call | flops 5905580032 | bytes 6291456 | tf_op jit(solution)/shard_map/decode/pallas_call | solution.py:406
  110.1 4.1 %collective-permute-start.21 = (bf16[1,128,896]{2,1,0:T(8,128)(2,1)S(1)}, bf16[1,128,896]{2,1,0:T(8,128)(2,1)S(1)}, u32[]{:S(2)}, u32[]{:S(2)}) collective-permute-start(bf16[1,128,896]{2,1,0:T(8,128)(2,1)S(1)} %slice.19), channel_id=1, source_target_pairs={{0,9},{1,8},{2,11},{3,10},{4,13},{5,12},{6,15},{7,14},{8,17},{9,16... | collective-permute-start | bytes 688136 | tf_op jit(solution)/shard_map/ppermute | solution.py:518
  114.3 3.8 %collective-permute-start.20 = (bf16[1,128,896]{2,1,0:T(8,128)(2,1)S(1)}, bf16[1,128,896]{2,1,0:T(8,128)(2,1)S(1)}, u32[]{:S(2)}, u32[]{:S(2)}) collective-permute-start(bf16[1,128,896]{2,1,0:T(8,128)(2,1)S(1)} %slice.19), channel_id=1, source_target_pairs={{0,8},{1,9},{2,10},{3,11},{4,12},{5,13},{6,14},{7,15},{8,16},{9,17... | collective-permute-start | bytes 688136 | tf_op jit(solution)/shard_map/ppermute | solution.py:518
  118.1 6.5 %decode.4 = (bf16[4,256,512]{2,1,0:T(8,128)(2,1)S(1)}, bf16[4,256,512]{2,1,0:T(8,128)(2,1)S(1)}) custom-call(s32[8]{0:T(128)S(1)} %pad_add_fusion.pair_ref.refs_0_, bf16[8,128,896]{2,1,0:T(8,128)(2,1)S(1)} %encode.3.refs_6_.refs_1_, bf16[8,128,896]{2,1,0:T(8,128)(2,1)S(1)} %collective-permute-done.19.refs_2_, ...), custom_call_target="tpu_custom_call" | custom-call | flops 2952790016 | bytes 6291456 | tf_op jit(solution)/shard_map/decode/pallas_call | solution.py:406
  124.6 0.6 collective-permute-start.24
  125.2 1.2 collective-permute-done.20.refs_7_
  126.4 6.5 %decode.5 = (bf16[4,256,512]{2,1,0:T(8,128)(2,1)S(1)}, bf16[4,256,512]{2,1,0:T(8,128)(2,1)S(1)}) custom-call(s32[8]{0:T(128)S(1)} %pad_add_fusion.pair_ref.refs_0_, bf16[8,128,896]{2,1,0:T(8,128)(2,1)S(1)} %encode.3.refs_6_.refs_1_, bf16[8,128,896]{2,1,0:T(8,128)(2,1)S(1)} %collective-permute-done.19.refs_2_, ...), custom_call_target="tpu_custom_call" | custom-call | flops 2952790016 | bytes 6291456 | tf_op jit(solution)/shard_map/decode/pallas_call | solution.py:406
  132.9 0.9 collective-permute-start.23
  134.0 2.0 %collective-permute-done.23.taken_ref = bf16[4,256,512]{2,1,0:T(8,128)(2,1)S(1)} collective-permute-done((bf16[4,256,512]{2,1,0:T(8,128)(2,1)S(1)}, bf16[4,256,512]{2,1,0:T(8,128)(2,1)S(1)}, u32[]{:S(2)}, u32[]{:S(2)}) %collective-permute-start.23) | collective-permute-done | bytes 1048608 | tf_op jit(solution)/shard_map/ppermute | solution.py:60
  136.8 1.0 collective-permute-start.26
  137.9 1.7 collective-permute-start.27
  139.6 2.1 %collective-permute-start.28 = (bf16[256,512]{1,0:T(8,128)(2,1)S(1)}, bf16[256,512]{1,0:T(8,128)(2,1)S(1)}, u32[]{:S(2)}, u32[]{:S(2)}) collective-permute-start(bf16[256,512]{1,0:T(8,128)(2,1)S(1)} %get-tuple-element.31.refs_0_), channel_id=1, source_target_pairs={{0,6},{1,7},{2,0},{3,1},{4,2},{5,3},{6,4},{7,5},{8,14},{9,15},{10,... | collective-permute-start | bytes 786440 | tf_op jit(solution)/shard_map/ppermute | solution.py:91
  141.6 5.5 %collective-permute-done.25 = bf16[256,512]{1,0:T(8,128)(2,1)S(1)} collective-permute-done((bf16[256,512]{1,0:T(8,128)(2,1)S(1)}, bf16[256,512]{1,0:T(8,128)(2,1)S(1)}, u32[]{:S(2)}, u32[]{:S(2)}) %collective-permute-start.25) | collective-permute-done | bytes 262176 | tf_op jit(solution)/shard_map/ppermute | solution.py:91
  147.1 1.3 collective-permute-start.30
  148.6 8.0 %collective-permute-done.27 = bf16[256,512]{1,0:T(8,128)(2,1)S(1)} collective-permute-done((bf16[256,512]{1,0:T(8,128)(2,1)S(1)}, bf16[256,512]{1,0:T(8,128)(2,1)S(1)}, u32[]{:S(2)}, u32[]{:S(2)}) %collective-permute-start.27) | collective-permute-done | bytes 262176 | tf_op jit(solution)/shard_map/ppermute | solution.py:91
  156.7 4.2 %collective-permute-done.28 = bf16[256,512]{1,0:T(8,128)(2,1)S(1)} collective-permute-done((bf16[256,512]{1,0:T(8,128)(2,1)S(1)}, bf16[256,512]{1,0:T(8,128)(2,1)S(1)}, u32[]{:S(2)}, u32[]{:S(2)}) %collective-permute-start.28) | collective-permute-done | bytes 262176 | tf_op jit(solution)/shard_map/ppermute | solution.py:91
  160.9 2.1 %collective-permute-done.29 = bf16[256,512]{1,0:T(8,128)(2,1)S(1)} collective-permute-done((bf16[256,512]{1,0:T(8,128)(2,1)S(1)}, bf16[256,512]{1,0:T(8,128)(2,1)S(1)}, u32[]{:S(2)}, u32[]{:S(2)}) %collective-permute-start.29) | collective-permute-done | bytes 262176 | tf_op jit(solution)/shard_map/ppermute | solution.py:91
  163.0 4.9 %collective-permute-done.30 = bf16[256,512]{1,0:T(8,128)(2,1)S(1)} collective-permute-done((bf16[256,512]{1,0:T(8,128)(2,1)S(1)}, bf16[256,512]{1,0:T(8,128)(2,1)S(1)}, u32[]{:S(2)}, u32[]{:S(2)}) %collective-permute-start.30) | collective-permute-done | bytes 262176 | tf_op jit(solution)/shard_map/ppermute | solution.py:91
  168.0 2.1 %pad_maximum_fusion = bf16[1024,512]{1,0:T(8,128)(2,1)} fusion(bf16[512,512]{1,0:T(8,128)(2,1)} %reduce-scatter.2.cloned.1.call-done, bf16[256,512]{1,0:T(8,128)(2,1)S(1)} %add_convert_fusion, bf16[256,512]{1,0:T(8,128)(2,1)S(1)} %add_convert_fusion.1), kind=kLoop, calls=%fused_computation.3 | loop fusion | flops 3145728 | bytes 2097152 | tf_op jit(solution)/shard_map/concatenate | solution.py:551
  (68 shorter events, 5.2 us)
Async XLA Ops:
  6.5 2.7 %copy-start = (bf16[8,128,896]{2,1,0:T(8,128)(2,1)S(1)}, bf16[8,128,896]{2,1,0:T(8,128)(2,1)}, u32[]{:S(2)}) copy-start(bf16[8,128,896]{2,1,0:T(8,128)(2,1)} %param.13) | copy-start | bytes 5505028
  6.5 65.5 %all-gather.3.cloned.1.call-start = ((), (), s32[]{:S(2)}) async-start(), calls=%async_computation.2 | async-start | bytes 8257536 | tf_op jit(solution)/shard_map/all_gather | solution.py:475
  11.0 157.0 %reduce-scatter.2.cloned.1.call-start = ((), (), s32[]{:S(2)}) async-start(), calls=%async_computation.1 | async-start | bytes 4718592 | tf_op jit(solution)/shard_map/reduce_scatter | solution.py:536
  12.0 7.6 %collective-permute-start.5 = (bf16[128,256]{1,0:T(8,128)(2,1)S(1)}, bf16[128,256]{1,0:T(8,128)(2,1)S(1)}, u32[]{:S(2)}, u32[]{:S(2)}) collective-permute-start(bf16[128,256]{1,0:T(8,128)(2,1)S(1)} %get-tuple-element.41.refs_4_), channel_id=1, source_target_pairs={{0,64},{8,72},{16,80},{24,88},{32,96},{40,104},{48,112},{56,120},{... | collective-permute-start | bytes 196616 | tf_op jit(solution)/shard_map/ppermute | solution.py:44
  14.1 6.5 %collective-permute-start.4 = (bf16[128,256]{1,0:T(8,128)(2,1)S(1)}, bf16[128,256]{1,0:T(8,128)(2,1)S(1)}, u32[]{:S(2)}, u32[]{:S(2)}) collective-permute-start(bf16[128,256]{1,0:T(8,128)(2,1)S(1)} %get-tuple-element.41.refs_4_), channel_id=1, source_target_pairs={{0,96},{8,104},{16,112},{24,120},{32,0},{40,8},{48,16},{56,24},{64... | collective-permute-start | bytes 196616 | tf_op jit(solution)/shard_map/ppermute | solution.py:44
  15.1 5.5 %collective-permute-start.3 = (bf16[128,256]{1,0:T(8,128)(2,1)S(1)}, bf16[128,256]{1,0:T(8,128)(2,1)S(1)}, u32[]{:S(2)}, u32[]{:S(2)}) collective-permute-start(bf16[128,256]{1,0:T(8,128)(2,1)S(1)} %get-tuple-element.41.refs_4_), channel_id=1, source_target_pairs={{0,32},{8,40},{16,48},{24,56},{32,64},{40,72},{48,80},{56,88},{64,... | collective-permute-start | bytes 196616 | tf_op jit(solution)/shard_map/ppermute | solution.py:44
  15.5 5.2 %collective-permute-start.2 = (bf16[128,256]{1,0:T(8,128)(2,1)S(1)}, bf16[128,256]{1,0:T(8,128)(2,1)S(1)}, u32[]{:S(2)}, u32[]{:S(2)}) collective-permute-start(bf16[128,256]{1,0:T(8,128)(2,1)S(1)} %get-tuple-element.42.refs_0_), channel_id=1, source_target_pairs={{0,16},{8,24},{16,0},{24,8},{32,48},{40,56},{48,32},{56,40},{64,80... | collective-permute-start | bytes 196616 | tf_op jit(solution)/shard_map/ppermute | solution.py:44
  19.1 3.4 %collective-permute-start.1 = (bf16[128,256]{1,0:T(8,128)(2,1)S(1)}, bf16[128,256]{1,0:T(8,128)(2,1)S(1)}, u32[]{:S(2)}, u32[]{:S(2)}) collective-permute-start(bf16[128,256]{1,0:T(8,128)(2,1)S(1)} %get-tuple-element.42.refs_0_), channel_id=1, source_target_pairs={{0,24},{8,0},{16,8},{24,16},{32,56},{40,32},{48,40},{56,48},{64,88... | collective-permute-start | bytes 196616 | tf_op jit(solution)/shard_map/ppermute | solution.py:44
  19.6 4.3 %collective-permute-start = (bf16[128,256]{1,0:T(8,128)(2,1)S(1)}, bf16[128,256]{1,0:T(8,128)(2,1)S(1)}, u32[]{:S(2)}, u32[]{:S(2)}) collective-permute-start(bf16[128,256]{1,0:T(8,128)(2,1)S(1)} %get-tuple-element.42.refs_0_), channel_id=1, source_target_pairs={{0,8},{8,16},{16,24},{24,0},{32,40},{40,48},{48,56},{56,32},{64,72... | collective-permute-start | bytes 196616 | tf_op jit(solution)/shard_map/ppermute | solution.py:44
  23.9 7.2 %collective-permute-start.8 = (bf16[4,128,256]{2,1,0:T(8,128)(2,1)S(1)}, bf16[4,128,256]{2,1,0:T(8,128)(2,1)S(1)}, u32[]{:S(2)}, u32[]{:S(2)}) collective-permute-start(bf16[4,128,256]{2,1,0:T(8,128)(2,1)S(1)} %get-tuple-element.22.refs_0_), channel_id=1, source_target_pairs={{0,64},{8,72},{16,80},{24,88},{32,96},{40,104},{48,112},{56,120},{... | collective-permute-start | bytes 786440 | tf_op jit(solution)/shard_map/ppermute | solution.py:44
  26.2 15.4 %collective-permute-start.7 = (bf16[4,128,256]{2,1,0:T(8,128)(2,1)S(1)}, bf16[4,128,256]{2,1,0:T(8,128)(2,1)S(1)}, u32[]{:S(2)}, u32[]{:S(2)}) collective-permute-start(bf16[4,128,256]{2,1,0:T(8,128)(2,1)S(1)} %get-tuple-element.22.refs_0_), channel_id=1, source_target_pairs={{0,96},{8,104},{16,112},{24,120},{32,0},{40,8},{48,16},{56,24},{64... | collective-permute-start | bytes 786440 | tf_op jit(solution)/shard_map/ppermute | solution.py:44
  26.2 15.4 %collective-permute-start.6 = (bf16[4,128,256]{2,1,0:T(8,128)(2,1)S(1)}, bf16[4,128,256]{2,1,0:T(8,128)(2,1)S(1)}, u32[]{:S(2)}, u32[]{:S(2)}) collective-permute-start(bf16[4,128,256]{2,1,0:T(8,128)(2,1)S(1)} %get-tuple-element.22.refs_0_), channel_id=1, source_target_pairs={{0,32},{8,40},{16,48},{24,56},{32,64},{40,72},{48,80},{56,88},{64,... | collective-permute-start | bytes 786440 | tf_op jit(solution)/shard_map/ppermute | solution.py:44
  27.6 14.0 %collective-permute-start.11 = (bf16[4,128,256]{2,1,0:T(8,128)(2,1)S(1)}, bf16[4,128,256]{2,1,0:T(8,128)(2,1)S(1)}, u32[]{:S(2)}, u32[]{:S(2)}) collective-permute-start(bf16[4,128,256]{2,1,0:T(8,128)(2,1)S(1)} %get-tuple-element.23.refs_4_), channel_id=1, source_target_pairs={{0,16},{8,24},{16,0},{24,8},{32,48},{40,56},{48,32},{56,40},{64,80... | collective-permute-start | bytes 786440 | tf_op jit(solution)/shard_map/ppermute | solution.py:44
  28.8 12.8 %collective-permute-start.10 = (bf16[4,128,256]{2,1,0:T(8,128)(2,1)S(1)}, bf16[4,128,256]{2,1,0:T(8,128)(2,1)S(1)}, u32[]{:S(2)}, u32[]{:S(2)}) collective-permute-start(bf16[4,128,256]{2,1,0:T(8,128)(2,1)S(1)} %get-tuple-element.23.refs_4_), channel_id=1, source_target_pairs={{0,24},{8,0},{16,8},{24,16},{32,56},{40,32},{48,40},{56,48},{64,88... | collective-permute-start | bytes 786440 | tf_op jit(solution)/shard_map/ppermute | solution.py:44
  31.2 10.5 %collective-permute-start.9 = (bf16[4,128,256]{2,1,0:T(8,128)(2,1)S(1)}, bf16[4,128,256]{2,1,0:T(8,128)(2,1)S(1)}, u32[]{:S(2)}, u32[]{:S(2)}) collective-permute-start(bf16[4,128,256]{2,1,0:T(8,128)(2,1)S(1)} %get-tuple-element.23.refs_4_), channel_id=1, source_target_pairs={{0,8},{8,16},{16,24},{24,0},{32,40},{40,48},{48,56},{56,32},{64,72... | collective-permute-start | bytes 786440 | tf_op jit(solution)/shard_map/ppermute | solution.py:44
  47.9 32.3 %collective-permute-start.14 = (bf16[16,64,256]{2,1,0:T(8,128)(2,1)S(1)}, bf16[16,64,256]{2,1,0:T(8,128)(2,1)S(1)}, u32[]{:S(2)}, u32[]{:S(2)}) collective-permute-start(bf16[16,64,256]{2,1,0:T(8,128)(2,1)S(1)} %bitcast.7), channel_id=1, source_target_pairs={{0,4},{1,5},{2,6},{3,7},{4,0},{5,1},{6,2},{7,3},{8,12},{9,13},{10,... | collective-permute-start | bytes 1572872 | tf_op jit(solution)/shard_map/ppermute | solution.py:54
  50.4 29.8 %collective-permute-start.13 = (bf16[16,64,256]{2,1,0:T(8,128)(2,1)S(1)}, bf16[16,64,256]{2,1,0:T(8,128)(2,1)S(1)}, u32[]{:S(2)}, u32[]{:S(2)}) collective-permute-start(bf16[16,64,256]{2,1,0:T(8,128)(2,1)S(1)} %bitcast.8), channel_id=1, source_target_pairs={{0,6},{1,7},{2,0},{3,1},{4,2},{5,3},{6,4},{7,5},{8,14},{9,15},{10,... | collective-permute-start | bytes 1572872 | tf_op jit(solution)/shard_map/ppermute | solution.py:54
  51.3 28.9 %collective-permute-start.12 = (bf16[16,64,256]{2,1,0:T(8,128)(2,1)S(1)}, bf16[16,64,256]{2,1,0:T(8,128)(2,1)S(1)}, u32[]{:S(2)}, u32[]{:S(2)}) collective-permute-start(bf16[16,64,256]{2,1,0:T(8,128)(2,1)S(1)} %bitcast.9), channel_id=1, source_target_pairs={{0,2},{1,3},{2,4},{3,5},{4,6},{5,7},{6,0},{7,1},{8,10},{9,11},{10,... | collective-permute-start | bytes 1572872 | tf_op jit(solution)/shard_map/ppermute | solution.py:54
  52.1 29.2 %collective-permute-start.15 = (bf16[16,64,256]{2,1,0:T(8,128)(2,1)S(1)}, bf16[16,64,256]{2,1,0:T(8,128)(2,1)S(1)}, u32[]{:S(2)}, u32[]{:S(2)}) collective-permute-start(bf16[16,64,256]{2,1,0:T(8,128)(2,1)S(1)} %bitcast.10), channel_id=1, source_target_pairs={{0,1},{1,0},{2,3},{3,2},{4,5},{5,4},{6,7},{7,6},{8,9},{9,8},{10,11... | collective-permute-start | bytes 1572872 | tf_op jit(solution)/shard_map/ppermute | solution.py:60
  80.2 3.7 %copy-start.3 = (bf16[896,896]{1,0:T(8,128)(2,1)S(1)}, bf16[896,896]{1,0:T(8,128)(2,1)}, u32[]{:S(2)}) copy-start(bf16[896,896]{1,0:T(8,128)(2,1)} %refs_13_.3) | copy-start | bytes 4816900
  80.3 2.0 %collective-permute-start.16 = (bf16[16,64,256]{2,1,0:T(8,128)(2,1)S(1)}, bf16[16,64,256]{2,1,0:T(8,128)(2,1)S(1)}, u32[]{:S(2)}, u32[]{:S(2)}) collective-permute-start(bf16[16,64,256]{2,1,0:T(8,128)(2,1)S(1)} %get-tuple-element.24.refs_5_), channel_id=1, source_target_pairs={{0,1},{1,0},{2,3},{3,2},{4,5},{5,4},{6,7},{7,6},{8,9},{9,8},{10,11... | collective-permute-start | bytes 1572872 | tf_op jit(solution)/shard_map/ppermute | solution.py:60
  80.7 2.4 %collective-permute-start.17 = (bf16[16,64,256]{2,1,0:T(8,128)(2,1)S(1)}, bf16[16,64,256]{2,1,0:T(8,128)(2,1)S(1)}, u32[]{:S(2)}, u32[]{:S(2)}) collective-permute-start(bf16[16,64,256]{2,1,0:T(8,128)(2,1)S(1)} %get-tuple-element.25.refs_6_), channel_id=1, source_target_pairs={{0,1},{1,0},{2,3},{3,2},{4,5},{5,4},{6,7},{7,6},{8,9},{9,8},{10,11... | collective-permute-start | bytes 1572872 | tf_op jit(solution)/shard_map/ppermute | solution.py:60
  80.9 2.9 %collective-permute-start.18 = (bf16[16,64,256]{2,1,0:T(8,128)(2,1)S(1)}, bf16[16,64,256]{2,1,0:T(8,128)(2,1)S(1)}, u32[]{:S(2)}, u32[]{:S(2)}) collective-permute-start(bf16[16,64,256]{2,1,0:T(8,128)(2,1)S(1)} %get-tuple-element.26.refs_7_), channel_id=1, source_target_pairs={{0,1},{1,0},{2,3},{3,2},{4,5},{5,4},{6,7},{7,6},{8,9},{9,8},{10,11... | collective-permute-start | bytes 1572872 | tf_op jit(solution)/shard_map/ppermute | solution.py:60
  81.3 2.6 %copy-start.6 = (bf16[16,64,256]{2,1,0:T(8,128)(2,1)}, bf16[16,64,256]{2,1,0:T(8,128)(2,1)S(1)}, u32[]{:S(2)}) copy-start(bf16[16,64,256]{2,1,0:T(8,128)(2,1)S(1)} %collective-permute-done.15.refs_8_) | copy-start | bytes 1572868
  91.1 8.1 %copy-start.2 = (bf16[512,4096]{1,0:T(8,128)(2,1)S(1)}, bf16[512,4096]{1,0:T(8,128)(2,1)}, u32[]{:S(2)}) copy-start(bf16[512,4096]{1,0:T(8,128)(2,1)} %refs_6_.3) | copy-start | bytes 12582916
  91.2 8.1 %copy-start.4 = (bf16[896,512]{1,0:T(8,128)(2,1)S(1)}, bf16[896,512]{1,0:T(8,128)(2,1)}, u32[]{:S(2)}) copy-start(bf16[896,512]{1,0:T(8,128)(2,1)} %refs_4_.7) | copy-start | bytes 2752516
  91.2 8.1 %copy-start.5 = (bf16[896,512]{1,0:T(8,128)(2,1)S(1)}, bf16[896,512]{1,0:T(8,128)(2,1)}, u32[]{:S(2)}) copy-start(bf16[896,512]{1,0:T(8,128)(2,1)} %refs_5_.5) | copy-start | bytes 2752516
  91.2 8.1 %collective-permute-start.22 = (bf16[8,128,896]{2,1,0:T(8,128)(2,1)S(1)}, bf16[8,128,896]{2,1,0:T(8,128)(2,1)S(1)}, u32[]{:S(2)}, u32[]{:S(2)}) collective-permute-start(bf16[8,128,896]{2,1,0:T(8,128)(2,1)S(1)} %encode.2.refs_14_.refs_0_), channel_id=1, source_target_pairs={{0,1},{1,0},{2,3},{3,2},{4,5},{5,4},{6,7},{7,6},{8,9},{9,8},{10,11... | collective-permute-start | bytes 5505032 | tf_op jit(solution)/shard_map/ppermute | solution.py:60
  109.8 8.4 %collective-permute-start.19 = (bf16[8,128,896]{2,1,0:T(8,128)(2,1)S(1)}, bf16[8,128,896]{2,1,0:T(8,128)(2,1)S(1)}, u32[]{:S(2)}, u32[]{:S(2)}) collective-permute-start(bf16[8,128,896]{2,1,0:T(8,128)(2,1)S(1)} %encode.3.refs_6_.refs_1_), channel_id=1, source_target_pairs={{0,1},{1,0},{2,3},{3,2},{4,5},{5,4},{6,7},{7,6},{8,9},{9,8},{10,11... | collective-permute-start | bytes 5505032 | tf_op jit(solution)/shard_map/ppermute | solution.py:60
  110.1 15.1 %collective-permute-start.21 = (bf16[1,128,896]{2,1,0:T(8,128)(2,1)S(1)}, bf16[1,128,896]{2,1,0:T(8,128)(2,1)S(1)}, u32[]{:S(2)}, u32[]{:S(2)}) collective-permute-start(bf16[1,128,896]{2,1,0:T(8,128)(2,1)S(1)} %slice.19), channel_id=1, source_target_pairs={{0,9},{1,8},{2,11},{3,10},{4,13},{5,12},{6,15},{7,14},{8,17},{9,16... | collective-permute-start | bytes 688136 | tf_op jit(solution)/shard_map/ppermute | solution.py:518
  114.3 12.2 %collective-permute-start.20 = (bf16[1,128,896]{2,1,0:T(8,128)(2,1)S(1)}, bf16[1,128,896]{2,1,0:T(8,128)(2,1)S(1)}, u32[]{:S(2)}, u32[]{:S(2)}) collective-permute-start(bf16[1,128,896]{2,1,0:T(8,128)(2,1)S(1)} %slice.19), channel_id=1, source_target_pairs={{0,8},{1,9},{2,10},{3,11},{4,12},{5,13},{6,14},{7,15},{8,16},{9,17... | collective-permute-start | bytes 688136 | tf_op jit(solution)/shard_map/ppermute | solution.py:518
  124.6 9.2 %collective-permute-start.24 = (bf16[4,256,512]{2,1,0:T(8,128)(2,1)S(1)}, bf16[4,256,512]{2,1,0:T(8,128)(2,1)S(1)}, u32[]{:S(2)}, u32[]{:S(2)}) collective-permute-start(bf16[4,256,512]{2,1,0:T(8,128)(2,1)S(1)} %get-tuple-element.30), channel_id=1, source_target_pairs={{0,1},{1,0},{2,3},{3,2},{4,5},{5,4},{6,7},{7,6},{8,9},{9,8},{10,11... | collective-permute-start | bytes 3145736 | tf_op jit(solution)/shard_map/ppermute | solution.py:60
  132.9 3.1 %collective-permute-start.23 = (bf16[4,256,512]{2,1,0:T(8,128)(2,1)S(1)}, bf16[4,256,512]{2,1,0:T(8,128)(2,1)S(1)}, u32[]{:S(2)}, u32[]{:S(2)}) collective-permute-start(bf16[4,256,512]{2,1,0:T(8,128)(2,1)S(1)} %get-tuple-element.29), channel_id=1, source_target_pairs={{0,1},{1,0},{2,3},{3,2},{4,5},{5,4},{6,7},{7,6},{8,9},{9,8},{10,11... | collective-permute-start | bytes 3145736 | tf_op jit(solution)/shard_map/ppermute | solution.py:60
  136.3 10.8 %collective-permute-start.25 = (bf16[256,512]{1,0:T(8,128)(2,1)S(1)}, bf16[256,512]{1,0:T(8,128)(2,1)S(1)}, u32[]{:S(2)}, u32[]{:S(2)}) collective-permute-start(bf16[256,512]{1,0:T(8,128)(2,1)S(1)} %get-tuple-element.35), channel_id=1, source_target_pairs={{0,6},{1,7},{2,0},{3,1},{4,2},{5,3},{6,4},{7,5},{8,14},{9,15},{10,... | collective-permute-start | bytes 786440 | tf_op jit(solution)/shard_map/ppermute | solution.py:91
  136.8 11.8 %collective-permute-start.26 = (bf16[256,512]{1,0:T(8,128)(2,1)S(1)}, bf16[256,512]{1,0:T(8,128)(2,1)S(1)}, u32[]{:S(2)}, u32[]{:S(2)}) collective-permute-start(bf16[256,512]{1,0:T(8,128)(2,1)S(1)} %get-tuple-element.36), channel_id=1, source_target_pairs={{0,2},{1,3},{2,4},{3,5},{4,6},{5,7},{6,0},{7,1},{8,10},{9,11},{10,... | collective-permute-start | bytes 786440 | tf_op jit(solution)/shard_map/ppermute | solution.py:91
  137.9 18.7 %collective-permute-start.27 = (bf16[256,512]{1,0:T(8,128)(2,1)S(1)}, bf16[256,512]{1,0:T(8,128)(2,1)S(1)}, u32[]{:S(2)}, u32[]{:S(2)}) collective-permute-start(bf16[256,512]{1,0:T(8,128)(2,1)S(1)} %get-tuple-element.37), channel_id=1, source_target_pairs={{0,4},{1,5},{2,6},{3,7},{4,0},{5,1},{6,2},{7,3},{8,12},{9,13},{10,... | collective-permute-start | bytes 786440 | tf_op jit(solution)/shard_map/ppermute | solution.py:91
  139.6 21.3 %collective-permute-start.28 = (bf16[256,512]{1,0:T(8,128)(2,1)S(1)}, bf16[256,512]{1,0:T(8,128)(2,1)S(1)}, u32[]{:S(2)}, u32[]{:S(2)}) collective-permute-start(bf16[256,512]{1,0:T(8,128)(2,1)S(1)} %get-tuple-element.31.refs_0_), channel_id=1, source_target_pairs={{0,6},{1,7},{2,0},{3,1},{4,2},{5,3},{6,4},{7,5},{8,14},{9,15},{10,... | collective-permute-start | bytes 786440 | tf_op jit(solution)/shard_map/ppermute | solution.py:91
  141.6 21.3 %collective-permute-start.29 = (bf16[256,512]{1,0:T(8,128)(2,1)S(1)}, bf16[256,512]{1,0:T(8,128)(2,1)S(1)}, u32[]{:S(2)}, u32[]{:S(2)}) collective-permute-start(bf16[256,512]{1,0:T(8,128)(2,1)S(1)} %get-tuple-element.32.refs_1_), channel_id=1, source_target_pairs={{0,2},{1,3},{2,4},{3,5},{4,6},{5,7},{6,0},{7,1},{8,10},{9,11},{10,... | collective-permute-start | bytes 786440 | tf_op jit(solution)/shard_map/ppermute | solution.py:91
  147.1 20.7 %collective-permute-start.30 = (bf16[256,512]{1,0:T(8,128)(2,1)S(1)}, bf16[256,512]{1,0:T(8,128)(2,1)S(1)}, u32[]{:S(2)}, u32[]{:S(2)}) collective-permute-start(bf16[256,512]{1,0:T(8,128)(2,1)S(1)} %get-tuple-element.33.refs_2_), channel_id=1, source_target_pairs={{0,4},{1,5},{2,6},{3,7},{4,0},{5,1},{6,2},{7,3},{8,12},{9,13},{10,... | collective-permute-start | bytes 786440 | tf_op jit(solution)/shard_map/ppermute | solution.py:91
  156.6 13.5 %copy-start.1 = (bf16[8,128,896]{2,1,0:T(8,128)(2,1)S(1)}, bf16[8,128,896]{2,1,0:T(8,128)(2,1)}, u32[]{:S(2)}) copy-start(bf16[8,128,896]{2,1,0:T(8,128)(2,1)} %param.13) | copy-start | bytes 5505028
Sparse Core Ops, SparseCore 0:
  11.1 60.9 all-gather.2
  109.9 47.1 reduce-scatter.1

commit v11 on v10

--- a/solution.py
+++ b/solution.py
@@ -184,12 +184,12 @@
 def enc_query_kernel(pos_ref, *refs):
     del pos_ref
     sources, w_ref, out_ref = refs[:4], refs[4], refs[-1]
-    rows = []
+    scales = []
     for source in sources:
         block = source[0].astype(F32)
-        scale = lax.rsqrt(jnp.mean(block * block, axis=-1, keepdims=True) + EPSILON)
-        rows.append((block * scale).astype(BF16))
-    got = dot(jnp.concatenate(rows, axis=0), w_ref[...]).astype(BF16)
+        scales.append(lax.rsqrt(jnp.mean(block * block, axis=-1, keepdims=True) + EPSILON))
+    got = dot(jnp.concatenate([source[0] for source in sources], axis=0), w_ref[...])
+    got = (got * jnp.concatenate(scales, axis=0)).astype(BF16)
     for n in range(4):
         out_ref[n] = got[n * NLEN : (n + 1) * NLEN]
 

time: 179 us -> 179 us (level)
  transfers between devices with their start and end apart: 33 -> 33, of which waited for: 16 -> 15; matrix products, arithmetic and copies ran while one was open for 7% -> 7% of each run, Pallas kernels for 20% -> 20%
where the time goes in v11:
time: 179 us; the launch traced here: 177 us
  Pallas kernels  52.9 us (30%)
  waiting for transfers between devices  47.5 us (27%)
  starting transfers between devices  44.7 us (25%)
  between operations  13.7 us (8%)
  matrix products  10.2 us (6%)
  local copies, waits for them, and re-layouts  4.24 us (2%)
  other arithmetic  3.79 us (2%)
    ppermute x6, waiting for transfers between devices, send_over_x(): got.append(lax.ppermute(sums[j], 'store', route))  24.9 us
    pallas_call x3, Pallas kernels, decode(): pl.pallas_call(lambda *refs: decode_kernel(len(carried) > 0, split, *refs...  23.4 us
    pallas_call x2, Pallas kernels, encode(): pl.pallas_call(encode_kernel, out_shape=jax.ShapeDtypeStruct((count, NLEN...  15.1 us
    ppermute x12, starting transfers between devices, around(): got.append(lax.ppermute(block, 'seq', route))  15.1 us
    all_gather x1, waiting for transfers between devices, body(): gathered = lax.all_gather(sources, 'store', axis=0, tiled=True)  12.3 us
    ppermute x8, starting transfers between devices, swap_cores(): return lax.ppermute(block, 'store', [(i, i ^ 1) for i in range(count)])  10.6 us
    dot_general x1, matrix products, dot(): return jnp.dot(a, b, preferred_element_type=F32)  10.2 us
    ppermute x2, starting transfers between devices, body(): lax.ppermute(low[:1], ('seq', 'store'), [(i * store_count + k, (i + 1) *...  8 us
  transfers between devices with their start and end apart: 33, of which 15 were waited for; matrix products, arithmetic and copies ran while one was open for 7% of the time, Pallas kernels for 20%

profile of v11, /device:TPU:9, one launch (start us, length us, event | category | flops | bytes accessed | tf_op | source)
XLA Modules:
  0.0 177.0 jit_solution(12900950239920646351)
XLA Ops:
  6.5 0.9 copy.16
  7.9 0.7 broadcast_add_fusion
  8.6 0.6 gather_fusion
  9.3 1.7 gather_fusion.1
  11.0 0.9 constant_dynamic-slice_fusion
  12.0 2.1 %collective-permute-start.5 = (bf16[128,256]{1,0:T(8,128)(2,1)S(1)}, bf16[128,256]{1,0:T(8,128)(2,1)S(1)}, u32[]{:S(2)}, u32[]{:S(2)}) collective-permute-start(bf16[128,256]{1,0:T(8,128)(2,1)S(1)} %get-tuple-element.41.refs_4_), channel_id=1, source_target_pairs={{0,64},{8,72},{16,80},{24,88},{32,96},{40,104},{48,112},{56,120},{... | collective-permute-start | bytes 196616 | tf_op jit(solution)/shard_map/ppermute | solution.py:44
  14.1 1.1 collective-permute-start.4
  15.5 3.6 %collective-permute-start.2 = (bf16[128,256]{1,0:T(8,128)(2,1)S(1)}, bf16[128,256]{1,0:T(8,128)(2,1)S(1)}, u32[]{:S(2)}, u32[]{:S(2)}) collective-permute-start(bf16[128,256]{1,0:T(8,128)(2,1)S(1)} %get-tuple-element.42.refs_0_), channel_id=1, source_target_pairs={{0,16},{8,24},{16,0},{24,8},{32,48},{40,56},{48,32},{56,40},{64,80... | collective-permute-start | bytes 196616 | tf_op jit(solution)/shard_map/ppermute | solution.py:44
  19.6 1.0 collective-permute-start
  20.8 1.8 collective-permute-done.1.refs_2_
  22.5 1.4 collective-permute-done.refs_1_
  23.9 2.2 %collective-permute-start.8 = (bf16[4,128,256]{2,1,0:T(8,128)(2,1)S(1)}, bf16[4,128,256]{2,1,0:T(8,128)(2,1)S(1)}, u32[]{:S(2)}, u32[]{:S(2)}) collective-permute-start(bf16[4,128,256]{2,1,0:T(8,128)(2,1)S(1)} %get-tuple-element.22.refs_0_), channel_id=1, source_target_pairs={{0,64},{8,72},{16,80},{24,88},{32,96},{40,104},{48,112},{56,120},{... | collective-permute-start | bytes 786440 | tf_op jit(solution)/shard_map/ppermute | solution.py:44
  26.2 1.5 collective-permute-start.6
  27.6 1.2 collective-permute-start.11
  28.8 1.4 collective-permute-start.10
  30.2 1.0 collective-permute-done.8.refs_3_
  31.3 10.2 %convolution_convert_fusion.refs_8_.refs_2_.refs_3_ = bf16[1024,512]{1,0:T(8,128)(2,1)} fusion(bf16[1024,4096]{1,0:T(8,128)(2,1)} %hidden_ref.1, bf16[4096,512]{1,0:T(8,128)(2,1)} %param.15), kind=kOutput, calls=%fused_computation.2 | convolution fusion | flops 4295491584 | bytes 13631488 | tf_op jit(solution)/shard_map/dot_general | solution.py:29
  41.6 6.3 %cond_rows.1 = bf16[1024,256]{1,0:T(8,128)(2,1)S(1)} custom-call(s32[8]{0:T(128)S(1)} %pad_add_fusion.1.src_ref, bf16[1024,4096]{1,0:T(8,128)(2,1)} %hidden_ref.1, bf16[4,128,256]{2,1,0:T(8,128)(2,1)S(1)} %get-tuple-element.22.refs_0_, bf16[4,128,256]{2,1,0:T(8,128)(2,1)S(1)} %collective-permute-done.6.refs_1_, ...), custom_call_target="tpu_custom_call" | custom-call | flops 2147483648 | bytes 12582912 | tf_op jit(solution)/shard_map/cond_rows/pallas_call | solution.py:122
  47.9 2.5 %collective-permute-start.14 = (bf16[16,64,256]{2,1,0:T(8,128)(2,1)S(1)}, bf16[16,64,256]{2,1,0:T(8,128)(2,1)S(1)}, u32[]{:S(2)}, u32[]{:S(2)}) collective-permute-start(bf16[16,64,256]{2,1,0:T(8,128)(2,1)S(1)} %bitcast.7), channel_id=1, source_target_pairs={{0,4},{1,5},{2,6},{3,7},{4,0},{5,1},{6,2},{7,3},{8,12},{9,13},{10,... | collective-permute-start | bytes 1572872 | tf_op jit(solution)/shard_map/ppermute | solution.py:54
  50.4 0.9 collective-permute-start.13
  51.3 0.6 collective-permute-start.12
  52.1 7.7 %collective-permute-start.15 = (bf16[16,64,256]{2,1,0:T(8,128)(2,1)S(1)}, bf16[16,64,256]{2,1,0:T(8,128)(2,1)S(1)}, u32[]{:S(2)}, u32[]{:S(2)}) collective-permute-start(bf16[16,64,256]{2,1,0:T(8,128)(2,1)S(1)} %bitcast.10), channel_id=1, source_target_pairs={{0,1},{1,0},{2,3},{3,2},{4,5},{5,4},{6,7},{7,6},{8,9},{9,8},{10,11... | collective-permute-start | bytes 1572872 | tf_op jit(solution)/shard_map/ppermute | solution.py:60
  59.8 12.3 %all-gather.3.cloned.1.call-done.refs_0_.refs_1_.refs_2_.refs_3_ = bf16[32,128,896]{2,1,0:T(8,128)(2,1)} async-done(((bf16[4,128,896]{2,1,0:T(8,128)(2,1)}), bf16[32,128,896]{2,1,0:T(8,128)(2,1)}) %all-gather.3.cloned.1.call-update) | async-done | bytes 7340048 | tf_op jit(solution)/shard_map/all_gather | solution.py:475
  72.1 7.6 %enc_queries.1.refs_3_.refs_12_ = bf16[16,128,896]{2,1,0:T(8,128)(2,1)S(1)} custom-call(s32[16]{0:T(128)S(1)} %select_reduce_fusion.1.pos_ref, bf16[32,128,896]{2,1,0:T(8,128)(2,1)} %all-gather.3.cloned.1.call-done.refs_0_.refs_1_.refs_2_.refs_3_, bf16[32,128,896]{2,1,0:T(8,128)(2,1)} %all-gather.3.cloned.1.call-done.refs_0_.refs_1_.refs_2_.refs_3_, ...), custom_call_target="tpu_custom_call" | custom-call | flops 3288334336 | bytes 10485760 | tf_op jit(solution)/shard_map/enc_queries/pallas_call | solution.py:203
  80.8 1.0 collective-permute-done.16.refs_9_
  81.8 0.7 collective-permute-done.17.refs_10_
  82.6 0.7 collective-permute-done.18.refs_11_
  83.3 7.3 %encode.2.refs_14_.refs_0_ = bf16[8,128,896]{2,1,0:T(8,128)(2,1)S(1)} custom-call(s32[16]{0:T(128)S(1)} %select_reduce_fusion.1.pos_ref, s32[8]{0:T(128)S(1)} %pad_add_fusion.pair_ref.refs_0_, bf16[32,128,896]{2,1,0:T(8,128)(2,1)} %all-gather.3.cloned.1.call-done.refs_0_.refs_1_.refs_2_.refs_3_, ...), custom_call_target="tpu_custom_call" | custom-call | flops 2466250752 | bytes 8388608 | tf_op jit(solution)/shard_map/encode/pallas_call | solution.py:277
  91.1 7.8 %encode.3.refs_6_.refs_1_ = bf16[8,128,896]{2,1,0:T(8,128)(2,1)S(1)} custom-call(s32[16]{0:T(128)S(1)} %select_reduce_fusion.1.pos_ref, s32[8]{0:T(128)S(1)} %pad_add_fusion.pair_ref.refs_0_, bf16[32,128,896]{2,1,0:T(8,128)(2,1)} %all-gather.3.cloned.1.call-done.refs_0_.refs_1_.refs_2_.refs_3_, ...), custom_call_target="tpu_custom_call" | custom-call | flops 2466250752 | bytes 8388608 | tf_op jit(solution)/shard_map/encode/pallas_call | solution.py:277
  98.9 10.4 %decode.3.refs_7_ = bf16[512,4096]{1,0:T(8,128)(2,1)} custom-call(bf16[8,128,896]{2,1,0:T(8,128)(2,1)S(1)} %encode.2.refs_14_.refs_0_, bf16[8,128,896]{2,1,0:T(8,128)(2,1)S(1)} %collective-permute-done.22.refs_1_, bf16[1024,512]{1,0:T(8,128)(2,1)} %convolution_convert_fusion.refs_8_.refs_2_.refs_3_, bf16[896,512]{1,0:T(8,128)(2,1)S(1)} %copy-done.4, ...), custom_call_target="tpu_custom_call" | custom-call | flops 5905580032 | bytes 6291456 | tf_op jit(solution)/shard_map/decode/pallas_call | solution.py:406
  109.6 4.2 %collective-permute-start.21 = (bf16[1,128,896]{2,1,0:T(8,128)(2,1)S(1)}, bf16[1,128,896]{2,1,0:T(8,128)(2,1)S(1)}, u32[]{:S(2)}, u32[]{:S(2)}) collective-permute-start(bf16[1,128,896]{2,1,0:T(8,128)(2,1)S(1)} %slice.19), channel_id=1, source_target_pairs={{0,9},{1,8},{2,11},{3,10},{4,13},{5,12},{6,15},{7,14},{8,17},{9,16... | collective-permute-start | bytes 688136 | tf_op jit(solution)/shard_map/ppermute | solution.py:518
  113.8 3.8 %collective-permute-start.20 = (bf16[1,128,896]{2,1,0:T(8,128)(2,1)S(1)}, bf16[1,128,896]{2,1,0:T(8,128)(2,1)S(1)}, u32[]{:S(2)}, u32[]{:S(2)}) collective-permute-start(bf16[1,128,896]{2,1,0:T(8,128)(2,1)S(1)} %slice.19), channel_id=1, source_target_pairs={{0,8},{1,9},{2,10},{3,11},{4,12},{5,13},{6,14},{7,15},{8,16},{9,17... | collective-permute-start | bytes 688136 | tf_op jit(solution)/shard_map/ppermute | solution.py:518
  117.6 6.5 %decode.4 = (bf16[4,256,512]{2,1,0:T(8,128)(2,1)S(1)}, bf16[4,256,512]{2,1,0:T(8,128)(2,1)S(1)}) custom-call(s32[8]{0:T(128)S(1)} %pad_add_fusion.pair_ref.refs_0_, bf16[8,128,896]{2,1,0:T(8,128)(2,1)S(1)} %encode.3.refs_6_.refs_1_, bf16[8,128,896]{2,1,0:T(8,128)(2,1)S(1)} %collective-permute-done.19.refs_2_, ...), custom_call_target="tpu_custom_call" | custom-call | flops 2952790016 | bytes 6291456 | tf_op jit(solution)/shard_map/decode/pallas_call | solution.py:406
  124.1 0.6 collective-permute-start.24
  124.7 1.4 collective-permute-done.20.refs_7_
  126.2 6.5 %decode.5 = (bf16[4,256,512]{2,1,0:T(8,128)(2,1)S(1)}, bf16[4,256,512]{2,1,0:T(8,128)(2,1)S(1)}) custom-call(s32[8]{0:T(128)S(1)} %pad_add_fusion.pair_ref.refs_0_, bf16[8,128,896]{2,1,0:T(8,128)(2,1)S(1)} %encode.3.refs_6_.refs_1_, bf16[8,128,896]{2,1,0:T(8,128)(2,1)S(1)} %collective-permute-done.19.refs_2_, ...), custom_call_target="tpu_custom_call" | custom-call | flops 2952790016 | bytes 6291456 | tf_op jit(solution)/shard_map/decode/pallas_call | solution.py:406
  132.6 0.8 collective-permute-start.23
  133.6 2.0 %collective-permute-done.23.taken_ref = bf16[4,256,512]{2,1,0:T(8,128)(2,1)S(1)} collective-permute-done((bf16[4,256,512]{2,1,0:T(8,128)(2,1)S(1)}, bf16[4,256,512]{2,1,0:T(8,128)(2,1)S(1)}, u32[]{:S(2)}, u32[]{:S(2)}) %collective-permute-start.23) | collective-permute-done | bytes 1048608 | tf_op jit(solution)/shard_map/ppermute | solution.py:60
  135.9 1.0 collective-permute-start.25
  136.9 0.6 collective-permute-start.26
  137.4 1.7 collective-permute-start.27
  139.2 2.0 %collective-permute-start.28 = (bf16[256,512]{1,0:T(8,128)(2,1)S(1)}, bf16[256,512]{1,0:T(8,128)(2,1)S(1)}, u32[]{:S(2)}, u32[]{:S(2)}) collective-permute-start(bf16[256,512]{1,0:T(8,128)(2,1)S(1)} %get-tuple-element.31.refs_0_), channel_id=1, source_target_pairs={{0,6},{1,7},{2,0},{3,1},{4,2},{5,3},{6,4},{7,5},{8,14},{9,15},{10,... | collective-permute-start | bytes 786440 | tf_op jit(solution)/shard_map/ppermute | solution.py:91
  141.2 5.6 %collective-permute-done.25 = bf16[256,512]{1,0:T(8,128)(2,1)S(1)} collective-permute-done((bf16[256,512]{1,0:T(8,128)(2,1)S(1)}, bf16[256,512]{1,0:T(8,128)(2,1)S(1)}, u32[]{:S(2)}, u32[]{:S(2)}) %collective-permute-start.25) | collective-permute-done | bytes 262176 | tf_op jit(solution)/shard_map/ppermute | solution.py:91
  146.7 1.7 collective-permute-start.30
  148.8 7.0 %collective-permute-done.27 = bf16[256,512]{1,0:T(8,128)(2,1)S(1)} collective-permute-done((bf16[256,512]{1,0:T(8,128)(2,1)S(1)}, bf16[256,512]{1,0:T(8,128)(2,1)S(1)}, u32[]{:S(2)}, u32[]{:S(2)}) %collective-permute-start.27) | collective-permute-done | bytes 262176 | tf_op jit(solution)/shard_map/ppermute | solution.py:91
  156.0 4.4 %collective-permute-done.28 = bf16[256,512]{1,0:T(8,128)(2,1)S(1)} collective-permute-done((bf16[256,512]{1,0:T(8,128)(2,1)S(1)}, bf16[256,512]{1,0:T(8,128)(2,1)S(1)}, u32[]{:S(2)}, u32[]{:S(2)}) %collective-permute-start.28) | collective-permute-done | bytes 262176 | tf_op jit(solution)/shard_map/ppermute | solution.py:91
  160.4 7.6 %collective-permute-done.29 = bf16[256,512]{1,0:T(8,128)(2,1)S(1)} collective-permute-done((bf16[256,512]{1,0:T(8,128)(2,1)S(1)}, bf16[256,512]{1,0:T(8,128)(2,1)S(1)}, u32[]{:S(2)}, u32[]{:S(2)}) %collective-permute-start.29) | collective-permute-done | bytes 262176 | tf_op jit(solution)/shard_map/ppermute | solution.py:91
  168.1 2.1 %pad_maximum_fusion = bf16[1024,512]{1,0:T(8,128)(2,1)} fusion(bf16[512,512]{1,0:T(8,128)(2,1)} %reduce-scatter.2.cloned.1.call-done, bf16[256,512]{1,0:T(8,128)(2,1)S(1)} %add_convert_fusion, bf16[256,512]{1,0:T(8,128)(2,1)S(1)} %add_convert_fusion.1), kind=kLoop, calls=%fused_computation.3 | loop fusion | flops 3145728 | bytes 2097152 | tf_op jit(solution)/shard_map/concatenate | solution.py:551
  (68 shorter events, 4.9 us)
Async XLA Ops:
  6.5 2.7 %copy-start = (bf16[8,128,896]{2,1,0:T(8,128)(2,1)S(1)}, bf16[8,128,896]{2,1,0:T(8,128)(2,1)}, u32[]{:S(2)}) copy-start(bf16[8,128,896]{2,1,0:T(8,128)(2,1)} %param.13) | copy-start | bytes 5505028
  6.5 65.5 %all-gather.3.cloned.1.call-start = ((), (), s32[]{:S(2)}) async-start(), calls=%async_computation.2 | async-start | bytes 8257536 | tf_op jit(solution)/shard_map/all_gather | solution.py:475
  11.0 157.1 %reduce-scatter.2.cloned.1.call-start = ((), (), s32[]{:S(2)}) async-start(), calls=%async_computation.1 | async-start | bytes 4718592 | tf_op jit(solution)/shard_map/reduce_scatter | solution.py:536
  12.0 7.6 %collective-permute-start.5 = (bf16[128,256]{1,0:T(8,128)(2,1)S(1)}, bf16[128,256]{1,0:T(8,128)(2,1)S(1)}, u32[]{:S(2)}, u32[]{:S(2)}) collective-permute-start(bf16[128,256]{1,0:T(8,128)(2,1)S(1)} %get-tuple-element.41.refs_4_), channel_id=1, source_target_pairs={{0,64},{8,72},{16,80},{24,88},{32,96},{40,104},{48,112},{56,120},{... | collective-permute-start | bytes 196616 | tf_op jit(solution)/shard_map/ppermute | solution.py:44
  14.1 6.5 %collective-permute-start.4 = (bf16[128,256]{1,0:T(8,128)(2,1)S(1)}, bf16[128,256]{1,0:T(8,128)(2,1)S(1)}, u32[]{:S(2)}, u32[]{:S(2)}) collective-permute-start(bf16[128,256]{1,0:T(8,128)(2,1)S(1)} %get-tuple-element.41.refs_4_), channel_id=1, source_target_pairs={{0,96},{8,104},{16,112},{24,120},{32,0},{40,8},{48,16},{56,24},{64... | collective-permute-start | bytes 196616 | tf_op jit(solution)/shard_map/ppermute | solution.py:44
  15.1 5.5 %collective-permute-start.3 = (bf16[128,256]{1,0:T(8,128)(2,1)S(1)}, bf16[128,256]{1,0:T(8,128)(2,1)S(1)}, u32[]{:S(2)}, u32[]{:S(2)}) collective-permute-start(bf16[128,256]{1,0:T(8,128)(2,1)S(1)} %get-tuple-element.41.refs_4_), channel_id=1, source_target_pairs={{0,32},{8,40},{16,48},{24,56},{32,64},{40,72},{48,80},{56,88},{64,... | collective-permute-start | bytes 196616 | tf_op jit(solution)/shard_map/ppermute | solution.py:44
  15.5 5.2 %collective-permute-start.2 = (bf16[128,256]{1,0:T(8,128)(2,1)S(1)}, bf16[128,256]{1,0:T(8,128)(2,1)S(1)}, u32[]{:S(2)}, u32[]{:S(2)}) collective-permute-start(bf16[128,256]{1,0:T(8,128)(2,1)S(1)} %get-tuple-element.42.refs_0_), channel_id=1, source_target_pairs={{0,16},{8,24},{16,0},{24,8},{32,48},{40,56},{48,32},{56,40},{64,80... | collective-permute-start | bytes 196616 | tf_op jit(solution)/shard_map/ppermute | solution.py:44
  19.1 3.4 %collective-permute-start.1 = (bf16[128,256]{1,0:T(8,128)(2,1)S(1)}, bf16[128,256]{1,0:T(8,128)(2,1)S(1)}, u32[]{:S(2)}, u32[]{:S(2)}) collective-permute-start(bf16[128,256]{1,0:T(8,128)(2,1)S(1)} %get-tuple-element.42.refs_0_), channel_id=1, source_target_pairs={{0,24},{8,0},{16,8},{24,16},{32,56},{40,32},{48,40},{56,48},{64,88... | collective-permute-start | bytes 196616 | tf_op jit(solution)/shard_map/ppermute | solution.py:44
  19.6 4.3 %collective-permute-start = (bf16[128,256]{1,0:T(8,128)(2,1)S(1)}, bf16[128,256]{1,0:T(8,128)(2,1)S(1)}, u32[]{:S(2)}, u32[]{:S(2)}) collective-permute-start(bf16[128,256]{1,0:T(8,128)(2,1)S(1)} %get-tuple-element.42.refs_0_), channel_id=1, source_target_pairs={{0,8},{8,16},{16,24},{24,0},{32,40},{40,48},{48,56},{56,32},{64,72... | collective-permute-start | bytes 196616 | tf_op jit(solution)/shard_map/ppermute | solution.py:44
  23.9 7.2 %collective-permute-start.8 = (bf16[4,128,256]{2,1,0:T(8,128)(2,1)S(1)}, bf16[4,128,256]{2,1,0:T(8,128)(2,1)S(1)}, u32[]{:S(2)}, u32[]{:S(2)}) collective-permute-start(bf16[4,128,256]{2,1,0:T(8,128)(2,1)S(1)} %get-tuple-element.22.refs_0_), channel_id=1, source_target_pairs={{0,64},{8,72},{16,80},{24,88},{32,96},{40,104},{48,112},{56,120},{... | collective-permute-start | bytes 786440 | tf_op jit(solution)/shard_map/ppermute | solution.py:44
  26.2 15.4 %collective-permute-start.7 = (bf16[4,128,256]{2,1,0:T(8,128)(2,1)S(1)}, bf16[4,128,256]{2,1,0:T(8,128)(2,1)S(1)}, u32[]{:S(2)}, u32[]{:S(2)}) collective-permute-start(bf16[4,128,256]{2,1,0:T(8,128)(2,1)S(1)} %get-tuple-element.22.refs_0_), channel_id=1, source_target_pairs={{0,96},{8,104},{16,112},{24,120},{32,0},{40,8},{48,16},{56,24},{64... | collective-permute-start | bytes 786440 | tf_op jit(solution)/shard_map/ppermute | solution.py:44
  26.2 15.4 %collective-permute-start.6 = (bf16[4,128,256]{2,1,0:T(8,128)(2,1)S(1)}, bf16[4,128,256]{2,1,0:T(8,128)(2,1)S(1)}, u32[]{:S(2)}, u32[]{:S(2)}) collective-permute-start(bf16[4,128,256]{2,1,0:T(8,128)(2,1)S(1)} %get-tuple-element.22.refs_0_), channel_id=1, source_target_pairs={{0,32},{8,40},{16,48},{24,56},{32,64},{40,72},{48,80},{56,88},{64,... | collective-permute-start | bytes 786440 | tf_op jit(solution)/shard_map/ppermute | solution.py:44
  27.6 14.0 %collective-permute-start.11 = (bf16[4,128,256]{2,1,0:T(8,128)(2,1)S(1)}, bf16[4,128,256]{2,1,0:T(8,128)(2,1)S(1)}, u32[]{:S(2)}, u32[]{:S(2)}) collective-permute-start(bf16[4,128,256]{2,1,0:T(8,128)(2,1)S(1)} %get-tuple-element.23.refs_4_), channel_id=1, source_target_pairs={{0,16},{8,24},{16,0},{24,8},{32,48},{40,56},{48,32},{56,40},{64,80... | collective-permute-start | bytes 786440 | tf_op jit(solution)/shard_map/ppermute | solution.py:44
  28.8 12.8 %collective-permute-start.10 = (bf16[4,128,256]{2,1,0:T(8,128)(2,1)S(1)}, bf16[4,128,256]{2,1,0:T(8,128)(2,1)S(1)}, u32[]{:S(2)}, u32[]{:S(2)}) collective-permute-start(bf16[4,128,256]{2,1,0:T(8,128)(2,1)S(1)} %get-tuple-element.23.refs_4_), channel_id=1, source_target_pairs={{0,24},{8,0},{16,8},{24,16},{32,56},{40,32},{48,40},{56,48},{64,88... | collective-permute-start | bytes 786440 | tf_op jit(solution)/shard_map/ppermute | solution.py:44
  31.2 10.5 %collective-permute-start.9 = (bf16[4,128,256]{2,1,0:T(8,128)(2,1)S(1)}, bf16[4,128,256]{2,1,0:T(8,128)(2,1)S(1)}, u32[]{:S(2)}, u32[]{:S(2)}) collective-permute-start(bf16[4,128,256]{2,1,0:T(8,128)(2,1)S(1)} %get-tuple-element.23.refs_4_), channel_id=1, source_target_pairs={{0,8},{8,16},{16,24},{24,0},{32,40},{40,48},{48,56},{56,32},{64,72... | collective-permute-start | bytes 786440 | tf_op jit(solution)/shard_map/ppermute | solution.py:44
  47.9 31.8 %collective-permute-start.14 = (bf16[16,64,256]{2,1,0:T(8,128)(2,1)S(1)}, bf16[16,64,256]{2,1,0:T(8,128)(2,1)S(1)}, u32[]{:S(2)}, u32[]{:S(2)}) collective-permute-start(bf16[16,64,256]{2,1,0:T(8,128)(2,1)S(1)} %bitcast.7), channel_id=1, source_target_pairs={{0,4},{1,5},{2,6},{3,7},{4,0},{5,1},{6,2},{7,3},{8,12},{9,13},{10,... | collective-permute-start | bytes 1572872 | tf_op jit(solution)/shard_map/ppermute | solution.py:54
  50.4 29.3 %collective-permute-start.13 = (bf16[16,64,256]{2,1,0:T(8,128)(2,1)S(1)}, bf16[16,64,256]{2,1,0:T(8,128)(2,1)S(1)}, u32[]{:S(2)}, u32[]{:S(2)}) collective-permute-start(bf16[16,64,256]{2,1,0:T(8,128)(2,1)S(1)} %bitcast.8), channel_id=1, source_target_pairs={{0,6},{1,7},{2,0},{3,1},{4,2},{5,3},{6,4},{7,5},{8,14},{9,15},{10,... | collective-permute-start | bytes 1572872 | tf_op jit(solution)/shard_map/ppermute | solution.py:54
  51.3 28.4 %collective-permute-start.12 = (bf16[16,64,256]{2,1,0:T(8,128)(2,1)S(1)}, bf16[16,64,256]{2,1,0:T(8,128)(2,1)S(1)}, u32[]{:S(2)}, u32[]{:S(2)}) collective-permute-start(bf16[16,64,256]{2,1,0:T(8,128)(2,1)S(1)} %bitcast.9), channel_id=1, source_target_pairs={{0,2},{1,3},{2,4},{3,5},{4,6},{5,7},{6,0},{7,1},{8,10},{9,11},{10,... | collective-permute-start | bytes 1572872 | tf_op jit(solution)/shard_map/ppermute | solution.py:54
  52.1 28.8 %collective-permute-start.15 = (bf16[16,64,256]{2,1,0:T(8,128)(2,1)S(1)}, bf16[16,64,256]{2,1,0:T(8,128)(2,1)S(1)}, u32[]{:S(2)}, u32[]{:S(2)}) collective-permute-start(bf16[16,64,256]{2,1,0:T(8,128)(2,1)S(1)} %bitcast.10), channel_id=1, source_target_pairs={{0,1},{1,0},{2,3},{3,2},{4,5},{5,4},{6,7},{7,6},{8,9},{9,8},{10,11... | collective-permute-start | bytes 1572872 | tf_op jit(solution)/shard_map/ppermute | solution.py:60
  79.7 3.7 %copy-start.3 = (bf16[896,896]{1,0:T(8,128)(2,1)S(1)}, bf16[896,896]{1,0:T(8,128)(2,1)}, u32[]{:S(2)}) copy-start(bf16[896,896]{1,0:T(8,128)(2,1)} %refs_13_.3) | copy-start | bytes 4816900
  79.8 2.0 %collective-permute-start.16 = (bf16[16,64,256]{2,1,0:T(8,128)(2,1)S(1)}, bf16[16,64,256]{2,1,0:T(8,128)(2,1)S(1)}, u32[]{:S(2)}, u32[]{:S(2)}) collective-permute-start(bf16[16,64,256]{2,1,0:T(8,128)(2,1)S(1)} %get-tuple-element.24.refs_5_), channel_id=1, source_target_pairs={{0,1},{1,0},{2,3},{3,2},{4,5},{5,4},{6,7},{7,6},{8,9},{9,8},{10,11... | collective-permute-start | bytes 1572872 | tf_op jit(solution)/shard_map/ppermute | solution.py:60
  80.2 2.3 %collective-permute-start.17 = (bf16[16,64,256]{2,1,0:T(8,128)(2,1)S(1)}, bf16[16,64,256]{2,1,0:T(8,128)(2,1)S(1)}, u32[]{:S(2)}, u32[]{:S(2)}) collective-permute-start(bf16[16,64,256]{2,1,0:T(8,128)(2,1)S(1)} %get-tuple-element.25.refs_6_), channel_id=1, source_target_pairs={{0,1},{1,0},{2,3},{3,2},{4,5},{5,4},{6,7},{7,6},{8,9},{9,8},{10,11... | collective-permute-start | bytes 1572872 | tf_op jit(solution)/shard_map/ppermute | solution.py:60
  80.4 2.9 %collective-permute-start.18 = (bf16[16,64,256]{2,1,0:T(8,128)(2,1)S(1)}, bf16[16,64,256]{2,1,0:T(8,128)(2,1)S(1)}, u32[]{:S(2)}, u32[]{:S(2)}) collective-permute-start(bf16[16,64,256]{2,1,0:T(8,128)(2,1)S(1)} %get-tuple-element.26.refs_7_), channel_id=1, source_target_pairs={{0,1},{1,0},{2,3},{3,2},{4,5},{5,4},{6,7},{7,6},{8,9},{9,8},{10,11... | collective-permute-start | bytes 1572872 | tf_op jit(solution)/shard_map/ppermute | solution.py:60
  80.8 2.5 %copy-start.6 = (bf16[16,64,256]{2,1,0:T(8,128)(2,1)}, bf16[16,64,256]{2,1,0:T(8,128)(2,1)S(1)}, u32[]{:S(2)}) copy-start(bf16[16,64,256]{2,1,0:T(8,128)(2,1)S(1)} %collective-permute-done.15.refs_8_) | copy-start | bytes 1572868
  90.6 8.3 %copy-start.2 = (bf16[512,4096]{1,0:T(8,128)(2,1)S(1)}, bf16[512,4096]{1,0:T(8,128)(2,1)}, u32[]{:S(2)}) copy-start(bf16[512,4096]{1,0:T(8,128)(2,1)} %refs_6_.3) | copy-start | bytes 12582916
  90.7 8.3 %copy-start.4 = (bf16[896,512]{1,0:T(8,128)(2,1)S(1)}, bf16[896,512]{1,0:T(8,128)(2,1)}, u32[]{:S(2)}) copy-start(bf16[896,512]{1,0:T(8,128)(2,1)} %refs_4_.7) | copy-start | bytes 2752516
  90.7 8.3 %copy-start.5 = (bf16[896,512]{1,0:T(8,128)(2,1)S(1)}, bf16[896,512]{1,0:T(8,128)(2,1)}, u32[]{:S(2)}) copy-start(bf16[896,512]{1,0:T(8,128)(2,1)} %refs_5_.5) | copy-start | bytes 2752516
  90.7 8.2 %collective-permute-start.22 = (bf16[8,128,896]{2,1,0:T(8,128)(2,1)S(1)}, bf16[8,128,896]{2,1,0:T(8,128)(2,1)S(1)}, u32[]{:S(2)}, u32[]{:S(2)}) collective-permute-start(bf16[8,128,896]{2,1,0:T(8,128)(2,1)S(1)} %encode.2.refs_14_.refs_0_), channel_id=1, source_target_pairs={{0,1},{1,0},{2,3},{3,2},{4,5},{5,4},{6,7},{7,6},{8,9},{9,8},{10,11... | collective-permute-start | bytes 5505032 | tf_op jit(solution)/shard_map/ppermute | solution.py:60
  109.4 8.2 %collective-permute-start.19 = (bf16[8,128,896]{2,1,0:T(8,128)(2,1)S(1)}, bf16[8,128,896]{2,1,0:T(8,128)(2,1)S(1)}, u32[]{:S(2)}, u32[]{:S(2)}) collective-permute-start(bf16[8,128,896]{2,1,0:T(8,128)(2,1)S(1)} %encode.3.refs_6_.refs_1_), channel_id=1, source_target_pairs={{0,1},{1,0},{2,3},{3,2},{4,5},{5,4},{6,7},{7,6},{8,9},{9,8},{10,11... | collective-permute-start | bytes 5505032 | tf_op jit(solution)/shard_map/ppermute | solution.py:60
  109.6 15.1 %collective-permute-start.21 = (bf16[1,128,896]{2,1,0:T(8,128)(2,1)S(1)}, bf16[1,128,896]{2,1,0:T(8,128)(2,1)S(1)}, u32[]{:S(2)}, u32[]{:S(2)}) collective-permute-start(bf16[1,128,896]{2,1,0:T(8,128)(2,1)S(1)} %slice.19), channel_id=1, source_target_pairs={{0,9},{1,8},{2,11},{3,10},{4,13},{5,12},{6,15},{7,14},{8,17},{9,16... | collective-permute-start | bytes 688136 | tf_op jit(solution)/shard_map/ppermute | solution.py:518
  113.8 12.4 %collective-permute-start.20 = (bf16[1,128,896]{2,1,0:T(8,128)(2,1)S(1)}, bf16[1,128,896]{2,1,0:T(8,128)(2,1)S(1)}, u32[]{:S(2)}, u32[]{:S(2)}) collective-permute-start(bf16[1,128,896]{2,1,0:T(8,128)(2,1)S(1)} %slice.19), channel_id=1, source_target_pairs={{0,8},{1,9},{2,10},{3,11},{4,12},{5,13},{6,14},{7,15},{8,16},{9,17... | collective-permute-start | bytes 688136 | tf_op jit(solution)/shard_map/ppermute | solution.py:518
  124.1 9.3 %collective-permute-start.24 = (bf16[4,256,512]{2,1,0:T(8,128)(2,1)S(1)}, bf16[4,256,512]{2,1,0:T(8,128)(2,1)S(1)}, u32[]{:S(2)}, u32[]{:S(2)}) collective-permute-start(bf16[4,256,512]{2,1,0:T(8,128)(2,1)S(1)} %get-tuple-element.30), channel_id=1, source_target_pairs={{0,1},{1,0},{2,3},{3,2},{4,5},{5,4},{6,7},{7,6},{8,9},{9,8},{10,11... | collective-permute-start | bytes 3145736 | tf_op jit(solution)/shard_map/ppermute | solution.py:60
  132.6 3.0 %collective-permute-start.23 = (bf16[4,256,512]{2,1,0:T(8,128)(2,1)S(1)}, bf16[4,256,512]{2,1,0:T(8,128)(2,1)S(1)}, u32[]{:S(2)}, u32[]{:S(2)}) collective-permute-start(bf16[4,256,512]{2,1,0:T(8,128)(2,1)S(1)} %get-tuple-element.29), channel_id=1, source_target_pairs={{0,1},{1,0},{2,3},{3,2},{4,5},{5,4},{6,7},{7,6},{8,9},{9,8},{10,11... | collective-permute-start | bytes 3145736 | tf_op jit(solution)/shard_map/ppermute | solution.py:60
  135.9 10.8 %collective-permute-start.25 = (bf16[256,512]{1,0:T(8,128)(2,1)S(1)}, bf16[256,512]{1,0:T(8,128)(2,1)S(1)}, u32[]{:S(2)}, u32[]{:S(2)}) collective-permute-start(bf16[256,512]{1,0:T(8,128)(2,1)S(1)} %get-tuple-element.35), channel_id=1, source_target_pairs={{0,6},{1,7},{2,0},{3,1},{4,2},{5,3},{6,4},{7,5},{8,14},{9,15},{10,... | collective-permute-start | bytes 786440 | tf_op jit(solution)/shard_map/ppermute | solution.py:91
  136.9 11.9 %collective-permute-start.26 = (bf16[256,512]{1,0:T(8,128)(2,1)S(1)}, bf16[256,512]{1,0:T(8,128)(2,1)S(1)}, u32[]{:S(2)}, u32[]{:S(2)}) collective-permute-start(bf16[256,512]{1,0:T(8,128)(2,1)S(1)} %get-tuple-element.36), channel_id=1, source_target_pairs={{0,2},{1,3},{2,4},{3,5},{4,6},{5,7},{6,0},{7,1},{8,10},{9,11},{10,... | collective-permute-start | bytes 786440 | tf_op jit(solution)/shard_map/ppermute | solution.py:91
  137.4 18.4 %collective-permute-start.27 = (bf16[256,512]{1,0:T(8,128)(2,1)S(1)}, bf16[256,512]{1,0:T(8,128)(2,1)S(1)}, u32[]{:S(2)}, u32[]{:S(2)}) collective-permute-start(bf16[256,512]{1,0:T(8,128)(2,1)S(1)} %get-tuple-element.37), channel_id=1, source_target_pairs={{0,4},{1,5},{2,6},{3,7},{4,0},{5,1},{6,2},{7,3},{8,12},{9,13},{10,... | collective-permute-start | bytes 786440 | tf_op jit(solution)/shard_map/ppermute | solution.py:91
  139.2 21.2 %collective-permute-start.28 = (bf16[256,512]{1,0:T(8,128)(2,1)S(1)}, bf16[256,512]{1,0:T(8,128)(2,1)S(1)}, u32[]{:S(2)}, u32[]{:S(2)}) collective-permute-start(bf16[256,512]{1,0:T(8,128)(2,1)S(1)} %get-tuple-element.31.refs_0_), channel_id=1, source_target_pairs={{0,6},{1,7},{2,0},{3,1},{4,2},{5,3},{6,4},{7,5},{8,14},{9,15},{10,... | collective-permute-start | bytes 786440 | tf_op jit(solution)/shard_map/ppermute | solution.py:91
  141.2 26.8 %collective-permute-start.29 = (bf16[256,512]{1,0:T(8,128)(2,1)S(1)}, bf16[256,512]{1,0:T(8,128)(2,1)S(1)}, u32[]{:S(2)}, u32[]{:S(2)}) collective-permute-start(bf16[256,512]{1,0:T(8,128)(2,1)S(1)} %get-tuple-element.32.refs_1_), channel_id=1, source_target_pairs={{0,2},{1,3},{2,4},{3,5},{4,6},{5,7},{6,0},{7,1},{8,10},{9,11},{10,... | collective-permute-start | bytes 786440 | tf_op jit(solution)/shard_map/ppermute | solution.py:91
  146.7 21.2 %collective-permute-start.30 = (bf16[256,512]{1,0:T(8,128)(2,1)S(1)}, bf16[256,512]{1,0:T(8,128)(2,1)S(1)}, u32[]{:S(2)}, u32[]{:S(2)}) collective-permute-start(bf16[256,512]{1,0:T(8,128)(2,1)S(1)} %get-tuple-element.33.refs_2_), channel_id=1, source_target_pairs={{0,4},{1,5},{2,6},{3,7},{4,0},{5,1},{6,2},{7,3},{8,12},{9,13},{10,... | collective-permute-start | bytes 786440 | tf_op jit(solution)/shard_map/ppermute | solution.py:91
  155.8 14.4 %copy-start.1 = (bf16[8,128,896]{2,1,0:T(8,128)(2,1)S(1)}, bf16[8,128,896]{2,1,0:T(8,128)(2,1)}, u32[]{:S(2)}) copy-start(bf16[8,128,896]{2,1,0:T(8,128)(2,1)} %param.13) | copy-start | bytes 5505028
Sparse Core Ops, SparseCore 0:
  11.1 60.9 all-gather.2
  109.5 45.3 reduce-scatter.1
